TPU v7x, 32 devices: a whole 2x2x4 slice. The times are simulated.
32 devices in a mesh: dp: 4 (over y, x), tm: 2 (over core), space: 4 (over z).
Axes of the slice: x: 2, y: 2, z: 4, core: 2. Of those that a mesh axis runs over, the one named last changes fastest.
Arguments:
- video: bfloat16 [4, 8, 64, 128, 128], P('dp', 'tm', 'space'), may hold values from -6 to 6
- lengths: int32 [4], P('dp'), may hold values from 2 to 8
- norm_gain: float32 [128], replicated, may hold values from 0.25 to 1.75
- norm_shift: float32 [128], replicated, may hold values from -3 to 3
- kernel: bfloat16 [3, 3, 3, 128, 128], replicated, may hold values from -0.109375 to 0.109375
- conv_bias: float32 [128], replicated, may hold values from -3 to 3
- cotangent: bfloat16 [4, 8, 64, 128, 128], P('dp', 'tm', 'space'), may hold values from -0.01171875 to 0.01171875
Outputs:
- output: bfloat16 [4, 8, 64, 128, 128], P('dp', 'tm', 'space')
- grad_kernel: float32 [3, 3, 3, 128, 128], replicated
- grad_bias: float32 [128], replicated
All inputs are finite; a program needn't handle non-finite values.
Results may differ from a plain program's by a relative error of at most 0.0032.
Values may be sent and summed in bfloat16 or wider, within the bound.
No kernel may reach another device: no remote copies, remote signals or barrier semaphores. Data moves between devices by JAX's collectives and lax.ppermute only.
A program may use at most 128 MiB of HBM per device.

v0:
```python
import jax
import jax.numpy as jnp
from jax import lax
from jax.sharding import PartitionSpec as P

GROUPS = 32


def shifted(array, axis, by):
    length = lax.axis_size(axis)
    pairs = [(i, i + by) for i in range(length) if 0 <= i + by < length]
    return lax.ppermute(array, axis, pairs)


def padded_2(block, sides, width):
    for axis, dim in sides:
        count = lax.axis_size(axis)
        forward = [(i, i + 1) for i in range(count - 1)]
        backward = [(target, source) for source, target in forward]
        low = lax.ppermute(
            lax.slice_in_dim(block, block.shape[dim] - width, None, axis=dim), axis, forward
        )
        high = lax.ppermute(lax.slice_in_dim(block, 0, width, axis=dim), axis, backward)
        block = jnp.concatenate([low, block, high], axis=dim)
    return block


def body(video, lengths, norm_gain, norm_shift, kernel, conv_bias, cotangent):
    frames = video.shape[1]
    rows = video.shape[2]
    cols = video.shape[3]
    chans = video.shape[4]
    per = chans // GROUPS
    first = lax.axis_index("tm") * frames
    valid = (first + jnp.arange(frames, dtype=jnp.int32) < lengths[0]).astype(jnp.float32)
    mask = valid[:, None, None, None]
    grouped = video[0].reshape(frames, rows, cols, GROUPS, per)
    gmask = valid[:, None, None, None, None]
    count = lengths[0].astype(jnp.float32) * (rows * lax.axis_size("space")) * cols * per
    local_sum = jnp.sum(grouped * gmask, axis=(0, 1, 2, 4), dtype=jnp.float32)
    mean = lax.psum(local_sum, ("tm", "space")) / count
    spread = (grouped.astype(jnp.float32) - mean[:, None]) * gmask
    variance = lax.psum(jnp.sum(spread * spread, axis=(0, 1, 2, 4)), ("tm", "space")) / count
    normed = (grouped.astype(jnp.float32) - mean[:, None]) * lax.rsqrt(variance + 1e-05)[:, None]
    normed = normed.reshape(frames, rows, cols, chans) * norm_gain + norm_shift
    activated = (jax.nn.silu(normed) * mask).astype(jnp.bfloat16)[None]
    earlier = shifted(activated[:, frames - 2 :], "tm", 1)
    timed = jnp.concatenate([earlier, activated], axis=1)
    extended = padded_2(timed, (("space", 2),), 1)
    padded = jnp.pad(extended[0], ((0, 0), (0, 0), (1, 1), (0, 0)))
    masked = (cotangent[0].astype(jnp.float32) * mask).astype(jnp.bfloat16)
    stacked = jnp.concatenate(
        [
            jnp.pad(masked, ((0, 0), (0, 0), (shift_cols, 2 - shift_cols), (0, 0)))
            for shift_cols in range(3)
        ],
        axis=-1,
    )
    stacked = stacked.reshape(-1, 3 * chans)
    wide_rows = frames * rows * (cols + 2)
    partial_value = jnp.zeros((wide_rows, 3 * chans), jnp.float32)
    grads = []
    for kt in range(3):
        for ky in range(3):
            band = padded[kt : kt + frames, ky : ky + rows].reshape(wide_rows, chans)
            taps = jnp.transpose(kernel[kt, ky], (1, 0, 2)).reshape(chans, 3 * chans)
            partial_value = partial_value + jnp.dot(band, taps, preferred_element_type=jnp.float32)
            product = lax.dot_general(
                band, stacked, (((0,), (0,)), ((), ())), preferred_element_type=jnp.float32
            )
            grads.append(
                jnp.transpose(product.reshape(chans, 3, chans), (1, 0, 2)).reshape(3 * chans, chans)
            )
    partial_value = partial_value.reshape(frames, rows, cols + 2, 3 * chans)
    conv = (
        partial_value[:, :, 0:cols, 0:chans]
        + partial_value[:, :, 1 : cols + 1, chans : 2 * chans]
        + partial_value[:, :, 2 : cols + 2, 2 * chans : 3 * chans]
    )
    output = ((video[0].astype(jnp.float32) + conv + conv_bias) * mask).astype(jnp.bfloat16)[None]
    local_kernel = jnp.concatenate(grads, axis=0)
    local_bias = jnp.sum(masked.reshape(-1, chans).astype(jnp.float32), axis=0)
    summed, grad_bias = lax.psum((local_kernel, local_bias), ("dp", "tm", "space"))
    return (output, summed.reshape(3, 3, 3, chans, chans), grad_bias)


def solution(mesh):
    return jax.shard_map(
        body,
        mesh=mesh,
        in_specs=(
            P("dp", "tm", "space", None, None),
            P("dp"),
            P(),
            P(),
            P(),
            P(),
            P("dp", "tm", "space", None, None),
        ),
        out_specs=(P("dp", "tm", "space", None, None), P(), P()),
        check_vma=False,
    )
```

profile of v0, /device:TPU:0, one launch (start us, length us, event | category | flops | bytes accessed | tf_op | source)
XLA Modules:
  0.0 367.2 jit_solution(12672691524185307099)
XLA Ops:
  8.0 2.8 fusion.26
  11.1 18.5 %psum.28 = f32[32]{0:T(128)S(1)} all-reduce(f32[32]{0:T(128)S(1)} %reduce_sum.36), channel_id=1, replica_groups=mesh['dp'=4,'tm'=2,'space'=4] {'tm','space'}, use_global_device_ids=true, to_apply=%region_2.0 | all-reduce | flops 32 | bytes 256 | tf_op jit(solution)/shard_map/psum | solution.py:41
  29.8 3.3 convert_reduce_fusion
  33.3 13.7 %psum.29 = f32[32]{0:T(128)S(1)} all-reduce(f32[32]{0:T(128)S(1)} %reduce_sum.46), channel_id=1, replica_groups=mesh['dp'=4,'tm'=2,'space'=4] {'tm','space'}, use_global_device_ids=true, to_apply=%region_5.6 | all-reduce | flops 32 | bytes 256 | tf_op jit(solution)/shard_map/psum | solution.py:43
  47.2 1.6 fusion.18
  49.0 2.6 collective-permute-start
  51.6 2.2 collective-permute-done
  54.6 3.9 %collective-permute-start.1 = (bf16[1,6,1,128,128]{4,3,2,1,0:T(8,128)(2,1)}, bf16[1,6,1,128,128]{4,3,2,1,0:T(8,128)(2,1)}, u32[]{:S(2)}, u32[]{:S(2)}) collective-permute-start(bf16[1,6,1,128,128]{4,3,2,1,0:T(8,128)(2,1)} %get-tuple-element.14), channel_id=1, source_target_pairs={{0,1},{1,2},{2,3},{4,5},{5,6},{6,7},{8,9},{9,10},{10,11},{12,13},{... | collective-permute-start | bytes 589832 | tf_op jit(solution)/shard_map/ppermute | solution.py:20
  60.9 1.6 copy.65
  64.2 1.6 copy.63
  69.0 1.6 copy.60
  71.7 2.0 maximum_bitcast_fusion
  73.7 10.9 %pad_slice_fusion = (bf16[4,16,130,128]{3,2,1,0:T(8,128)(2,1)}, bf16[4,16,130,128]{3,2,1,0:T(8,128)(2,1)}, bf16[4,16,130,128]{3,2,1,0:T(8,128)(2,1)}, bf16[4,16,...) fusion(bf16[6,18,128,128]{3,2,1,0:T(8,128)(2,1)S(1)} %maximum_b, ...), kind=kLoop, calls=%fused_computation.67 | loop fusion | bytes 22708224 | tf_op jit(solution)/shard_map/slice | solution.py:65
  84.6 4.1 %reshape.166 = bf16[8320,128]{1,0:T(8,128)(2,1)} reshape(bf16[4,16,130,128]{3,2,1,0:T(8,128)(2,1)} %get-tuple-element.5) | data formatting | bytes 4259840 | tf_op jit(solution)/shard_map/reshape | solution.py:65
  88.7 4.0 %reshape.152 = bf16[8320,128]{1,0:T(8,128)(2,1)} reshape(bf16[4,16,130,128]{3,2,1,0:T(8,128)(2,1)} %get-tuple-element.6) | data formatting | bytes 4259840 | tf_op jit(solution)/shard_map/reshape | solution.py:65
  92.7 4.0 %reshape.154 = bf16[8320,128]{1,0:T(8,128)(2,1)} reshape(bf16[4,16,130,128]{3,2,1,0:T(8,128)(2,1)} %get-tuple-element.7) | data formatting | bytes 4259840 | tf_op jit(solution)/shard_map/reshape | solution.py:65
  96.8 4.0 %reshape.156 = bf16[8320,128]{1,0:T(8,128)(2,1)} reshape(bf16[4,16,130,128]{3,2,1,0:T(8,128)(2,1)} %get-tuple-element.8) | data formatting | bytes 4259840 | tf_op jit(solution)/shard_map/reshape | solution.py:65
  100.8 4.0 %reshape.158 = bf16[8320,128]{1,0:T(8,128)(2,1)} reshape(bf16[4,16,130,128]{3,2,1,0:T(8,128)(2,1)} %get-tuple-element.9) | data formatting | bytes 4259840 | tf_op jit(solution)/shard_map/reshape | solution.py:65
  104.9 4.1 %reshape.160 = bf16[8320,128]{1,0:T(8,128)(2,1)} reshape(bf16[4,16,130,128]{3,2,1,0:T(8,128)(2,1)} %get-tuple-element.10) | data formatting | bytes 4259840 | tf_op jit(solution)/shard_map/reshape | solution.py:65
  109.0 4.0 %reshape.162 = bf16[8320,128]{1,0:T(8,128)(2,1)} reshape(bf16[4,16,130,128]{3,2,1,0:T(8,128)(2,1)} %get-tuple-element.11) | data formatting | bytes 4259840 | tf_op jit(solution)/shard_map/reshape | solution.py:65
  113.0 4.0 %reshape.164 = bf16[8320,128]{1,0:T(8,128)(2,1)} reshape(bf16[4,16,130,128]{3,2,1,0:T(8,128)(2,1)} %get-tuple-element.12) | data formatting | bytes 4259840 | tf_op jit(solution)/shard_map/reshape | solution.py:65
  117.0 4.4 %reshape.150 = bf16[8320,128]{1,0:T(8,128)(2,1)} reshape(bf16[4,16,130,128]{3,2,1,0:T(8,128)(2,1)} %get-tuple-element.13) | data formatting | bytes 4259840 | tf_op jit(solution)/shard_map/reshape | solution.py:65
  121.5 3.4 fusion.47
  124.9 3.6 convolution_add_fusion.7
  128.5 3.6 convolution_add_fusion.6
  132.1 3.6 convolution_add_fusion.5
  135.8 3.6 convolution_add_fusion.4
  139.4 3.6 convolution_add_fusion.3
  143.0 3.6 convolution_add_fusion.2
  146.6 3.8 %convolution_add_fusion.1 = f32[8320,384]{1,0:T(8,128)S(1)} fusion(f32[8320,384]{1,0:T(8,128)S(1)} %convolution_add_fusion.2, bf16[8320,128]{1,0:T(8,128)(2,1)} %reshape.164, bf16[128,384]{0,1:T(8,128)(2,1)S(1)} %bitcast.176), kind=kOutput, calls=%fused_computation.3 | convolution fusion | flops 821084160 | bytes 27787264 | tf_op jit(solution)/shard_map/dot_general | solution.py:67
  150.4 8.2 %convolution_add_fusion = f32[8320,384]{1,0:T(8,128)} fusion(f32[8320,384]{1,0:T(8,128)S(1)} %convolution_add_fusion.1, bf16[8320,128]{1,0:T(8,128)(2,1)} %reshape.166, bf16[128,384]{0,1:T(8,128)(2,1)S(1)} %bitcast.175), kind=kOutput, calls=%fused_computation.2 | convolution fusion | flops 821084160 | bytes 27787264 | tf_op jit(solution)/shard_map/dot_general | solution.py:67
  158.6 12.0 %reshape.168 = f32[4,16,130,384]{3,2,1,0:T(8,128)} reshape(f32[8320,384]{1,0:T(8,128)} %convolution_add_fusion) | data formatting | bytes 25559040 | tf_op jit(solution)/shard_map/reshape | solution.py:74
  170.6 7.8 %fusion.20 = (bf16[4,16,128,128]{3,2,1,0:T(8,128)(2,1)S(1)}, bf16[1,4,16,128,128]{4,3,2,1,0:T(8,128)(2,1)}) fusion(bf16[1,4,16,128,128]{4,3,2,1,0:T(8,128)(2,1)} %param.13, f32[4]{0:T(128)S(1)} %compare_convert_fusion, f32[128]{0:T(128)S(1)} %copy-done.23, f32[4,16,130,384]{3,2,1,0:T(8,128)} %reshape.168, bf16[1,4,16,128,128]{4,3,2,1,0:T(8,128)(2,1)S(1)} %copy-done.1), kind=kLoop, calls=%fused_computation.37 | loop fusion | flops 10485760 | bytes 20972048 | tf_op jit(solution)/shard_map/convert_element_type | solution.py:51
  178.4 3.9 %fusion.5 = bf16[4,16,130,384]{3,2,1,0:T(8,128)(2,1)} fusion(bf16[4,16,128,128]{3,2,1,0:T(8,128)(2,1)S(1)} %get-tuple-element.25), kind=kLoop, calls=%fused_computation.17 | loop fusion | flops 44728320 | bytes 8486912 | tf_op jit(solution)/shard_map/concatenate | solution.py:52
  182.4 8.5 %reshape.169 = bf16[8320,384]{1,0:T(8,128)(2,1)} reshape(bf16[4,16,130,384]{3,2,1,0:T(8,128)(2,1)} %fusion.5) | data formatting | bytes 12779520 | tf_op jit(solution)/shard_map/reshape | solution.py:59
  190.9 9.4 %copy.29 = bf16[384,8320]{1,0:T(8,128)(2,1)} copy(bf16[384,8320]{0,1:T(8,128)(2,1)} %bitcast.163) | data formatting | bytes 12779520 | tf_op jit(solution)/shard_map/dot_general | solution.py:68
  200.3 4.9 %fusion.27 = f32[128,3,128]{2,0,1:T(8,128)S(1)} fusion(bf16[3,128,8320]{2,1,0:T(8,128)(2,1)} %bitcast.154, bf16[8320,128]{1,0:T(8,128)(2,1)S(1)} %copy-done.5), kind=kOutput, calls=%fused_computation.48 | convolution fusion | flops 817889280 | bytes 8716288 | tf_op jit(solution)/shard_map/dot_general | solution.py:68
  205.6 2.0 fusion.29
  207.6 2.0 fusion.31
  209.6 2.0 fusion.33
  211.6 2.0 fusion.35
  213.6 2.0 fusion.37
  215.6 2.0 fusion.39
  217.7 2.0 fusion.41
  219.7 2.0 fusion.43
  223.1 41.4 %psum.31 = f32[128]{0:T(128)} all-reduce(f32[128]{0:T(128)S(1)} %copy-done.24), channel_id=1, replica_groups=mesh['dp'=4,'tm'=2,'space'=4] {'dp','tm','space'}, use_global_device_ids=true, to_apply=%region_8.9 | all-reduce | flops 128 | bytes 1024 | tf_op jit(solution)/shard_map/psum | solution.py:83
  264.5 92.8 %all-reduce.6.cloned.1.call-done = f32[3,3,3,128,128]{4,3,2,1,0:T(8,128)} async-done(((f32[3,3,3,128,128]{4,3,2,1,0:T(8,128)}), f32[3,3,3,128,128]{4,3,2,1,0:T(8,128)}) %all-reduce.6.cloned.1.call-update) | async-done | bytes 1769488 | tf_op jit(solution)/shard_map/psum | solution.py:83
  357.3 2.9 copy.76
  (84 shorter events, 11.7 us)
Async XLA Ops:
  7.2 22.6 %copy-start.1 = (bf16[1,4,16,128,128]{4,3,2,1,0:T(8,128)(2,1)S(1)}, bf16[1,4,16,128,128]{4,3,2,1,0:T(8,128)(2,1)}, u32[]{:S(2)}) copy-start(bf16[1,4,16,128,128]{4,3,2,1,0:T(8,128)(2,1)} %param.7) | copy-start | bytes 6291460
  7.2 40.0 %copy-start.21 = (f32[128]{0:T(128)S(1)}, f32[128]{0:T(128)}, u32[]{:S(2)}) copy-start(f32[128]{0:T(128)} %param.10) | copy-start | bytes 1540
  7.2 40.0 %copy-start.22 = (f32[128]{0:T(128)S(1)}, f32[128]{0:T(128)}, u32[]{:S(2)}) copy-start(f32[128]{0:T(128)} %param.9) | copy-start | bytes 1540
  7.2 350.1 %all-reduce.6.cloned.1.call-start = ((), (), s32[]{:S(2)}) async-start(), calls=%async_computation | async-start | bytes 3538944 | tf_op jit(solution)/shard_map/psum | solution.py:83
  48.9 12.0 %copy-start.10 = (bf16[1,4,16,128,128]{4,3,2,1,0:T(8,128)(2,1)}, bf16[1,4,16,128,128]{4,3,2,1,0:T(8,128)(2,1)S(1)}, u32[]{:S(2)}) copy-start(bf16[1,4,16,128,128]{4,3,2,1,0:T(8,128)(2,1)S(1)} %fusion.18) | copy-start | bytes 6291460
  48.9 11.1 %copy-start.13 = (bf16[3,3,3,128,128]{4,3,2,1,0:T(8,128)(2,1)S(1)}, bf16[3,3,3,128,128]{4,3,2,1,0:T(8,128)(2,1)}, u32[]{:S(2)}) copy-start(bf16[3,3,3,128,128]{4,3,2,1,0:T(8,128)(2,1)} %param.11) | copy-start | bytes 2654212
  49.0 4.8 %collective-permute-start = (bf16[1,2,16,128,128]{4,3,2,1,0:T(8,128)(2,1)S(1)}, bf16[1,2,16,128,128]{4,3,2,1,0:T(8,128)(2,1)S(1)}, u32[]{:S(2)}, u32[]{:S(2)}) collective-permute-start(bf16[1,2,16,128,128]{4,3,2,1,0:T(8,128)(2,1)S(1)} %slice.96), channel_id=1, source_target_pairs={{0,4},{1,5},{2,6},{3,7},{8,12},{9,13},{10,14},{11,15},{16,20},{17,... | collective-permute-start | bytes 3145736 | tf_op jit(solution)/shard_map/ppermute | solution.py:12
  54.6 17.1 %collective-permute-start.1 = (bf16[1,6,1,128,128]{4,3,2,1,0:T(8,128)(2,1)}, bf16[1,6,1,128,128]{4,3,2,1,0:T(8,128)(2,1)}, u32[]{:S(2)}, u32[]{:S(2)}) collective-permute-start(bf16[1,6,1,128,128]{4,3,2,1,0:T(8,128)(2,1)} %get-tuple-element.14), channel_id=1, source_target_pairs={{0,1},{1,2},{2,3},{4,5},{5,6},{6,7},{8,9},{9,10},{10,11},{12,13},{... | collective-permute-start | bytes 589832 | tf_op jit(solution)/shard_map/ppermute | solution.py:20
  58.5 13.2 %collective-permute-start.2 = (bf16[1,6,1,128,128]{4,3,2,1,0:T(8,128)(2,1)}, bf16[1,6,1,128,128]{4,3,2,1,0:T(8,128)(2,1)}, u32[]{:S(2)}, u32[]{:S(2)}) collective-permute-start(bf16[1,6,1,128,128]{4,3,2,1,0:T(8,128)(2,1)} %get-tuple-element.15), channel_id=1, source_target_pairs={{1,0},{2,1},{3,2},{5,4},{6,5},{7,6},{9,8},{10,9},{11,10},{13,12},{... | collective-permute-start | bytes 589832 | tf_op jit(solution)/shard_map/ppermute | solution.py:23
  124.9 3.6 copy-start.20
  128.5 3.6 copy-start.19
  132.1 3.6 copy-start.18
  135.8 3.6 copy-start.17
  139.4 3.6 copy-start.16
  143.0 3.6 copy-start.15
  146.6 3.8 %copy-start.14 = (bf16[1,1,3,128,128]{3,4,2,1,0:T(8,128)(2,1)S(1)}, bf16[1,1,3,128,128]{3,4,2,1,0:T(8,128)(2,1)}, u32[]{:S(2)}) copy-start(bf16[1,1,3,128,128]{3,4,2,1,0:T(8,128)(2,1)} %copy.65) | copy-start | bytes 294916
  158.6 12.0 %copy-start.23 = (f32[128]{0:T(128)S(1)}, f32[128]{0:T(128)}, u32[]{:S(2)}) copy-start(f32[128]{0:T(128)} %param.12) | copy-start | bytes 1540
  190.9 9.4 %copy-start.5 = (bf16[8320,128]{1,0:T(8,128)(2,1)S(1)}, bf16[8320,128]{1,0:T(8,128)(2,1)}, u32[]{:S(2)}) copy-start(bf16[8320,128]{1,0:T(8,128)(2,1)} %reshape.166) | copy-start | bytes 6389764
  200.3 4.9 %copy-start = (bf16[384,8320]{1,0:T(8,128)(2,1)S(1)}, bf16[384,8320]{1,0:T(8,128)(2,1)}, u32[]{:S(2)}) copy-start(bf16[384,8320]{1,0:T(8,128)(2,1)} %copy.29) | copy-start | bytes 19169284
  200.3 5.3 %copy-start.9 = (bf16[8320,128]{1,0:T(8,128)(2,1)S(1)}, bf16[8320,128]{1,0:T(8,128)(2,1)}, u32[]{:S(2)}) copy-start(bf16[8320,128]{1,0:T(8,128)(2,1)} %reshape.164) | copy-start | bytes 6389764
  205.6 2.0 copy-start.8
  207.6 2.0 copy-start.7
  209.6 2.0 copy-start.6
  211.6 2.0 copy-start.4
  213.6 2.0 copy-start.3
  215.6 2.0 copy-start.2
  217.6 2.0 copy-start.11
  221.6 1.5 copy-start.24
  221.9 1.2 copy-start.12
Sparse Core Ops, SparseCore 0:
  223.2 134.0 all-reduce.5
where the time goes:
time: 373 us; the launch traced here: 367 us
  waiting for transfers between devices  95 us (25%)
  local copies, waits for them, and re-layouts  94.6 us (25%)
  blocking collectives  73.7 us (20%)
  matrix products  57.7 us (15%)
  other arithmetic  22.5 us (6%)
  between operations  15.6 us (4%)
  starting transfers between devices  8.1 us (2%)
    psum x1, waiting for transfers between devices, body(): lax.psum((local_kernel, local_bias), ('dp', 'tm', 'space'))  92.8 us
    psum x1, blocking collectives, body(): lax.psum((local_kernel, local_bias), ('dp', 'tm', 'space'))  41.4 us
    dot_general x9, matrix products, body(): jnp.dot(band, taps, preferred_element_type=jnp.float32)  36.9 us
    reshape x9, local copies, waits for them, and re-layouts, body(): band = padded[kt:kt + frames, ky:ky + rows].reshape(wide_rows, chans)  36.8 us
    dot_general x9, matrix products, body(): lax.dot_general(band, stacked, (((0,), (0,)), ((), ())), preferred_elemen...  20.8 us
    psum x1, blocking collectives, body(): mean = lax.psum(local_sum, ('tm', 'space')) / count  18.5 us
    unnamed x68, local copies, waits for them, and re-layouts  15.4 us
    psum x1, blocking collectives, body(): lax.psum(jnp.sum(spread * spread, axis=(0, 1, 2, 4)), ('tm', 'space'))  13.7 us
  transfers between devices with their start and end apart: 4, of which 2 were waited for; matrix products, arithmetic and copies ran while one was open for 3% of the time, Pallas kernels for 0%

commit v1 on v0

v1 whole, which is shorter than its diff:
```python
import functools

import jax
import jax.numpy as jnp
from jax import lax
from jax.experimental import pallas as pl
from jax.experimental.pallas import tpu as pltpu
from jax.sharding import PartitionSpec as P

GROUPS = 32
TILE = 16
F32 = jnp.float32
BF16 = jnp.bfloat16
VMEM = pl.BlockSpec(memory_space=pltpu.VMEM)
SMEM = pl.BlockSpec(memory_space=pltpu.SMEM)


def params(mib):
    return pltpu.CompilerParams(vmem_limit_bytes=mib * 1024 * 1024)


def swap(array, axis, by):
    length = lax.axis_size(axis)
    assert length & (length - 1) == 0
    return lax.ppermute(array, axis, [(i, i ^ by) for i in range(length)])


def shifted(array, axis, by):
    length = lax.axis_size(axis)
    return lax.ppermute(array, axis, [(i, i + by) for i in range(length) if 0 <= i + by < length])


def group_sum(row, per):
    value = jnp.broadcast_to(row, (8, row.shape[1]))
    lane = lax.broadcasted_iota(jnp.int32, value.shape, 1)
    size = value.shape[1]
    step = 1
    while step < per:
        up = pltpu.roll(value, size - step, 1)
        down = pltpu.roll(value, step, 1)
        value = value + jnp.where((lane & step) == 0, up, down)
        step *= 2
    return value[0:1]


def merged(parts):
    count = sum(part[0:1] for part in parts)
    total = sum(part[1:2] for part in parts)
    mean = total / jnp.maximum(count, 1.0)
    squares = jnp.zeros_like(mean)
    for part in parts:
        away = part[1:2] / jnp.maximum(part[0:1], 1.0) - mean
        squares = squares + (part[2:3] + part[0:1] * (away * away))
    return count, total, mean, squares


def stats_kernel(per, info_ref, video_ref, out_ref, sums, squares):
    frames = pl.num_programs(0)
    t = pl.program_id(0)
    rows, cols, chans = video_ref.shape[2:]
    size = float(rows * cols * per)

    def add(y, acc):
        return acc + jnp.sum(video_ref[0, 0, y].astype(F32).reshape(cols // 8, 8, chans), axis=0)

    acc = lax.fori_loop(0, rows, add, jnp.zeros((8, chans), F32), unroll=4)
    total = group_sum(jnp.sum(acc, axis=0, keepdims=True), per)
    mean = total / size

    def deviate(y, acc):
        away = video_ref[0, 0, y].astype(F32).reshape(cols // 8, 8, chans) - mean
        return acc + jnp.sum(away * away, axis=0)

    acc = lax.fori_loop(0, rows, deviate, jnp.zeros((8, chans), F32), unroll=4)
    sums[t] = jnp.broadcast_to(total, (8, chans))
    squares[t] = jnp.broadcast_to(group_sum(jnp.sum(acc, axis=0, keepdims=True), per), (8, chans))

    @pl.when(t == frames - 1)
    def _():
        inside = info_ref[0]
        parts = []
        for f in range(sums.shape[0]):
            keep = (f < inside).astype(F32)
            parts.append(
                jnp.concatenate(
                    [jnp.full((1, chans), size, F32), sums[f, 0:1], squares[f, 0:1]], axis=0
                )
                * keep
            )
        count, total, _, deviations = merged(parts)
        out_ref[...] = jnp.concatenate(
            [count, total, deviations, jnp.zeros((5, chans), F32)], axis=0
        )


def merge_kernel(*refs):
    count, total, _, deviations = merged([ref[...] for ref in refs[:-1]])
    refs[-1][...] = jnp.concatenate(
        [count, total, deviations, jnp.zeros((5, count.shape[1]), F32)], axis=0
    )


def cotangent_kernel(info_ref, cot_ref, turned_ref, bias_ref, wide):
    t = pl.program_id(0)
    rows, cols, chans = cot_ref.shape[2:]
    step = cols // TILE
    keep = (t < info_ref[0]).astype(F32)

    @pl.when(t == 0)
    def _():
        bias_ref[...] = jnp.zeros_like(bias_ref)

    def row(y, acc):
        value = cot_ref[0, 0, y].astype(F32) * keep
        slot = wide.at[y % wide.shape[0]]
        slot[...] = value
        order = jnp.concatenate(
            [slot[pl.ds(r, TILE, stride=step), :] for r in range(step)], axis=0
        )
        turned_ref[0, y] = order.T.astype(BF16)
        return acc + jnp.sum(value.reshape(cols // 8, 8, chans), axis=0)

    acc = lax.fori_loop(0, rows, row, jnp.zeros((8, chans), F32), unroll=4)
    bias_ref[0:1, :] += jnp.sum(acc, axis=0, keepdims=True)


def activate_kernel(
    parts_n, info_ref, video_ref, early_ref, low_ref, high_ref, gain_ref, shift_ref, *refs
):
    parts, out_ref, wide = refs[:parts_n], refs[parts_n], refs[parts_n + 1]
    frames, rows, cols, chans = video_ref.shape[1:]
    before = early_ref.shape[1]
    step = cols // TILE
    inside, first, has_low, has_high = info_ref[0], info_ref[1], info_ref[2], info_ref[3]
    count, _, mean, squares = merged([ref[...] for ref in parts])
    scale = 0.5 * lax.rsqrt(squares / count + 1e-05) * gain_ref[...]
    offset = 0.5 * shift_ref[...] - mean * scale
    slots = wide.shape[0]
    wide[:, 0:8, :] = jnp.zeros((slots, 8, chans), F32)
    wide[:, 8 + cols : 16 + cols, :] = jnp.zeros((slots, 8, chans), F32)

    def row(values, keep, slot, f, y):
        half = values.astype(F32) * (scale * keep) + offset * keep
        wide[slot, 8 : 8 + cols, :] = half + half * jnp.tanh(half)
        for r in range(-1, step + 1):
            out_ref[f, y, r + 1] = wide[slot, pl.ds(8 + r, TILE, stride=step), :].astype(BF16)

    for f in range(frames + before):
        local = f - before
        ok = (local < inside) & (first + local >= 0)
        keep = ok.astype(F32)
        source = early_ref.at[0, f] if local < 0 else video_ref.at[0, local]

        def inner(y, carry, source=source, keep=keep, f=f):
            row(source[y], keep, y % slots, f, y + 1)
            return carry

        lax.fori_loop(0, rows, inner, 0, unroll=4)
        row(low_ref[0, f, 0], keep * has_low.astype(F32), 0, f, 0)
        row(high_ref[0, f, 0], keep * has_high.astype(F32), 1, f, rows + 1)


def packed(value):
    per = value.shape[0] - TILE
    total = value[per : per + 1] + value[per + 1 : per + 2] + value[per + 2 : per + 3]
    top = total.astype(BF16).astype(F32)
    mid = (total - top).astype(BF16).astype(F32)
    rest = total - top - mid
    tail = jnp.concatenate([top, mid, rest, jnp.zeros((TILE - 3, value.shape[1]), F32)], axis=0)
    return jnp.concatenate([value[:per].astype(BF16), tail.astype(BF16)], axis=0)


def weights_kernel(info_ref, turned_ref, act_ref, bias_ref, keep_ref, *refs):
    send_refs, acc = refs[:-2], refs[-2:]
    acc, shards = acc
    frames, rows = turned_ref.shape[:2]
    chans = turned_ref.shape[2]
    k = turned_ref.shape[3]
    step = act_ref.shape[2] - 2
    taps = [(kt, ky, kx) for kt in range(3) for ky in range(3) for kx in range(3)]
    pair = 2

    def frame(t, carry):
        left = jnp.concatenate([turned_ref[t, y] for y in range(rows)], axis=1)
        for j in range(0, len(taps), pair):
            chosen = taps[j : j + pair]
            right = jnp.concatenate(
                [
                    act_ref[t + kt, ky : ky + rows, kx : kx + step].reshape(rows * k, chans)
                    for kt, ky, kx in chosen
                ],
                axis=1,
            )
            product = jnp.dot(left, right, preferred_element_type=F32)
            where = slice(j * chans, (j + len(chosen)) * chans)
            acc[:, where] = jnp.where(t == 0, product, acc[:, where] + product)
        return carry

    lax.fori_loop(0, frames, frame, 0)
    tms, dps, per = shards.shape[:3]
    per -= TILE
    for tap in range(len(taps)):
        block = acc[:, tap * chans : (tap + 1) * chans].T
        done = 0
        while done < chans:
            shard, at = divmod(tap * chans + done, per)
            take = min(chans - done, per - at)
            shards[shard // dps, shard % dps, at : at + take, :] = block[done : done + take]
            done += take
    tail = jnp.concatenate([bias_ref[0:1], jnp.zeros((TILE - 1, chans), F32)], axis=0)
    for i in range(tms):
        for j in range(dps):
            shards[i, j, per : per + TILE, :] = tail
    me = info_ref[4]
    keep_ref[...] = shards[me]
    for r in range(1, tms):
        send_refs[r - 1][...] = shards[me ^ r]


def spread_kernel(count, info_ref, keep_ref, *refs):
    incoming, own_ref, send_refs = refs[:count], refs[count], refs[count + 1 :]
    me = info_ref[5]
    for r in range(len(send_refs) + 1):
        value = keep_ref[me ^ r]
        for ref in incoming:
            value = value + ref[me ^ r]
        if r == 0:
            own_ref[...] = value
        else:
            send_refs[r - 1][...] = packed(value)


def add_kernel(*refs):
    value = refs[0][...].astype(F32)
    for ref in refs[1:-1]:
        value = value + ref[...].astype(F32)
    refs[-1][...] = packed(value) if refs[-1].dtype == BF16 else value


def conv_kernel(t0, info_ref, act_ref, taps_ref, video_ref, bias_ref, out_ref, wide):
    block = pl.program_id(0)
    frames_out, rows, cols, chans = out_ref.shape[1:]
    step = cols // TILE
    y0 = block * rows
    left = jnp.concatenate(
        [
            act_ref[f, pl.ds(y0 + ky, rows), kx : kx + step].reshape(rows * cols, chans)
            for f in range(frames_out + 2)
            for ky in range(3)
            for kx in range(3)
        ],
        axis=1,
    )
    result = jnp.dot(left, taps_ref[...], preferred_element_type=F32)
    for f in range(frames_out):
        keep = (t0 + f < info_ref[0]).astype(F32)
        for y in range(rows):
            slot = f * rows + y
            for r in range(step):
                at = y * cols + r * TILE
                wide[slot, pl.ds(r, TILE, stride=step), :] = result[
                    at : at + TILE, f * chans : (f + 1) * chans
                ]
            value = video_ref[0, f, y].astype(F32) + wide[slot] + bias_ref[...]
            out_ref[0, f, y] = (value * keep).astype(BF16)


def body(video, lengths, norm_gain, norm_shift, kernel, conv_bias, cotangent):
    frames, rows, cols, chans = video.shape[1:]
    per = chans // GROUPS
    step = cols // TILE
    before = kernel.shape[0] - 1
    tms, dps, spaces = (lax.axis_size(axis) for axis in ("tm", "dp", "space"))
    tm, dp, space = (lax.axis_index(axis) for axis in ("tm", "dp", "space"))
    first = tm * frames
    inside = jnp.clip(lengths[0] - first, -before, frames)
    info = jnp.stack(
        [
            inside,
            first,
            (space > 0).astype(jnp.int32),
            (space < spaces - 1).astype(jnp.int32),
            tm,
            dp,
        ]
    ).astype(jnp.int32)

    early = shifted(video[:, frames - before :], "tm", 1)

    frame_spec = pl.BlockSpec((1, 1, rows, cols, chans), lambda t: (0, t, 0, 0, 0))
    stats = pl.pallas_call(
        functools.partial(stats_kernel, per),
        grid=(frames,),
        in_specs=[SMEM, frame_spec],
        out_specs=pl.BlockSpec((8, chans), lambda t: (0, 0)),
        out_shape=jax.ShapeDtypeStruct((8, chans), F32),
        scratch_shapes=[pltpu.VMEM((frames, 8, chans), F32), pltpu.VMEM((frames, 8, chans), F32)],
        name="stats",
    )(info, video)
    stats = pl.pallas_call(
        merge_kernel,
        in_specs=[VMEM] * tms,
        out_specs=VMEM,
        out_shape=jax.ShapeDtypeStruct((8, chans), F32),
        name="merge",
    )(stats, *[swap(stats, "tm", r) for r in range(1, tms)])
    parts = [stats] + [swap(stats, "space", r) for r in range(1, spaces)]

    edge_low = jnp.concatenate([early[:, :, rows - 1 :], video[:, :, rows - 1 :]], axis=1)
    edge_high = jnp.concatenate([early[:, :, :1], video[:, :, :1]], axis=1)
    low = shifted(edge_low, "space", 1)
    high = shifted(edge_high, "space", -1)

    turned, bias = pl.pallas_call(
        cotangent_kernel,
        grid=(frames,),
        in_specs=[SMEM, frame_spec],
        out_specs=[
            pl.BlockSpec((1, rows, chans, cols), lambda t: (t, 0, 0, 0)),
            pl.BlockSpec((8, chans), lambda t: (0, 0)),
        ],
        out_shape=[
            jax.ShapeDtypeStruct((frames, rows, chans, cols), BF16),
            jax.ShapeDtypeStruct((8, chans), F32),
        ],
        scratch_shapes=[pltpu.VMEM((4, cols, chans), F32)],
        name="cotangent",
    )(info, cotangent)

    act = pl.pallas_call(
        functools.partial(activate_kernel, spaces),
        in_specs=[SMEM] + [VMEM] * (6 + spaces),
        out_specs=VMEM,
        out_shape=jax.ShapeDtypeStruct(
            (frames + before, rows + 2, step + 2, TILE, chans), BF16
        ),
        scratch_shapes=[pltpu.VMEM((4, cols + 16, chans), F32)],
        compiler_params=params(24),
        name="activate",
    )(
        info,
        video,
        early,
        low,
        high,
        norm_gain.reshape(1, chans),
        norm_shift.reshape(1, chans),
        *parts,
    )

    count = kernel.shape[0] * kernel.shape[1] * kernel.shape[2] * chans
    shards_n = tms * dps
    assert count % shards_n == 0
    shard = count // shards_n
    full = shard + TILE
    keep, *sends = pl.pallas_call(
        weights_kernel,
        in_specs=[SMEM, VMEM, VMEM, VMEM],
        out_specs=[VMEM] * tms,
        out_shape=[jax.ShapeDtypeStruct((dps, full, chans), F32)] * tms,
        scratch_shapes=[
            pltpu.VMEM((chans, count), F32),
            pltpu.VMEM((tms, dps, full, chans), F32),
        ],
        compiler_params=params(40),
        name="weights",
    )(info, turned, act, bias)

    incoming = [swap(send, "tm", r + 1) for r, send in enumerate(sends)]
    own, *sends = pl.pallas_call(
        functools.partial(spread_kernel, len(incoming)),
        in_specs=[SMEM] + [VMEM] * (1 + len(incoming)),
        out_specs=[VMEM] * dps,
        out_shape=[jax.ShapeDtypeStruct((full, chans), F32)]
        + [jax.ShapeDtypeStruct((full, chans), BF16)] * (dps - 1),
        name="spread",
    )(info, keep, *incoming)

    def added(dtype, *arrays):
        return pl.pallas_call(
            add_kernel,
            in_specs=[VMEM] * len(arrays),
            out_specs=VMEM,
            out_shape=jax.ShapeDtypeStruct((full, chans), dtype),
            name="added",
        )(*arrays)

    total = added(F32, own, *[swap(send, "dp", r + 1) for r, send in enumerate(sends)])
    by = 1
    while by < spaces:
        total = added(F32 if 2 * by < spaces else BF16, total, swap(total, "space", by))
        by *= 2
    mine = [total] + [swap(total, "dp", r) for r in range(1, dps)]
    shards = {(0, r): array for r, array in enumerate(mine)}
    for q in range(1, tms):
        for r, array in enumerate(mine):
            shards[q, r] = swap(array, "tm", q)
    order = list(shards)

    def collect(info_ref, *refs):
        out_ref, sum_ref = refs[-2:]
        for (q, r), ref in zip(order, refs):
            at = (info_ref[4] ^ q) * dps + (info_ref[5] ^ r)
            out_ref[at] = ref[0:shard, :].astype(F32)
        tail = refs[0][shard : shard + TILE, :].astype(F32)
        sum_ref[...] = tail[0:1] + tail[1:2] + tail[2:3]

    grad_kernel, grad_bias = pl.pallas_call(
        collect,
        in_specs=[SMEM] + [VMEM] * len(order),
        out_specs=[VMEM, VMEM],
        out_shape=[
            jax.ShapeDtypeStruct((shards_n, shard, chans), F32),
            jax.ShapeDtypeStruct((1, chans), F32),
        ],
        name="collect",
    )(info, *[shards[key] for key in order])

    zero = jnp.zeros(kernel.shape[1:], BF16)
    taps = jnp.concatenate(
        [
            jnp.concatenate(
                [
                    kernel[f - g] if 0 <= f - g < kernel.shape[0] else zero
                    for g in range(2)
                ],
                axis=-1,
            ).reshape(-1, 2 * chans)
            for f in range(kernel.shape[0] + 1)
        ],
        axis=0,
    )
    block = 4
    outputs = []
    for t0 in range(0, frames, 2):
        outputs.append(
            pl.pallas_call(
                functools.partial(conv_kernel, t0),
                grid=(rows // block,),
                in_specs=[
                    SMEM,
                    VMEM,
                    VMEM,
                    pl.BlockSpec((1, 2, block, cols, chans), lambda y, t0=t0: (0, t0 // 2, y, 0, 0)),
                    VMEM,
                ],
                out_specs=pl.BlockSpec((1, 2, block, cols, chans), lambda y: (0, 0, y, 0, 0)),
                out_shape=jax.ShapeDtypeStruct((1, 2, rows, cols, chans), BF16),
                scratch_shapes=[pltpu.VMEM((2 * block, cols, chans), F32)],
                compiler_params=params(40),
                name="conv",
            )(info, act[t0 : t0 + 4], taps, video, conv_bias.reshape(1, chans))
        )
    output = jnp.concatenate(outputs, axis=1)
    return output, grad_kernel.reshape(kernel.shape), grad_bias.reshape(chans)


def solution(mesh):
    return jax.shard_map(
        body,
        mesh=mesh,
        in_specs=(
            P("dp", "tm", "space", None, None),
            P("dp"),
            P(),
            P(),
            P(),
            P(),
            P("dp", "tm", "space", None, None),
        ),
        out_specs=(P("dp", "tm", "space", None, None), P(), P()),
        check_vma=False,
    )
```

time: 373 us -> 119 us (0.32); the launches traced: 367 us -> 118 us
  waiting for transfers between devices: 95 us -> 15.8 us
  local copies, waits for them, and re-layouts: 94.6 us -> 16.9 us
  blocking collectives: 73.7 us -> 0 us
  matrix products: 57.7 us -> 0 us
  Pallas kernels: 0 us -> 47.2 us
  starting transfers between devices: 8.1 us -> 25.1 us
  between operations: 15.6 us -> 1.62 us
  other arithmetic: 22.5 us -> 11.7 us
    psum x1 -> x0, waiting for transfers between devices: 92.8 us -> none  [body(): lax.psum((local_kernel, local_bias), ('dp', 'tm', 'space'))]
    psum x3 -> x0, blocking collectives: 73.7 us -> none  [the longest x1 41.4 us: body(): lax.psum((local_kernel, local_bias), ('dp', 'tm', 'space'))]
    dot_general x18 -> x0, matrix products: 57.7 us -> none  [the longest x9 36.9 us: body(): jnp.dot(band, taps, preferred_element_type=jnp.float32)]
    reshape x11 -> x0, local copies, waits for them, and re-layouts: 57.3 us -> none  [the longest x9 36.8 us: body(): band = padded[kt:kt + frames, ky:ky + rows].reshape(wide_rows, chans)]
    pallas_call x0 -> x12, Pallas kernels: none -> 47.2 us  [the longest x2 13.1 us: body(): pl.pallas_call(functools.partial(conv_kernel, t0), grid=(rows // block,),...]
    ppermute x3 -> x20, starting transfers between devices: 8.06 us -> 25.1 us  [the longest x17 16.9 us: swap(): return lax.ppermute(array, axis, [(i, i ^ by) for i in range(length)])]
    ppermute x3 -> x20, waiting for transfers between devices: 2.21 us -> 15.8 us  [the longest x17 14.6 us: swap(): return lax.ppermute(array, axis, [(i, i ^ by) for i in range(length)])]
    convert_element_type x3 -> x0, other arithmetic: 9.49 us -> none  [the longest x1 7.84 us: body(): masked = (cotangent[0].astype(jnp.float32) * mask).astype(jnp.bfloat16)]
  transfers between devices with their start and end apart: 4 -> 20, of which waited for: 2 -> 8; matrix products, arithmetic and copies ran while one was open for 3% -> 16% of each run, Pallas kernels for 0% -> 20%
where the time goes in v1:
time: 119 us; the launch traced here: 118 us
  Pallas kernels  47.2 us (40%)
  starting transfers between devices  25.1 us (21%)
  local copies, waits for them, and re-layouts  16.9 us (14%)
  waiting for transfers between devices  15.8 us (13%)
  other arithmetic  11.7 us (10%)
  between operations  1.62 us (1%)
    ppermute x17, starting transfers between devices, swap(): return lax.ppermute(array, axis, [(i, i ^ by) for i in range(length)])  16.9 us
    ppermute x17, waiting for transfers between devices, swap(): return lax.ppermute(array, axis, [(i, i ^ by) for i in range(length)])  14.6 us
    pallas_call x2, Pallas kernels, body(): pl.pallas_call(functools.partial(conv_kernel, t0), grid=(rows // block,),...  13.1 us
    pallas_call x1, Pallas kernels, body(): pl.pallas_call(weights_kernel, in_specs=[SMEM, VMEM, VMEM, VMEM], out_spe...  9.5 us
    concatenate x1, other arithmetic, body(): jnp.concatenate([jnp.concatenate([kernel[f - g] if 0 <= f - g < kernel.sh...  8.76 us
    ppermute x3, starting transfers between devices, shifted(): lax.ppermute(array, axis, [(i, i + by) for i in range(length) if 0 <= i +...  8.17 us
    unnamed x54, local copies, waits for them, and re-layouts  7.83 us
    pallas_call x3, Pallas kernels, added(): pl.pallas_call(add_kernel, in_specs=[VMEM] * len(arrays), out_specs=VMEM,...  5.35 us
  transfers between devices with their start and end apart: 20, of which 8 were waited for; matrix products, arithmetic and copies ran while one was open for 16% of the time, Pallas kernels for 20%

profile of v1, /device:TPU:0, one launch (start us, length us, event | category | flops | bytes accessed | tf_op | source)
XLA Modules:
  0.0 118.1 jit_solution(16511251186162040122)
XLA Ops:
  0.6 1.3 %slice.33 = bf16[1,2,16,128,128]{4,3,2,1,0:T(8,128)(2,1)S(1)} slice(bf16[1,4,16,128,128]{4,3,2,1,0:T(8,128)(2,1)} %video_ref.7), slice={[0:1], [2:4], [0:16], [0:128], [0:128]} | slice | bytes 2097152 | tf_op jit(solution)/shard_map/slice | solution.py:288
  1.9 2.6 %collective-permute-start = (bf16[1,2,16,128,128]{4,3,2,1,0:T(8,128)(2,1)S(1)}, bf16[1,2,16,128,128]{4,3,2,1,0:T(8,128)(2,1)S(1)}, u32[]{:S(2)}, u32[]{:S(2)}) collective-permute-start(bf16[1,2,16,128,128]{4,3,2,1,0:T(8,128)(2,1)S(1)} %slice.33), channel_id=1, source_target_pairs={{0,4},{1,5},{2,6},{3,7},{8,12},{9,13},{10,14},{11,15},{16,20},{17,... | collective-permute-start | bytes 3145736 | tf_op jit(solution)/shard_map/ppermute | solution.py:30
  4.5 1.0 fusion.1
  5.5 1.2 %collective-permute-done.early_ref = bf16[1,2,16,128,128]{4,3,2,1,0:T(8,128)(2,1)S(1)} collective-permute-done((bf16[1,2,16,128,128]{4,3,2,1,0:T(8,128)(2,1)S(1)}, bf16[1,2,16,128,128]{4,3,2,1,0:T(8,128)(2,1)S(1)}, u32[]{:S(2)}, u32[]{:S(2)}) %collective-permute-start) | collective-permute-done | bytes 1048608 | tf_op jit(solution)/shard_map/ppermute | solution.py:30
  6.8 0.7 pad_maximum_fusion.2
  7.5 4.3 %collective-permute-start.1 = (bf16[1,6,1,128,128]{4,3,2,1,0:T(8,128)(2,1)}, bf16[1,6,1,128,128]{4,3,2,1,0:T(8,128)(2,1)S(1)}, u32[]{:S(2)}, u32[]{:S(2)}) collective-permute-start(bf16[1,6,1,128,128]{4,3,2,1,0:T(8,128)(2,1)} %pad_maximum_fusion.2), channel_id=1, source_target_pairs={{0,1},{1,2},{2,3},{4,5},{5,6},{6,7},{8,9},{9,10},{10,11},{12,13},{... | collective-permute-start | bytes 589832 | tf_op jit(solution)/shard_map/ppermute | solution.py:30
  11.8 0.7 pad_maximum_fusion.3
  12.5 1.3 %collective-permute-start.2 = (bf16[1,6,1,128,128]{4,3,2,1,0:T(8,128)(2,1)}, bf16[1,6,1,128,128]{4,3,2,1,0:T(8,128)(2,1)S(1)}, u32[]{:S(2)}, u32[]{:S(2)}) collective-permute-start(bf16[1,6,1,128,128]{4,3,2,1,0:T(8,128)(2,1)} %pad_maximum_fusion.3), channel_id=1, source_target_pairs={{1,0},{2,1},{3,2},{5,4},{6,5},{7,6},{9,8},{10,9},{11,10},{13,12},{... | collective-permute-start | bytes 589832 | tf_op jit(solution)/shard_map/ppermute | solution.py:30
  14.4 0.6 stack.35.info_ref
  15.0 4.5 %stats.1.refs_0_ = f32[8,128]{1,0:T(8,128)} custom-call(s32[6]{0:T(128)} %stack.35.info_ref, bf16[1,4,16,128,128]{4,3,2,1,0:T(8,128)(2,1)} %video_ref.7), custom_call_target="tpu_custom_call" | custom-call | tf_op jit(solution)/shard_map/stats/pallas_call | solution.py:291
  19.5 1.3 %collective-permute-done.3.refs_1_ = f32[8,128]{1,0:T(8,128)S(1)} collective-permute-done((f32[8,128]{1,0:T(8,128)}, f32[8,128]{1,0:T(8,128)S(1)}, u32[]{:S(2)}, u32[]{:S(2)}) %collective-permute-start.3) | collective-permute-done | bytes 4128 | tf_op jit(solution)/shard_map/ppermute | solution.py:25
  20.8 0.6 copy-done.26
  21.4 1.3 %merge.1.refs_0_ = f32[8,128]{1,0:T(8,128)} custom-call(f32[8,128]{1,0:T(8,128)} %stats.1.refs_0_, f32[8,128]{1,0:T(8,128)} %copy-done.26), custom_call_target="tpu_custom_call" | custom-call | tf_op jit(solution)/shard_map/merge/pallas_call | solution.py:300
  22.7 2.6 %collective-permute-start.4 = (f32[8,128]{1,0:T(8,128)}, f32[8,128]{1,0:T(8,128)S(1)}, u32[]{:S(2)}, u32[]{:S(2)}) collective-permute-start(f32[8,128]{1,0:T(8,128)} %merge.1.refs_0_), channel_id=1, source_target_pairs={{0,1},{1,0},{2,3},{3,2},{4,5},{5,4},{6,7},{7,6},{8,9},{9,8},{10,11... | collective-permute-start | bytes 12296 | tf_op jit(solution)/shard_map/ppermute | solution.py:25
  25.4 2.6 %collective-permute-start.5 = (f32[8,128]{1,0:T(8,128)}, f32[8,128]{1,0:T(8,128)S(1)}, u32[]{:S(2)}, u32[]{:S(2)}) collective-permute-start(f32[8,128]{1,0:T(8,128)} %merge.1.refs_0_), channel_id=1, source_target_pairs={{0,2},{1,3},{2,0},{3,1},{4,6},{5,7},{6,4},{7,5},{8,10},{9,11},{10,... | collective-permute-start | bytes 12296 | tf_op jit(solution)/shard_map/ppermute | solution.py:25
  28.0 5.2 %cotangent.1 = (bf16[4,16,128,128]{3,2,1,0:T(8,128)(2,1)}, f32[8,128]{1,0:T(8,128)}) custom-call(s32[6]{0:T(128)} %stack.35.info_ref, bf16[1,4,16,128,128]{4,3,2,1,0:T(8,128)(2,1)} %cot_ref.1), custom_call_target="tpu_custom_call" | custom-call | tf_op jit(solution)/shard_map/cotangent/pallas_call | solution.py:314
  33.6 0.7 copy-done.7
  34.3 0.7 copy-done.10
  34.9 0.7 copy-done.11
  35.6 3.2 %activate.1.act_ref = bf16[6,18,10,16,128]{4,3,2,1,0:T(8,128)(2,1)S(1)} custom-call(s32[6]{0:T(128)S(1)} %copy-done.5, bf16[1,4,16,128,128]{4,3,2,1,0:T(8,128)(2,1)S(1)} %copy-done.1, bf16[1,2,16,128,128]{4,3,2,1,0:T(8,128)(2,1)S(1)} %collective-permute-done.early_ref, bf16[1,6,1,128,128]{4,3,2,1,0:T(8,128)(2,1)S(1)} %collective-permute-done.1.low_ref, ...), custom_call_target="tpu_custom_call" | custom-call | tf_op jit(solution)/shard_map/activate/pallas_call | solution.py:330
  38.9 9.5 %weights.1 = (f32[4,448,128]{2,1,0:T(8,128)S(1)}, f32[4,448,128]{2,1,0:T(8,128)S(1)}) custom-call(s32[6]{0:T(128)S(1)} %copy-done.5, bf16[4,16,128,128]{3,2,1,0:T(8,128)(2,1)S(1)} %copy-done.3, bf16[6,18,10,16,128]{4,3,2,1,0:T(8,128)(2,1)S(1)} %activate.1.act_ref, f32[8,128]{1,0:T(8,128)S(1)} %copy-done.8), custom_call_target="tpu_custom_call" | custom-call | tf_op jit(solution)/shard_map/weights/pallas_call | solution.py:356
  48.4 0.9 copy-done.4
  49.3 2.5 %collective-permute-done.7.refs_0_ = f32[4,448,128]{2,1,0:T(8,128)S(1)} collective-permute-done((f32[4,448,128]{2,1,0:T(8,128)S(1)}, f32[4,448,128]{2,1,0:T(8,128)S(1)}, u32[]{:S(2)}, u32[]{:S(2)}) %collective-permute-start.7) | collective-permute-done | bytes 917536 | tf_op jit(solution)/shard_map/ppermute | solution.py:25
  51.8 0.9 copy-done.12
  52.7 2.4 %spread.1 = (f32[448,128]{1,0:T(8,128)}, bf16[448,128]{1,0:T(8,128)(2,1)}, bf16[448,128]{1,0:T(8,128)(2,1)}, bf16[448,128]{1,0:T(8,128)(2,1)}) custom-call(s32[6]{0:T(128)} %stack.35.info_ref, f32[4,448,128]{2,1,0:T(8,128)} %copy-done.4, f32[4,448,128]{2,1,0:T(8,128)} %copy-done.12), custom_call_target="tpu_custom_call" | custom-call | tf_op jit(solution)/shard_map/spread/pallas_call | solution.py:370
  55.1 2.4 %collective-permute-start.10 = (bf16[448,128]{1,0:T(8,128)(2,1)}, bf16[448,128]{1,0:T(8,128)(2,1)S(1)}, u32[]{:S(2)}, u32[]{:S(2)}) collective-permute-start(bf16[448,128]{1,0:T(8,128)(2,1)} %get-tuple-element.20), channel_id=1, source_target_pairs={{0,24},{8,16},{16,8},{24,0},{1,25},{9,17},{17,9},{25,1},{2,26},{10... | collective-permute-start | bytes 344072 | tf_op jit(solution)/shard_map/ppermute | solution.py:25
  58.6 3.6 %collective-permute-done.10.refs_3_ = bf16[448,128]{1,0:T(8,128)(2,1)S(1)} collective-permute-done((bf16[448,128]{1,0:T(8,128)(2,1)}, bf16[448,128]{1,0:T(8,128)(2,1)S(1)}, u32[]{:S(2)}, u32[]{:S(2)}) %collective-permute-start.10) | collective-permute-done | bytes 114720 | tf_op jit(solution)/shard_map/ppermute | solution.py:25
  62.2 1.7 %collective-permute-done.8.refs_1_ = bf16[448,128]{1,0:T(8,128)(2,1)S(1)} collective-permute-done((bf16[448,128]{1,0:T(8,128)(2,1)}, bf16[448,128]{1,0:T(8,128)(2,1)S(1)}, u32[]{:S(2)}, u32[]{:S(2)}) %collective-permute-start.8) | collective-permute-done | bytes 114720 | tf_op jit(solution)/shard_map/ppermute | solution.py:25
  63.9 0.6 copy-done.24
  64.6 1.9 %added.3.refs_0_ = f32[448,128]{1,0:T(8,128)} custom-call(f32[448,128]{1,0:T(8,128)} %get-tuple-element.17.refs_0_, bf16[448,128]{1,0:T(8,128)(2,1)} %copy-done.24, bf16[448,128]{1,0:T(8,128)(2,1)} %copy-done.25, bf16[448,128]{1,0:T(8,128)(2,1)} %copy-done.23), custom_call_target="tpu_custom_call" | custom-call | tf_op jit(solution)/shard_map/added/pallas_call | solution.py:380
  67.0 2.2 %slice_bitcast_fusion.1 = (bf16[3,3,128,128]{3,2,1,0:T(8,128)(2,1)S(1)}, bf16[3,3,128,128]{3,2,1,0:T(8,128)(2,1)S(1)}, bf16[1,3,3,128,128]{4,3,2,1,0:T(8,128)(2,...) fusion(bf16[3,3,3,128,128]{4,3,2,1,0:T(8,128)(2,1)} %param.11), kind=kLoop, calls=%fused_computation.5 | loop fusion | bytes 2359296 | tf_op jit(solution)/shard_map/squeeze | solution.py:424
  69.4 4.2 %collective-permute-done.11.refs_1_ = f32[448,128]{1,0:T(8,128)S(1)} collective-permute-done((f32[448,128]{1,0:T(8,128)}, f32[448,128]{1,0:T(8,128)S(1)}, u32[]{:S(2)}, u32[]{:S(2)}) %collective-permute-start.11) | collective-permute-done | bytes 229408 | tf_op jit(solution)/shard_map/ppermute | solution.py:25
  73.5 0.7 copy-done.15
  74.2 1.8 %added.4.refs_0_ = f32[448,128]{1,0:T(8,128)} custom-call(f32[448,128]{1,0:T(8,128)} %added.3.refs_0_, f32[448,128]{1,0:T(8,128)} %copy-done.15), custom_call_target="tpu_custom_call" | custom-call | tf_op jit(solution)/shard_map/added/pallas_call | solution.py:380
  76.0 2.3 %collective-permute-start.12 = (f32[448,128]{1,0:T(8,128)}, f32[448,128]{1,0:T(8,128)S(1)}, u32[]{:S(2)}, u32[]{:S(2)}) collective-permute-start(f32[448,128]{1,0:T(8,128)} %added.4.refs_0_), channel_id=1, source_target_pairs={{0,2},{1,3},{2,0},{3,1},{4,6},{5,7},{6,4},{7,5},{8,10},{9,11},{10,... | collective-permute-start | bytes 688136 | tf_op jit(solution)/shard_map/ppermute | solution.py:25
  78.3 8.8 %pad_maximum_fusion.taps_ref = bf16[4608,256]{1,0:T(8,128)(2,1)} fusion(bf16[1152,256]{1,0:T(8,128)(2,1)S(1)} %bitcast.27, bf16[1152,128]{1,0:T(8,128)(2,1)} %bitcast.30, bf16[1152,128]{1,0:T(8,128)(2,1)} %bitcast.29, bf16[1152,128]{1,0:T(8,128)(2,1)} %bitcast.28, bf16[1152,256]{1,0:T(8,128)(2,1)S(1)} %bitcast.26), kind=kLoop, calls=%fused_computation | loop fusion | flops 14155776 | bytes 4423680 | tf_op jit(solution)/shard_map/concatenate | solution.py:420
  87.1 1.0 collective-permute-done.12.refs_1_
  88.0 0.7 copy-done.14
  88.7 1.7 %added.5.refs_0_ = bf16[448,128]{1,0:T(8,128)(2,1)} custom-call(f32[448,128]{1,0:T(8,128)} %added.4.refs_0_, f32[448,128]{1,0:T(8,128)} %copy-done.14), custom_call_target="tpu_custom_call" | custom-call | tf_op jit(solution)/shard_map/added/pallas_call | solution.py:380
  90.4 1.5 %collective-permute-start.13 = (bf16[448,128]{1,0:T(8,128)(2,1)}, bf16[448,128]{1,0:T(8,128)(2,1)S(1)}, u32[]{:S(2)}, u32[]{:S(2)}) collective-permute-start(bf16[448,128]{1,0:T(8,128)(2,1)} %added.5.refs_0_), channel_id=1, source_target_pairs={{0,8},{8,0},{16,24},{24,16},{1,9},{9,1},{17,25},{25,17},{2,10},{10... | collective-permute-start | bytes 344072 | tf_op jit(solution)/shard_map/ppermute | solution.py:25
  92.0 2.6 %collective-permute-start.14 = (bf16[448,128]{1,0:T(8,128)(2,1)}, bf16[448,128]{1,0:T(8,128)(2,1)S(1)}, u32[]{:S(2)}, u32[]{:S(2)}) collective-permute-start(bf16[448,128]{1,0:T(8,128)(2,1)} %added.5.refs_0_), channel_id=1, source_target_pairs={{0,16},{8,24},{16,0},{24,8},{1,17},{9,25},{17,1},{25,9},{2,18},{10... | collective-permute-start | bytes 344072 | tf_op jit(solution)/shard_map/ppermute | solution.py:25
  94.6 3.8 %fusion = (bf16[4,18,10,16,128]{4,3,2,1,0:T(8,128)(2,1)S(1)}, bf16[4,18,10,16,128]{4,3,2,1,0:T(8,128)(2,1)S(1)}) fusion(bf16[6,18,10,16,128]{4,3,2,1,0:T(8,128)(2,1)} %copy-done), kind=kLoop, calls=%fused_computation.6 | loop fusion | bytes 11796480 | tf_op jit(solution)/shard_map/slice | solution.py:452
  98.4 6.5 %conv.2 = bf16[1,2,16,128,128]{4,3,2,1,0:T(8,128)(2,1)S(1)} custom-call(s32[6]{0:T(128)S(1)} %copy-done.6, bf16[4,18,10,16,128]{4,3,2,1,0:T(8,128)(2,1)S(1)} %get-tuple-element.23.act_ref, bf16[4608,256]{1,0:T(8,128)(2,1)S(1)} %copy-done.2, bf16[1,4,16,128,128]{4,3,2,1,0:T(8,128)(2,1)S(1)} %copy-done.1, f32[1,128]{1,0:T(1,128)S(1)} %bitcast.22), custom_call_target="tpu_custom_call" | custom-call | tf_op jit(solution)/shard_map/conv/pallas_call | solution.py:437
  105.0 6.5 %conv.3 = bf16[1,2,16,128,128]{4,3,2,1,0:T(8,128)(2,1)S(1)} custom-call(s32[6]{0:T(128)S(1)} %copy-done.6, bf16[4,18,10,16,128]{4,3,2,1,0:T(8,128)(2,1)S(1)} %get-tuple-element.24.act_ref, bf16[4608,256]{1,0:T(8,128)(2,1)S(1)} %copy-done.2, bf16[1,4,16,128,128]{4,3,2,1,0:T(8,128)(2,1)S(1)} %copy-done.1, f32[1,128]{1,0:T(1,128)S(1)} %bitcast.23), custom_call_target="tpu_custom_call" | custom-call | tf_op jit(solution)/shard_map/conv/pallas_call | solution.py:437
  112.7 1.5 %pad_maximum_fusion.1 = bf16[1,4,16,128,128]{4,3,2,1,0:T(8,128)(2,1)} fusion(bf16[1,2,16,128,128]{4,3,2,1,0:T(8,128)(2,1)S(1)} %conv.3, bf16[1,2,16,128,128]{4,3,2,1,0:T(8,128)(2,1)S(1)} %conv.2), kind=kLoop, calls=%fused_computation.1 | loop fusion | flops 1048576 | bytes 4194304 | tf_op jit(solution)/shard_map/concatenate | solution.py:454
  114.2 0.6 copy-done.19
  114.9 0.6 copy-done.22
  115.6 2.6 %collect.1 = (f32[8,432,128]{2,1,0:T(8,128)}, f32[1,128]{1,0:T(1,128)}) custom-call(s32[6]{0:T(128)} %stack.35.info_ref, bf16[448,128]{1,0:T(8,128)(2,1)} %added.5.refs_0_, bf16[448,128]{1,0:T(8,128)(2,1)} %copy-done.16, bf16[448,128]{1,0:T(8,128)(2,1)} %copy-done.17, bf16[448,128]{1,0:T(8,128)(2,1)} %copy-done.18, bf16[448,128]{1,0:T(8,128)(2,1)} %copy-done.19, ...), custom_call_target="tpu_custom_call" | custom-call | tf_op jit(solution)/shard_map/collect/pallas_call | solution.py:408
  (70 shorter events, 3.5 us)
Async XLA Ops:
  1.9 31.6 %copy-start.1 = (bf16[1,4,16,128,128]{4,3,2,1,0:T(8,128)(2,1)S(1)}, bf16[1,4,16,128,128]{4,3,2,1,0:T(8,128)(2,1)}, u32[]{:S(2)}) copy-start(bf16[1,4,16,128,128]{4,3,2,1,0:T(8,128)(2,1)} %video_ref.7) | copy-start | bytes 6291460
  1.9 4.8 %collective-permute-start = (bf16[1,2,16,128,128]{4,3,2,1,0:T(8,128)(2,1)S(1)}, bf16[1,2,16,128,128]{4,3,2,1,0:T(8,128)(2,1)S(1)}, u32[]{:S(2)}, u32[]{:S(2)}) collective-permute-start(bf16[1,2,16,128,128]{4,3,2,1,0:T(8,128)(2,1)S(1)} %slice.33), channel_id=1, source_target_pairs={{0,4},{1,5},{2,6},{3,7},{8,12},{9,13},{10,14},{11,15},{16,20},{17,... | collective-permute-start | bytes 3145736 | tf_op jit(solution)/shard_map/ppermute | solution.py:30
  7.5 26.1 %collective-permute-start.1 = (bf16[1,6,1,128,128]{4,3,2,1,0:T(8,128)(2,1)}, bf16[1,6,1,128,128]{4,3,2,1,0:T(8,128)(2,1)S(1)}, u32[]{:S(2)}, u32[]{:S(2)}) collective-permute-start(bf16[1,6,1,128,128]{4,3,2,1,0:T(8,128)(2,1)} %pad_maximum_fusion.2), channel_id=1, source_target_pairs={{0,1},{1,2},{2,3},{4,5},{5,6},{6,7},{8,9},{9,10},{10,11},{12,13},{... | collective-permute-start | bytes 589832 | tf_op jit(solution)/shard_map/ppermute | solution.py:30
  12.5 21.1 %collective-permute-start.2 = (bf16[1,6,1,128,128]{4,3,2,1,0:T(8,128)(2,1)}, bf16[1,6,1,128,128]{4,3,2,1,0:T(8,128)(2,1)S(1)}, u32[]{:S(2)}, u32[]{:S(2)}) collective-permute-start(bf16[1,6,1,128,128]{4,3,2,1,0:T(8,128)(2,1)} %pad_maximum_fusion.3), channel_id=1, source_target_pairs={{1,0},{2,1},{3,2},{5,4},{6,5},{7,6},{9,8},{10,9},{11,10},{13,12},{... | collective-permute-start | bytes 589832 | tf_op jit(solution)/shard_map/ppermute | solution.py:30
  15.0 18.6 %copy-start.5 = (s32[6]{0:T(128)S(1)}, s32[6]{0:T(128)}, u32[]{:S(2)}) copy-start(s32[6]{0:T(128)} %stack.35.info_ref) | copy-start | bytes 76
  19.5 1.4 %collective-permute-start.3 = (f32[8,128]{1,0:T(8,128)}, f32[8,128]{1,0:T(8,128)S(1)}, u32[]{:S(2)}, u32[]{:S(2)}) collective-permute-start(f32[8,128]{1,0:T(8,128)} %stats.1.refs_0_), channel_id=1, source_target_pairs={{0,4},{4,0},{1,5},{5,1},{2,6},{6,2},{3,7},{7,3},{8,12},{12,8},{9,1... | collective-permute-start | bytes 12296 | tf_op jit(solution)/shard_map/ppermute | solution.py:25
  20.8 0.6 copy-start.26
  22.7 10.5 %collective-permute-start.4 = (f32[8,128]{1,0:T(8,128)}, f32[8,128]{1,0:T(8,128)S(1)}, u32[]{:S(2)}, u32[]{:S(2)}) collective-permute-start(f32[8,128]{1,0:T(8,128)} %merge.1.refs_0_), channel_id=1, source_target_pairs={{0,1},{1,0},{2,3},{3,2},{4,5},{5,4},{6,7},{7,6},{8,9},{9,8},{10,11... | collective-permute-start | bytes 12296 | tf_op jit(solution)/shard_map/ppermute | solution.py:25
  25.4 7.8 %collective-permute-start.5 = (f32[8,128]{1,0:T(8,128)}, f32[8,128]{1,0:T(8,128)S(1)}, u32[]{:S(2)}, u32[]{:S(2)}) collective-permute-start(f32[8,128]{1,0:T(8,128)} %merge.1.refs_0_), channel_id=1, source_target_pairs={{0,2},{1,3},{2,0},{3,1},{4,6},{5,7},{6,4},{7,5},{8,10},{9,11},{10,... | collective-permute-start | bytes 12296 | tf_op jit(solution)/shard_map/ppermute | solution.py:25
  28.0 5.6 %collective-permute-start.6 = (f32[8,128]{1,0:T(8,128)}, f32[8,128]{1,0:T(8,128)S(1)}, u32[]{:S(2)}, u32[]{:S(2)}) collective-permute-start(f32[8,128]{1,0:T(8,128)} %merge.1.refs_0_), channel_id=1, source_target_pairs={{0,3},{1,2},{2,1},{3,0},{4,7},{5,6},{6,5},{7,4},{8,11},{9,10},{10,... | collective-permute-start | bytes 12296 | tf_op jit(solution)/shard_map/ppermute | solution.py:25
  33.6 0.7 copy-start.7
  34.3 0.7 copy-start.10
  34.9 0.7 copy-start.11
  35.6 3.3 %copy-start.3 = (bf16[4,16,128,128]{3,2,1,0:T(8,128)(2,1)S(1)}, bf16[4,16,128,128]{3,2,1,0:T(8,128)(2,1)}, u32[]{:S(2)}) copy-start(bf16[4,16,128,128]{3,2,1,0:T(8,128)(2,1)} %get-tuple-element.13.turned_ref) | copy-start | bytes 6291460
  35.6 3.3 %copy-start.8 = (f32[8,128]{1,0:T(8,128)S(1)}, f32[8,128]{1,0:T(8,128)}, u32[]{:S(2)}) copy-start(f32[8,128]{1,0:T(8,128)} %get-tuple-element.14.bias_ref) | copy-start | bytes 12292
  38.8 9.5 %copy-start = (bf16[6,18,10,16,128]{4,3,2,1,0:T(8,128)(2,1)}, bf16[6,18,10,16,128]{4,3,2,1,0:T(8,128)(2,1)S(1)}, u32[]{:S(2)}) copy-start(bf16[6,18,10,16,128]{4,3,2,1,0:T(8,128)(2,1)S(1)} %activate.1.act_ref) | copy-start | bytes 13271044
  48.4 0.9 copy-start.4
  49.3 2.5 %collective-permute-start.7 = (f32[4,448,128]{2,1,0:T(8,128)S(1)}, f32[4,448,128]{2,1,0:T(8,128)S(1)}, u32[]{:S(2)}, u32[]{:S(2)}) collective-permute-start(f32[4,448,128]{2,1,0:T(8,128)S(1)} %get-tuple-element.16), channel_id=1, source_target_pairs={{0,4},{4,0},{1,5},{5,1},{2,6},{6,2},{3,7},{7,3},{8,12},{12,8},{9,1... | collective-permute-start | bytes 2752520 | tf_op jit(solution)/shard_map/ppermute | solution.py:25
  51.8 0.9 copy-start.12
  55.1 7.1 %collective-permute-start.10 = (bf16[448,128]{1,0:T(8,128)(2,1)}, bf16[448,128]{1,0:T(8,128)(2,1)S(1)}, u32[]{:S(2)}, u32[]{:S(2)}) collective-permute-start(bf16[448,128]{1,0:T(8,128)(2,1)} %get-tuple-element.20), channel_id=1, source_target_pairs={{0,24},{8,16},{16,8},{24,0},{1,25},{9,17},{17,9},{25,1},{2,26},{10... | collective-permute-start | bytes 344072 | tf_op jit(solution)/shard_map/ppermute | solution.py:25
  57.5 6.4 %collective-permute-start.8 = (bf16[448,128]{1,0:T(8,128)(2,1)}, bf16[448,128]{1,0:T(8,128)(2,1)S(1)}, u32[]{:S(2)}, u32[]{:S(2)}) collective-permute-start(bf16[448,128]{1,0:T(8,128)(2,1)} %get-tuple-element.18), channel_id=1, source_target_pairs={{0,8},{8,0},{16,24},{24,16},{1,9},{9,1},{17,25},{25,17},{2,10},{10... | collective-permute-start | bytes 344072 | tf_op jit(solution)/shard_map/ppermute | solution.py:25
  58.1 5.8 %collective-permute-start.9 = (bf16[448,128]{1,0:T(8,128)(2,1)}, bf16[448,128]{1,0:T(8,128)(2,1)S(1)}, u32[]{:S(2)}, u32[]{:S(2)}) collective-permute-start(bf16[448,128]{1,0:T(8,128)(2,1)} %get-tuple-element.19), channel_id=1, source_target_pairs={{0,16},{8,24},{16,0},{24,8},{1,17},{9,25},{17,1},{25,9},{2,18},{10... | collective-permute-start | bytes 344072 | tf_op jit(solution)/shard_map/ppermute | solution.py:25
  62.2 1.7 %copy-start.23 = (bf16[448,128]{1,0:T(8,128)(2,1)}, bf16[448,128]{1,0:T(8,128)(2,1)S(1)}, u32[]{:S(2)}) copy-start(bf16[448,128]{1,0:T(8,128)(2,1)S(1)} %collective-permute-done.10.refs_3_) | copy-start | bytes 344068
  63.9 0.6 copy-start.24
  63.9 0.7 copy-start.25
  66.4 7.1 %collective-permute-start.11 = (f32[448,128]{1,0:T(8,128)}, f32[448,128]{1,0:T(8,128)S(1)}, u32[]{:S(2)}, u32[]{:S(2)}) collective-permute-start(f32[448,128]{1,0:T(8,128)} %added.3.refs_0_), channel_id=1, source_target_pairs={{0,1},{1,0},{2,3},{3,2},{4,5},{5,4},{6,7},{7,6},{8,9},{9,8},{10,11... | collective-permute-start | bytes 688136 | tf_op jit(solution)/shard_map/ppermute | solution.py:25
  73.5 0.7 copy-start.15
  76.0 12.0 %collective-permute-start.12 = (f32[448,128]{1,0:T(8,128)}, f32[448,128]{1,0:T(8,128)S(1)}, u32[]{:S(2)}, u32[]{:S(2)}) collective-permute-start(f32[448,128]{1,0:T(8,128)} %added.4.refs_0_), channel_id=1, source_target_pairs={{0,2},{1,3},{2,0},{3,1},{4,6},{5,7},{6,4},{7,5},{8,10},{9,11},{10,... | collective-permute-start | bytes 688136 | tf_op jit(solution)/shard_map/ppermute | solution.py:25
  88.0 0.7 copy-start.14
  90.4 8.0 %copy-start.2 = (bf16[4608,256]{1,0:T(8,128)(2,1)S(1)}, bf16[4608,256]{1,0:T(8,128)(2,1)}, u32[]{:S(2)}) copy-start(bf16[4608,256]{1,0:T(8,128)(2,1)} %pad_maximum_fusion.taps_ref) | copy-start | bytes 7077892
  90.4 8.0 %copy-start.6 = (s32[6]{0:T(128)S(1)}, s32[6]{0:T(128)}, u32[]{:S(2)}) copy-start(s32[6]{0:T(128)} %stack.35.info_ref) | copy-start | bytes 76
  90.4 8.0 %copy-start.9 = (f32[128]{0:T(128)S(1)}, f32[128]{0:T(128)}, u32[]{:S(2)}) copy-start(f32[128]{0:T(128)} %param.12) | copy-start | bytes 1540
  90.4 21.2 %collective-permute-start.13 = (bf16[448,128]{1,0:T(8,128)(2,1)}, bf16[448,128]{1,0:T(8,128)(2,1)S(1)}, u32[]{:S(2)}, u32[]{:S(2)}) collective-permute-start(bf16[448,128]{1,0:T(8,128)(2,1)} %added.5.refs_0_), channel_id=1, source_target_pairs={{0,8},{8,0},{16,24},{24,16},{1,9},{9,1},{17,25},{25,17},{2,10},{10... | collective-permute-start | bytes 344072 | tf_op jit(solution)/shard_map/ppermute | solution.py:25
  92.0 20.2 %collective-permute-start.14 = (bf16[448,128]{1,0:T(8,128)(2,1)}, bf16[448,128]{1,0:T(8,128)(2,1)S(1)}, u32[]{:S(2)}, u32[]{:S(2)}) collective-permute-start(bf16[448,128]{1,0:T(8,128)(2,1)} %added.5.refs_0_), channel_id=1, source_target_pairs={{0,16},{8,24},{16,0},{24,8},{1,17},{9,25},{17,1},{25,9},{2,18},{10... | collective-permute-start | bytes 344072 | tf_op jit(solution)/shard_map/ppermute | solution.py:25
  94.6 17.7 %collective-permute-start.15 = (bf16[448,128]{1,0:T(8,128)(2,1)}, bf16[448,128]{1,0:T(8,128)(2,1)S(1)}, u32[]{:S(2)}, u32[]{:S(2)}) collective-permute-start(bf16[448,128]{1,0:T(8,128)(2,1)} %added.5.refs_0_), channel_id=1, source_target_pairs={{0,24},{8,16},{16,8},{24,0},{1,25},{9,17},{17,9},{25,1},{2,26},{10... | collective-permute-start | bytes 344072 | tf_op jit(solution)/shard_map/ppermute | solution.py:25
  105.0 6.6 %copy-start.13 = (bf16[448,128]{1,0:T(8,128)(2,1)S(1)}, bf16[448,128]{1,0:T(8,128)(2,1)}, u32[]{:S(2)}) copy-start(bf16[448,128]{1,0:T(8,128)(2,1)} %added.5.refs_0_) | copy-start | bytes 344068
  111.6 2.6 %collective-permute-start.16 = (bf16[448,128]{1,0:T(8,128)(2,1)S(1)}, bf16[448,128]{1,0:T(8,128)(2,1)S(1)}, u32[]{:S(2)}, u32[]{:S(2)}) collective-permute-start(bf16[448,128]{1,0:T(8,128)(2,1)S(1)} %copy-done.13), channel_id=1, source_target_pairs={{0,4},{4,0},{1,5},{5,1},{2,6},{6,2},{3,7},{7,3},{8,12},{12,8},{9,1... | collective-permute-start | bytes 344072 | tf_op jit(solution)/shard_map/ppermute | solution.py:25
  111.6 2.6 %copy-start.16 = (bf16[448,128]{1,0:T(8,128)(2,1)}, bf16[448,128]{1,0:T(8,128)(2,1)S(1)}, u32[]{:S(2)}) copy-start(bf16[448,128]{1,0:T(8,128)(2,1)S(1)} %collective-permute-done.13.refs_1_) | copy-start | bytes 344068
  111.7 2.5 %collective-permute-start.17 = (bf16[448,128]{1,0:T(8,128)(2,1)S(1)}, bf16[448,128]{1,0:T(8,128)(2,1)S(1)}, u32[]{:S(2)}, u32[]{:S(2)}) collective-permute-start(bf16[448,128]{1,0:T(8,128)(2,1)S(1)} %collective-permute-done.13.refs_1_), channel_id=1, source_target_pairs={{0,4},{4,0},{1,5},{5,1},{2,6},{6,2},{3,7},{7,3},{8,12},{12,8},{9,1... | collective-permute-start | bytes 344072 | tf_op jit(solution)/shard_map/ppermute | solution.py:25
  112.1 2.1 %copy-start.17 = (bf16[448,128]{1,0:T(8,128)(2,1)}, bf16[448,128]{1,0:T(8,128)(2,1)S(1)}, u32[]{:S(2)}) copy-start(bf16[448,128]{1,0:T(8,128)(2,1)S(1)} %collective-permute-done.14.refs_2_) | copy-start | bytes 344068
  112.1 2.0 %collective-permute-start.18 = (bf16[448,128]{1,0:T(8,128)(2,1)S(1)}, bf16[448,128]{1,0:T(8,128)(2,1)S(1)}, u32[]{:S(2)}, u32[]{:S(2)}) collective-permute-start(bf16[448,128]{1,0:T(8,128)(2,1)S(1)} %collective-permute-done.14.refs_2_), channel_id=1, source_target_pairs={{0,4},{4,0},{1,5},{5,1},{2,6},{6,2},{3,7},{7,3},{8,12},{12,8},{9,1... | collective-permute-start | bytes 344072 | tf_op jit(solution)/shard_map/ppermute | solution.py:25
  112.2 2.0 %copy-start.18 = (bf16[448,128]{1,0:T(8,128)(2,1)}, bf16[448,128]{1,0:T(8,128)(2,1)S(1)}, u32[]{:S(2)}) copy-start(bf16[448,128]{1,0:T(8,128)(2,1)S(1)} %collective-permute-done.15.refs_3_) | copy-start | bytes 344068
  112.2 2.0 %collective-permute-start.19 = (bf16[448,128]{1,0:T(8,128)(2,1)S(1)}, bf16[448,128]{1,0:T(8,128)(2,1)S(1)}, u32[]{:S(2)}, u32[]{:S(2)}) collective-permute-start(bf16[448,128]{1,0:T(8,128)(2,1)S(1)} %collective-permute-done.15.refs_3_), channel_id=1, source_target_pairs={{0,4},{4,0},{1,5},{5,1},{2,6},{6,2},{3,7},{7,3},{8,12},{12,8},{9,1... | collective-permute-start | bytes 344072 | tf_op jit(solution)/shard_map/ppermute | solution.py:25
  114.2 0.6 copy-start.19
  114.2 0.7 copy-start.20
  114.2 0.7 copy-start.21
  114.9 0.6 copy-start.22

commit v2 on v1

--- a/solution.py
+++ b/solution.py
@@ -54,26 +54,35 @@
     return count, total, mean, squares
 
 
-def stats_kernel(per, info_ref, video_ref, out_ref, sums, squares):
+def stats_kernel(per, before, info_ref, video_ref, out_ref, tail_ref, ends_ref, sums, squares):
     frames = pl.num_programs(0)
     t = pl.program_id(0)
     rows, cols, chans = video_ref.shape[2:]
     size = float(rows * cols * per)
+    lanes = 4
+    split = (cols // (8 * lanes), lanes, 8, chans)
 
     def add(y, acc):
-        return acc + jnp.sum(video_ref[0, 0, y].astype(F32).reshape(cols // 8, 8, chans), axis=0)
-
-    acc = lax.fori_loop(0, rows, add, jnp.zeros((8, chans), F32), unroll=4)
+        return acc + jnp.sum(video_ref[0, 0, y].astype(F32).reshape(split), axis=0)
+
+    start = jnp.zeros((lanes, 8, chans), F32)
+    acc = jnp.sum(lax.fori_loop(0, rows, add, start, unroll=4), axis=0)
     total = group_sum(jnp.sum(acc, axis=0, keepdims=True), per)
     mean = total / size
 
     def deviate(y, acc):
-        away = video_ref[0, 0, y].astype(F32).reshape(cols // 8, 8, chans) - mean
+        away = video_ref[0, 0, y].astype(F32).reshape(split) - mean
         return acc + jnp.sum(away * away, axis=0)
 
-    acc = lax.fori_loop(0, rows, deviate, jnp.zeros((8, chans), F32), unroll=4)
+    acc = jnp.sum(lax.fori_loop(0, rows, deviate, start, unroll=4), axis=0)
     sums[t] = jnp.broadcast_to(total, (8, chans))
     squares[t] = jnp.broadcast_to(group_sum(jnp.sum(acc, axis=0, keepdims=True), per), (8, chans))
+    ends_ref[0, t] = video_ref[0, 0, rows - 1]
+    ends_ref[1, t] = video_ref[0, 0, 0]
+
+    @pl.when(t >= frames - before)
+    def _():
+        tail_ref[0, t - (frames - before)] = video_ref[0, 0]
 
     @pl.when(t == frames - 1)
     def _():
@@ -93,11 +102,16 @@
         )
 
 
-def merge_kernel(*refs):
-    count, total, _, deviations = merged([ref[...] for ref in refs[:-1]])
-    refs[-1][...] = jnp.concatenate(
+def merge_kernel(parts_n, ends_ref, early_ref, *refs):
+    parts, (out_ref, low_ref, high_ref) = refs[:parts_n], refs[parts_n:]
+    count, total, _, deviations = merged([ref[...] for ref in parts])
+    out_ref[...] = jnp.concatenate(
         [count, total, deviations, jnp.zeros((5, count.shape[1]), F32)], axis=0
     )
+    before = early_ref.shape[1]
+    for side, ref in enumerate((low_ref, high_ref)):
+        ref[0:before] = early_ref[side]
+        ref[before:] = ends_ref[side]
 
 
 def cotangent_kernel(info_ref, cot_ref, turned_ref, bias_ref, wide):
@@ -156,8 +170,8 @@
             return carry
 
         lax.fori_loop(0, rows, inner, 0, unroll=4)
-        row(low_ref[0, f, 0], keep * has_low.astype(F32), 0, f, 0)
-        row(high_ref[0, f, 0], keep * has_high.astype(F32), 1, f, rows + 1)
+        row(low_ref[f], keep * has_low.astype(F32), 0, f, 0)
+        row(high_ref[f], keep * has_high.astype(F32), 1, f, rows + 1)
 
 
 def packed(value):
@@ -217,7 +231,7 @@
         send_refs[r - 1][...] = shards[me ^ r]
 
 
-def spread_kernel(count, info_ref, keep_ref, *refs):
+def spread_kernel(count, info_ref, after_ref, keep_ref, *refs):
     incoming, own_ref, send_refs = refs[:count], refs[count], refs[count + 1 :]
     me = info_ref[5]
     for r in range(len(send_refs) + 1):
@@ -230,28 +244,43 @@
             send_refs[r - 1][...] = packed(value)
 
 
-def add_kernel(*refs):
+def add_kernel(after_ref, *refs):
     value = refs[0][...].astype(F32)
     for ref in refs[1:-1]:
         value = value + ref[...].astype(F32)
     refs[-1][...] = packed(value) if refs[-1].dtype == BF16 else value
 
 
-def conv_kernel(t0, info_ref, act_ref, taps_ref, video_ref, bias_ref, out_ref, wide):
-    block = pl.program_id(0)
+def conv_kernel(t0, y0, info_ref, after_ref, act_ref, kernel_ref, video_ref, bias_ref, *refs):
+    out_ref, token_ref, wide = refs[-3:]
     frames_out, rows, cols, chans = out_ref.shape[1:]
+    kts, kys, kxs = kernel_ref.shape[:3]
     step = cols // TILE
-    y0 = block * rows
+    start = y0 + pl.program_id(0) * rows
+    taps = [(ky, kx) for ky in range(kys) for kx in range(kxs)]
+    used = [(f, ky, kx) for f in range(frames_out + kts - 1) for ky, kx in taps]
     left = jnp.concatenate(
         [
-            act_ref[f, pl.ds(y0 + ky, rows), kx : kx + step].reshape(rows * cols, chans)
-            for f in range(frames_out + 2)
-            for ky in range(3)
-            for kx in range(3)
+            act_ref[t0 + f, pl.ds(start + ky, rows), kx : kx + step].reshape(rows * cols, chans)
+            for f, ky, kx in used
         ],
         axis=1,
     )
-    result = jnp.dot(left, taps_ref[...], preferred_element_type=F32)
+    zero = jnp.zeros((chans, chans), BF16)
+    right = jnp.concatenate(
+        [
+            jnp.concatenate(
+                [
+                    kernel_ref[f - g, ky, kx] if 0 <= f - g < kts else zero
+                    for g in range(frames_out)
+                ],
+                axis=1,
+            )
+            for f, ky, kx in used
+        ],
+        axis=0,
+    )
+    result = jnp.dot(left, right, preferred_element_type=F32)
     for f in range(frames_out):
         keep = (t0 + f < info_ref[0]).astype(F32)
         for y in range(rows):
@@ -263,6 +292,7 @@
                 ]
             value = video_ref[0, f, y].astype(F32) + wide[slot] + bias_ref[...]
             out_ref[0, f, y] = (value * keep).astype(BF16)
+    token_ref[...] = jnp.zeros_like(token_ref)
 
 
 def body(video, lengths, norm_gain, norm_shift, kernel, conv_bias, cotangent):
@@ -285,29 +315,38 @@
         ]
     ).astype(jnp.int32)
 
-    early = shifted(video[:, frames - before :], "tm", 1)
-
     frame_spec = pl.BlockSpec((1, 1, rows, cols, chans), lambda t: (0, t, 0, 0, 0))
-    stats = pl.pallas_call(
-        functools.partial(stats_kernel, per),
+    stats, tail, ends = pl.pallas_call(
+        functools.partial(stats_kernel, per, before),
         grid=(frames,),
         in_specs=[SMEM, frame_spec],
-        out_specs=pl.BlockSpec((8, chans), lambda t: (0, 0)),
-        out_shape=jax.ShapeDtypeStruct((8, chans), F32),
+        out_specs=[
+            pl.BlockSpec((8, chans), lambda t: (0, 0)),
+            pl.BlockSpec((1, before, rows, cols, chans), lambda t: (0, 0, 0, 0, 0)),
+            pl.BlockSpec((2, frames, cols, chans), lambda t: (0, 0, 0, 0)),
+        ],
+        out_shape=[
+            jax.ShapeDtypeStruct((8, chans), F32),
+            jax.ShapeDtypeStruct((1, before, rows, cols, chans), BF16),
+            jax.ShapeDtypeStruct((2, frames, cols, chans), BF16),
+        ],
         scratch_shapes=[pltpu.VMEM((frames, 8, chans), F32), pltpu.VMEM((frames, 8, chans), F32)],
+        compiler_params=params(8),
         name="stats",
     )(info, video)
-    stats = pl.pallas_call(
-        merge_kernel,
-        in_specs=[VMEM] * tms,
-        out_specs=VMEM,
-        out_shape=jax.ShapeDtypeStruct((8, chans), F32),
+    gathered = [stats] + [swap(stats, "tm", r) for r in range(1, tms)]
+    early_ends = shifted(ends[:, frames - before :], "tm", 1)
+    early = shifted(tail, "tm", 1)
+    border = jax.ShapeDtypeStruct((before + frames, cols, chans), BF16)
+    stats, edge_low, edge_high = pl.pallas_call(
+        functools.partial(merge_kernel, tms),
+        in_specs=[VMEM] * (2 + tms),
+        out_specs=[VMEM] * 3,
+        out_shape=[jax.ShapeDtypeStruct((8, chans), F32), border, border],
+        compiler_params=params(2),
         name="merge",
-    )(stats, *[swap(stats, "tm", r) for r in range(1, tms)])
+    )(ends, early_ends, *gathered)
     parts = [stats] + [swap(stats, "space", r) for r in range(1, spaces)]
-
-    edge_low = jnp.concatenate([early[:, :, rows - 1 :], video[:, :, rows - 1 :]], axis=1)
-    edge_high = jnp.concatenate([early[:, :, :1], video[:, :, :1]], axis=1)
     low = shifted(edge_low, "space", 1)
     high = shifted(edge_high, "space", -1)
 
@@ -324,6 +363,7 @@
             jax.ShapeDtypeStruct((8, chans), F32),
         ],
         scratch_shapes=[pltpu.VMEM((4, cols, chans), F32)],
+        compiler_params=params(8),
         name="cotangent",
     )(info, cotangent)
 
@@ -335,7 +375,7 @@
             (frames + before, rows + 2, step + 2, TILE, chans), BF16
         ),
         scratch_shapes=[pltpu.VMEM((4, cols + 16, chans), F32)],
-        compiler_params=params(24),
+        compiler_params=params(8),
         name="activate",
     )(
         info,
@@ -362,34 +402,84 @@
             pltpu.VMEM((chans, count), F32),
             pltpu.VMEM((tms, dps, full, chans), F32),
         ],
-        compiler_params=params(40),
+        compiler_params=params(16),
         name="weights",
     )(info, turned, act, bias)
 
+    ANY = pl.BlockSpec(memory_space=pl.ANY)
+    block = 4
+    output = None
+    half = rows // 2
+
+    def conv(after, output, t0, y0):
+        given = [] if output is None else [output]
+        where = lambda y: (0, t0 // 2, y0 // block + y, 0, 0)
+        return pl.pallas_call(
+            functools.partial(conv_kernel, t0, y0),
+            grid=(half // block,),
+            in_specs=[
+                SMEM,
+                ANY,
+                VMEM,
+                VMEM,
+                pl.BlockSpec((1, 2, block, cols, chans), where),
+                VMEM,
+            ]
+            + [ANY] * len(given),
+            out_specs=[
+                pl.BlockSpec((1, 2, block, cols, chans), where),
+                pl.BlockSpec((8, chans), lambda y: (0, 0)),
+            ],
+            out_shape=[
+                jax.ShapeDtypeStruct(video.shape, BF16),
+                jax.ShapeDtypeStruct((8, chans), F32),
+            ],
+            scratch_shapes=[pltpu.VMEM((2 * block, cols, chans), F32)],
+            input_output_aliases={6: 0} if given else {},
+            compiler_params=params(12),
+            name="conv",
+        )(info, after, act, kernel, video, conv_bias.reshape(1, chans), *given)
+
+    pieces = [(t0, y0) for t0 in range(0, frames, 2) for y0 in range(0, rows, half)]
+
+    def cover(after, output):
+        if not pieces:
+            return output, after
+        return conv(after, output, *pieces.pop(0))
+
     incoming = [swap(send, "tm", r + 1) for r, send in enumerate(sends)]
+    output, token = cover(keep, output)
     own, *sends = pl.pallas_call(
         functools.partial(spread_kernel, len(incoming)),
-        in_specs=[SMEM] + [VMEM] * (1 + len(incoming)),
+        in_specs=[SMEM, ANY] + [VMEM] * (1 + len(incoming)),
         out_specs=[VMEM] * dps,
         out_shape=[jax.ShapeDtypeStruct((full, chans), F32)]
         + [jax.ShapeDtypeStruct((full, chans), BF16)] * (dps - 1),
+        compiler_params=params(4),
         name="spread",
-    )(info, keep, *incoming)
-
-    def added(dtype, *arrays):
+    )(info, token, keep, *incoming)
+
+    def added(dtype, after, *arrays):
         return pl.pallas_call(
             add_kernel,
-            in_specs=[VMEM] * len(arrays),
+            in_specs=[ANY] + [VMEM] * len(arrays),
             out_specs=VMEM,
             out_shape=jax.ShapeDtypeStruct((full, chans), dtype),
+            compiler_params=params(2),
             name="added",
-        )(*arrays)
-
-    total = added(F32, own, *[swap(send, "dp", r + 1) for r, send in enumerate(sends)])
+        )(after, *arrays)
+
+    incoming = [swap(send, "dp", r + 1) for r, send in enumerate(sends)]
+    output, token = cover(own, output)
+    total = added(F32, token, own, *incoming)
     by = 1
     while by < spaces:
-        total = added(F32 if 2 * by < spaces else BF16, total, swap(total, "space", by))
+        other = swap(total, "space", by)
+        output, token = cover(total, output)
         by *= 2
+        total = added(F32 if by < spaces else BF16, token, total, other)
+    while pieces:
+        output, token = cover(total, output)
     mine = [total] + [swap(total, "dp", r) for r in range(1, dps)]
     shards = {(0, r): array for r, array in enumerate(mine)}
     for q in range(1, tms):
@@ -413,45 +503,10 @@
             jax.ShapeDtypeStruct((shards_n, shard, chans), F32),
             jax.ShapeDtypeStruct((1, chans), F32),
         ],
+        compiler_params=params(4),
         name="collect",
     )(info, *[shards[key] for key in order])
 
-    zero = jnp.zeros(kernel.shape[1:], BF16)
-    taps = jnp.concatenate(
-        [
-            jnp.concatenate(
-                [
-                    kernel[f - g] if 0 <= f - g < kernel.shape[0] else zero
-                    for g in range(2)
-                ],
-                axis=-1,
-            ).reshape(-1, 2 * chans)
-            for f in range(kernel.shape[0] + 1)
-        ],
-        axis=0,
-    )
-    block = 4
-    outputs = []
-    for t0 in range(0, frames, 2):
-        outputs.append(
-            pl.pallas_call(
-                functools.partial(conv_kernel, t0),
-                grid=(rows // block,),
-                in_specs=[
-                    SMEM,
-                    VMEM,
-                    VMEM,
-                    pl.BlockSpec((1, 2, block, cols, chans), lambda y, t0=t0: (0, t0 // 2, y, 0, 0)),
-                    VMEM,
-                ],
-                out_specs=pl.BlockSpec((1, 2, block, cols, chans), lambda y: (0, 0, y, 0, 0)),
-                out_shape=jax.ShapeDtypeStruct((1, 2, rows, cols, chans), BF16),
-                scratch_shapes=[pltpu.VMEM((2 * block, cols, chans), F32)],
-                compiler_params=params(40),
-                name="conv",
-            )(info, act[t0 : t0 + 4], taps, video, conv_bias.reshape(1, chans))
-        )
-    output = jnp.concatenate(outputs, axis=1)
     return output, grad_kernel.reshape(kernel.shape), grad_bias.reshape(chans)
 
 

time: 119 us -> 89.2 us (0.75)
  local copies, waits for them, and re-layouts: 16.9 us -> 3.3 us
  other arithmetic: 11.7 us -> 0 us
  Pallas kernels: 47.2 us -> 38.5 us
  waiting for transfers between devices: 15.8 us -> 20.6 us
    concatenate x4 -> x0, other arithmetic: 11.7 us -> none  [the longest x1 8.76 us: body(): jnp.concatenate([jnp.concatenate([kernel[f - g] if 0 <= f - g < kernel.sh...]
    slice x4 -> x1, local copies, waits for them, and re-layouts: 6.12 us -> 0.01 us  [body(): early_ends = shifted(ends[:, frames - before:], 'tm', 1)]
    ppermute x17, waiting for transfers between devices: 14.6 us -> 20.6 us  [swap(): return lax.ppermute(array, axis, [(i, i ^ by) for i in range(length)])]
    pallas_call x7 -> x9, Pallas kernels: 24.2 us -> 19.6 us  [the longest x4 16.7 us: conv(): pl.pallas_call(functools.partial(conv_kernel, t0, y0), grid=(half // bloc...]
    unnamed x54 -> x14, local copies, waits for them, and re-layouts: 7.83 us -> 3.21 us
    squeeze x1 -> x0, local copies, waits for them, and re-layouts: 2.24 us -> none  [body(): kernel[f - g]]
    pallas_call x1, Pallas kernels: 5.24 us -> 3.35 us  [body(): pl.pallas_call(cotangent_kernel, grid=(frames,), in_specs=[SMEM, frame_sp...]
    pallas_call x1, Pallas kernels: 2.36 us -> 0.64 us  [body(): pl.pallas_call(functools.partial(spread_kernel, len(incoming)), in_specs=...]
  transfers between devices with their start and end apart: 20 -> 21, of which waited for: 8 -> 9; matrix products, arithmetic and copies ran while one was open for 16% -> 0% of each run, Pallas kernels for 20% -> 23%
where the time goes in v2:
time: 89.2 us; the launch traced here: 89 us
  Pallas kernels  38.5 us (43%)
  starting transfers between devices  25.1 us (28%)
  waiting for transfers between devices  20.6 us (23%)
  local copies, waits for them, and re-layouts  3.3 us (4%)
  between operations  1.52 us (2%)
    ppermute x17, waiting for transfers between devices, swap(): return lax.ppermute(array, axis, [(i, i ^ by) for i in range(length)])  20.6 us
    pallas_call x4, Pallas kernels, conv(): pl.pallas_call(functools.partial(conv_kernel, t0, y0), grid=(half // bloc...  16.7 us
    ppermute x17, starting transfers between devices, swap(): return lax.ppermute(array, axis, [(i, i ^ by) for i in range(length)])  15.7 us
    pallas_call x1, Pallas kernels, body(): pl.pallas_call(weights_kernel, in_specs=[SMEM, VMEM, VMEM, VMEM], out_spe...  9.77 us
    ppermute x4, starting transfers between devices, shifted(): lax.ppermute(array, axis, [(i, i + by) for i in range(length) if 0 <= i +...  9.36 us
    pallas_call x1, Pallas kernels, body(): pl.pallas_call(cotangent_kernel, grid=(frames,), in_specs=[SMEM, frame_sp...  3.35 us
    pallas_call x1, Pallas kernels, body(): pl.pallas_call(functools.partial(activate_kernel, spaces), in_specs=[SMEM...  3.25 us
    unnamed x14, local copies, waits for them, and re-layouts  3.21 us
  transfers between devices with their start and end apart: 21, of which 9 were waited for; matrix products, arithmetic and copies ran while one was open for 0% of the time, Pallas kernels for 23%

profile of v2, /device:TPU:0, one launch (start us, length us, event | category | flops | bytes accessed | tf_op | source)
XLA Modules:
  0.0 89.0 jit_solution(15159421581286757223)
XLA Ops:
  1.3 0.1 stack.35.info_ref
  1.4 1.6 %copy-done = bf16[1,4,16,128,128]{4,3,2,1,0:T(8,128)(2,1)S(1)} copy-done((bf16[1,4,16,128,128]{4,3,2,1,0:T(8,128)(2,1)S(1)}, bf16[1,4,16,128,128]{4,3,2,1,0:T(8,128)(2,1)}, u32[]{:S(2)}) %copy-start) | copy-done | bytes 2097176
  3.0 2.8 %stats.1 = (f32[8,128]{1,0:T(8,128)S(1)}, bf16[1,2,16,128,128]{4,3,2,1,0:T(8,128)(2,1)S(1)}, bf16[2,4,128,128]{3,2,1,0:T(8,128)(2,1)S(1)}) custom-call(s32[6]{0:T(128)S(1)} %stack.35.info_ref, bf16[1,4,16,128,128]{4,3,2,1,0:T(8,128)(2,1)S(1)} %copy-done), custom_call_target="tpu_custom_call" | custom-call | tf_op jit(solution)/shard_map/stats/pallas_call | solution.py:319
  5.7 2.5 %collective-permute-start = (bf16[1,2,16,128,128]{4,3,2,1,0:T(8,128)(2,1)S(1)}, bf16[1,2,16,128,128]{4,3,2,1,0:T(8,128)(2,1)S(1)}, u32[]{:S(2)}, u32[]{:S(2)}) collective-permute-start(bf16[1,2,16,128,128]{4,3,2,1,0:T(8,128)(2,1)S(1)} %get-tuple-element.28), channel_id=1, source_target_pairs={{0,4},{1,5},{2,6},{3,7},{8,12},{9,13},{10,14},{11,15},{16,20},{17,... | collective-permute-start | bytes 3145736 | tf_op jit(solution)/shard_map/ppermute | solution.py:30
  8.2 1.3 %collective-permute-start.1 = (bf16[2,2,128,128]{3,2,1,0:T(8,128)(2,1)S(1)}, bf16[2,2,128,128]{3,2,1,0:T(8,128)(2,1)S(1)}, u32[]{:S(2)}, u32[]{:S(2)}) collective-permute-start(bf16[2,2,128,128]{3,2,1,0:T(8,128)(2,1)S(1)} %slice.3), channel_id=1, source_target_pairs={{0,4},{1,5},{2,6},{3,7},{8,12},{9,13},{10,14},{11,15},{16,20},{17,... | collective-permute-start | bytes 393224 | tf_op jit(solution)/shard_map/ppermute | solution.py:30
  9.5 0.1 collective-permute-start.2
  9.6 1.2 %collective-permute-done.2.refs_1_ = f32[8,128]{1,0:T(8,128)S(1)} collective-permute-done((f32[8,128]{1,0:T(8,128)S(1)}, f32[8,128]{1,0:T(8,128)S(1)}, u32[]{:S(2)}, u32[]{:S(2)}) %collective-permute-start.2) | collective-permute-done | bytes 4128 | tf_op jit(solution)/shard_map/ppermute | solution.py:25
  10.8 0.0 collective-permute-done.1.early_ref
  10.8 4.3 %collective-permute-start.3 = (bf16[6,128,128]{2,1,0:T(8,128)(2,1)S(1)}, bf16[6,128,128]{2,1,0:T(8,128)(2,1)S(1)}, u32[]{:S(2)}, u32[]{:S(2)}) collective-permute-start(bf16[6,128,128]{2,1,0:T(8,128)(2,1)S(1)} %get-tuple-element.31), channel_id=1, source_target_pairs={{0,1},{1,2},{2,3},{4,5},{5,6},{6,7},{8,9},{9,10},{10,11},{12,13},{... | collective-permute-start | bytes 589832 | tf_op jit(solution)/shard_map/ppermute | solution.py:30
  15.1 1.3 %collective-permute-start.4 = (bf16[6,128,128]{2,1,0:T(8,128)(2,1)S(1)}, bf16[6,128,128]{2,1,0:T(8,128)(2,1)S(1)}, u32[]{:S(2)}, u32[]{:S(2)}) collective-permute-start(bf16[6,128,128]{2,1,0:T(8,128)(2,1)S(1)} %get-tuple-element.32), channel_id=1, source_target_pairs={{1,0},{2,1},{3,2},{5,4},{6,5},{7,6},{9,8},{10,9},{11,10},{13,12},{... | collective-permute-start | bytes 589832 | tf_op jit(solution)/shard_map/ppermute | solution.py:30
  16.4 4.7 %collective-permute-start.7 = (f32[8,128]{1,0:T(8,128)S(1)}, f32[8,128]{1,0:T(8,128)S(1)}, u32[]{:S(2)}, u32[]{:S(2)}) collective-permute-start(f32[8,128]{1,0:T(8,128)S(1)} %get-tuple-element.33.refs_0_), channel_id=1, source_target_pairs={{0,3},{1,2},{2,1},{3,0},{4,7},{5,6},{6,5},{7,4},{8,11},{9,10},{10,... | collective-permute-start | bytes 12296 | tf_op jit(solution)/shard_map/ppermute | solution.py:25
  21.2 4.7 %collective-permute-done.7.refs_3_ = f32[8,128]{1,0:T(8,128)S(1)} collective-permute-done((f32[8,128]{1,0:T(8,128)S(1)}, f32[8,128]{1,0:T(8,128)S(1)}, u32[]{:S(2)}, u32[]{:S(2)}) %collective-permute-start.7) | collective-permute-done | bytes 4128 | tf_op jit(solution)/shard_map/ppermute | solution.py:25
  25.9 0.0 collective-permute-start.5
  25.9 1.6 %copy-done.3 = bf16[1,4,16,128,128]{4,3,2,1,0:T(8,128)(2,1)S(1)} copy-done((bf16[1,4,16,128,128]{4,3,2,1,0:T(8,128)(2,1)S(1)}, bf16[1,4,16,128,128]{4,3,2,1,0:T(8,128)(2,1)}, u32[]{:S(2)}) %copy-start.3) | copy-done | bytes 2097176
  27.5 3.4 %cotangent.1 = (bf16[4,16,128,128]{3,2,1,0:T(8,128)(2,1)S(1)}, f32[8,128]{1,0:T(8,128)S(1)}) custom-call(s32[6]{0:T(128)S(1)} %stack.35.info_ref, bf16[1,4,16,128,128]{4,3,2,1,0:T(8,128)(2,1)S(1)} %copy-done.3), custom_call_target="tpu_custom_call" | custom-call | tf_op jit(solution)/shard_map/cotangent/pallas_call | solution.py:353
  30.9 0.0 collective-permute-done.6.refs_2_
  30.9 0.0 collective-permute-done.4.high_ref
  30.9 0.0 collective-permute-done.early_ref
  30.9 3.2 %activate.1.act_ref = bf16[6,18,10,16,128]{4,3,2,1,0:T(8,128)(2,1)S(1)} custom-call(s32[6]{0:T(128)S(1)} %stack.35.info_ref, bf16[1,4,16,128,128]{4,3,2,1,0:T(8,128)(2,1)S(1)} %copy-done.1, bf16[1,2,16,128,128]{4,3,2,1,0:T(8,128)(2,1)S(1)} %collective-permute-done.early_ref, bf16[6,128,128]{2,1,0:T(8,128)(2,1)S(1)} %collective-permute-done.3.low_ref, ...), custom_call_target="tpu_custom_call" | custom-call | tf_op jit(solution)/shard_map/activate/pallas_call | solution.py:370
  34.2 0.0 copy-start.2
  34.2 0.0 copy-start.4
  34.2 9.8 %weights.1 = (f32[4,448,128]{2,1,0:T(8,128)S(1)}, f32[4,448,128]{2,1,0:T(8,128)S(1)}) custom-call(s32[6]{0:T(128)S(1)} %stack.35.info_ref, bf16[4,16,128,128]{3,2,1,0:T(8,128)(2,1)S(1)} %get-tuple-element.27.turned_ref, bf16[6,18,10,16,128]{4,3,2,1,0:T(8,128)(2,1)S(1)} %activate.1.act_ref, f32[8,128]{1,0:T(8,128)S(1)} %get-tuple-element.34.bias_ref), custom_call_target="tpu_custom_call" | custom-call | tf_op jit(solution)/shard_map/weights/pallas_call | solution.py:396
  44.0 0.1 collective-permute-start.8
  44.1 4.2 %conv.4 = (bf16[1,4,16,128,128]{4,3,2,1,0:T(8,128)(2,1)}, f32[8,128]{1,0:T(8,128)S(1)}) custom-call(s32[6]{0:T(128)S(1)} %stack.35.info_ref, f32[4,448,128]{2,1,0:T(8,128)S(1)} %get-tuple-element.35.after_ref.keep_ref, bf16[6,18,10,16,128]{4,3,2,1,0:T(8,128)(2,1)S(1)} %activate.1.act_ref, bf16[3,3,3,128,128]{4,3,2,1,0:T(8,128)(2,1)S(1)} %copy-done.2, ...), custom_call_target="tpu_custom_call" | custom-call | tf_op jit(solution)/shard_map/conv/pallas_call | solution.py:417
  48.3 0.6 spread.1
  48.9 1.6 %collective-permute-start.9 = (bf16[448,128]{1,0:T(8,128)(2,1)S(1)}, bf16[448,128]{1,0:T(8,128)(2,1)S(1)}, u32[]{:S(2)}, u32[]{:S(2)}) collective-permute-start(bf16[448,128]{1,0:T(8,128)(2,1)S(1)} %get-tuple-element.41), channel_id=1, source_target_pairs={{0,8},{8,0},{16,24},{24,16},{1,9},{9,1},{17,25},{25,17},{2,10},{10... | collective-permute-start | bytes 344072 | tf_op jit(solution)/shard_map/ppermute | solution.py:25
  50.5 1.5 %collective-permute-start.10 = (bf16[448,128]{1,0:T(8,128)(2,1)S(1)}, bf16[448,128]{1,0:T(8,128)(2,1)S(1)}, u32[]{:S(2)}, u32[]{:S(2)}) collective-permute-start(bf16[448,128]{1,0:T(8,128)(2,1)S(1)} %get-tuple-element.42), channel_id=1, source_target_pairs={{0,16},{8,24},{16,0},{24,8},{1,17},{9,25},{17,1},{25,9},{2,18},{10... | collective-permute-start | bytes 344072 | tf_op jit(solution)/shard_map/ppermute | solution.py:25
  52.0 0.5 collective-permute-start.11
  52.5 4.2 %conv.5 = (bf16[1,4,16,128,128]{4,3,2,1,0:T(8,128)(2,1)}, f32[8,128]{1,0:T(8,128)S(1)}) custom-call(s32[6]{0:T(128)S(1)} %stack.35.info_ref, f32[448,128]{1,0:T(8,128)S(1)} %get-tuple-element.38.after_ref.refs_0_, bf16[6,18,10,16,128]{4,3,2,1,0:T(8,128)(2,1)S(1)} %activate.1.act_ref, ...), custom_call_target="tpu_custom_call", output_to_operand_aliasing={{0}: (6, {})} | custom-call | tf_op jit(solution)/shard_map/conv/pallas_call | solution.py:417
  56.7 0.0 collective-permute-done.9.refs_1_
  56.7 1.5 %collective-permute-done.10.refs_2_ = bf16[448,128]{1,0:T(8,128)(2,1)S(1)} collective-permute-done((bf16[448,128]{1,0:T(8,128)(2,1)S(1)}, bf16[448,128]{1,0:T(8,128)(2,1)S(1)}, u32[]{:S(2)}, u32[]{:S(2)}) %collective-permute-start.10) | collective-permute-done | bytes 114720 | tf_op jit(solution)/shard_map/ppermute | solution.py:25
  58.2 0.1 added.3.after_ref.refs_0_
  58.2 2.1 %collective-permute-start.12 = (f32[448,128]{1,0:T(8,128)S(1)}, f32[448,128]{1,0:T(8,128)S(1)}, u32[]{:S(2)}, u32[]{:S(2)}) collective-permute-start(f32[448,128]{1,0:T(8,128)S(1)} %added.3.after_ref.refs_0_), channel_id=1, source_target_pairs={{0,1},{1,0},{2,3},{3,2},{4,5},{5,4},{6,7},{7,6},{8,9},{9,8},{10,11... | collective-permute-start | bytes 688136 | tf_op jit(solution)/shard_map/ppermute | solution.py:25
  60.3 4.2 %conv.6 = (bf16[1,4,16,128,128]{4,3,2,1,0:T(8,128)(2,1)}, f32[8,128]{1,0:T(8,128)S(1)}) custom-call(s32[6]{0:T(128)S(1)} %stack.35.info_ref, f32[448,128]{1,0:T(8,128)S(1)} %added.3.after_ref.refs_0_, bf16[6,18,10,16,128]{4,3,2,1,0:T(8,128)(2,1)S(1)} %activate.1.act_ref, bf16[3,3,3,128,128]{4,3,2,1,0:T(8,128)(2,1)S(1)} %copy-done.2, ...), custom_call_target="tpu_custom_call", output_to_operand_aliasing={{0}: (6, {})} | custom-call | tf_op jit(solution)/shard_map/conv/pallas_call | solution.py:417
  64.5 0.5 collective-permute-done.12.refs_1_
  65.0 1.0 %collective-permute-start.13 = (f32[448,128]{1,0:T(8,128)S(1)}, f32[448,128]{1,0:T(8,128)S(1)}, u32[]{:S(2)}, u32[]{:S(2)}) collective-permute-start(f32[448,128]{1,0:T(8,128)S(1)} %added.4.after_ref.refs_0_), channel_id=1, source_target_pairs={{0,2},{1,3},{2,0},{3,1},{4,6},{5,7},{6,4},{7,5},{8,10},{9,11},{10,... | collective-permute-start | bytes 688136 | tf_op jit(solution)/shard_map/ppermute | solution.py:25
  66.0 4.2 %conv.7 = (bf16[1,4,16,128,128]{4,3,2,1,0:T(8,128)(2,1)}, f32[8,128]{1,0:T(8,128)S(1)}) custom-call(s32[6]{0:T(128)S(1)} %stack.35.info_ref, f32[448,128]{1,0:T(8,128)S(1)} %added.4.after_ref.refs_0_, bf16[6,18,10,16,128]{4,3,2,1,0:T(8,128)(2,1)S(1)} %activate.1.act_ref, bf16[3,3,3,128,128]{4,3,2,1,0:T(8,128)(2,1)S(1)} %copy-done.2, ...), custom_call_target="tpu_custom_call", output_to_operand_aliasing={{0}: (6, {})} | custom-call | tf_op jit(solution)/shard_map/conv/pallas_call | solution.py:417
  70.2 6.5 %collective-permute-done.13.refs_1_ = f32[448,128]{1,0:T(8,128)S(1)} collective-permute-done((f32[448,128]{1,0:T(8,128)S(1)}, f32[448,128]{1,0:T(8,128)S(1)}, u32[]{:S(2)}, u32[]{:S(2)}) %collective-permute-start.13) | collective-permute-done | bytes 229408 | tf_op jit(solution)/shard_map/ppermute | solution.py:25
  76.8 2.4 %collective-permute-start.16 = (bf16[448,128]{1,0:T(8,128)(2,1)S(1)}, bf16[448,128]{1,0:T(8,128)(2,1)S(1)}, u32[]{:S(2)}, u32[]{:S(2)}) collective-permute-start(bf16[448,128]{1,0:T(8,128)(2,1)S(1)} %added.5.refs_0_), channel_id=1, source_target_pairs={{0,24},{8,16},{16,8},{24,0},{1,25},{9,17},{17,9},{25,1},{2,26},{10... | collective-permute-start | bytes 344072 | tf_op jit(solution)/shard_map/ppermute | solution.py:25
  79.2 1.7 %collective-permute-start.15 = (bf16[448,128]{1,0:T(8,128)(2,1)S(1)}, bf16[448,128]{1,0:T(8,128)(2,1)S(1)}, u32[]{:S(2)}, u32[]{:S(2)}) collective-permute-start(bf16[448,128]{1,0:T(8,128)(2,1)S(1)} %added.5.refs_0_), channel_id=1, source_target_pairs={{0,16},{8,24},{16,0},{24,8},{1,17},{9,25},{17,1},{25,9},{2,18},{10... | collective-permute-start | bytes 344072 | tf_op jit(solution)/shard_map/ppermute | solution.py:25
  80.9 2.3 %collective-permute-done.16.refs_3_ = bf16[448,128]{1,0:T(8,128)(2,1)S(1)} collective-permute-done((bf16[448,128]{1,0:T(8,128)(2,1)S(1)}, bf16[448,128]{1,0:T(8,128)(2,1)S(1)}, u32[]{:S(2)}, u32[]{:S(2)}) %collective-permute-start.16) | collective-permute-done | bytes 114720 | tf_op jit(solution)/shard_map/ppermute | solution.py:25
  83.2 0.0 collective-permute-start.20
  83.2 1.1 %collective-permute-done.15.refs_2_ = bf16[448,128]{1,0:T(8,128)(2,1)S(1)} collective-permute-done((bf16[448,128]{1,0:T(8,128)(2,1)S(1)}, bf16[448,128]{1,0:T(8,128)(2,1)S(1)}, u32[]{:S(2)}, u32[]{:S(2)}) %collective-permute-start.15) | collective-permute-done | bytes 114720 | tf_op jit(solution)/shard_map/ppermute | solution.py:25
  84.4 1.4 %collective-permute-done.14.refs_1_ = bf16[448,128]{1,0:T(8,128)(2,1)S(1)} collective-permute-done((bf16[448,128]{1,0:T(8,128)(2,1)S(1)}, bf16[448,128]{1,0:T(8,128)(2,1)S(1)}, u32[]{:S(2)}, u32[]{:S(2)}) %collective-permute-start.14) | collective-permute-done | bytes 114720 | tf_op jit(solution)/shard_map/ppermute | solution.py:25
  85.8 0.0 collective-permute-start.18
  85.8 0.0 collective-permute-done.17.refs_4_
  85.8 1.3 %collective-permute-done.18.refs_5_ = bf16[448,128]{1,0:T(8,128)(2,1)S(1)} collective-permute-done((bf16[448,128]{1,0:T(8,128)(2,1)S(1)}, bf16[448,128]{1,0:T(8,128)(2,1)S(1)}, u32[]{:S(2)}, u32[]{:S(2)}) %collective-permute-start.18) | collective-permute-done | bytes 114720 | tf_op jit(solution)/shard_map/ppermute | solution.py:25
  87.1 1.9 %collect.1 = (f32[8,432,128]{2,1,0:T(8,128)}, f32[1,128]{1,0:T(1,128)}) custom-call(s32[6]{0:T(128)S(1)} %stack.35.info_ref, bf16[448,128]{1,0:T(8,128)(2,1)S(1)} %added.5.refs_0_, bf16[448,128]{1,0:T(8,128)(2,1)S(1)} %collective-permute-done.14.refs_1_, bf16[448,128]{1,0:T(8,128)(2,1)S(1)} %collective-permute-done.15.refs_2_, ...), custom_call_target="tpu_custom_call" | custom-call | tf_op jit(solution)/shard_map/collect/pallas_call | solution.py:498
  (24 shorter events, 0.1 us)
Async XLA Ops:
  1.4 1.6 %copy-start = (bf16[1,4,16,128,128]{4,3,2,1,0:T(8,128)(2,1)S(1)}, bf16[1,4,16,128,128]{4,3,2,1,0:T(8,128)(2,1)}, u32[]{:S(2)}) copy-start(bf16[1,4,16,128,128]{4,3,2,1,0:T(8,128)(2,1)} %video_ref.11) | copy-start | bytes 6291460
  3.0 27.9 %copy-start.1 = (bf16[1,4,16,128,128]{4,3,2,1,0:T(8,128)(2,1)S(1)}, bf16[1,4,16,128,128]{4,3,2,1,0:T(8,128)(2,1)}, u32[]{:S(2)}) copy-start(bf16[1,4,16,128,128]{4,3,2,1,0:T(8,128)(2,1)} %video_ref.11) | copy-start | bytes 6291460
  3.0 28.0 %copy-start.5 = (f32[128]{0:T(128)S(1)}, f32[128]{0:T(128)}, u32[]{:S(2)}) copy-start(f32[128]{0:T(128)} %param.9) | copy-start | bytes 1540
  3.0 28.0 %copy-start.6 = (f32[128]{0:T(128)S(1)}, f32[128]{0:T(128)}, u32[]{:S(2)}) copy-start(f32[128]{0:T(128)} %param.10) | copy-start | bytes 1540
  5.7 25.2 %collective-permute-start = (bf16[1,2,16,128,128]{4,3,2,1,0:T(8,128)(2,1)S(1)}, bf16[1,2,16,128,128]{4,3,2,1,0:T(8,128)(2,1)S(1)}, u32[]{:S(2)}, u32[]{:S(2)}) collective-permute-start(bf16[1,2,16,128,128]{4,3,2,1,0:T(8,128)(2,1)S(1)} %get-tuple-element.28), channel_id=1, source_target_pairs={{0,4},{1,5},{2,6},{3,7},{8,12},{9,13},{10,14},{11,15},{16,20},{17,... | collective-permute-start | bytes 3145736 | tf_op jit(solution)/shard_map/ppermute | solution.py:30
  8.2 2.5 %collective-permute-start.1 = (bf16[2,2,128,128]{3,2,1,0:T(8,128)(2,1)S(1)}, bf16[2,2,128,128]{3,2,1,0:T(8,128)(2,1)S(1)}, u32[]{:S(2)}, u32[]{:S(2)}) collective-permute-start(bf16[2,2,128,128]{3,2,1,0:T(8,128)(2,1)S(1)} %slice.3), channel_id=1, source_target_pairs={{0,4},{1,5},{2,6},{3,7},{8,12},{9,13},{10,14},{11,15},{16,20},{17,... | collective-permute-start | bytes 393224 | tf_op jit(solution)/shard_map/ppermute | solution.py:30
  9.5 1.2 %collective-permute-start.2 = (f32[8,128]{1,0:T(8,128)S(1)}, f32[8,128]{1,0:T(8,128)S(1)}, u32[]{:S(2)}, u32[]{:S(2)}) collective-permute-start(f32[8,128]{1,0:T(8,128)S(1)} %get-tuple-element.30.refs_0_), channel_id=1, source_target_pairs={{0,4},{4,0},{1,5},{5,1},{2,6},{6,2},{3,7},{7,3},{8,12},{12,8},{9,1... | collective-permute-start | bytes 12296 | tf_op jit(solution)/shard_map/ppermute | solution.py:25
  10.8 20.1 %collective-permute-start.3 = (bf16[6,128,128]{2,1,0:T(8,128)(2,1)S(1)}, bf16[6,128,128]{2,1,0:T(8,128)(2,1)S(1)}, u32[]{:S(2)}, u32[]{:S(2)}) collective-permute-start(bf16[6,128,128]{2,1,0:T(8,128)(2,1)S(1)} %get-tuple-element.31), channel_id=1, source_target_pairs={{0,1},{1,2},{2,3},{4,5},{5,6},{6,7},{8,9},{9,10},{10,11},{12,13},{... | collective-permute-start | bytes 589832 | tf_op jit(solution)/shard_map/ppermute | solution.py:30
  15.1 15.8 %collective-permute-start.4 = (bf16[6,128,128]{2,1,0:T(8,128)(2,1)S(1)}, bf16[6,128,128]{2,1,0:T(8,128)(2,1)S(1)}, u32[]{:S(2)}, u32[]{:S(2)}) collective-permute-start(bf16[6,128,128]{2,1,0:T(8,128)(2,1)S(1)} %get-tuple-element.32), channel_id=1, source_target_pairs={{1,0},{2,1},{3,2},{5,4},{6,5},{7,6},{9,8},{10,9},{11,10},{13,12},{... | collective-permute-start | bytes 589832 | tf_op jit(solution)/shard_map/ppermute | solution.py:30
  16.4 9.5 %collective-permute-start.7 = (f32[8,128]{1,0:T(8,128)S(1)}, f32[8,128]{1,0:T(8,128)S(1)}, u32[]{:S(2)}, u32[]{:S(2)}) collective-permute-start(f32[8,128]{1,0:T(8,128)S(1)} %get-tuple-element.33.refs_0_), channel_id=1, source_target_pairs={{0,3},{1,2},{2,1},{3,0},{4,7},{5,6},{6,5},{7,4},{8,11},{9,10},{10,... | collective-permute-start | bytes 12296 | tf_op jit(solution)/shard_map/ppermute | solution.py:25
  21.2 9.7 %collective-permute-start.6 = (f32[8,128]{1,0:T(8,128)S(1)}, f32[8,128]{1,0:T(8,128)S(1)}, u32[]{:S(2)}, u32[]{:S(2)}) collective-permute-start(f32[8,128]{1,0:T(8,128)S(1)} %get-tuple-element.33.refs_0_), channel_id=1, source_target_pairs={{0,2},{1,3},{2,0},{3,1},{4,6},{5,7},{6,4},{7,5},{8,10},{9,11},{10,... | collective-permute-start | bytes 12296 | tf_op jit(solution)/shard_map/ppermute | solution.py:25
  25.9 5.0 %collective-permute-start.5 = (f32[8,128]{1,0:T(8,128)S(1)}, f32[8,128]{1,0:T(8,128)S(1)}, u32[]{:S(2)}, u32[]{:S(2)}) collective-permute-start(f32[8,128]{1,0:T(8,128)S(1)} %get-tuple-element.33.refs_0_), channel_id=1, source_target_pairs={{0,1},{1,0},{2,3},{3,2},{4,5},{5,4},{6,7},{7,6},{8,9},{9,8},{10,11... | collective-permute-start | bytes 12296 | tf_op jit(solution)/shard_map/ppermute | solution.py:25
  25.9 1.6 %copy-start.3 = (bf16[1,4,16,128,128]{4,3,2,1,0:T(8,128)(2,1)S(1)}, bf16[1,4,16,128,128]{4,3,2,1,0:T(8,128)(2,1)}, u32[]{:S(2)}) copy-start(bf16[1,4,16,128,128]{4,3,2,1,0:T(8,128)(2,1)} %cot_ref.1) | copy-start | bytes 6291460
  34.2 9.9 %copy-start.2 = (bf16[3,3,3,128,128]{4,3,2,1,0:T(8,128)(2,1)S(1)}, bf16[3,3,3,128,128]{4,3,2,1,0:T(8,128)(2,1)}, u32[]{:S(2)}) copy-start(bf16[3,3,3,128,128]{4,3,2,1,0:T(8,128)(2,1)} %kernel_ref.7) | copy-start | bytes 2654212
  34.2 9.9 %copy-start.4 = (f32[128]{0:T(128)S(1)}, f32[128]{0:T(128)}, u32[]{:S(2)}) copy-start(f32[128]{0:T(128)} %param.12) | copy-start | bytes 1540
  44.0 4.3 %collective-permute-start.8 = (f32[4,448,128]{2,1,0:T(8,128)S(1)}, f32[4,448,128]{2,1,0:T(8,128)S(1)}, u32[]{:S(2)}, u32[]{:S(2)}) collective-permute-start(f32[4,448,128]{2,1,0:T(8,128)S(1)} %get-tuple-element.37), channel_id=1, source_target_pairs={{0,4},{4,0},{1,5},{5,1},{2,6},{6,2},{3,7},{7,3},{8,12},{12,8},{9,1... | collective-permute-start | bytes 2752520 | tf_op jit(solution)/shard_map/ppermute | solution.py:25
  48.9 7.7 %collective-permute-start.9 = (bf16[448,128]{1,0:T(8,128)(2,1)S(1)}, bf16[448,128]{1,0:T(8,128)(2,1)S(1)}, u32[]{:S(2)}, u32[]{:S(2)}) collective-permute-start(bf16[448,128]{1,0:T(8,128)(2,1)S(1)} %get-tuple-element.41), channel_id=1, source_target_pairs={{0,8},{8,0},{16,24},{24,16},{1,9},{9,1},{17,25},{25,17},{2,10},{10... | collective-permute-start | bytes 344072 | tf_op jit(solution)/shard_map/ppermute | solution.py:25
  50.5 7.7 %collective-permute-start.10 = (bf16[448,128]{1,0:T(8,128)(2,1)S(1)}, bf16[448,128]{1,0:T(8,128)(2,1)S(1)}, u32[]{:S(2)}, u32[]{:S(2)}) collective-permute-start(bf16[448,128]{1,0:T(8,128)(2,1)S(1)} %get-tuple-element.42), channel_id=1, source_target_pairs={{0,16},{8,24},{16,0},{24,8},{1,17},{9,25},{17,1},{25,9},{2,18},{10... | collective-permute-start | bytes 344072 | tf_op jit(solution)/shard_map/ppermute | solution.py:25
  52.0 6.2 %collective-permute-start.11 = (bf16[448,128]{1,0:T(8,128)(2,1)S(1)}, bf16[448,128]{1,0:T(8,128)(2,1)S(1)}, u32[]{:S(2)}, u32[]{:S(2)}) collective-permute-start(bf16[448,128]{1,0:T(8,128)(2,1)S(1)} %get-tuple-element.43), channel_id=1, source_target_pairs={{0,24},{8,16},{16,8},{24,0},{1,25},{9,17},{17,9},{25,1},{2,26},{10... | collective-permute-start | bytes 344072 | tf_op jit(solution)/shard_map/ppermute | solution.py:25
  58.2 6.8 %collective-permute-start.12 = (f32[448,128]{1,0:T(8,128)S(1)}, f32[448,128]{1,0:T(8,128)S(1)}, u32[]{:S(2)}, u32[]{:S(2)}) collective-permute-start(f32[448,128]{1,0:T(8,128)S(1)} %added.3.after_ref.refs_0_), channel_id=1, source_target_pairs={{0,1},{1,0},{2,3},{3,2},{4,5},{5,4},{6,7},{7,6},{8,9},{9,8},{10,11... | collective-permute-start | bytes 688136 | tf_op jit(solution)/shard_map/ppermute | solution.py:25
  65.0 11.7 %collective-permute-start.13 = (f32[448,128]{1,0:T(8,128)S(1)}, f32[448,128]{1,0:T(8,128)S(1)}, u32[]{:S(2)}, u32[]{:S(2)}) collective-permute-start(f32[448,128]{1,0:T(8,128)S(1)} %added.4.after_ref.refs_0_), channel_id=1, source_target_pairs={{0,2},{1,3},{2,0},{3,1},{4,6},{5,7},{6,4},{7,5},{8,10},{9,11},{10,... | collective-permute-start | bytes 688136 | tf_op jit(solution)/shard_map/ppermute | solution.py:25
  76.8 6.4 %collective-permute-start.16 = (bf16[448,128]{1,0:T(8,128)(2,1)S(1)}, bf16[448,128]{1,0:T(8,128)(2,1)S(1)}, u32[]{:S(2)}, u32[]{:S(2)}) collective-permute-start(bf16[448,128]{1,0:T(8,128)(2,1)S(1)} %added.5.refs_0_), channel_id=1, source_target_pairs={{0,24},{8,16},{16,8},{24,0},{1,25},{9,17},{17,9},{25,1},{2,26},{10... | collective-permute-start | bytes 344072 | tf_op jit(solution)/shard_map/ppermute | solution.py:25
  79.2 5.1 %collective-permute-start.15 = (bf16[448,128]{1,0:T(8,128)(2,1)S(1)}, bf16[448,128]{1,0:T(8,128)(2,1)S(1)}, u32[]{:S(2)}, u32[]{:S(2)}) collective-permute-start(bf16[448,128]{1,0:T(8,128)(2,1)S(1)} %added.5.refs_0_), channel_id=1, source_target_pairs={{0,16},{8,24},{16,0},{24,8},{1,17},{9,25},{17,1},{25,9},{2,18},{10... | collective-permute-start | bytes 344072 | tf_op jit(solution)/shard_map/ppermute | solution.py:25
  80.9 4.8 %collective-permute-start.14 = (bf16[448,128]{1,0:T(8,128)(2,1)S(1)}, bf16[448,128]{1,0:T(8,128)(2,1)S(1)}, u32[]{:S(2)}, u32[]{:S(2)}) collective-permute-start(bf16[448,128]{1,0:T(8,128)(2,1)S(1)} %added.5.refs_0_), channel_id=1, source_target_pairs={{0,8},{8,0},{16,24},{24,16},{1,9},{9,1},{17,25},{25,17},{2,10},{10... | collective-permute-start | bytes 344072 | tf_op jit(solution)/shard_map/ppermute | solution.py:25
  80.9 4.8 %collective-permute-start.17 = (bf16[448,128]{1,0:T(8,128)(2,1)S(1)}, bf16[448,128]{1,0:T(8,128)(2,1)S(1)}, u32[]{:S(2)}, u32[]{:S(2)}) collective-permute-start(bf16[448,128]{1,0:T(8,128)(2,1)S(1)} %added.5.refs_0_), channel_id=1, source_target_pairs={{0,4},{4,0},{1,5},{5,1},{2,6},{6,2},{3,7},{7,3},{8,12},{12,8},{9,1... | collective-permute-start | bytes 344072 | tf_op jit(solution)/shard_map/ppermute | solution.py:25
  83.2 2.6 %collective-permute-start.20 = (bf16[448,128]{1,0:T(8,128)(2,1)S(1)}, bf16[448,128]{1,0:T(8,128)(2,1)S(1)}, u32[]{:S(2)}, u32[]{:S(2)}) collective-permute-start(bf16[448,128]{1,0:T(8,128)(2,1)S(1)} %collective-permute-done.16.refs_3_), channel_id=1, source_target_pairs={{0,4},{4,0},{1,5},{5,1},{2,6},{6,2},{3,7},{7,3},{8,12},{12,8},{9,1... | collective-permute-start | bytes 344072 | tf_op jit(solution)/shard_map/ppermute | solution.py:25
  84.4 1.4 %collective-permute-start.19 = (bf16[448,128]{1,0:T(8,128)(2,1)S(1)}, bf16[448,128]{1,0:T(8,128)(2,1)S(1)}, u32[]{:S(2)}, u32[]{:S(2)}) collective-permute-start(bf16[448,128]{1,0:T(8,128)(2,1)S(1)} %collective-permute-done.15.refs_2_), channel_id=1, source_target_pairs={{0,4},{4,0},{1,5},{5,1},{2,6},{6,2},{3,7},{7,3},{8,12},{12,8},{9,1... | collective-permute-start | bytes 344072 | tf_op jit(solution)/shard_map/ppermute | solution.py:25
  85.8 1.3 %collective-permute-start.18 = (bf16[448,128]{1,0:T(8,128)(2,1)S(1)}, bf16[448,128]{1,0:T(8,128)(2,1)S(1)}, u32[]{:S(2)}, u32[]{:S(2)}) collective-permute-start(bf16[448,128]{1,0:T(8,128)(2,1)S(1)} %collective-permute-done.14.refs_1_), channel_id=1, source_target_pairs={{0,4},{4,0},{1,5},{5,1},{2,6},{6,2},{3,7},{7,3},{8,12},{12,8},{9,1... | collective-permute-start | bytes 344072 | tf_op jit(solution)/shard_map/ppermute | solution.py:25

commit v3 on v2

--- a/solution.py
+++ b/solution.py
@@ -7,11 +7,13 @@
 from jax.experimental.pallas import tpu as pltpu
 from jax.sharding import PartitionSpec as P
 
+
 GROUPS = 32
 TILE = 16
 F32 = jnp.float32
 BF16 = jnp.bfloat16
 VMEM = pl.BlockSpec(memory_space=pltpu.VMEM)
+ANY = pl.BlockSpec(memory_space=pl.ANY)
 SMEM = pl.BlockSpec(memory_space=pltpu.SMEM)
 
 
@@ -251,14 +253,31 @@
     refs[-1][...] = packed(value) if refs[-1].dtype == BF16 else value
 
 
-def conv_kernel(t0, y0, info_ref, after_ref, act_ref, kernel_ref, video_ref, bias_ref, *refs):
+def taps_kernel(after_ref, kernel_ref, out_ref):
+    kts, kys, kxs, chans = kernel_ref.shape[:4]
+    pair = out_ref.shape[1] // chans
+    zero = jnp.zeros((kys * kxs * chans, chans), BF16)
+    span = kys * kxs * chans
+    for f in range(kts + pair - 1):
+        for g in range(pair):
+            if 0 <= f - g < kts:
+                value = kernel_ref[f - g].reshape(span, chans)
+            else:
+                value = zero
+            out_ref[f * span : (f + 1) * span, g * chans : (g + 1) * chans] = value
+
+
+def conv_kernel(t0, y0, info_ref, after_ref, act_ref, taps_ref, video_ref, bias_ref, *refs):
     out_ref, token_ref, wide = refs[-3:]
     frames_out, rows, cols, chans = out_ref.shape[1:]
-    kts, kys, kxs = kernel_ref.shape[:3]
     step = cols // TILE
     start = y0 + pl.program_id(0) * rows
-    taps = [(ky, kx) for ky in range(kys) for kx in range(kxs)]
-    used = [(f, ky, kx) for f in range(frames_out + kts - 1) for ky, kx in taps]
+    used = [
+        (f, ky, kx)
+        for f in range(taps_ref.shape[0] // (9 * chans))
+        for ky in range(3)
+        for kx in range(3)
+    ]
     left = jnp.concatenate(
         [
             act_ref[t0 + f, pl.ds(start + ky, rows), kx : kx + step].reshape(rows * cols, chans)
@@ -266,21 +285,7 @@
         ],
         axis=1,
     )
-    zero = jnp.zeros((chans, chans), BF16)
-    right = jnp.concatenate(
-        [
-            jnp.concatenate(
-                [
-                    kernel_ref[f - g, ky, kx] if 0 <= f - g < kts else zero
-                    for g in range(frames_out)
-                ],
-                axis=1,
-            )
-            for f, ky, kx in used
-        ],
-        axis=0,
-    )
-    result = jnp.dot(left, right, preferred_element_type=F32)
+    result = jnp.dot(left, taps_ref[...], preferred_element_type=F32)
     for f in range(frames_out):
         keep = (t0 + f < info_ref[0]).astype(F32)
         for y in range(rows):
@@ -295,7 +300,7 @@
     token_ref[...] = jnp.zeros_like(token_ref)
 
 
-def body(video, lengths, norm_gain, norm_shift, kernel, conv_bias, cotangent):
+def step_of(video, lengths, norm_gain, norm_shift, kernel, conv_bias, cotangent):
     frames, rows, cols, chans = video.shape[1:]
     per = chans // GROUPS
     step = cols // TILE
@@ -333,7 +338,7 @@
         scratch_shapes=[pltpu.VMEM((frames, 8, chans), F32), pltpu.VMEM((frames, 8, chans), F32)],
         compiler_params=params(8),
         name="stats",
-    )(info, video)
+    )(info, pltpu.with_memory_space_constraint(video, pltpu.HBM))
     gathered = [stats] + [swap(stats, "tm", r) for r in range(1, tms)]
     early_ends = shifted(ends[:, frames - before :], "tm", 1)
     early = shifted(tail, "tm", 1)
@@ -349,6 +354,17 @@
     parts = [stats] + [swap(stats, "space", r) for r in range(1, spaces)]
     low = shifted(edge_low, "space", 1)
     high = shifted(edge_high, "space", -1)
+    pair = 2
+    taps = pl.pallas_call(
+        taps_kernel,
+        in_specs=[ANY, VMEM],
+        out_specs=VMEM,
+        out_shape=jax.ShapeDtypeStruct(
+            ((kernel.shape[0] + pair - 1) * 9 * chans, pair * chans), BF16
+        ),
+        compiler_params=params(2),
+        name="taps",
+    )(ends, kernel)
 
     turned, bias = pl.pallas_call(
         cotangent_kernel,
@@ -365,7 +381,7 @@
         scratch_shapes=[pltpu.VMEM((4, cols, chans), F32)],
         compiler_params=params(8),
         name="cotangent",
-    )(info, cotangent)
+    )(info, pltpu.with_memory_space_constraint(cotangent, pltpu.HBM))
 
     act = pl.pallas_call(
         functools.partial(activate_kernel, spaces),
@@ -406,10 +422,9 @@
         name="weights",
     )(info, turned, act, bias)
 
-    ANY = pl.BlockSpec(memory_space=pl.ANY)
     block = 4
     output = None
-    half = rows // 2
+    half = block
 
     def conv(after, output, t0, y0):
         given = [] if output is None else [output]
@@ -438,17 +453,17 @@
             input_output_aliases={6: 0} if given else {},
             compiler_params=params(12),
             name="conv",
-        )(info, after, act, kernel, video, conv_bias.reshape(1, chans), *given)
+        )(info, after, act, taps, video, conv_bias.reshape(1, chans), *given)
 
     pieces = [(t0, y0) for t0 in range(0, frames, 2) for y0 in range(0, rows, half)]
 
-    def cover(after, output):
-        if not pieces:
-            return output, after
-        return conv(after, output, *pieces.pop(0))
+    def cover(after, output, number):
+        for _ in range(min(number, len(pieces))):
+            output, after = conv(after, output, *pieces.pop(0))
+        return output, after
 
     incoming = [swap(send, "tm", r + 1) for r, send in enumerate(sends)]
-    output, token = cover(keep, output)
+    output, token = cover(keep, output, 2)
     own, *sends = pl.pallas_call(
         functools.partial(spread_kernel, len(incoming)),
         in_specs=[SMEM, ANY] + [VMEM] * (1 + len(incoming)),
@@ -470,17 +485,16 @@
         )(after, *arrays)
 
     incoming = [swap(send, "dp", r + 1) for r, send in enumerate(sends)]
-    output, token = cover(own, output)
-    total = added(F32, token, own, *incoming)
+    output, token = cover(own, output, 1)
+    total = added(F32 if spaces > 2 else BF16, token, own, *incoming)
     by = 1
     while by < spaces:
         other = swap(total, "space", by)
-        output, token = cover(total, output)
+        output, token = cover(total, output, 2)
         by *= 2
-        total = added(F32 if by < spaces else BF16, token, total, other)
-    while pieces:
-        output, token = cover(total, output)
+        total = added(F32 if 2 * by < spaces else BF16, token, total, other)
     mine = [total] + [swap(total, "dp", r) for r in range(1, dps)]
+    output, token = cover(total, output, len(pieces))
     shards = {(0, r): array for r, array in enumerate(mine)}
     for q in range(1, tms):
         for r, array in enumerate(mine):
@@ -512,7 +526,7 @@
 
 def solution(mesh):
     return jax.shard_map(
-        body,
+        step_of,
         mesh=mesh,
         in_specs=(
             P("dp", "tm", "space", None, None),

time: 89.2 us -> 87 us (0.975)
  Pallas kernels: 38.5 us -> 45.9 us
  waiting for transfers between devices: 20.6 us -> 15.3 us
  local copies, waits for them, and re-layouts: 3.3 us -> 0.3 us
  starting transfers between devices: 25.1 us -> 23.6 us
    ppermute x17, waiting for transfers between devices: 20.6 us -> 15.3 us  [swap(): return lax.ppermute(array, axis, [(i, i ^ by) for i in range(length)])]
    pallas_call x4 -> x8, Pallas kernels: 16.7 us -> 21.5 us  [conv(): pl.pallas_call(functools.partial(conv_kernel, t0, y0), grid=(half // bloc...]
    unnamed x14 -> x10, local copies, waits for them, and re-layouts: 3.21 us -> 0.2 us
    pallas_call x7 -> x8, Pallas kernels: 21.7 us -> 24.3 us  [the longest x1 9.95 us: step_of(): pl.pallas_call(weights_kernel, in_specs=[SMEM, VMEM, VMEM, VMEM], out_spe...]
    ppermute x17, starting transfers between devices: 15.7 us -> 14.3 us  [swap(): return lax.ppermute(array, axis, [(i, i ^ by) for i in range(length)])]
  transfers between devices with their start and end apart: 21 -> 21, of which waited for: 9 -> 7; matrix products, arithmetic and copies ran while one was open for 0% -> 0% of each run, Pallas kernels for 23% -> 30%
where the time goes in v3:
time: 87 us; the launch traced here: 86.7 us
  Pallas kernels  45.9 us (53%)
  starting transfers between devices  23.6 us (27%)
  waiting for transfers between devices  15.3 us (18%)
  between operations  1.53 us (2%)
    pallas_call x8, Pallas kernels, conv(): pl.pallas_call(functools.partial(conv_kernel, t0, y0), grid=(half // bloc...  21.5 us
    ppermute x17, waiting for transfers between devices, swap(): return lax.ppermute(array, axis, [(i, i ^ by) for i in range(length)])  15.3 us
    ppermute x17, starting transfers between devices, swap(): return lax.ppermute(array, axis, [(i, i ^ by) for i in range(length)])  14.3 us
    pallas_call x1, Pallas kernels, step_of(): pl.pallas_call(weights_kernel, in_specs=[SMEM, VMEM, VMEM, VMEM], out_spe...  9.95 us
    ppermute x4, starting transfers between devices, shifted(): lax.ppermute(array, axis, [(i, i + by) for i in range(length) if 0 <= i +...  9.36 us
    pallas_call x1, Pallas kernels, step_of(): pl.pallas_call(cotangent_kernel, grid=(frames,), in_specs=[SMEM, frame_sp...  4.25 us
    pallas_call x1, Pallas kernels, step_of(): pl.pallas_call(functools.partial(stats_kernel, per, before), grid=(frames...  3.96 us
    pallas_call x1, Pallas kernels, step_of(): pl.pallas_call(functools.partial(activate_kernel, spaces), in_specs=[SMEM...  3.25 us
  transfers between devices with their start and end apart: 21, of which 7 were waited for; matrix products, arithmetic and copies ran while one was open for 0% of the time, Pallas kernels for 30%

profile of v3, /device:TPU:0, one launch (start us, length us, event | category | flops | bytes accessed | tf_op | source)
XLA Modules:
  0.0 86.7 jit_solution(17661265056388838422)
XLA Ops:
  1.3 0.1 stack.35.info_ref
  1.4 4.0 %stats.1 = (f32[8,128]{1,0:T(8,128)S(1)}, bf16[1,2,16,128,128]{4,3,2,1,0:T(8,128)(2,1)S(1)}, bf16[2,4,128,128]{3,2,1,0:T(8,128)(2,1)S(1)}) custom-call(s32[6]{0:T(128)S(1)} %stack.35.info_ref, bf16[1,4,16,128,128]{4,3,2,1,0:T(8,128)(2,1)} %video_ref.19), custom_call_target="tpu_custom_call" | custom-call | tf_op jit(solution)/shard_map/stats/pallas_call | solution.py:324
  5.3 2.5 %collective-permute-start = (bf16[1,2,16,128,128]{4,3,2,1,0:T(8,128)(2,1)S(1)}, bf16[1,2,16,128,128]{4,3,2,1,0:T(8,128)(2,1)S(1)}, u32[]{:S(2)}, u32[]{:S(2)}) collective-permute-start(bf16[1,2,16,128,128]{4,3,2,1,0:T(8,128)(2,1)S(1)} %get-tuple-element.35), channel_id=1, source_target_pairs={{0,4},{1,5},{2,6},{3,7},{8,12},{9,13},{10,14},{11,15},{16,20},{17,... | collective-permute-start | bytes 3145736 | tf_op jit(solution)/shard_map/ppermute | solution.py:32
  7.8 1.3 %collective-permute-start.1 = (bf16[2,2,128,128]{3,2,1,0:T(8,128)(2,1)S(1)}, bf16[2,2,128,128]{3,2,1,0:T(8,128)(2,1)S(1)}, u32[]{:S(2)}, u32[]{:S(2)}) collective-permute-start(bf16[2,2,128,128]{3,2,1,0:T(8,128)(2,1)S(1)} %slice.3), channel_id=1, source_target_pairs={{0,4},{1,5},{2,6},{3,7},{8,12},{9,13},{10,14},{11,15},{16,20},{17,... | collective-permute-start | bytes 393224 | tf_op jit(solution)/shard_map/ppermute | solution.py:32
  9.1 0.1 collective-permute-start.2
  9.2 1.2 %collective-permute-done.2.refs_1_ = f32[8,128]{1,0:T(8,128)S(1)} collective-permute-done((f32[8,128]{1,0:T(8,128)S(1)}, f32[8,128]{1,0:T(8,128)S(1)}, u32[]{:S(2)}, u32[]{:S(2)}) %collective-permute-start.2) | collective-permute-done | bytes 4128 | tf_op jit(solution)/shard_map/ppermute | solution.py:27
  10.4 0.0 collective-permute-done.1.early_ref
  10.4 4.3 %collective-permute-start.3 = (bf16[6,128,128]{2,1,0:T(8,128)(2,1)S(1)}, bf16[6,128,128]{2,1,0:T(8,128)(2,1)S(1)}, u32[]{:S(2)}, u32[]{:S(2)}) collective-permute-start(bf16[6,128,128]{2,1,0:T(8,128)(2,1)S(1)} %get-tuple-element.38), channel_id=1, source_target_pairs={{0,1},{1,2},{2,3},{4,5},{5,6},{6,7},{8,9},{9,10},{10,11},{12,13},{... | collective-permute-start | bytes 589832 | tf_op jit(solution)/shard_map/ppermute | solution.py:32
  14.7 1.3 %collective-permute-start.4 = (bf16[6,128,128]{2,1,0:T(8,128)(2,1)S(1)}, bf16[6,128,128]{2,1,0:T(8,128)(2,1)S(1)}, u32[]{:S(2)}, u32[]{:S(2)}) collective-permute-start(bf16[6,128,128]{2,1,0:T(8,128)(2,1)S(1)} %get-tuple-element.39), channel_id=1, source_target_pairs={{1,0},{2,1},{3,2},{5,4},{6,5},{7,6},{9,8},{10,9},{11,10},{13,12},{... | collective-permute-start | bytes 589832 | tf_op jit(solution)/shard_map/ppermute | solution.py:32
  16.0 4.7 %collective-permute-start.7 = (f32[8,128]{1,0:T(8,128)S(1)}, f32[8,128]{1,0:T(8,128)S(1)}, u32[]{:S(2)}, u32[]{:S(2)}) collective-permute-start(f32[8,128]{1,0:T(8,128)S(1)} %get-tuple-element.40.refs_0_), channel_id=1, source_target_pairs={{0,3},{1,2},{2,1},{3,0},{4,7},{5,6},{6,5},{7,4},{8,11},{9,10},{10,... | collective-permute-start | bytes 12296 | tf_op jit(solution)/shard_map/ppermute | solution.py:27
  20.8 4.7 %collective-permute-done.7.refs_3_ = f32[8,128]{1,0:T(8,128)S(1)} collective-permute-done((f32[8,128]{1,0:T(8,128)S(1)}, f32[8,128]{1,0:T(8,128)S(1)}, u32[]{:S(2)}, u32[]{:S(2)}) %collective-permute-start.7) | collective-permute-done | bytes 4128 | tf_op jit(solution)/shard_map/ppermute | solution.py:27
  25.5 0.0 collective-permute-start.5
  25.5 4.3 %cotangent.1 = (bf16[4,16,128,128]{3,2,1,0:T(8,128)(2,1)S(1)}, f32[8,128]{1,0:T(8,128)S(1)}) custom-call(s32[6]{0:T(128)S(1)} %stack.35.info_ref, bf16[1,4,16,128,128]{4,3,2,1,0:T(8,128)(2,1)} %cot_ref.1), custom_call_target="tpu_custom_call" | custom-call | tf_op jit(solution)/shard_map/cotangent/pallas_call | solution.py:369
  29.8 0.0 collective-permute-done.5.refs_1_
  29.8 0.0 collective-permute-done.3.low_ref
  29.8 0.0 collective-permute-done.early_ref
  29.9 3.2 %activate.1.act_ref = bf16[6,18,10,16,128]{4,3,2,1,0:T(8,128)(2,1)S(1)} custom-call(s32[6]{0:T(128)S(1)} %stack.35.info_ref, bf16[1,4,16,128,128]{4,3,2,1,0:T(8,128)(2,1)S(1)} %copy-done, bf16[1,2,16,128,128]{4,3,2,1,0:T(8,128)(2,1)S(1)} %collective-permute-done.early_ref, bf16[6,128,128]{2,1,0:T(8,128)(2,1)S(1)} %collective-permute-done.3.low_ref, ...), custom_call_target="tpu_custom_call" | custom-call | tf_op jit(solution)/shard_map/activate/pallas_call | solution.py:386
  33.1 0.0 copy-start.1
  33.1 10.0 %weights.1 = (f32[4,448,128]{2,1,0:T(8,128)S(1)}, f32[4,448,128]{2,1,0:T(8,128)S(1)}) custom-call(s32[6]{0:T(128)S(1)} %stack.35.info_ref, bf16[4,16,128,128]{3,2,1,0:T(8,128)(2,1)S(1)} %get-tuple-element.34.turned_ref, bf16[6,18,10,16,128]{4,3,2,1,0:T(8,128)(2,1)S(1)} %activate.1.act_ref, f32[8,128]{1,0:T(8,128)S(1)} %get-tuple-element.41.bias_ref), custom_call_target="tpu_custom_call" | custom-call | tf_op jit(solution)/shard_map/weights/pallas_call | solution.py:412
  43.1 0.0 copy-start.2
  43.1 0.1 collective-permute-start.8
  43.2 0.4 taps.1.taps_ref
  43.6 0.2 copy-done.2
  43.7 2.7 %conv.8 = (bf16[1,4,16,128,128]{4,3,2,1,0:T(8,128)(2,1)}, f32[8,128]{1,0:T(8,128)S(1)}) custom-call(s32[6]{0:T(128)S(1)} %stack.35.info_ref, f32[4,448,128]{2,1,0:T(8,128)S(1)} %get-tuple-element.42.after_ref.keep_ref, bf16[6,18,10,16,128]{4,3,2,1,0:T(8,128)(2,1)S(1)} %activate.1.act_ref, bf16[4608,256]{1,0:T(8,128)(2,1)S(1)} %taps.1.taps_ref, ...), custom_call_target="tpu_custom_call" | custom-call | tf_op jit(solution)/shard_map/conv/pallas_call | solution.py:432
  46.4 2.7 %conv.9 = (bf16[1,4,16,128,128]{4,3,2,1,0:T(8,128)(2,1)}, f32[8,128]{1,0:T(8,128)S(1)}) custom-call(s32[6]{0:T(128)S(1)} %stack.35.info_ref, f32[8,128]{1,0:T(8,128)S(1)} %get-tuple-element.43.after_ref, bf16[6,18,10,16,128]{4,3,2,1,0:T(8,128)(2,1)S(1)} %activate.1.act_ref, bf16[4608,256]{1,0:T(8,128)(2,1)S(1)} %taps.1.taps_ref, ...), custom_call_target="tpu_custom_call", output_to_operand_aliasing={{0}: (6, {})} | custom-call | tf_op jit(solution)/shard_map/conv/pallas_call | solution.py:432
  49.1 0.0 collective-permute-done.8.refs_0_
  49.1 0.6 spread.1
  49.8 1.6 %collective-permute-start.9 = (bf16[448,128]{1,0:T(8,128)(2,1)S(1)}, bf16[448,128]{1,0:T(8,128)(2,1)S(1)}, u32[]{:S(2)}, u32[]{:S(2)}) collective-permute-start(bf16[448,128]{1,0:T(8,128)(2,1)S(1)} %get-tuple-element.50), channel_id=1, source_target_pairs={{0,8},{8,0},{16,24},{24,16},{1,9},{9,1},{17,25},{25,17},{2,10},{10... | collective-permute-start | bytes 344072 | tf_op jit(solution)/shard_map/ppermute | solution.py:27
  51.3 1.5 %collective-permute-start.10 = (bf16[448,128]{1,0:T(8,128)(2,1)S(1)}, bf16[448,128]{1,0:T(8,128)(2,1)S(1)}, u32[]{:S(2)}, u32[]{:S(2)}) collective-permute-start(bf16[448,128]{1,0:T(8,128)(2,1)S(1)} %get-tuple-element.51), channel_id=1, source_target_pairs={{0,16},{8,24},{16,0},{24,8},{1,17},{9,25},{17,1},{25,9},{2,18},{10... | collective-permute-start | bytes 344072 | tf_op jit(solution)/shard_map/ppermute | solution.py:27
  52.8 0.5 collective-permute-start.11
  53.3 2.7 %conv.10 = (bf16[1,4,16,128,128]{4,3,2,1,0:T(8,128)(2,1)}, f32[8,128]{1,0:T(8,128)S(1)}) custom-call(s32[6]{0:T(128)S(1)} %stack.35.info_ref, f32[448,128]{1,0:T(8,128)S(1)} %get-tuple-element.47.after_ref.refs_0_, bf16[6,18,10,16,128]{4,3,2,1,0:T(8,128)(2,1)S(1)} %activate.1.act_ref, ...), custom_call_target="tpu_custom_call", output_to_operand_aliasing={{0}: (6, {})} | custom-call | tf_op jit(solution)/shard_map/conv/pallas_call | solution.py:432
  56.0 2.9 %collective-permute-done.10.refs_2_ = bf16[448,128]{1,0:T(8,128)(2,1)S(1)} collective-permute-done((bf16[448,128]{1,0:T(8,128)(2,1)S(1)}, bf16[448,128]{1,0:T(8,128)(2,1)S(1)}, u32[]{:S(2)}, u32[]{:S(2)}) %collective-permute-start.10) | collective-permute-done | bytes 114720 | tf_op jit(solution)/shard_map/ppermute | solution.py:27
  58.9 0.1 added.3.after_ref.refs_0_
  58.9 2.1 %collective-permute-start.12 = (f32[448,128]{1,0:T(8,128)S(1)}, f32[448,128]{1,0:T(8,128)S(1)}, u32[]{:S(2)}, u32[]{:S(2)}) collective-permute-start(f32[448,128]{1,0:T(8,128)S(1)} %added.3.after_ref.refs_0_), channel_id=1, source_target_pairs={{0,1},{1,0},{2,3},{3,2},{4,5},{5,4},{6,7},{7,6},{8,9},{9,8},{10,11... | collective-permute-start | bytes 688136 | tf_op jit(solution)/shard_map/ppermute | solution.py:27
  61.0 2.7 %conv.11 = (bf16[1,4,16,128,128]{4,3,2,1,0:T(8,128)(2,1)}, f32[8,128]{1,0:T(8,128)S(1)}) custom-call(s32[6]{0:T(128)S(1)} %stack.35.info_ref, f32[448,128]{1,0:T(8,128)S(1)} %added.3.after_ref.refs_0_, bf16[6,18,10,16,128]{4,3,2,1,0:T(8,128)(2,1)S(1)} %activate.1.act_ref, bf16[4608,256]{1,0:T(8,128)(2,1)S(1)} %taps.1.taps_ref, ...), custom_call_target="tpu_custom_call", output_to_operand_aliasing={{0}: (6, {})} | custom-call | tf_op jit(solution)/shard_map/conv/pallas_call | solution.py:432
  63.7 2.7 %conv.12 = (bf16[1,4,16,128,128]{4,3,2,1,0:T(8,128)(2,1)}, f32[8,128]{1,0:T(8,128)S(1)}) custom-call(s32[6]{0:T(128)S(1)} %stack.35.info_ref, f32[8,128]{1,0:T(8,128)S(1)} %get-tuple-element.54.after_ref, bf16[6,18,10,16,128]{4,3,2,1,0:T(8,128)(2,1)S(1)} %activate.1.act_ref, bf16[4608,256]{1,0:T(8,128)(2,1)S(1)} %taps.1.taps_ref, ...), custom_call_target="tpu_custom_call", output_to_operand_aliasing={{0}: (6, {})} | custom-call | tf_op jit(solution)/shard_map/conv/pallas_call | solution.py:432
  66.4 0.2 collective-permute-start.13
  66.6 2.7 %conv.13 = (bf16[1,4,16,128,128]{4,3,2,1,0:T(8,128)(2,1)}, f32[8,128]{1,0:T(8,128)S(1)}) custom-call(s32[6]{0:T(128)S(1)} %stack.35.info_ref, bf16[448,128]{1,0:T(8,128)(2,1)S(1)} %added.4.after_ref.refs_0_, bf16[6,18,10,16,128]{4,3,2,1,0:T(8,128)(2,1)S(1)} %activate.1.act_ref, bf16[4608,256]{1,0:T(8,128)(2,1)S(1)} %taps.1.taps_ref, ...), custom_call_target="tpu_custom_call", output_to_operand_aliasing={{0}: (6, {})} | custom-call | tf_op jit(solution)/shard_map/conv/pallas_call | solution.py:432
  69.3 2.7 %conv.14 = (bf16[1,4,16,128,128]{4,3,2,1,0:T(8,128)(2,1)}, f32[8,128]{1,0:T(8,128)S(1)}) custom-call(s32[6]{0:T(128)S(1)} %stack.35.info_ref, f32[8,128]{1,0:T(8,128)S(1)} %get-tuple-element.58.after_ref, bf16[6,18,10,16,128]{4,3,2,1,0:T(8,128)(2,1)S(1)} %activate.1.act_ref, bf16[4608,256]{1,0:T(8,128)(2,1)S(1)} %taps.1.taps_ref, ...), custom_call_target="tpu_custom_call", output_to_operand_aliasing={{0}: (6, {})} | custom-call | tf_op jit(solution)/shard_map/conv/pallas_call | solution.py:432
  72.0 1.4 %collective-permute-done.13.refs_1_ = bf16[448,128]{1,0:T(8,128)(2,1)S(1)} collective-permute-done((bf16[448,128]{1,0:T(8,128)(2,1)S(1)}, bf16[448,128]{1,0:T(8,128)(2,1)S(1)}, u32[]{:S(2)}, u32[]{:S(2)}) %collective-permute-start.13) | collective-permute-done | bytes 114720 | tf_op jit(solution)/shard_map/ppermute | solution.py:27
  73.5 2.0 %collective-permute-start.16 = (bf16[448,128]{1,0:T(8,128)(2,1)S(1)}, bf16[448,128]{1,0:T(8,128)(2,1)S(1)}, u32[]{:S(2)}, u32[]{:S(2)}) collective-permute-start(bf16[448,128]{1,0:T(8,128)(2,1)S(1)} %added.5.after_ref.refs_0_), channel_id=1, source_target_pairs={{0,24},{8,16},{16,8},{24,0},{1,25},{9,17},{17,9},{25,1},{2,26},{10... | collective-permute-start | bytes 344072 | tf_op jit(solution)/shard_map/ppermute | solution.py:27
  75.4 1.5 %collective-permute-start.15 = (bf16[448,128]{1,0:T(8,128)(2,1)S(1)}, bf16[448,128]{1,0:T(8,128)(2,1)S(1)}, u32[]{:S(2)}, u32[]{:S(2)}) collective-permute-start(bf16[448,128]{1,0:T(8,128)(2,1)S(1)} %added.5.after_ref.refs_0_), channel_id=1, source_target_pairs={{0,16},{8,24},{16,0},{24,8},{1,17},{9,25},{17,1},{25,9},{2,18},{10... | collective-permute-start | bytes 344072 | tf_op jit(solution)/shard_map/ppermute | solution.py:27
  76.9 0.1 collective-permute-start.14
  77.0 3.2 %collective-permute-done.16.refs_3_ = bf16[448,128]{1,0:T(8,128)(2,1)S(1)} collective-permute-done((bf16[448,128]{1,0:T(8,128)(2,1)S(1)}, bf16[448,128]{1,0:T(8,128)(2,1)S(1)}, u32[]{:S(2)}, u32[]{:S(2)}) %collective-permute-start.16) | collective-permute-done | bytes 114720 | tf_op jit(solution)/shard_map/ppermute | solution.py:27
  80.2 0.6 collective-permute-done.15.refs_2_
  80.8 1.3 %collective-permute-done.14.refs_1_ = bf16[448,128]{1,0:T(8,128)(2,1)S(1)} collective-permute-done((bf16[448,128]{1,0:T(8,128)(2,1)S(1)}, bf16[448,128]{1,0:T(8,128)(2,1)S(1)}, u32[]{:S(2)}, u32[]{:S(2)}) %collective-permute-start.14) | collective-permute-done | bytes 114720 | tf_op jit(solution)/shard_map/ppermute | solution.py:27
  82.1 2.7 %conv.15 = (bf16[1,4,16,128,128]{4,3,2,1,0:T(8,128)(2,1)}, f32[8,128]{1,0:T(8,128)}) custom-call(s32[6]{0:T(128)S(1)} %stack.35.info_ref, bf16[448,128]{1,0:T(8,128)(2,1)S(1)} %added.5.after_ref.refs_0_, bf16[6,18,10,16,128]{4,3,2,1,0:T(8,128)(2,1)S(1)} %activate.1.act_ref, bf16[4608,256]{1,0:T(8,128)(2,1)S(1)} %taps.1.taps_ref, ...), custom_call_target="tpu_custom_call", output_to_operand_aliasing={{0}: (6, {})} | custom-call | tf_op jit(solution)/shard_map/conv/pallas_call | solution.py:432
  84.8 1.9 %collect.1 = (f32[8,432,128]{2,1,0:T(8,128)}, f32[1,128]{1,0:T(1,128)}) custom-call(s32[6]{0:T(128)S(1)} %stack.35.info_ref, bf16[448,128]{1,0:T(8,128)(2,1)S(1)} %added.5.after_ref.refs_0_, bf16[448,128]{1,0:T(8,128)(2,1)S(1)} %collective-permute-done.14.refs_1_, bf16[448,128]{1,0:T(8,128)(2,1)S(1)} %collective-permute-done.15.refs_2_, ...), custom_call_target="tpu_custom_call" | custom-call | tf_op jit(solution)/shard_map/collect/pallas_call | solution.py:512
  (25 shorter events, 0.2 us)
Async XLA Ops:
  1.4 28.5 %copy-start = (bf16[1,4,16,128,128]{4,3,2,1,0:T(8,128)(2,1)S(1)}, bf16[1,4,16,128,128]{4,3,2,1,0:T(8,128)(2,1)}, u32[]{:S(2)}) copy-start(bf16[1,4,16,128,128]{4,3,2,1,0:T(8,128)(2,1)} %video_ref.19) | copy-start | bytes 6291460
  1.4 28.5 %copy-start.3 = (f32[128]{0:T(128)S(1)}, f32[128]{0:T(128)}, u32[]{:S(2)}) copy-start(f32[128]{0:T(128)} %param.9) | copy-start | bytes 1540
  1.4 28.5 %copy-start.4 = (f32[128]{0:T(128)S(1)}, f32[128]{0:T(128)}, u32[]{:S(2)}) copy-start(f32[128]{0:T(128)} %param.10) | copy-start | bytes 1540
  5.3 24.5 %collective-permute-start = (bf16[1,2,16,128,128]{4,3,2,1,0:T(8,128)(2,1)S(1)}, bf16[1,2,16,128,128]{4,3,2,1,0:T(8,128)(2,1)S(1)}, u32[]{:S(2)}, u32[]{:S(2)}) collective-permute-start(bf16[1,2,16,128,128]{4,3,2,1,0:T(8,128)(2,1)S(1)} %get-tuple-element.35), channel_id=1, source_target_pairs={{0,4},{1,5},{2,6},{3,7},{8,12},{9,13},{10,14},{11,15},{16,20},{17,... | collective-permute-start | bytes 3145736 | tf_op jit(solution)/shard_map/ppermute | solution.py:32
  7.8 2.5 %collective-permute-start.1 = (bf16[2,2,128,128]{3,2,1,0:T(8,128)(2,1)S(1)}, bf16[2,2,128,128]{3,2,1,0:T(8,128)(2,1)S(1)}, u32[]{:S(2)}, u32[]{:S(2)}) collective-permute-start(bf16[2,2,128,128]{3,2,1,0:T(8,128)(2,1)S(1)} %slice.3), channel_id=1, source_target_pairs={{0,4},{1,5},{2,6},{3,7},{8,12},{9,13},{10,14},{11,15},{16,20},{17,... | collective-permute-start | bytes 393224 | tf_op jit(solution)/shard_map/ppermute | solution.py:32
  9.1 1.2 %collective-permute-start.2 = (f32[8,128]{1,0:T(8,128)S(1)}, f32[8,128]{1,0:T(8,128)S(1)}, u32[]{:S(2)}, u32[]{:S(2)}) collective-permute-start(f32[8,128]{1,0:T(8,128)S(1)} %get-tuple-element.37.refs_0_), channel_id=1, source_target_pairs={{0,4},{4,0},{1,5},{5,1},{2,6},{6,2},{3,7},{7,3},{8,12},{12,8},{9,1... | collective-permute-start | bytes 12296 | tf_op jit(solution)/shard_map/ppermute | solution.py:27
  10.4 19.4 %collective-permute-start.3 = (bf16[6,128,128]{2,1,0:T(8,128)(2,1)S(1)}, bf16[6,128,128]{2,1,0:T(8,128)(2,1)S(1)}, u32[]{:S(2)}, u32[]{:S(2)}) collective-permute-start(bf16[6,128,128]{2,1,0:T(8,128)(2,1)S(1)} %get-tuple-element.38), channel_id=1, source_target_pairs={{0,1},{1,2},{2,3},{4,5},{5,6},{6,7},{8,9},{9,10},{10,11},{12,13},{... | collective-permute-start | bytes 589832 | tf_op jit(solution)/shard_map/ppermute | solution.py:32
  14.7 15.1 %collective-permute-start.4 = (bf16[6,128,128]{2,1,0:T(8,128)(2,1)S(1)}, bf16[6,128,128]{2,1,0:T(8,128)(2,1)S(1)}, u32[]{:S(2)}, u32[]{:S(2)}) collective-permute-start(bf16[6,128,128]{2,1,0:T(8,128)(2,1)S(1)} %get-tuple-element.39), channel_id=1, source_target_pairs={{1,0},{2,1},{3,2},{5,4},{6,5},{7,6},{9,8},{10,9},{11,10},{13,12},{... | collective-permute-start | bytes 589832 | tf_op jit(solution)/shard_map/ppermute | solution.py:32
  16.0 9.5 %collective-permute-start.7 = (f32[8,128]{1,0:T(8,128)S(1)}, f32[8,128]{1,0:T(8,128)S(1)}, u32[]{:S(2)}, u32[]{:S(2)}) collective-permute-start(f32[8,128]{1,0:T(8,128)S(1)} %get-tuple-element.40.refs_0_), channel_id=1, source_target_pairs={{0,3},{1,2},{2,1},{3,0},{4,7},{5,6},{6,5},{7,4},{8,11},{9,10},{10,... | collective-permute-start | bytes 12296 | tf_op jit(solution)/shard_map/ppermute | solution.py:27
  20.8 9.0 %collective-permute-start.6 = (f32[8,128]{1,0:T(8,128)S(1)}, f32[8,128]{1,0:T(8,128)S(1)}, u32[]{:S(2)}, u32[]{:S(2)}) collective-permute-start(f32[8,128]{1,0:T(8,128)S(1)} %get-tuple-element.40.refs_0_), channel_id=1, source_target_pairs={{0,2},{1,3},{2,0},{3,1},{4,6},{5,7},{6,4},{7,5},{8,10},{9,11},{10,... | collective-permute-start | bytes 12296 | tf_op jit(solution)/shard_map/ppermute | solution.py:27
  25.5 4.3 %collective-permute-start.5 = (f32[8,128]{1,0:T(8,128)S(1)}, f32[8,128]{1,0:T(8,128)S(1)}, u32[]{:S(2)}, u32[]{:S(2)}) collective-permute-start(f32[8,128]{1,0:T(8,128)S(1)} %get-tuple-element.40.refs_0_), channel_id=1, source_target_pairs={{0,1},{1,0},{2,3},{3,2},{4,5},{5,4},{6,7},{7,6},{8,9},{9,8},{10,11... | collective-permute-start | bytes 12296 | tf_op jit(solution)/shard_map/ppermute | solution.py:27
  33.1 10.1 %copy-start.1 = (bf16[3,3,3,128,128]{4,3,2,1,0:T(8,128)(2,1)S(1)}, bf16[3,3,3,128,128]{4,3,2,1,0:T(8,128)(2,1)}, u32[]{:S(2)}) copy-start(bf16[3,3,3,128,128]{4,3,2,1,0:T(8,128)(2,1)} %kernel_ref.1) | copy-start | bytes 2654212
  43.1 0.7 copy-start.2
  43.1 6.0 %collective-permute-start.8 = (f32[4,448,128]{2,1,0:T(8,128)S(1)}, f32[4,448,128]{2,1,0:T(8,128)S(1)}, u32[]{:S(2)}, u32[]{:S(2)}) collective-permute-start(f32[4,448,128]{2,1,0:T(8,128)S(1)} %get-tuple-element.46), channel_id=1, source_target_pairs={{0,4},{4,0},{1,5},{5,1},{2,6},{6,2},{3,7},{7,3},{8,12},{12,8},{9,1... | collective-permute-start | bytes 2752520 | tf_op jit(solution)/shard_map/ppermute | solution.py:27
  49.8 6.2 %collective-permute-start.9 = (bf16[448,128]{1,0:T(8,128)(2,1)S(1)}, bf16[448,128]{1,0:T(8,128)(2,1)S(1)}, u32[]{:S(2)}, u32[]{:S(2)}) collective-permute-start(bf16[448,128]{1,0:T(8,128)(2,1)S(1)} %get-tuple-element.50), channel_id=1, source_target_pairs={{0,8},{8,0},{16,24},{24,16},{1,9},{9,1},{17,25},{25,17},{2,10},{10... | collective-permute-start | bytes 344072 | tf_op jit(solution)/shard_map/ppermute | solution.py:27
  51.3 7.5 %collective-permute-start.10 = (bf16[448,128]{1,0:T(8,128)(2,1)S(1)}, bf16[448,128]{1,0:T(8,128)(2,1)S(1)}, u32[]{:S(2)}, u32[]{:S(2)}) collective-permute-start(bf16[448,128]{1,0:T(8,128)(2,1)S(1)} %get-tuple-element.51), channel_id=1, source_target_pairs={{0,16},{8,24},{16,0},{24,8},{1,17},{9,25},{17,1},{25,9},{2,18},{10... | collective-permute-start | bytes 344072 | tf_op jit(solution)/shard_map/ppermute | solution.py:27
  52.8 6.0 %collective-permute-start.11 = (bf16[448,128]{1,0:T(8,128)(2,1)S(1)}, bf16[448,128]{1,0:T(8,128)(2,1)S(1)}, u32[]{:S(2)}, u32[]{:S(2)}) collective-permute-start(bf16[448,128]{1,0:T(8,128)(2,1)S(1)} %get-tuple-element.52), channel_id=1, source_target_pairs={{0,24},{8,16},{16,8},{24,0},{1,25},{9,17},{17,9},{25,1},{2,26},{10... | collective-permute-start | bytes 344072 | tf_op jit(solution)/shard_map/ppermute | solution.py:27
  58.9 7.5 %collective-permute-start.12 = (f32[448,128]{1,0:T(8,128)S(1)}, f32[448,128]{1,0:T(8,128)S(1)}, u32[]{:S(2)}, u32[]{:S(2)}) collective-permute-start(f32[448,128]{1,0:T(8,128)S(1)} %added.3.after_ref.refs_0_), channel_id=1, source_target_pairs={{0,1},{1,0},{2,3},{3,2},{4,5},{5,4},{6,7},{7,6},{8,9},{9,8},{10,11... | collective-permute-start | bytes 688136 | tf_op jit(solution)/shard_map/ppermute | solution.py:27
  66.4 7.0 %collective-permute-start.13 = (bf16[448,128]{1,0:T(8,128)(2,1)S(1)}, bf16[448,128]{1,0:T(8,128)(2,1)S(1)}, u32[]{:S(2)}, u32[]{:S(2)}) collective-permute-start(bf16[448,128]{1,0:T(8,128)(2,1)S(1)} %added.4.after_ref.refs_0_), channel_id=1, source_target_pairs={{0,2},{1,3},{2,0},{3,1},{4,6},{5,7},{6,4},{7,5},{8,10},{9,11},{10,... | collective-permute-start | bytes 344072 | tf_op jit(solution)/shard_map/ppermute | solution.py:27
  73.5 6.8 %collective-permute-start.16 = (bf16[448,128]{1,0:T(8,128)(2,1)S(1)}, bf16[448,128]{1,0:T(8,128)(2,1)S(1)}, u32[]{:S(2)}, u32[]{:S(2)}) collective-permute-start(bf16[448,128]{1,0:T(8,128)(2,1)S(1)} %added.5.after_ref.refs_0_), channel_id=1, source_target_pairs={{0,24},{8,16},{16,8},{24,0},{1,25},{9,17},{17,9},{25,1},{2,26},{10... | collective-permute-start | bytes 344072 | tf_op jit(solution)/shard_map/ppermute | solution.py:27
  75.4 5.4 %collective-permute-start.15 = (bf16[448,128]{1,0:T(8,128)(2,1)S(1)}, bf16[448,128]{1,0:T(8,128)(2,1)S(1)}, u32[]{:S(2)}, u32[]{:S(2)}) collective-permute-start(bf16[448,128]{1,0:T(8,128)(2,1)S(1)} %added.5.after_ref.refs_0_), channel_id=1, source_target_pairs={{0,16},{8,24},{16,0},{24,8},{1,17},{9,25},{17,1},{25,9},{2,18},{10... | collective-permute-start | bytes 344072 | tf_op jit(solution)/shard_map/ppermute | solution.py:27
  76.9 5.2 %collective-permute-start.14 = (bf16[448,128]{1,0:T(8,128)(2,1)S(1)}, bf16[448,128]{1,0:T(8,128)(2,1)S(1)}, u32[]{:S(2)}, u32[]{:S(2)}) collective-permute-start(bf16[448,128]{1,0:T(8,128)(2,1)S(1)} %added.5.after_ref.refs_0_), channel_id=1, source_target_pairs={{0,8},{8,0},{16,24},{24,16},{1,9},{9,1},{17,25},{25,17},{2,10},{10... | collective-permute-start | bytes 344072 | tf_op jit(solution)/shard_map/ppermute | solution.py:27
  77.0 7.8 %collective-permute-start.17 = (bf16[448,128]{1,0:T(8,128)(2,1)S(1)}, bf16[448,128]{1,0:T(8,128)(2,1)S(1)}, u32[]{:S(2)}, u32[]{:S(2)}) collective-permute-start(bf16[448,128]{1,0:T(8,128)(2,1)S(1)} %added.5.after_ref.refs_0_), channel_id=1, source_target_pairs={{0,4},{4,0},{1,5},{5,1},{2,6},{6,2},{3,7},{7,3},{8,12},{12,8},{9,1... | collective-permute-start | bytes 344072 | tf_op jit(solution)/shard_map/ppermute | solution.py:27
  80.2 4.6 %collective-permute-start.20 = (bf16[448,128]{1,0:T(8,128)(2,1)S(1)}, bf16[448,128]{1,0:T(8,128)(2,1)S(1)}, u32[]{:S(2)}, u32[]{:S(2)}) collective-permute-start(bf16[448,128]{1,0:T(8,128)(2,1)S(1)} %collective-permute-done.16.refs_3_), channel_id=1, source_target_pairs={{0,4},{4,0},{1,5},{5,1},{2,6},{6,2},{3,7},{7,3},{8,12},{12,8},{9,1... | collective-permute-start | bytes 344072 | tf_op jit(solution)/shard_map/ppermute | solution.py:27
  80.8 4.0 %collective-permute-start.19 = (bf16[448,128]{1,0:T(8,128)(2,1)S(1)}, bf16[448,128]{1,0:T(8,128)(2,1)S(1)}, u32[]{:S(2)}, u32[]{:S(2)}) collective-permute-start(bf16[448,128]{1,0:T(8,128)(2,1)S(1)} %collective-permute-done.15.refs_2_), channel_id=1, source_target_pairs={{0,4},{4,0},{1,5},{5,1},{2,6},{6,2},{3,7},{7,3},{8,12},{12,8},{9,1... | collective-permute-start | bytes 344072 | tf_op jit(solution)/shard_map/ppermute | solution.py:27
  82.1 2.7 %collective-permute-start.18 = (bf16[448,128]{1,0:T(8,128)(2,1)S(1)}, bf16[448,128]{1,0:T(8,128)(2,1)S(1)}, u32[]{:S(2)}, u32[]{:S(2)}) collective-permute-start(bf16[448,128]{1,0:T(8,128)(2,1)S(1)} %collective-permute-done.14.refs_1_), channel_id=1, source_target_pairs={{0,4},{4,0},{1,5},{5,1},{2,6},{6,2},{3,7},{7,3},{8,12},{12,8},{9,1... | collective-permute-start | bytes 344072 | tf_op jit(solution)/shard_map/ppermute | solution.py:27

commit v4 on v3

--- a/solution.py
+++ b/solution.py
@@ -267,11 +267,11 @@
             out_ref[f * span : (f + 1) * span, g * chans : (g + 1) * chans] = value
 
 
-def conv_kernel(t0, y0, info_ref, after_ref, act_ref, taps_ref, video_ref, bias_ref, *refs):
-    out_ref, token_ref, wide = refs[-3:]
-    frames_out, rows, cols, chans = out_ref.shape[1:]
+def conv_kernel(t0, y0, rows, info_ref, after_ref, act_ref, taps_ref, video_ref, bias_ref, *refs):
+    out_ref, wide = refs
+    cols, chans = out_ref.shape[2:]
     step = cols // TILE
-    start = y0 + pl.program_id(0) * rows
+    pair = taps_ref.shape[1] // chans
     used = [
         (f, ky, kx)
         for f in range(taps_ref.shape[0] // (9 * chans))
@@ -280,13 +280,13 @@
     ]
     left = jnp.concatenate(
         [
-            act_ref[t0 + f, pl.ds(start + ky, rows), kx : kx + step].reshape(rows * cols, chans)
+            act_ref[t0 + f, y0 + ky : y0 + ky + rows, kx : kx + step].reshape(rows * cols, chans)
             for f, ky, kx in used
         ],
         axis=1,
     )
     result = jnp.dot(left, taps_ref[...], preferred_element_type=F32)
-    for f in range(frames_out):
+    for f in range(pair):
         keep = (t0 + f < info_ref[0]).astype(F32)
         for y in range(rows):
             slot = f * rows + y
@@ -295,9 +295,8 @@
                 wide[slot, pl.ds(r, TILE, stride=step), :] = result[
                     at : at + TILE, f * chans : (f + 1) * chans
                 ]
-            value = video_ref[0, f, y].astype(F32) + wide[slot] + bias_ref[...]
-            out_ref[0, f, y] = (value * keep).astype(BF16)
-    token_ref[...] = jnp.zeros_like(token_ref)
+            value = video_ref[0, t0 + f, y0 + y].astype(F32) + wide[slot] + bias_ref[...]
+            out_ref[f, y] = (value * keep).astype(BF16)
 
 
 def step_of(video, lengths, norm_gain, norm_shift, kernel, conv_bias, cotangent):
@@ -340,8 +339,9 @@
         name="stats",
     )(info, pltpu.with_memory_space_constraint(video, pltpu.HBM))
     gathered = [stats] + [swap(stats, "tm", r) for r in range(1, tms)]
-    early_ends = shifted(ends[:, frames - before :], "tm", 1)
-    early = shifted(tail, "tm", 1)
+    following = [(i, (i + 1) % tms) for i in range(tms)]
+    early_ends = lax.ppermute(ends[:, frames - before :], "tm", following)
+    early = lax.ppermute(tail, "tm", following)
     border = jax.ShapeDtypeStruct((before + frames, cols, chans), BF16)
     stats, edge_low, edge_high = pl.pallas_call(
         functools.partial(merge_kernel, tms),
@@ -423,47 +423,26 @@
     )(info, turned, act, bias)
 
     block = 4
-    output = None
-    half = block
-
-    def conv(after, output, t0, y0):
-        given = [] if output is None else [output]
-        where = lambda y: (0, t0 // 2, y0 // block + y, 0, 0)
-        return pl.pallas_call(
-            functools.partial(conv_kernel, t0, y0),
-            grid=(half // block,),
-            in_specs=[
-                SMEM,
-                ANY,
-                VMEM,
-                VMEM,
-                pl.BlockSpec((1, 2, block, cols, chans), where),
-                VMEM,
-            ]
-            + [ANY] * len(given),
-            out_specs=[
-                pl.BlockSpec((1, 2, block, cols, chans), where),
-                pl.BlockSpec((8, chans), lambda y: (0, 0)),
-            ],
-            out_shape=[
-                jax.ShapeDtypeStruct(video.shape, BF16),
-                jax.ShapeDtypeStruct((8, chans), F32),
-            ],
-            scratch_shapes=[pltpu.VMEM((2 * block, cols, chans), F32)],
-            input_output_aliases={6: 0} if given else {},
-            compiler_params=params(12),
-            name="conv",
-        )(info, after, act, taps, video, conv_bias.reshape(1, chans), *given)
-
-    pieces = [(t0, y0) for t0 in range(0, frames, 2) for y0 in range(0, rows, half)]
-
-    def cover(after, output, number):
-        for _ in range(min(number, len(pieces))):
-            output, after = conv(after, output, *pieces.pop(0))
-        return output, after
+    pieces = [(t0, y0) for t0 in range(0, frames, pair) for y0 in range(0, rows, block)]
+    done = []
+
+    def cover(after, number):
+        for _ in range(min(number, len(pieces) - len(done))):
+            t0, y0 = pieces[len(done)]
+            after = pl.pallas_call(
+                functools.partial(conv_kernel, t0, y0, block),
+                in_specs=[SMEM, ANY, VMEM, VMEM, VMEM, VMEM],
+                out_specs=VMEM,
+                out_shape=jax.ShapeDtypeStruct((pair, block, cols, chans), BF16),
+                scratch_shapes=[pltpu.VMEM((pair * block, cols, chans), F32)],
+                compiler_params=params(6),
+                name="conv",
+            )(info, after, act, taps, video, conv_bias.reshape(1, chans))
+            done.append(after)
+        return after
 
     incoming = [swap(send, "tm", r + 1) for r, send in enumerate(sends)]
-    output, token = cover(keep, output, 2)
+    token = cover(keep, 2)
     own, *sends = pl.pallas_call(
         functools.partial(spread_kernel, len(incoming)),
         in_specs=[SMEM, ANY] + [VMEM] * (1 + len(incoming)),
@@ -485,16 +464,16 @@
         )(after, *arrays)
 
     incoming = [swap(send, "dp", r + 1) for r, send in enumerate(sends)]
-    output, token = cover(own, output, 1)
+    token = cover(own, 1)
     total = added(F32 if spaces > 2 else BF16, token, own, *incoming)
     by = 1
     while by < spaces:
         other = swap(total, "space", by)
-        output, token = cover(total, output, 2)
+        token = cover(total, 2)
         by *= 2
         total = added(F32 if 2 * by < spaces else BF16, token, total, other)
     mine = [total] + [swap(total, "dp", r) for r in range(1, dps)]
-    output, token = cover(total, output, len(pieces))
+    cover(total, len(pieces))
     shards = {(0, r): array for r, array in enumerate(mine)}
     for q in range(1, tms):
         for r, array in enumerate(mine):
@@ -502,24 +481,34 @@
     order = list(shards)
 
     def collect(info_ref, *refs):
-        out_ref, sum_ref = refs[-2:]
-        for (q, r), ref in zip(order, refs):
+        shard_refs, piece_refs = refs[: len(order)], refs[len(order) : len(order) + len(done)]
+        out_ref, sum_ref, output_ref, sems = refs[-4:]
+        copies = []
+        for n, (t0, y0) in enumerate(pieces):
+            target = output_ref.at[0, t0 : t0 + pair, y0 : y0 + block]
+            copies.append(pltpu.make_async_copy(piece_refs[n], target, sems.at[n]))
+            copies[-1].start()
+        for (q, r), ref in zip(order, shard_refs):
             at = (info_ref[4] ^ q) * dps + (info_ref[5] ^ r)
             out_ref[at] = ref[0:shard, :].astype(F32)
-        tail = refs[0][shard : shard + TILE, :].astype(F32)
+        tail = shard_refs[0][shard : shard + TILE, :].astype(F32)
         sum_ref[...] = tail[0:1] + tail[1:2] + tail[2:3]
-
-    grad_kernel, grad_bias = pl.pallas_call(
+        for copy in copies:
+            copy.wait()
+
+    grad_kernel, grad_bias, output = pl.pallas_call(
         collect,
-        in_specs=[SMEM] + [VMEM] * len(order),
-        out_specs=[VMEM, VMEM],
+        in_specs=[SMEM] + [VMEM] * (len(order) + len(done)),
+        out_specs=[VMEM, VMEM, ANY],
         out_shape=[
             jax.ShapeDtypeStruct((shards_n, shard, chans), F32),
             jax.ShapeDtypeStruct((1, chans), F32),
-        ],
+            jax.ShapeDtypeStruct(video.shape, BF16),
+        ],
+        scratch_shapes=[pltpu.SemaphoreType.DMA((len(pieces),))],
         compiler_params=params(4),
         name="collect",
-    )(info, *[shards[key] for key in order])
+    )(info, *[shards[key] for key in order], *done)
 
     return output, grad_kernel.reshape(kernel.shape), grad_bias.reshape(chans)
 

time: 87 us -> 83.7 us (0.962)
  Pallas kernels: 45.9 us -> 41.4 us
    pallas_call x9, Pallas kernels: 23.4 us -> 18.9 us  [the longest x8 15.7 us: cover(): pl.pallas_call(functools.partial(conv_kernel, t0, y0, block), in_specs=[S...]
    ppermute x4 -> x2, starting transfers between devices: 9.36 us -> 6.14 us  [shifted(): lax.ppermute(array, axis, [(i, i + by) for i in range(length) if 0 <= i +...]
    ppermute x17, starting transfers between devices: 14.3 us -> 17.3 us  [swap(): return lax.ppermute(array, axis, [(i, i ^ by) for i in range(length)])]
  transfers between devices with their start and end apart: 21 -> 21, of which waited for: 7 -> 10; matrix products, arithmetic and copies ran while one was open for 0% -> 0% of each run, Pallas kernels for 30% -> 24%
where the time goes in v4:
time: 83.7 us; the launch traced here: 83.4 us
  Pallas kernels  41.4 us (49%)
  starting transfers between devices  24.1 us (29%)
  waiting for transfers between devices  15.9 us (19%)
  between operations  1.73 us (2%)
    ppermute x17, starting transfers between devices, swap(): return lax.ppermute(array, axis, [(i, i ^ by) for i in range(length)])  17.3 us
    ppermute x17, waiting for transfers between devices, swap(): return lax.ppermute(array, axis, [(i, i ^ by) for i in range(length)])  15.8 us
    pallas_call x8, Pallas kernels, cover(): pl.pallas_call(functools.partial(conv_kernel, t0, y0, block), in_specs=[S...  15.7 us
    pallas_call x1, Pallas kernels, step_of(): pl.pallas_call(weights_kernel, in_specs=[SMEM, VMEM, VMEM, VMEM], out_spe...  9.94 us
    ppermute x2, starting transfers between devices, shifted(): lax.ppermute(array, axis, [(i, i + by) for i in range(length) if 0 <= i +...  6.14 us
    pallas_call x1, Pallas kernels, step_of(): pl.pallas_call(cotangent_kernel, grid=(frames,), in_specs=[SMEM, frame_sp...  4.25 us
    pallas_call x1, Pallas kernels, step_of(): pl.pallas_call(functools.partial(stats_kernel, per, before), grid=(frames...  3.96 us
    pallas_call x1, Pallas kernels, step_of(): pl.pallas_call(functools.partial(activate_kernel, spaces), in_specs=[SMEM...  3.25 us
  transfers between devices with their start and end apart: 21, of which 10 were waited for; matrix products, arithmetic and copies ran while one was open for 0% of the time, Pallas kernels for 24%

profile of v4, /device:TPU:0, one launch (start us, length us, event | category | flops | bytes accessed | tf_op | source)
XLA Modules:
  0.0 83.4 jit_solution(3149673056769402389)
XLA Ops:
  1.3 0.1 stack.35.info_ref
  1.4 4.0 %stats.1 = (f32[8,128]{1,0:T(8,128)S(1)}, bf16[1,2,16,128,128]{4,3,2,1,0:T(8,128)(2,1)S(1)}, bf16[2,4,128,128]{3,2,1,0:T(8,128)(2,1)S(1)}) custom-call(s32[6]{0:T(128)S(1)} %stack.35.info_ref, bf16[1,4,16,128,128]{4,3,2,1,0:T(8,128)(2,1)} %video_ref.19), custom_call_target="tpu_custom_call" | custom-call | tf_op jit(solution)/shard_map/stats/pallas_call | solution.py:323
  5.4 0.6 collective-permute-start
  5.9 0.1 collective-permute-start.1
  6.0 0.5 collective-permute-start.2
  6.5 1.9 %collective-permute-done.2.refs_1_ = f32[8,128]{1,0:T(8,128)S(1)} collective-permute-done((f32[8,128]{1,0:T(8,128)S(1)}, f32[8,128]{1,0:T(8,128)S(1)}, u32[]{:S(2)}, u32[]{:S(2)}) %collective-permute-start.2) | collective-permute-done | bytes 4128 | tf_op jit(solution)/shard_map/ppermute | solution.py:27
  8.4 4.8 %collective-permute-start.3 = (bf16[6,128,128]{2,1,0:T(8,128)(2,1)S(1)}, bf16[6,128,128]{2,1,0:T(8,128)(2,1)S(1)}, u32[]{:S(2)}, u32[]{:S(2)}) collective-permute-start(bf16[6,128,128]{2,1,0:T(8,128)(2,1)S(1)} %get-tuple-element.24), channel_id=1, source_target_pairs={{0,1},{1,2},{2,3},{4,5},{5,6},{6,7},{8,9},{9,10},{10,11},{12,13},{... | collective-permute-start | bytes 589832 | tf_op jit(solution)/shard_map/ppermute | solution.py:32
  13.3 1.3 %collective-permute-start.4 = (bf16[6,128,128]{2,1,0:T(8,128)(2,1)S(1)}, bf16[6,128,128]{2,1,0:T(8,128)(2,1)S(1)}, u32[]{:S(2)}, u32[]{:S(2)}) collective-permute-start(bf16[6,128,128]{2,1,0:T(8,128)(2,1)S(1)} %get-tuple-element.25), channel_id=1, source_target_pairs={{1,0},{2,1},{3,2},{5,4},{6,5},{7,6},{9,8},{10,9},{11,10},{13,12},{... | collective-permute-start | bytes 589832 | tf_op jit(solution)/shard_map/ppermute | solution.py:32
  14.6 2.7 %collective-permute-start.5 = (f32[8,128]{1,0:T(8,128)S(1)}, f32[8,128]{1,0:T(8,128)S(1)}, u32[]{:S(2)}, u32[]{:S(2)}) collective-permute-start(f32[8,128]{1,0:T(8,128)S(1)} %get-tuple-element.26.refs_0_), channel_id=1, source_target_pairs={{0,1},{1,0},{2,3},{3,2},{4,5},{5,4},{6,7},{7,6},{8,9},{9,8},{10,11... | collective-permute-start | bytes 12296 | tf_op jit(solution)/shard_map/ppermute | solution.py:27
  17.3 2.6 %collective-permute-start.6 = (f32[8,128]{1,0:T(8,128)S(1)}, f32[8,128]{1,0:T(8,128)S(1)}, u32[]{:S(2)}, u32[]{:S(2)}) collective-permute-start(f32[8,128]{1,0:T(8,128)S(1)} %get-tuple-element.26.refs_0_), channel_id=1, source_target_pairs={{0,2},{1,3},{2,0},{3,1},{4,6},{5,7},{6,4},{7,5},{8,10},{9,11},{10,... | collective-permute-start | bytes 12296 | tf_op jit(solution)/shard_map/ppermute | solution.py:27
  19.9 2.1 %collective-permute-done.5.refs_1_ = f32[8,128]{1,0:T(8,128)S(1)} collective-permute-done((f32[8,128]{1,0:T(8,128)S(1)}, f32[8,128]{1,0:T(8,128)S(1)}, u32[]{:S(2)}, u32[]{:S(2)}) %collective-permute-start.5) | collective-permute-done | bytes 4128 | tf_op jit(solution)/shard_map/ppermute | solution.py:27
  22.0 1.6 %collective-permute-start.7 = (f32[8,128]{1,0:T(8,128)S(1)}, f32[8,128]{1,0:T(8,128)S(1)}, u32[]{:S(2)}, u32[]{:S(2)}) collective-permute-start(f32[8,128]{1,0:T(8,128)S(1)} %get-tuple-element.26.refs_0_), channel_id=1, source_target_pairs={{0,3},{1,2},{2,1},{3,0},{4,7},{5,6},{6,5},{7,4},{8,11},{9,10},{10,... | collective-permute-start | bytes 12296 | tf_op jit(solution)/shard_map/ppermute | solution.py:27
  23.5 4.3 %cotangent.1 = (bf16[4,16,128,128]{3,2,1,0:T(8,128)(2,1)S(1)}, f32[8,128]{1,0:T(8,128)S(1)}) custom-call(s32[6]{0:T(128)S(1)} %stack.35.info_ref, bf16[1,4,16,128,128]{4,3,2,1,0:T(8,128)(2,1)} %cot_ref.1), custom_call_target="tpu_custom_call" | custom-call | tf_op jit(solution)/shard_map/cotangent/pallas_call | solution.py:369
  27.8 0.0 collective-permute-done.7.refs_3_
  27.9 3.2 %activate.1.act_ref = bf16[6,18,10,16,128]{4,3,2,1,0:T(8,128)(2,1)S(1)} custom-call(s32[6]{0:T(128)S(1)} %stack.35.info_ref, bf16[1,4,16,128,128]{4,3,2,1,0:T(8,128)(2,1)S(1)} %copy-done, bf16[1,2,16,128,128]{4,3,2,1,0:T(8,128)(2,1)S(1)} %collective-permute-done.early_ref, bf16[6,128,128]{2,1,0:T(8,128)(2,1)S(1)} %collective-permute-done.3.low_ref, ...), custom_call_target="tpu_custom_call" | custom-call | tf_op jit(solution)/shard_map/activate/pallas_call | solution.py:386
  31.1 0.0 copy-start.1
  31.1 9.9 %weights.1 = (f32[4,448,128]{2,1,0:T(8,128)S(1)}, f32[4,448,128]{2,1,0:T(8,128)S(1)}) custom-call(s32[6]{0:T(128)S(1)} %stack.35.info_ref, bf16[4,16,128,128]{3,2,1,0:T(8,128)(2,1)S(1)} %get-tuple-element.20.turned_ref, bf16[6,18,10,16,128]{4,3,2,1,0:T(8,128)(2,1)S(1)} %activate.1.act_ref, f32[8,128]{1,0:T(8,128)S(1)} %get-tuple-element.27.bias_ref), custom_call_target="tpu_custom_call" | custom-call | tf_op jit(solution)/shard_map/weights/pallas_call | solution.py:412
  41.1 0.0 copy-start.2
  41.1 0.1 collective-permute-start.8
  41.2 0.4 taps.1.taps_ref
  41.6 0.2 copy-done.2
  41.8 2.0 %conv.8.after_ref.refs_8_ = bf16[2,4,128,128]{3,2,1,0:T(8,128)(2,1)S(1)} custom-call(s32[6]{0:T(128)S(1)} %stack.35.info_ref, f32[4,448,128]{2,1,0:T(8,128)S(1)} %get-tuple-element.28.after_ref.keep_ref, bf16[6,18,10,16,128]{4,3,2,1,0:T(8,128)(2,1)S(1)} %activate.1.act_ref, bf16[4608,256]{1,0:T(8,128)(2,1)S(1)} %taps.1.taps_ref, ...), custom_call_target="tpu_custom_call" | custom-call | tf_op jit(solution)/shard_map/conv/pallas_call | solution.py:432
  43.7 2.0 %conv.9.after_ref.refs_9_ = bf16[2,4,128,128]{3,2,1,0:T(8,128)(2,1)S(1)} custom-call(s32[6]{0:T(128)S(1)} %stack.35.info_ref, bf16[2,4,128,128]{3,2,1,0:T(8,128)(2,1)S(1)} %conv.8.after_ref.refs_8_, bf16[6,18,10,16,128]{4,3,2,1,0:T(8,128)(2,1)S(1)} %activate.1.act_ref, bf16[4608,256]{1,0:T(8,128)(2,1)S(1)} %taps.1.taps_ref, ...), custom_call_target="tpu_custom_call" | custom-call | tf_op jit(solution)/shard_map/conv/pallas_call | solution.py:432
  45.7 0.6 spread.1
  46.4 1.6 %collective-permute-start.10 = (bf16[448,128]{1,0:T(8,128)(2,1)S(1)}, bf16[448,128]{1,0:T(8,128)(2,1)S(1)}, u32[]{:S(2)}, u32[]{:S(2)}) collective-permute-start(bf16[448,128]{1,0:T(8,128)(2,1)S(1)} %get-tuple-element.32), channel_id=1, source_target_pairs={{0,16},{8,24},{16,0},{24,8},{1,17},{9,25},{17,1},{25,9},{2,18},{10... | collective-permute-start | bytes 344072 | tf_op jit(solution)/shard_map/ppermute | solution.py:27
  48.0 1.4 %collective-permute-start.11 = (bf16[448,128]{1,0:T(8,128)(2,1)S(1)}, bf16[448,128]{1,0:T(8,128)(2,1)S(1)}, u32[]{:S(2)}, u32[]{:S(2)}) collective-permute-start(bf16[448,128]{1,0:T(8,128)(2,1)S(1)} %get-tuple-element.33), channel_id=1, source_target_pairs={{0,24},{8,16},{16,8},{24,0},{1,25},{9,17},{17,9},{25,1},{2,26},{10... | collective-permute-start | bytes 344072 | tf_op jit(solution)/shard_map/ppermute | solution.py:27
  49.4 0.5 collective-permute-start.9
  49.9 2.0 %conv.10.after_ref.refs_10_ = bf16[2,4,128,128]{3,2,1,0:T(8,128)(2,1)S(1)} custom-call(s32[6]{0:T(128)S(1)} %stack.35.info_ref, f32[448,128]{1,0:T(8,128)S(1)} %get-tuple-element.30.after_ref.refs_0_, bf16[6,18,10,16,128]{4,3,2,1,0:T(8,128)(2,1)S(1)} %activate.1.act_ref, bf16[4608,256]{1,0:T(8,128)(2,1)S(1)} %taps.1.taps_ref, ...), custom_call_target="tpu_custom_call" | custom-call | tf_op jit(solution)/shard_map/conv/pallas_call | solution.py:432
  51.9 1.7 %collective-permute-done.10.refs_2_ = bf16[448,128]{1,0:T(8,128)(2,1)S(1)} collective-permute-done((bf16[448,128]{1,0:T(8,128)(2,1)S(1)}, bf16[448,128]{1,0:T(8,128)(2,1)S(1)}, u32[]{:S(2)}, u32[]{:S(2)}) %collective-permute-start.10) | collective-permute-done | bytes 114720 | tf_op jit(solution)/shard_map/ppermute | solution.py:27
  53.6 1.3 %collective-permute-done.11.refs_3_ = bf16[448,128]{1,0:T(8,128)(2,1)S(1)} collective-permute-done((bf16[448,128]{1,0:T(8,128)(2,1)S(1)}, bf16[448,128]{1,0:T(8,128)(2,1)S(1)}, u32[]{:S(2)}, u32[]{:S(2)}) %collective-permute-start.11) | collective-permute-done | bytes 114720 | tf_op jit(solution)/shard_map/ppermute | solution.py:27
  54.9 0.6 collective-permute-done.9.refs_1_
  55.5 0.1 added.3.after_ref.refs_0_
  55.5 1.6 %collective-permute-start.12 = (f32[448,128]{1,0:T(8,128)S(1)}, f32[448,128]{1,0:T(8,128)S(1)}, u32[]{:S(2)}, u32[]{:S(2)}) collective-permute-start(f32[448,128]{1,0:T(8,128)S(1)} %added.3.after_ref.refs_0_), channel_id=1, source_target_pairs={{0,1},{1,0},{2,3},{3,2},{4,5},{5,4},{6,7},{7,6},{8,9},{9,8},{10,11... | collective-permute-start | bytes 688136 | tf_op jit(solution)/shard_map/ppermute | solution.py:27
  57.2 2.0 %conv.11.after_ref.refs_11_ = bf16[2,4,128,128]{3,2,1,0:T(8,128)(2,1)S(1)} custom-call(s32[6]{0:T(128)S(1)} %stack.35.info_ref, f32[448,128]{1,0:T(8,128)S(1)} %added.3.after_ref.refs_0_, bf16[6,18,10,16,128]{4,3,2,1,0:T(8,128)(2,1)S(1)} %activate.1.act_ref, bf16[4608,256]{1,0:T(8,128)(2,1)S(1)} %taps.1.taps_ref, bf16[1,4,16,128,128]{4,3,2,1,0:T(8,128)(2,1)S(1)} %copy-done, ...), custom_call_target="tpu_custom_call" | custom-call | tf_op jit(solution)/shard_map/conv/pallas_call | solution.py:432
  59.2 2.0 %conv.12.after_ref.refs_12_ = bf16[2,4,128,128]{3,2,1,0:T(8,128)(2,1)S(1)} custom-call(s32[6]{0:T(128)S(1)} %stack.35.info_ref, bf16[2,4,128,128]{3,2,1,0:T(8,128)(2,1)S(1)} %conv.11.after_ref.refs_11_, bf16[6,18,10,16,128]{4,3,2,1,0:T(8,128)(2,1)S(1)} %activate.1.act_ref, bf16[4608,256]{1,0:T(8,128)(2,1)S(1)} %taps.1.taps_ref, ...), custom_call_target="tpu_custom_call" | custom-call | tf_op jit(solution)/shard_map/conv/pallas_call | solution.py:432
  61.1 1.2 %collective-permute-done.12.refs_1_ = f32[448,128]{1,0:T(8,128)S(1)} collective-permute-done((f32[448,128]{1,0:T(8,128)S(1)}, f32[448,128]{1,0:T(8,128)S(1)}, u32[]{:S(2)}, u32[]{:S(2)}) %collective-permute-start.12) | collective-permute-done | bytes 229408 | tf_op jit(solution)/shard_map/ppermute | solution.py:27
  62.3 1.1 %collective-permute-start.13 = (bf16[448,128]{1,0:T(8,128)(2,1)S(1)}, bf16[448,128]{1,0:T(8,128)(2,1)S(1)}, u32[]{:S(2)}, u32[]{:S(2)}) collective-permute-start(bf16[448,128]{1,0:T(8,128)(2,1)S(1)} %added.4.after_ref.refs_0_), channel_id=1, source_target_pairs={{0,2},{1,3},{2,0},{3,1},{4,6},{5,7},{6,4},{7,5},{8,10},{9,11},{10,... | collective-permute-start | bytes 344072 | tf_op jit(solution)/shard_map/ppermute | solution.py:27
  63.5 2.0 %conv.13.after_ref.refs_13_ = bf16[2,4,128,128]{3,2,1,0:T(8,128)(2,1)S(1)} custom-call(s32[6]{0:T(128)S(1)} %stack.35.info_ref, bf16[448,128]{1,0:T(8,128)(2,1)S(1)} %added.4.after_ref.refs_0_, bf16[6,18,10,16,128]{4,3,2,1,0:T(8,128)(2,1)S(1)} %activate.1.act_ref, bf16[4608,256]{1,0:T(8,128)(2,1)S(1)} %taps.1.taps_ref, ...), custom_call_target="tpu_custom_call" | custom-call | tf_op jit(solution)/shard_map/conv/pallas_call | solution.py:432
  65.5 2.0 %conv.14.after_ref.refs_14_ = bf16[2,4,128,128]{3,2,1,0:T(8,128)(2,1)S(1)} custom-call(s32[6]{0:T(128)S(1)} %stack.35.info_ref, bf16[2,4,128,128]{3,2,1,0:T(8,128)(2,1)S(1)} %conv.13.after_ref.refs_13_, bf16[6,18,10,16,128]{4,3,2,1,0:T(8,128)(2,1)S(1)} %activate.1.act_ref, bf16[4608,256]{1,0:T(8,128)(2,1)S(1)} %taps.1.taps_ref, ...), custom_call_target="tpu_custom_call" | custom-call | tf_op jit(solution)/shard_map/conv/pallas_call | solution.py:432
  67.4 1.9 %collective-permute-done.13.refs_1_ = bf16[448,128]{1,0:T(8,128)(2,1)S(1)} collective-permute-done((bf16[448,128]{1,0:T(8,128)(2,1)S(1)}, bf16[448,128]{1,0:T(8,128)(2,1)S(1)}, u32[]{:S(2)}, u32[]{:S(2)}) %collective-permute-start.13) | collective-permute-done | bytes 114720 | tf_op jit(solution)/shard_map/ppermute | solution.py:27
  69.4 1.6 %collective-permute-start.14 = (bf16[448,128]{1,0:T(8,128)(2,1)S(1)}, bf16[448,128]{1,0:T(8,128)(2,1)S(1)}, u32[]{:S(2)}, u32[]{:S(2)}) collective-permute-start(bf16[448,128]{1,0:T(8,128)(2,1)S(1)} %added.5.after_ref.refs_0_), channel_id=1, source_target_pairs={{0,8},{8,0},{16,24},{24,16},{1,9},{9,1},{17,25},{25,17},{2,10},{10... | collective-permute-start | bytes 344072 | tf_op jit(solution)/shard_map/ppermute | solution.py:27
  70.9 1.5 %collective-permute-start.15 = (bf16[448,128]{1,0:T(8,128)(2,1)S(1)}, bf16[448,128]{1,0:T(8,128)(2,1)S(1)}, u32[]{:S(2)}, u32[]{:S(2)}) collective-permute-start(bf16[448,128]{1,0:T(8,128)(2,1)S(1)} %added.5.after_ref.refs_0_), channel_id=1, source_target_pairs={{0,16},{8,24},{16,0},{24,8},{1,17},{9,25},{17,1},{25,9},{2,18},{10... | collective-permute-start | bytes 344072 | tf_op jit(solution)/shard_map/ppermute | solution.py:27
  72.4 0.5 collective-permute-start.16
  72.9 1.3 %collective-permute-done.14.refs_1_ = bf16[448,128]{1,0:T(8,128)(2,1)S(1)} collective-permute-done((bf16[448,128]{1,0:T(8,128)(2,1)S(1)}, bf16[448,128]{1,0:T(8,128)(2,1)S(1)}, u32[]{:S(2)}, u32[]{:S(2)}) %collective-permute-start.14) | collective-permute-done | bytes 114720 | tf_op jit(solution)/shard_map/ppermute | solution.py:27
  74.2 1.5 %collective-permute-done.15.refs_2_ = bf16[448,128]{1,0:T(8,128)(2,1)S(1)} collective-permute-done((bf16[448,128]{1,0:T(8,128)(2,1)S(1)}, bf16[448,128]{1,0:T(8,128)(2,1)S(1)}, u32[]{:S(2)}, u32[]{:S(2)}) %collective-permute-start.15) | collective-permute-done | bytes 114720 | tf_op jit(solution)/shard_map/ppermute | solution.py:27
  75.7 2.4 %collective-permute-done.16.refs_3_ = bf16[448,128]{1,0:T(8,128)(2,1)S(1)} collective-permute-done((bf16[448,128]{1,0:T(8,128)(2,1)S(1)}, bf16[448,128]{1,0:T(8,128)(2,1)S(1)}, u32[]{:S(2)}, u32[]{:S(2)}) %collective-permute-start.16) | collective-permute-done | bytes 114720 | tf_op jit(solution)/shard_map/ppermute | solution.py:27
  78.1 2.0 %conv.15.refs_15_ = bf16[2,4,128,128]{3,2,1,0:T(8,128)(2,1)S(1)} custom-call(s32[6]{0:T(128)S(1)} %stack.35.info_ref, bf16[448,128]{1,0:T(8,128)(2,1)S(1)} %added.5.after_ref.refs_0_, bf16[6,18,10,16,128]{4,3,2,1,0:T(8,128)(2,1)S(1)} %activate.1.act_ref, bf16[4608,256]{1,0:T(8,128)(2,1)S(1)} %taps.1.taps_ref, bf16[1,4,16,128,128]{4,3,2,1,0:T(8,128)(2,1)S(1)} %copy-done, ...), custom_call_target="tpu_custom_call" | custom-call | tf_op jit(solution)/shard_map/conv/pallas_call | solution.py:432
  80.1 3.1 %collect.1 = (f32[8,432,128]{2,1,0:T(8,128)}, f32[1,128]{1,0:T(1,128)}, bf16[1,4,16,128,128]{4,3,2,1,0:T(8,128)(2,1)}) custom-call(s32[6]{0:T(128)S(1)} %stack.35.info_ref, bf16[448,128]{1,0:T(8,128)(2,1)S(1)} %added.5.after_ref.refs_0_, bf16[448,128]{1,0:T(8,128)(2,1)S(1)} %collective-permute-done.14.refs_1_, ...), custom_call_target="tpu_custom_call" | custom-call | tf_op jit(solution)/shard_map/collect/pallas_call | solution.py:499
  (25 shorter events, 0.2 us)
Async XLA Ops:
  1.4 26.5 %copy-start = (bf16[1,4,16,128,128]{4,3,2,1,0:T(8,128)(2,1)S(1)}, bf16[1,4,16,128,128]{4,3,2,1,0:T(8,128)(2,1)}, u32[]{:S(2)}) copy-start(bf16[1,4,16,128,128]{4,3,2,1,0:T(8,128)(2,1)} %video_ref.19) | copy-start | bytes 6291460
  1.4 26.5 %copy-start.3 = (f32[128]{0:T(128)S(1)}, f32[128]{0:T(128)}, u32[]{:S(2)}) copy-start(f32[128]{0:T(128)} %param.9) | copy-start | bytes 1540
  1.4 26.5 %copy-start.4 = (f32[128]{0:T(128)S(1)}, f32[128]{0:T(128)}, u32[]{:S(2)}) copy-start(f32[128]{0:T(128)} %param.10) | copy-start | bytes 1540
  5.4 22.5 %collective-permute-start = (bf16[1,2,16,128,128]{4,3,2,1,0:T(8,128)(2,1)S(1)}, bf16[1,2,16,128,128]{4,3,2,1,0:T(8,128)(2,1)S(1)}, u32[]{:S(2)}, u32[]{:S(2)}) collective-permute-start(bf16[1,2,16,128,128]{4,3,2,1,0:T(8,128)(2,1)S(1)} %get-tuple-element.21), channel_id=1, source_target_pairs={{0,4},{4,0},{1,5},{5,1},{2,6},{6,2},{3,7},{7,3},{8,12},{12,8},{9,1... | collective-permute-start | bytes 3145736 | tf_op jit(solution)/shard_map/ppermute | solution.py:344
  5.9 2.5 %collective-permute-start.1 = (bf16[2,2,128,128]{3,2,1,0:T(8,128)(2,1)S(1)}, bf16[2,2,128,128]{3,2,1,0:T(8,128)(2,1)S(1)}, u32[]{:S(2)}, u32[]{:S(2)}) collective-permute-start(bf16[2,2,128,128]{3,2,1,0:T(8,128)(2,1)S(1)} %slice.3), channel_id=1, source_target_pairs={{0,4},{4,0},{1,5},{5,1},{2,6},{6,2},{3,7},{7,3},{8,12},{12,8},{9,1... | collective-permute-start | bytes 393224 | tf_op jit(solution)/shard_map/ppermute | solution.py:343
  6.0 2.4 %collective-permute-start.2 = (f32[8,128]{1,0:T(8,128)S(1)}, f32[8,128]{1,0:T(8,128)S(1)}, u32[]{:S(2)}, u32[]{:S(2)}) collective-permute-start(f32[8,128]{1,0:T(8,128)S(1)} %get-tuple-element.23.refs_0_), channel_id=1, source_target_pairs={{0,4},{4,0},{1,5},{5,1},{2,6},{6,2},{3,7},{7,3},{8,12},{12,8},{9,1... | collective-permute-start | bytes 12296 | tf_op jit(solution)/shard_map/ppermute | solution.py:27
  8.4 19.4 %collective-permute-start.3 = (bf16[6,128,128]{2,1,0:T(8,128)(2,1)S(1)}, bf16[6,128,128]{2,1,0:T(8,128)(2,1)S(1)}, u32[]{:S(2)}, u32[]{:S(2)}) collective-permute-start(bf16[6,128,128]{2,1,0:T(8,128)(2,1)S(1)} %get-tuple-element.24), channel_id=1, source_target_pairs={{0,1},{1,2},{2,3},{4,5},{5,6},{6,7},{8,9},{9,10},{10,11},{12,13},{... | collective-permute-start | bytes 589832 | tf_op jit(solution)/shard_map/ppermute | solution.py:32
  13.3 14.5 %collective-permute-start.4 = (bf16[6,128,128]{2,1,0:T(8,128)(2,1)S(1)}, bf16[6,128,128]{2,1,0:T(8,128)(2,1)S(1)}, u32[]{:S(2)}, u32[]{:S(2)}) collective-permute-start(bf16[6,128,128]{2,1,0:T(8,128)(2,1)S(1)} %get-tuple-element.25), channel_id=1, source_target_pairs={{1,0},{2,1},{3,2},{5,4},{6,5},{7,6},{9,8},{10,9},{11,10},{13,12},{... | collective-permute-start | bytes 589832 | tf_op jit(solution)/shard_map/ppermute | solution.py:32
  14.6 7.4 %collective-permute-start.5 = (f32[8,128]{1,0:T(8,128)S(1)}, f32[8,128]{1,0:T(8,128)S(1)}, u32[]{:S(2)}, u32[]{:S(2)}) collective-permute-start(f32[8,128]{1,0:T(8,128)S(1)} %get-tuple-element.26.refs_0_), channel_id=1, source_target_pairs={{0,1},{1,0},{2,3},{3,2},{4,5},{5,4},{6,7},{7,6},{8,9},{9,8},{10,11... | collective-permute-start | bytes 12296 | tf_op jit(solution)/shard_map/ppermute | solution.py:27
  17.3 10.5 %collective-permute-start.6 = (f32[8,128]{1,0:T(8,128)S(1)}, f32[8,128]{1,0:T(8,128)S(1)}, u32[]{:S(2)}, u32[]{:S(2)}) collective-permute-start(f32[8,128]{1,0:T(8,128)S(1)} %get-tuple-element.26.refs_0_), channel_id=1, source_target_pairs={{0,2},{1,3},{2,0},{3,1},{4,6},{5,7},{6,4},{7,5},{8,10},{9,11},{10,... | collective-permute-start | bytes 12296 | tf_op jit(solution)/shard_map/ppermute | solution.py:27
  22.0 5.8 %collective-permute-start.7 = (f32[8,128]{1,0:T(8,128)S(1)}, f32[8,128]{1,0:T(8,128)S(1)}, u32[]{:S(2)}, u32[]{:S(2)}) collective-permute-start(f32[8,128]{1,0:T(8,128)S(1)} %get-tuple-element.26.refs_0_), channel_id=1, source_target_pairs={{0,3},{1,2},{2,1},{3,0},{4,7},{5,6},{6,5},{7,4},{8,11},{9,10},{10,... | collective-permute-start | bytes 12296 | tf_op jit(solution)/shard_map/ppermute | solution.py:27
  31.1 10.1 %copy-start.1 = (bf16[3,3,3,128,128]{4,3,2,1,0:T(8,128)(2,1)S(1)}, bf16[3,3,3,128,128]{4,3,2,1,0:T(8,128)(2,1)}, u32[]{:S(2)}) copy-start(bf16[3,3,3,128,128]{4,3,2,1,0:T(8,128)(2,1)} %kernel_ref.1) | copy-start | bytes 2654212
  41.1 0.7 copy-start.2
  41.1 4.6 %collective-permute-start.8 = (f32[4,448,128]{2,1,0:T(8,128)S(1)}, f32[4,448,128]{2,1,0:T(8,128)S(1)}, u32[]{:S(2)}, u32[]{:S(2)}) collective-permute-start(f32[4,448,128]{2,1,0:T(8,128)S(1)} %get-tuple-element.29), channel_id=1, source_target_pairs={{0,4},{4,0},{1,5},{5,1},{2,6},{6,2},{3,7},{7,3},{8,12},{12,8},{9,1... | collective-permute-start | bytes 2752520 | tf_op jit(solution)/shard_map/ppermute | solution.py:27
  46.4 7.2 %collective-permute-start.10 = (bf16[448,128]{1,0:T(8,128)(2,1)S(1)}, bf16[448,128]{1,0:T(8,128)(2,1)S(1)}, u32[]{:S(2)}, u32[]{:S(2)}) collective-permute-start(bf16[448,128]{1,0:T(8,128)(2,1)S(1)} %get-tuple-element.32), channel_id=1, source_target_pairs={{0,16},{8,24},{16,0},{24,8},{1,17},{9,25},{17,1},{25,9},{2,18},{10... | collective-permute-start | bytes 344072 | tf_op jit(solution)/shard_map/ppermute | solution.py:27
  48.0 7.0 %collective-permute-start.11 = (bf16[448,128]{1,0:T(8,128)(2,1)S(1)}, bf16[448,128]{1,0:T(8,128)(2,1)S(1)}, u32[]{:S(2)}, u32[]{:S(2)}) collective-permute-start(bf16[448,128]{1,0:T(8,128)(2,1)S(1)} %get-tuple-element.33), channel_id=1, source_target_pairs={{0,24},{8,16},{16,8},{24,0},{1,25},{9,17},{17,9},{25,1},{2,26},{10... | collective-permute-start | bytes 344072 | tf_op jit(solution)/shard_map/ppermute | solution.py:27
  49.4 6.1 %collective-permute-start.9 = (bf16[448,128]{1,0:T(8,128)(2,1)S(1)}, bf16[448,128]{1,0:T(8,128)(2,1)S(1)}, u32[]{:S(2)}, u32[]{:S(2)}) collective-permute-start(bf16[448,128]{1,0:T(8,128)(2,1)S(1)} %get-tuple-element.31), channel_id=1, source_target_pairs={{0,8},{8,0},{16,24},{24,16},{1,9},{9,1},{17,25},{25,17},{2,10},{10... | collective-permute-start | bytes 344072 | tf_op jit(solution)/shard_map/ppermute | solution.py:27
  55.5 6.8 %collective-permute-start.12 = (f32[448,128]{1,0:T(8,128)S(1)}, f32[448,128]{1,0:T(8,128)S(1)}, u32[]{:S(2)}, u32[]{:S(2)}) collective-permute-start(f32[448,128]{1,0:T(8,128)S(1)} %added.3.after_ref.refs_0_), channel_id=1, source_target_pairs={{0,1},{1,0},{2,3},{3,2},{4,5},{5,4},{6,7},{7,6},{8,9},{9,8},{10,11... | collective-permute-start | bytes 688136 | tf_op jit(solution)/shard_map/ppermute | solution.py:27
  62.3 7.0 %collective-permute-start.13 = (bf16[448,128]{1,0:T(8,128)(2,1)S(1)}, bf16[448,128]{1,0:T(8,128)(2,1)S(1)}, u32[]{:S(2)}, u32[]{:S(2)}) collective-permute-start(bf16[448,128]{1,0:T(8,128)(2,1)S(1)} %added.4.after_ref.refs_0_), channel_id=1, source_target_pairs={{0,2},{1,3},{2,0},{3,1},{4,6},{5,7},{6,4},{7,5},{8,10},{9,11},{10,... | collective-permute-start | bytes 344072 | tf_op jit(solution)/shard_map/ppermute | solution.py:27
  69.4 4.9 %collective-permute-start.14 = (bf16[448,128]{1,0:T(8,128)(2,1)S(1)}, bf16[448,128]{1,0:T(8,128)(2,1)S(1)}, u32[]{:S(2)}, u32[]{:S(2)}) collective-permute-start(bf16[448,128]{1,0:T(8,128)(2,1)S(1)} %added.5.after_ref.refs_0_), channel_id=1, source_target_pairs={{0,8},{8,0},{16,24},{24,16},{1,9},{9,1},{17,25},{25,17},{2,10},{10... | collective-permute-start | bytes 344072 | tf_op jit(solution)/shard_map/ppermute | solution.py:27
  70.9 4.8 %collective-permute-start.15 = (bf16[448,128]{1,0:T(8,128)(2,1)S(1)}, bf16[448,128]{1,0:T(8,128)(2,1)S(1)}, u32[]{:S(2)}, u32[]{:S(2)}) collective-permute-start(bf16[448,128]{1,0:T(8,128)(2,1)S(1)} %added.5.after_ref.refs_0_), channel_id=1, source_target_pairs={{0,16},{8,24},{16,0},{24,8},{1,17},{9,25},{17,1},{25,9},{2,18},{10... | collective-permute-start | bytes 344072 | tf_op jit(solution)/shard_map/ppermute | solution.py:27
  72.4 5.7 %collective-permute-start.16 = (bf16[448,128]{1,0:T(8,128)(2,1)S(1)}, bf16[448,128]{1,0:T(8,128)(2,1)S(1)}, u32[]{:S(2)}, u32[]{:S(2)}) collective-permute-start(bf16[448,128]{1,0:T(8,128)(2,1)S(1)} %added.5.after_ref.refs_0_), channel_id=1, source_target_pairs={{0,24},{8,16},{16,8},{24,0},{1,25},{9,17},{17,9},{25,1},{2,26},{10... | collective-permute-start | bytes 344072 | tf_op jit(solution)/shard_map/ppermute | solution.py:27
  72.9 7.2 %collective-permute-start.17 = (bf16[448,128]{1,0:T(8,128)(2,1)S(1)}, bf16[448,128]{1,0:T(8,128)(2,1)S(1)}, u32[]{:S(2)}, u32[]{:S(2)}) collective-permute-start(bf16[448,128]{1,0:T(8,128)(2,1)S(1)} %added.5.after_ref.refs_0_), channel_id=1, source_target_pairs={{0,4},{4,0},{1,5},{5,1},{2,6},{6,2},{3,7},{7,3},{8,12},{12,8},{9,1... | collective-permute-start | bytes 344072 | tf_op jit(solution)/shard_map/ppermute | solution.py:27
  74.2 5.9 %collective-permute-start.18 = (bf16[448,128]{1,0:T(8,128)(2,1)S(1)}, bf16[448,128]{1,0:T(8,128)(2,1)S(1)}, u32[]{:S(2)}, u32[]{:S(2)}) collective-permute-start(bf16[448,128]{1,0:T(8,128)(2,1)S(1)} %collective-permute-done.14.refs_1_), channel_id=1, source_target_pairs={{0,4},{4,0},{1,5},{5,1},{2,6},{6,2},{3,7},{7,3},{8,12},{12,8},{9,1... | collective-permute-start | bytes 344072 | tf_op jit(solution)/shard_map/ppermute | solution.py:27
  75.7 4.4 %collective-permute-start.19 = (bf16[448,128]{1,0:T(8,128)(2,1)S(1)}, bf16[448,128]{1,0:T(8,128)(2,1)S(1)}, u32[]{:S(2)}, u32[]{:S(2)}) collective-permute-start(bf16[448,128]{1,0:T(8,128)(2,1)S(1)} %collective-permute-done.15.refs_2_), channel_id=1, source_target_pairs={{0,4},{4,0},{1,5},{5,1},{2,6},{6,2},{3,7},{7,3},{8,12},{12,8},{9,1... | collective-permute-start | bytes 344072 | tf_op jit(solution)/shard_map/ppermute | solution.py:27
  78.1 2.0 %collective-permute-start.20 = (bf16[448,128]{1,0:T(8,128)(2,1)S(1)}, bf16[448,128]{1,0:T(8,128)(2,1)S(1)}, u32[]{:S(2)}, u32[]{:S(2)}) collective-permute-start(bf16[448,128]{1,0:T(8,128)(2,1)S(1)} %collective-permute-done.16.refs_3_), channel_id=1, source_target_pairs={{0,4},{4,0},{1,5},{5,1},{2,6},{6,2},{3,7},{7,3},{8,12},{12,8},{9,1... | collective-permute-start | bytes 344072 | tf_op jit(solution)/shard_map/ppermute | solution.py:27

commit v5 on v4

--- a/solution.py
+++ b/solution.py
@@ -56,52 +56,59 @@
     return count, total, mean, squares
 
 
-def stats_kernel(per, before, info_ref, video_ref, out_ref, tail_ref, ends_ref, sums, squares):
-    frames = pl.num_programs(0)
-    t = pl.program_id(0)
-    rows, cols, chans = video_ref.shape[2:]
-    size = float(rows * cols * per)
+def stats_kernel(per, before, info_ref, video_hbm, cot_hbm, *refs):
+    out_ref, video_ref, cot_ref, tail_ref, ends_ref, early_ref, sems = refs
+    frames, rows, cols, chans = video_ref.shape[1:]
+    parts_n = 2 * frames
+    some = rows // 2
+    first = frames - before
+    copies = []
+    for n in range(parts_n):
+        at = (0, n // 2, pl.ds(n % 2 * some, some))
+        copies.append((video_hbm.at[at], video_ref.at[at]))
+    copies.append((video_hbm.at[:, first:], tail_ref))
+    for side, row in enumerate((rows - 1, 0)):
+        copies.append((video_hbm.at[0, :, row], ends_ref.at[side]))
+        copies.append((video_hbm.at[0, first:, row], early_ref.at[side]))
+    copies.append((cot_hbm, cot_ref))
+    copies = [
+        pltpu.make_async_copy(source, target, sems.at[n])
+        for n, (source, target) in enumerate(copies)
+    ]
+    for copy in copies:
+        copy.start()
+    size = float(some * cols * per)
     lanes = 4
     split = (cols // (8 * lanes), lanes, 8, chans)
-
-    def add(y, acc):
-        return acc + jnp.sum(video_ref[0, 0, y].astype(F32).reshape(split), axis=0)
-
     start = jnp.zeros((lanes, 8, chans), F32)
-    acc = jnp.sum(lax.fori_loop(0, rows, add, start, unroll=4), axis=0)
-    total = group_sum(jnp.sum(acc, axis=0, keepdims=True), per)
-    mean = total / size
-
-    def deviate(y, acc):
-        away = video_ref[0, 0, y].astype(F32).reshape(split) - mean
-        return acc + jnp.sum(away * away, axis=0)
-
-    acc = jnp.sum(lax.fori_loop(0, rows, deviate, start, unroll=4), axis=0)
-    sums[t] = jnp.broadcast_to(total, (8, chans))
-    squares[t] = jnp.broadcast_to(group_sum(jnp.sum(acc, axis=0, keepdims=True), per), (8, chans))
-    ends_ref[0, t] = video_ref[0, 0, rows - 1]
-    ends_ref[1, t] = video_ref[0, 0, 0]
-
-    @pl.when(t >= frames - before)
-    def _():
-        tail_ref[0, t - (frames - before)] = video_ref[0, 0]
-
-    @pl.when(t == frames - 1)
-    def _():
-        inside = info_ref[0]
-        parts = []
-        for f in range(sums.shape[0]):
-            keep = (f < inside).astype(F32)
-            parts.append(
-                jnp.concatenate(
-                    [jnp.full((1, chans), size, F32), sums[f, 0:1], squares[f, 0:1]], axis=0
-                )
-                * keep
-            )
-        count, total, _, deviations = merged(parts)
-        out_ref[...] = jnp.concatenate(
-            [count, total, deviations, jnp.zeros((5, chans), F32)], axis=0
+    parts = []
+    for n in range(parts_n):
+        copies[n].wait()
+        f, y0 = n // 2, n % 2 * some
+
+        def add(y, acc, f=f, y0=y0):
+            return acc + jnp.sum(video_ref[0, f, y0 + y].astype(F32).reshape(split), axis=0)
+
+        acc = jnp.sum(lax.fori_loop(0, some, add, start, unroll=4), axis=0)
+        total = group_sum(jnp.sum(acc, axis=0, keepdims=True), per)
+        mean = total / size
+
+        def deviate(y, acc, f=f, y0=y0, mean=mean):
+            away = video_ref[0, f, y0 + y].astype(F32).reshape(split) - mean
+            return acc + jnp.sum(away * away, axis=0)
+
+        acc = jnp.sum(lax.fori_loop(0, some, deviate, start, unroll=4), axis=0)
+        squares = group_sum(jnp.sum(acc, axis=0, keepdims=True), per)
+        keep = (f < info_ref[0]).astype(F32)
+        parts.append(
+            jnp.concatenate([jnp.full((1, chans), size, F32), total, squares], axis=0) * keep
         )
+    count, total, _, deviations = merged(parts)
+    out_ref[...] = jnp.concatenate(
+        [count, total, deviations, jnp.zeros((5, chans), F32)], axis=0
+    )
+    for copy in copies[parts_n:]:
+        copy.wait()
 
 
 def merge_kernel(parts_n, ends_ref, early_ref, *refs):
@@ -117,27 +124,26 @@
 
 
 def cotangent_kernel(info_ref, cot_ref, turned_ref, bias_ref, wide):
-    t = pl.program_id(0)
-    rows, cols, chans = cot_ref.shape[2:]
+    frames, rows, cols, chans = cot_ref.shape[1:]
     step = cols // TILE
-    keep = (t < info_ref[0]).astype(F32)
-
-    @pl.when(t == 0)
-    def _():
-        bias_ref[...] = jnp.zeros_like(bias_ref)
-
-    def row(y, acc):
-        value = cot_ref[0, 0, y].astype(F32) * keep
-        slot = wide.at[y % wide.shape[0]]
-        slot[...] = value
-        order = jnp.concatenate(
-            [slot[pl.ds(r, TILE, stride=step), :] for r in range(step)], axis=0
-        )
-        turned_ref[0, y] = order.T.astype(BF16)
-        return acc + jnp.sum(value.reshape(cols // 8, 8, chans), axis=0)
-
-    acc = lax.fori_loop(0, rows, row, jnp.zeros((8, chans), F32), unroll=4)
-    bias_ref[0:1, :] += jnp.sum(acc, axis=0, keepdims=True)
+    lanes = 4
+    bias = jnp.zeros((lanes, 8, chans), F32)
+    for t in range(frames):
+        keep = (t < info_ref[0]).astype(F32)
+
+        def row(y, acc, t=t, keep=keep):
+            value = cot_ref[0, t, y].astype(F32) * keep
+            slot = wide.at[y % wide.shape[0]]
+            slot[...] = value
+            order = jnp.concatenate(
+                [slot[pl.ds(r, TILE, stride=step), :] for r in range(step)], axis=0
+            )
+            turned_ref[t, y] = order.astype(BF16).T
+            return acc + jnp.sum(value.reshape(cols // (8 * lanes), lanes, 8, chans), axis=0)
+
+        bias = lax.fori_loop(0, rows, row, bias, unroll=8)
+    total = jnp.sum(jnp.sum(bias, axis=0), axis=0, keepdims=True)
+    bias_ref[...] = jnp.broadcast_to(total, bias_ref.shape)
 
 
 def activate_kernel(
@@ -247,10 +253,10 @@
 
 
 def add_kernel(after_ref, *refs):
-    value = refs[0][...].astype(F32)
-    for ref in refs[1:-1]:
-        value = value + ref[...].astype(F32)
-    refs[-1][...] = packed(value) if refs[-1].dtype == BF16 else value
+    values = [ref[...].astype(F32) for ref in refs[:-1]]
+    while len(values) > 1:
+        values = [sum(values[n : n + 2]) for n in range(0, len(values), 2)]
+    refs[-1][...] = packed(values[0])
 
 
 def taps_kernel(after_ref, kernel_ref, out_ref):
@@ -267,8 +273,15 @@
             out_ref[f * span : (f + 1) * span, g * chans : (g + 1) * chans] = value
 
 
-def conv_kernel(t0, y0, rows, info_ref, after_ref, act_ref, taps_ref, video_ref, bias_ref, *refs):
-    out_ref, wide = refs
+def conv_kernel(
+    piece, last, info_ref, after_ref, act_ref, taps_ref, video_ref, bias_ref, *refs
+):
+    out_ref, whole_ref, wide, sem = refs[-4:]
+    t0, y0 = piece
+    rows = out_ref.shape[1]
+    if last is not None:
+        out = pltpu.make_async_copy(refs[0], whole_ref.at[last], sem)
+        out.start()
     cols, chans = out_ref.shape[2:]
     step = cols // TILE
     pair = taps_ref.shape[1] // chans
@@ -297,6 +310,8 @@
                 ]
             value = video_ref[0, t0 + f, y0 + y].astype(F32) + wide[slot] + bias_ref[...]
             out_ref[f, y] = (value * keep).astype(BF16)
+    if last is not None:
+        out.wait()
 
 
 def step_of(video, lengths, norm_gain, norm_shift, kernel, conv_bias, cotangent):
@@ -319,28 +334,30 @@
         ]
     ).astype(jnp.int32)
 
-    frame_spec = pl.BlockSpec((1, 1, rows, cols, chans), lambda t: (0, t, 0, 0, 0))
-    stats, tail, ends = pl.pallas_call(
+    both = 2 * frames + 6
+    stats, local, masked_in, tail, ends, ends_tail = pl.pallas_call(
         functools.partial(stats_kernel, per, before),
-        grid=(frames,),
-        in_specs=[SMEM, frame_spec],
-        out_specs=[
-            pl.BlockSpec((8, chans), lambda t: (0, 0)),
-            pl.BlockSpec((1, before, rows, cols, chans), lambda t: (0, 0, 0, 0, 0)),
-            pl.BlockSpec((2, frames, cols, chans), lambda t: (0, 0, 0, 0)),
-        ],
+        in_specs=[SMEM, ANY, ANY],
+        out_specs=[VMEM] * 6,
         out_shape=[
             jax.ShapeDtypeStruct((8, chans), F32),
+            jax.ShapeDtypeStruct(video.shape, BF16),
+            jax.ShapeDtypeStruct(cotangent.shape, BF16),
             jax.ShapeDtypeStruct((1, before, rows, cols, chans), BF16),
             jax.ShapeDtypeStruct((2, frames, cols, chans), BF16),
+            jax.ShapeDtypeStruct((2, before, cols, chans), BF16),
         ],
-        scratch_shapes=[pltpu.VMEM((frames, 8, chans), F32), pltpu.VMEM((frames, 8, chans), F32)],
-        compiler_params=params(8),
+        scratch_shapes=[pltpu.SemaphoreType.DMA((both,))],
+        compiler_params=params(2),
         name="stats",
-    )(info, pltpu.with_memory_space_constraint(video, pltpu.HBM))
+    )(
+        info,
+        pltpu.with_memory_space_constraint(video, pltpu.HBM),
+        pltpu.with_memory_space_constraint(cotangent, pltpu.HBM),
+    )
     gathered = [stats] + [swap(stats, "tm", r) for r in range(1, tms)]
     following = [(i, (i + 1) % tms) for i in range(tms)]
-    early_ends = lax.ppermute(ends[:, frames - before :], "tm", following)
+    early_ends = lax.ppermute(ends_tail, "tm", following)
     early = lax.ppermute(tail, "tm", following)
     border = jax.ShapeDtypeStruct((before + frames, cols, chans), BF16)
     stats, edge_low, edge_high = pl.pallas_call(
@@ -368,20 +385,16 @@
 
     turned, bias = pl.pallas_call(
         cotangent_kernel,
-        grid=(frames,),
-        in_specs=[SMEM, frame_spec],
-        out_specs=[
-            pl.BlockSpec((1, rows, chans, cols), lambda t: (t, 0, 0, 0)),
-            pl.BlockSpec((8, chans), lambda t: (0, 0)),
-        ],
+        in_specs=[SMEM, VMEM],
+        out_specs=[VMEM, VMEM],
         out_shape=[
             jax.ShapeDtypeStruct((frames, rows, chans, cols), BF16),
             jax.ShapeDtypeStruct((8, chans), F32),
         ],
-        scratch_shapes=[pltpu.VMEM((4, cols, chans), F32)],
-        compiler_params=params(8),
+        scratch_shapes=[pltpu.VMEM((8, cols, chans), F32)],
+        compiler_params=params(4),
         name="cotangent",
-    )(info, pltpu.with_memory_space_constraint(cotangent, pltpu.HBM))
+    )(info, masked_in)
 
     act = pl.pallas_call(
         functools.partial(activate_kernel, spaces),
@@ -395,7 +408,7 @@
         name="activate",
     )(
         info,
-        video,
+        local,
         early,
         low,
         high,
@@ -426,23 +439,35 @@
     pieces = [(t0, y0) for t0 in range(0, frames, pair) for y0 in range(0, rows, block)]
     done = []
 
+    whole = jax.ShapeDtypeStruct(video.shape, BF16)
+
+    def where(n):
+        t0, y0 = pieces[n]
+        return 0, pl.ds(t0, pair), pl.ds(y0, block)
+
     def cover(after, number):
         for _ in range(min(number, len(pieces) - len(done))):
-            t0, y0 = pieces[len(done)]
-            after = pl.pallas_call(
-                functools.partial(conv_kernel, t0, y0, block),
-                in_specs=[SMEM, ANY, VMEM, VMEM, VMEM, VMEM],
-                out_specs=VMEM,
-                out_shape=jax.ShapeDtypeStruct((pair, block, cols, chans), BF16),
-                scratch_shapes=[pltpu.VMEM((pair * block, cols, chans), F32)],
+            n = len(done)
+            made = list(done[-1]) if done else []
+            piece, output = pl.pallas_call(
+                functools.partial(conv_kernel, pieces[n], where(n - 1) if made else None),
+                in_specs=[SMEM, ANY, VMEM, VMEM, VMEM, VMEM] + [VMEM, ANY][: len(made)],
+                out_specs=[VMEM, ANY],
+                out_shape=[jax.ShapeDtypeStruct((pair, block, cols, chans), BF16), whole],
+                scratch_shapes=[
+                    pltpu.VMEM((pair * block, cols, chans), F32),
+                    pltpu.SemaphoreType.DMA,
+                ],
+                input_output_aliases={7: 1} if made else {},
                 compiler_params=params(6),
                 name="conv",
-            )(info, after, act, taps, video, conv_bias.reshape(1, chans))
-            done.append(after)
+            )(info, after, act, taps, local, conv_bias.reshape(1, chans), *made)
+            done.append((piece, output))
+            after = piece
         return after
 
     incoming = [swap(send, "tm", r + 1) for r, send in enumerate(sends)]
-    token = cover(keep, 2)
+    token = cover(keep, 1)
     own, *sends = pl.pallas_call(
         functools.partial(spread_kernel, len(incoming)),
         in_specs=[SMEM, ANY] + [VMEM] * (1 + len(incoming)),
@@ -464,14 +489,11 @@
         )(after, *arrays)
 
     incoming = [swap(send, "dp", r + 1) for r, send in enumerate(sends)]
-    token = cover(own, 1)
-    total = added(F32 if spaces > 2 else BF16, token, own, *incoming)
-    by = 1
-    while by < spaces:
-        other = swap(total, "space", by)
-        token = cover(total, 2)
-        by *= 2
-        total = added(F32 if 2 * by < spaces else BF16, token, total, other)
+    token = cover(own, 3)
+    total = added(BF16, token, own, *incoming)
+    others = [swap(total, "space", r) for r in range(1, spaces)]
+    token = cover(total, 3)
+    total = added(BF16, token, total, *others)
     mine = [total] + [swap(total, "dp", r) for r in range(1, dps)]
     cover(total, len(pieces))
     shards = {(0, r): array for r, array in enumerate(mine)}
@@ -481,34 +503,31 @@
     order = list(shards)
 
     def collect(info_ref, *refs):
-        shard_refs, piece_refs = refs[: len(order)], refs[len(order) : len(order) + len(done)]
-        out_ref, sum_ref, output_ref, sems = refs[-4:]
-        copies = []
-        for n, (t0, y0) in enumerate(pieces):
-            target = output_ref.at[0, t0 : t0 + pair, y0 : y0 + block]
-            copies.append(pltpu.make_async_copy(piece_refs[n], target, sems.at[n]))
-            copies[-1].start()
+        shard_refs, piece_ref = refs[: len(order)], refs[len(order)]
+        out_ref, sum_ref, whole_ref, sem = refs[-4:]
+        copy = pltpu.make_async_copy(piece_ref, whole_ref.at[where(len(pieces) - 1)], sem)
+        copy.start()
         for (q, r), ref in zip(order, shard_refs):
             at = (info_ref[4] ^ q) * dps + (info_ref[5] ^ r)
             out_ref[at] = ref[0:shard, :].astype(F32)
         tail = shard_refs[0][shard : shard + TILE, :].astype(F32)
         sum_ref[...] = tail[0:1] + tail[1:2] + tail[2:3]
-        for copy in copies:
-            copy.wait()
+        copy.wait()
 
     grad_kernel, grad_bias, output = pl.pallas_call(
         collect,
-        in_specs=[SMEM] + [VMEM] * (len(order) + len(done)),
+        in_specs=[SMEM] + [VMEM] * (len(order) + 1) + [ANY],
         out_specs=[VMEM, VMEM, ANY],
         out_shape=[
             jax.ShapeDtypeStruct((shards_n, shard, chans), F32),
             jax.ShapeDtypeStruct((1, chans), F32),
-            jax.ShapeDtypeStruct(video.shape, BF16),
+            whole,
         ],
-        scratch_shapes=[pltpu.SemaphoreType.DMA((len(pieces),))],
+        scratch_shapes=[pltpu.SemaphoreType.DMA],
+        input_output_aliases={len(order) + 2: 2},
         compiler_params=params(4),
         name="collect",
-    )(info, *[shards[key] for key in order], *done)
+    )(info, *[shards[key] for key in order], *done[-1])
 
     return output, grad_kernel.reshape(kernel.shape), grad_bias.reshape(chans)
 

time: 83.7 us -> 81 us (0.968)
  waiting for transfers between devices: 15.9 us -> 13.9 us
    ppermute x17 -> x18, waiting for transfers between devices: 15.8 us -> 13.9 us  [swap(): return lax.ppermute(array, axis, [(i, i ^ by) for i in range(length)])]
    ppermute x17 -> x18, starting transfers between devices: 17.3 us -> 17.3 us  [swap(): return lax.ppermute(array, axis, [(i, i ^ by) for i in range(length)])]
  transfers between devices with their start and end apart: 21 -> 22, of which waited for: 10 -> 7; matrix products, arithmetic and copies ran while one was open for 0% -> 0% of each run, Pallas kernels for 24% -> 24%
where the time goes in v5:
time: 81 us; the launch traced here: 80.8 us
  Pallas kernels  40.8 us (50%)
  starting transfers between devices  24 us (30%)
  waiting for transfers between devices  13.9 us (17%)
  between operations  1.74 us (2%)
    ppermute x18, starting transfers between devices, swap(): return lax.ppermute(array, axis, [(i, i ^ by) for i in range(length)])  17.3 us
    pallas_call x8, Pallas kernels, cover(): pl.pallas_call(functools.partial(conv_kernel, pieces[n], where(n - 1) if...  16.4 us
    ppermute x18, waiting for transfers between devices, swap(): return lax.ppermute(array, axis, [(i, i ^ by) for i in range(length)])  13.9 us
    pallas_call x1, Pallas kernels, step_of(): pl.pallas_call(weights_kernel, in_specs=[SMEM, VMEM, VMEM, VMEM], out_spe...  9.95 us
    ppermute x2, starting transfers between devices, shifted(): lax.ppermute(array, axis, [(i, i + by) for i in range(length) if 0 <= i +...  6.14 us
    pallas_call x1, Pallas kernels, step_of(): pl.pallas_call(functools.partial(stats_kernel, per, before), in_specs=[SM...  5.01 us
    pallas_call x1, Pallas kernels, step_of(): pl.pallas_call(functools.partial(activate_kernel, spaces), in_specs=[SMEM...  3.25 us
    pallas_call x1, Pallas kernels, step_of(): pl.pallas_call(collect, in_specs=[SMEM] + [VMEM] * (len(order) + 1) + [AN...  2.54 us
  transfers between devices with their start and end apart: 22, of which 7 were waited for; matrix products, arithmetic and copies ran while one was open for 0% of the time, Pallas kernels for 24%

profile of v5, /device:TPU:0, one launch (start us, length us, event | category | flops | bytes accessed | tf_op | source)
XLA Modules:
  0.0 80.8 jit_solution(7851671142651980078)
XLA Ops:
  1.3 0.1 stack.35.info_ref
  1.4 5.0 %stats.1 = (f32[8,128]{1,0:T(8,128)S(1)}, bf16[1,4,16,128,128]{4,3,2,1,0:T(8,128)(2,1)S(1)}, bf16[1,4,16,128,128]{4,3,2,1,0:T(8,128)(2,1)S(1)}, bf16[1,2,16,128,...) custom-call(s32[6]{0:T(128)S(1)} %stack.35.info_ref, ...), custom_call_target="tpu_custom_call" | custom-call | tf_op jit(solution)/shard_map/stats/pallas_call | solution.py:338
  6.4 0.0 copy-start.2
  6.4 0.0 copy-start.3
  6.4 0.6 collective-permute-start
  7.0 0.1 collective-permute-start.1
  7.1 0.4 collective-permute-start.2
  7.5 2.0 %collective-permute-done.2.refs_1_ = f32[8,128]{1,0:T(8,128)S(1)} collective-permute-done((f32[8,128]{1,0:T(8,128)S(1)}, f32[8,128]{1,0:T(8,128)S(1)}, u32[]{:S(2)}, u32[]{:S(2)}) %collective-permute-start.2) | collective-permute-done | bytes 4128 | tf_op jit(solution)/shard_map/ppermute | solution.py:27
  9.5 4.8 %collective-permute-start.3 = (bf16[6,128,128]{2,1,0:T(8,128)(2,1)S(1)}, bf16[6,128,128]{2,1,0:T(8,128)(2,1)S(1)}, u32[]{:S(2)}, u32[]{:S(2)}) collective-permute-start(bf16[6,128,128]{2,1,0:T(8,128)(2,1)S(1)} %get-tuple-element.46), channel_id=1, source_target_pairs={{0,1},{1,2},{2,3},{4,5},{5,6},{6,7},{8,9},{9,10},{10,11},{12,13},{... | collective-permute-start | bytes 589832 | tf_op jit(solution)/shard_map/ppermute | solution.py:32
  14.4 1.3 %collective-permute-start.4 = (bf16[6,128,128]{2,1,0:T(8,128)(2,1)S(1)}, bf16[6,128,128]{2,1,0:T(8,128)(2,1)S(1)}, u32[]{:S(2)}, u32[]{:S(2)}) collective-permute-start(bf16[6,128,128]{2,1,0:T(8,128)(2,1)S(1)} %get-tuple-element.47), channel_id=1, source_target_pairs={{1,0},{2,1},{3,2},{5,4},{6,5},{7,6},{9,8},{10,9},{11,10},{13,12},{... | collective-permute-start | bytes 589832 | tf_op jit(solution)/shard_map/ppermute | solution.py:32
  15.7 4.7 %collective-permute-start.7 = (f32[8,128]{1,0:T(8,128)S(1)}, f32[8,128]{1,0:T(8,128)S(1)}, u32[]{:S(2)}, u32[]{:S(2)}) collective-permute-start(f32[8,128]{1,0:T(8,128)S(1)} %get-tuple-element.48.refs_0_), channel_id=1, source_target_pairs={{0,3},{1,2},{2,1},{3,0},{4,7},{5,6},{6,5},{7,4},{8,11},{9,10},{10,... | collective-permute-start | bytes 12296 | tf_op jit(solution)/shard_map/ppermute | solution.py:27
  20.4 0.0 collective-permute-start.6
  20.4 4.7 %collective-permute-done.7.refs_3_ = f32[8,128]{1,0:T(8,128)S(1)} collective-permute-done((f32[8,128]{1,0:T(8,128)S(1)}, f32[8,128]{1,0:T(8,128)S(1)}, u32[]{:S(2)}, u32[]{:S(2)}) %collective-permute-start.7) | collective-permute-done | bytes 4128 | tf_op jit(solution)/shard_map/ppermute | solution.py:27
  25.1 2.5 %cotangent.1 = (bf16[4,16,128,128]{3,2,1,0:T(8,128)(2,1)S(1)}, f32[8,128]{1,0:T(8,128)S(1)}) custom-call(s32[6]{0:T(128)S(1)} %stack.35.info_ref, bf16[1,4,16,128,128]{4,3,2,1,0:T(8,128)(2,1)S(1)} %get-tuple-element.39.cot_ref), custom_call_target="tpu_custom_call" | custom-call | tf_op jit(solution)/shard_map/cotangent/pallas_call | solution.py:386
  27.6 1.1 %collective-permute-done.5.refs_1_ = f32[8,128]{1,0:T(8,128)S(1)} collective-permute-done((f32[8,128]{1,0:T(8,128)S(1)}, f32[8,128]{1,0:T(8,128)S(1)}, u32[]{:S(2)}, u32[]{:S(2)}) %collective-permute-start.5) | collective-permute-done | bytes 4128 | tf_op jit(solution)/shard_map/ppermute | solution.py:27
  28.7 3.2 %activate.1.act_ref = bf16[6,18,10,16,128]{4,3,2,1,0:T(8,128)(2,1)S(1)} custom-call(s32[6]{0:T(128)S(1)} %stack.35.info_ref, bf16[1,4,16,128,128]{4,3,2,1,0:T(8,128)(2,1)S(1)} %get-tuple-element.41.video_ref, bf16[1,2,16,128,128]{4,3,2,1,0:T(8,128)(2,1)S(1)} %collective-permute-done.early_ref, bf16[6,128,128]{2,1,0:T(8,128)(2,1)S(1)} %collective-permute-done.3.low_ref, ...), custom_call_target="tpu_custom_call" | custom-call | tf_op jit(solution)/shard_map/activate/pallas_call | solution.py:399
  32.0 0.0 copy-start
  32.0 10.0 %weights.1 = (f32[4,448,128]{2,1,0:T(8,128)S(1)}, f32[4,448,128]{2,1,0:T(8,128)S(1)}) custom-call(s32[6]{0:T(128)S(1)} %stack.35.info_ref, bf16[4,16,128,128]{3,2,1,0:T(8,128)(2,1)S(1)} %get-tuple-element.40.turned_ref, bf16[6,18,10,16,128]{4,3,2,1,0:T(8,128)(2,1)S(1)} %activate.1.act_ref, f32[8,128]{1,0:T(8,128)S(1)} %get-tuple-element.49.bias_ref), custom_call_target="tpu_custom_call" | custom-call | tf_op jit(solution)/shard_map/weights/pallas_call | solution.py:425
  41.9 0.0 copy-start.1
  41.9 0.1 collective-permute-start.8
  42.0 0.4 taps.1.taps_ref
  42.4 0.2 copy-done.1
  42.6 2.0 %conv.8 = (bf16[2,4,128,128]{3,2,1,0:T(8,128)(2,1)S(1)}, bf16[1,4,16,128,128]{4,3,2,1,0:T(8,128)(2,1)}) custom-call(s32[6]{0:T(128)S(1)} %stack.35.info_ref, f32[4,448,128]{2,1,0:T(8,128)S(1)} %get-tuple-element.50.after_ref.keep_ref, bf16[6,18,10,16,128]{4,3,2,1,0:T(8,128)(2,1)S(1)} %activate.1.act_ref, bf16[4608,256]{1,0:T(8,128)(2,1)S(1)} %taps.1.taps_ref, ...), custom_call_target="tpu_custom_call" | custom-call | tf_op jit(solution)/shard_map/conv/pallas_call | solution.py:452
  44.6 0.6 spread.1
  45.2 1.6 %collective-permute-start.9 = (bf16[448,128]{1,0:T(8,128)(2,1)S(1)}, bf16[448,128]{1,0:T(8,128)(2,1)S(1)}, u32[]{:S(2)}, u32[]{:S(2)}) collective-permute-start(bf16[448,128]{1,0:T(8,128)(2,1)S(1)} %get-tuple-element.60), channel_id=1, source_target_pairs={{0,8},{8,0},{16,24},{24,16},{1,9},{9,1},{17,25},{25,17},{2,10},{10... | collective-permute-start | bytes 344072 | tf_op jit(solution)/shard_map/ppermute | solution.py:27
  46.8 1.5 %collective-permute-start.10 = (bf16[448,128]{1,0:T(8,128)(2,1)S(1)}, bf16[448,128]{1,0:T(8,128)(2,1)S(1)}, u32[]{:S(2)}, u32[]{:S(2)}) collective-permute-start(bf16[448,128]{1,0:T(8,128)(2,1)S(1)} %get-tuple-element.61), channel_id=1, source_target_pairs={{0,16},{8,24},{16,0},{24,8},{1,17},{9,25},{17,1},{25,9},{2,18},{10... | collective-permute-start | bytes 344072 | tf_op jit(solution)/shard_map/ppermute | solution.py:27
  48.3 0.5 collective-permute-start.11
  48.8 2.5 %conv.9 = (bf16[2,4,128,128]{3,2,1,0:T(8,128)(2,1)S(1)}, bf16[1,4,16,128,128]{4,3,2,1,0:T(8,128)(2,1)}) custom-call(s32[6]{0:T(128)S(1)} %stack.35.info_ref, f32[448,128]{1,0:T(8,128)S(1)} %get-tuple-element.53.after_ref.refs_0_, bf16[6,18,10,16,128]{4,3,2,1,0:T(8,128)(2,1)S(1)} %activate.1.act_ref, ...), custom_call_target="tpu_custom_call", output_to_operand_aliasing={{1}: (7, {})} | custom-call | tf_op jit(solution)/shard_map/conv/pallas_call | solution.py:452
  51.3 2.0 %conv.10 = (bf16[2,4,128,128]{3,2,1,0:T(8,128)(2,1)S(1)}, bf16[1,4,16,128,128]{4,3,2,1,0:T(8,128)(2,1)}) custom-call(s32[6]{0:T(128)S(1)} %stack.35.info_ref, bf16[2,4,128,128]{3,2,1,0:T(8,128)(2,1)S(1)} %get-tuple-element.55.after_ref.refs_0_, bf16[6,18,10,16,128]{4,3,2,1,0:T(8,128)(2,1)S(1)} %activate.1.act_ref, ...), custom_call_target="tpu_custom_call", output_to_operand_aliasing={{1}: (7, {})} | custom-call | tf_op jit(solution)/shard_map/conv/pallas_call | solution.py:452
  53.3 2.0 %conv.11 = (bf16[2,4,128,128]{3,2,1,0:T(8,128)(2,1)S(1)}, bf16[1,4,16,128,128]{4,3,2,1,0:T(8,128)(2,1)}) custom-call(s32[6]{0:T(128)S(1)} %stack.35.info_ref, bf16[2,4,128,128]{3,2,1,0:T(8,128)(2,1)S(1)} %get-tuple-element.57.after_ref.refs_0_, bf16[6,18,10,16,128]{4,3,2,1,0:T(8,128)(2,1)S(1)} %activate.1.act_ref, ...), custom_call_target="tpu_custom_call", output_to_operand_aliasing={{1}: (7, {})} | custom-call | tf_op jit(solution)/shard_map/conv/pallas_call | solution.py:452
  55.3 0.1 added.2.after_ref.refs_0_
  55.4 0.8 collective-permute-start.14
  56.2 1.7 %collective-permute-start.13 = (bf16[448,128]{1,0:T(8,128)(2,1)S(1)}, bf16[448,128]{1,0:T(8,128)(2,1)S(1)}, u32[]{:S(2)}, u32[]{:S(2)}) collective-permute-start(bf16[448,128]{1,0:T(8,128)(2,1)S(1)} %added.2.after_ref.refs_0_), channel_id=1, source_target_pairs={{0,2},{1,3},{2,0},{3,1},{4,6},{5,7},{6,4},{7,5},{8,10},{9,11},{10,... | collective-permute-start | bytes 344072 | tf_op jit(solution)/shard_map/ppermute | solution.py:27
  57.8 2.0 %collective-permute-start.12 = (bf16[448,128]{1,0:T(8,128)(2,1)S(1)}, bf16[448,128]{1,0:T(8,128)(2,1)S(1)}, u32[]{:S(2)}, u32[]{:S(2)}) collective-permute-start(bf16[448,128]{1,0:T(8,128)(2,1)S(1)} %added.2.after_ref.refs_0_), channel_id=1, source_target_pairs={{0,1},{1,0},{2,3},{3,2},{4,5},{5,4},{6,7},{7,6},{8,9},{9,8},{10,11... | collective-permute-start | bytes 344072 | tf_op jit(solution)/shard_map/ppermute | solution.py:27
  59.8 2.0 %conv.12 = (bf16[2,4,128,128]{3,2,1,0:T(8,128)(2,1)S(1)}, bf16[1,4,16,128,128]{4,3,2,1,0:T(8,128)(2,1)}) custom-call(s32[6]{0:T(128)S(1)} %stack.35.info_ref, bf16[448,128]{1,0:T(8,128)(2,1)S(1)} %added.2.after_ref.refs_0_, bf16[6,18,10,16,128]{4,3,2,1,0:T(8,128)(2,1)S(1)} %activate.1.act_ref, ...), custom_call_target="tpu_custom_call", output_to_operand_aliasing={{1}: (7, {})} | custom-call | tf_op jit(solution)/shard_map/conv/pallas_call | solution.py:452
  61.8 2.0 %conv.13 = (bf16[2,4,128,128]{3,2,1,0:T(8,128)(2,1)S(1)}, bf16[1,4,16,128,128]{4,3,2,1,0:T(8,128)(2,1)}) custom-call(s32[6]{0:T(128)S(1)} %stack.35.info_ref, bf16[2,4,128,128]{3,2,1,0:T(8,128)(2,1)S(1)} %get-tuple-element.64.after_ref.refs_0_, bf16[6,18,10,16,128]{4,3,2,1,0:T(8,128)(2,1)S(1)} %activate.1.act_ref, ...), custom_call_target="tpu_custom_call", output_to_operand_aliasing={{1}: (7, {})} | custom-call | tf_op jit(solution)/shard_map/conv/pallas_call | solution.py:452
  63.8 2.0 %conv.14 = (bf16[2,4,128,128]{3,2,1,0:T(8,128)(2,1)S(1)}, bf16[1,4,16,128,128]{4,3,2,1,0:T(8,128)(2,1)}) custom-call(s32[6]{0:T(128)S(1)} %stack.35.info_ref, bf16[2,4,128,128]{3,2,1,0:T(8,128)(2,1)S(1)} %get-tuple-element.66.after_ref.refs_0_, bf16[6,18,10,16,128]{4,3,2,1,0:T(8,128)(2,1)S(1)} %activate.1.act_ref, ...), custom_call_target="tpu_custom_call", output_to_operand_aliasing={{1}: (7, {})} | custom-call | tf_op jit(solution)/shard_map/conv/pallas_call | solution.py:452
  65.8 1.9 %collective-permute-done.13.refs_2_ = bf16[448,128]{1,0:T(8,128)(2,1)S(1)} collective-permute-done((bf16[448,128]{1,0:T(8,128)(2,1)S(1)}, bf16[448,128]{1,0:T(8,128)(2,1)S(1)}, u32[]{:S(2)}, u32[]{:S(2)}) %collective-permute-start.13) | collective-permute-done | bytes 114720 | tf_op jit(solution)/shard_map/ppermute | solution.py:27
  67.7 0.1 added.3.after_ref.refs_0_
  67.8 2.5 %collective-permute-start.17 = (bf16[448,128]{1,0:T(8,128)(2,1)S(1)}, bf16[448,128]{1,0:T(8,128)(2,1)S(1)}, u32[]{:S(2)}, u32[]{:S(2)}) collective-permute-start(bf16[448,128]{1,0:T(8,128)(2,1)S(1)} %added.3.after_ref.refs_0_), channel_id=1, source_target_pairs={{0,24},{8,16},{16,8},{24,0},{1,25},{9,17},{17,9},{25,1},{2,26},{10... | collective-permute-start | bytes 344072 | tf_op jit(solution)/shard_map/ppermute | solution.py:27
  70.3 0.5 collective-permute-start.16
  70.8 0.5 collective-permute-start.15
  71.3 3.3 %collective-permute-done.17.refs_3_ = bf16[448,128]{1,0:T(8,128)(2,1)S(1)} collective-permute-done((bf16[448,128]{1,0:T(8,128)(2,1)S(1)}, bf16[448,128]{1,0:T(8,128)(2,1)S(1)}, u32[]{:S(2)}, u32[]{:S(2)}) %collective-permute-start.17) | collective-permute-done | bytes 114720 | tf_op jit(solution)/shard_map/ppermute | solution.py:27
  74.7 0.9 %collective-permute-done.16.refs_2_ = bf16[448,128]{1,0:T(8,128)(2,1)S(1)} collective-permute-done((bf16[448,128]{1,0:T(8,128)(2,1)S(1)}, bf16[448,128]{1,0:T(8,128)(2,1)S(1)}, u32[]{:S(2)}, u32[]{:S(2)}) %collective-permute-start.16) | collective-permute-done | bytes 114720 | tf_op jit(solution)/shard_map/ppermute | solution.py:27
  75.6 0.1 collective-permute-done.15.refs_1_
  75.6 0.5 collective-permute-start.19
  76.1 2.0 %conv.15 = (bf16[2,4,128,128]{3,2,1,0:T(8,128)(2,1)S(1)}, bf16[1,4,16,128,128]{4,3,2,1,0:T(8,128)(2,1)}) custom-call(s32[6]{0:T(128)S(1)} %stack.35.info_ref, bf16[448,128]{1,0:T(8,128)(2,1)S(1)} %added.3.after_ref.refs_0_, bf16[6,18,10,16,128]{4,3,2,1,0:T(8,128)(2,1)S(1)} %activate.1.act_ref, ...), custom_call_target="tpu_custom_call", output_to_operand_aliasing={{1}: (7, {})} | custom-call | tf_op jit(solution)/shard_map/conv/pallas_call | solution.py:452
  78.1 2.5 %collect.1 = (f32[8,432,128]{2,1,0:T(8,128)}, f32[1,128]{1,0:T(1,128)}, bf16[1,4,16,128,128]{4,3,2,1,0:T(8,128)(2,1)}) custom-call(s32[6]{0:T(128)S(1)} %stack.35.info_ref, bf16[448,128]{1,0:T(8,128)(2,1)S(1)} %added.3.after_ref.refs_0_, bf16[448,128]{1,0:T(8,128)(2,1)S(1)} %collective-permute-done.15.refs_1_, ...), custom_call_target="tpu_custom_call", output_to_operand_aliasing={{2}: (10, {})} | custom-call | tf_op jit(solution)/shard_map/collect/pallas_call | solution.py:517
  (23 shorter events, 0.1 us)
Async XLA Ops:
  6.4 22.3 %copy-start.2 = (f32[128]{0:T(128)S(1)}, f32[128]{0:T(128)}, u32[]{:S(2)}) copy-start(f32[128]{0:T(128)} %param.9) | copy-start | bytes 1540
  6.4 22.3 %copy-start.3 = (f32[128]{0:T(128)S(1)}, f32[128]{0:T(128)}, u32[]{:S(2)}) copy-start(f32[128]{0:T(128)} %param.10) | copy-start | bytes 1540
  6.4 22.3 %collective-permute-start = (bf16[1,2,16,128,128]{4,3,2,1,0:T(8,128)(2,1)S(1)}, bf16[1,2,16,128,128]{4,3,2,1,0:T(8,128)(2,1)S(1)}, u32[]{:S(2)}, u32[]{:S(2)}) collective-permute-start(bf16[1,2,16,128,128]{4,3,2,1,0:T(8,128)(2,1)S(1)} %get-tuple-element.42), channel_id=1, source_target_pairs={{0,4},{4,0},{1,5},{5,1},{2,6},{6,2},{3,7},{7,3},{8,12},{12,8},{9,1... | collective-permute-start | bytes 3145736 | tf_op jit(solution)/shard_map/ppermute | solution.py:361
  7.0 2.5 %collective-permute-start.1 = (bf16[2,2,128,128]{3,2,1,0:T(8,128)(2,1)S(1)}, bf16[2,2,128,128]{3,2,1,0:T(8,128)(2,1)S(1)}, u32[]{:S(2)}, u32[]{:S(2)}) collective-permute-start(bf16[2,2,128,128]{3,2,1,0:T(8,128)(2,1)S(1)} %get-tuple-element.44), channel_id=1, source_target_pairs={{0,4},{4,0},{1,5},{5,1},{2,6},{6,2},{3,7},{7,3},{8,12},{12,8},{9,1... | collective-permute-start | bytes 393224 | tf_op jit(solution)/shard_map/ppermute | solution.py:360
  7.1 2.4 %collective-permute-start.2 = (f32[8,128]{1,0:T(8,128)S(1)}, f32[8,128]{1,0:T(8,128)S(1)}, u32[]{:S(2)}, u32[]{:S(2)}) collective-permute-start(f32[8,128]{1,0:T(8,128)S(1)} %get-tuple-element.45.refs_0_), channel_id=1, source_target_pairs={{0,4},{4,0},{1,5},{5,1},{2,6},{6,2},{3,7},{7,3},{8,12},{12,8},{9,1... | collective-permute-start | bytes 12296 | tf_op jit(solution)/shard_map/ppermute | solution.py:27
  9.5 19.2 %collective-permute-start.3 = (bf16[6,128,128]{2,1,0:T(8,128)(2,1)S(1)}, bf16[6,128,128]{2,1,0:T(8,128)(2,1)S(1)}, u32[]{:S(2)}, u32[]{:S(2)}) collective-permute-start(bf16[6,128,128]{2,1,0:T(8,128)(2,1)S(1)} %get-tuple-element.46), channel_id=1, source_target_pairs={{0,1},{1,2},{2,3},{4,5},{5,6},{6,7},{8,9},{9,10},{10,11},{12,13},{... | collective-permute-start | bytes 589832 | tf_op jit(solution)/shard_map/ppermute | solution.py:32
  14.4 14.3 %collective-permute-start.4 = (bf16[6,128,128]{2,1,0:T(8,128)(2,1)S(1)}, bf16[6,128,128]{2,1,0:T(8,128)(2,1)S(1)}, u32[]{:S(2)}, u32[]{:S(2)}) collective-permute-start(bf16[6,128,128]{2,1,0:T(8,128)(2,1)S(1)} %get-tuple-element.47), channel_id=1, source_target_pairs={{1,0},{2,1},{3,2},{5,4},{6,5},{7,6},{9,8},{10,9},{11,10},{13,12},{... | collective-permute-start | bytes 589832 | tf_op jit(solution)/shard_map/ppermute | solution.py:32
  15.7 9.4 %collective-permute-start.7 = (f32[8,128]{1,0:T(8,128)S(1)}, f32[8,128]{1,0:T(8,128)S(1)}, u32[]{:S(2)}, u32[]{:S(2)}) collective-permute-start(f32[8,128]{1,0:T(8,128)S(1)} %get-tuple-element.48.refs_0_), channel_id=1, source_target_pairs={{0,3},{1,2},{2,1},{3,0},{4,7},{5,6},{6,5},{7,4},{8,11},{9,10},{10,... | collective-permute-start | bytes 12296 | tf_op jit(solution)/shard_map/ppermute | solution.py:27
  20.4 7.2 %collective-permute-start.6 = (f32[8,128]{1,0:T(8,128)S(1)}, f32[8,128]{1,0:T(8,128)S(1)}, u32[]{:S(2)}, u32[]{:S(2)}) collective-permute-start(f32[8,128]{1,0:T(8,128)S(1)} %get-tuple-element.48.refs_0_), channel_id=1, source_target_pairs={{0,2},{1,3},{2,0},{3,1},{4,6},{5,7},{6,4},{7,5},{8,10},{9,11},{10,... | collective-permute-start | bytes 12296 | tf_op jit(solution)/shard_map/ppermute | solution.py:27
  25.1 3.6 %collective-permute-start.5 = (f32[8,128]{1,0:T(8,128)S(1)}, f32[8,128]{1,0:T(8,128)S(1)}, u32[]{:S(2)}, u32[]{:S(2)}) collective-permute-start(f32[8,128]{1,0:T(8,128)S(1)} %get-tuple-element.48.refs_0_), channel_id=1, source_target_pairs={{0,1},{1,0},{2,3},{3,2},{4,5},{5,4},{6,7},{7,6},{8,9},{9,8},{10,11... | collective-permute-start | bytes 12296 | tf_op jit(solution)/shard_map/ppermute | solution.py:27
  32.0 10.1 %copy-start = (bf16[3,3,3,128,128]{4,3,2,1,0:T(8,128)(2,1)S(1)}, bf16[3,3,3,128,128]{4,3,2,1,0:T(8,128)(2,1)}, u32[]{:S(2)}) copy-start(bf16[3,3,3,128,128]{4,3,2,1,0:T(8,128)(2,1)} %kernel_ref.1) | copy-start | bytes 2654212
  41.9 0.7 copy-start.1
  41.9 2.6 %collective-permute-start.8 = (f32[4,448,128]{2,1,0:T(8,128)S(1)}, f32[4,448,128]{2,1,0:T(8,128)S(1)}, u32[]{:S(2)}, u32[]{:S(2)}) collective-permute-start(f32[4,448,128]{2,1,0:T(8,128)S(1)} %get-tuple-element.52), channel_id=1, source_target_pairs={{0,4},{4,0},{1,5},{5,1},{2,6},{6,2},{3,7},{7,3},{8,12},{12,8},{9,1... | collective-permute-start | bytes 2752520 | tf_op jit(solution)/shard_map/ppermute | solution.py:27
  45.2 10.0 %collective-permute-start.9 = (bf16[448,128]{1,0:T(8,128)(2,1)S(1)}, bf16[448,128]{1,0:T(8,128)(2,1)S(1)}, u32[]{:S(2)}, u32[]{:S(2)}) collective-permute-start(bf16[448,128]{1,0:T(8,128)(2,1)S(1)} %get-tuple-element.60), channel_id=1, source_target_pairs={{0,8},{8,0},{16,24},{24,16},{1,9},{9,1},{17,25},{25,17},{2,10},{10... | collective-permute-start | bytes 344072 | tf_op jit(solution)/shard_map/ppermute | solution.py:27
  46.8 8.5 %collective-permute-start.10 = (bf16[448,128]{1,0:T(8,128)(2,1)S(1)}, bf16[448,128]{1,0:T(8,128)(2,1)S(1)}, u32[]{:S(2)}, u32[]{:S(2)}) collective-permute-start(bf16[448,128]{1,0:T(8,128)(2,1)S(1)} %get-tuple-element.61), channel_id=1, source_target_pairs={{0,16},{8,24},{16,0},{24,8},{1,17},{9,25},{17,1},{25,9},{2,18},{10... | collective-permute-start | bytes 344072 | tf_op jit(solution)/shard_map/ppermute | solution.py:27
  48.3 7.0 %collective-permute-start.11 = (bf16[448,128]{1,0:T(8,128)(2,1)S(1)}, bf16[448,128]{1,0:T(8,128)(2,1)S(1)}, u32[]{:S(2)}, u32[]{:S(2)}) collective-permute-start(bf16[448,128]{1,0:T(8,128)(2,1)S(1)} %get-tuple-element.62), channel_id=1, source_target_pairs={{0,24},{8,16},{16,8},{24,0},{1,25},{9,17},{17,9},{25,1},{2,26},{10... | collective-permute-start | bytes 344072 | tf_op jit(solution)/shard_map/ppermute | solution.py:27
  55.4 10.4 %collective-permute-start.14 = (bf16[448,128]{1,0:T(8,128)(2,1)S(1)}, bf16[448,128]{1,0:T(8,128)(2,1)S(1)}, u32[]{:S(2)}, u32[]{:S(2)}) collective-permute-start(bf16[448,128]{1,0:T(8,128)(2,1)S(1)} %added.2.after_ref.refs_0_), channel_id=1, source_target_pairs={{0,3},{1,2},{2,1},{3,0},{4,7},{5,6},{6,5},{7,4},{8,11},{9,10},{10,... | collective-permute-start | bytes 344072 | tf_op jit(solution)/shard_map/ppermute | solution.py:27
  56.2 11.6 %collective-permute-start.13 = (bf16[448,128]{1,0:T(8,128)(2,1)S(1)}, bf16[448,128]{1,0:T(8,128)(2,1)S(1)}, u32[]{:S(2)}, u32[]{:S(2)}) collective-permute-start(bf16[448,128]{1,0:T(8,128)(2,1)S(1)} %added.2.after_ref.refs_0_), channel_id=1, source_target_pairs={{0,2},{1,3},{2,0},{3,1},{4,6},{5,7},{6,4},{7,5},{8,10},{9,11},{10,... | collective-permute-start | bytes 344072 | tf_op jit(solution)/shard_map/ppermute | solution.py:27
  57.8 9.9 %collective-permute-start.12 = (bf16[448,128]{1,0:T(8,128)(2,1)S(1)}, bf16[448,128]{1,0:T(8,128)(2,1)S(1)}, u32[]{:S(2)}, u32[]{:S(2)}) collective-permute-start(bf16[448,128]{1,0:T(8,128)(2,1)S(1)} %added.2.after_ref.refs_0_), channel_id=1, source_target_pairs={{0,1},{1,0},{2,3},{3,2},{4,5},{5,4},{6,7},{7,6},{8,9},{9,8},{10,11... | collective-permute-start | bytes 344072 | tf_op jit(solution)/shard_map/ppermute | solution.py:27
  67.8 6.9 %collective-permute-start.17 = (bf16[448,128]{1,0:T(8,128)(2,1)S(1)}, bf16[448,128]{1,0:T(8,128)(2,1)S(1)}, u32[]{:S(2)}, u32[]{:S(2)}) collective-permute-start(bf16[448,128]{1,0:T(8,128)(2,1)S(1)} %added.3.after_ref.refs_0_), channel_id=1, source_target_pairs={{0,24},{8,16},{16,8},{24,0},{1,25},{9,17},{17,9},{25,1},{2,26},{10... | collective-permute-start | bytes 344072 | tf_op jit(solution)/shard_map/ppermute | solution.py:27
  70.3 5.3 %collective-permute-start.16 = (bf16[448,128]{1,0:T(8,128)(2,1)S(1)}, bf16[448,128]{1,0:T(8,128)(2,1)S(1)}, u32[]{:S(2)}, u32[]{:S(2)}) collective-permute-start(bf16[448,128]{1,0:T(8,128)(2,1)S(1)} %added.3.after_ref.refs_0_), channel_id=1, source_target_pairs={{0,16},{8,24},{16,0},{24,8},{1,17},{9,25},{17,1},{25,9},{2,18},{10... | collective-permute-start | bytes 344072 | tf_op jit(solution)/shard_map/ppermute | solution.py:27
  70.8 4.8 %collective-permute-start.15 = (bf16[448,128]{1,0:T(8,128)(2,1)S(1)}, bf16[448,128]{1,0:T(8,128)(2,1)S(1)}, u32[]{:S(2)}, u32[]{:S(2)}) collective-permute-start(bf16[448,128]{1,0:T(8,128)(2,1)S(1)} %added.3.after_ref.refs_0_), channel_id=1, source_target_pairs={{0,8},{8,0},{16,24},{24,16},{1,9},{9,1},{17,25},{25,17},{2,10},{10... | collective-permute-start | bytes 344072 | tf_op jit(solution)/shard_map/ppermute | solution.py:27
  71.3 6.7 %collective-permute-start.18 = (bf16[448,128]{1,0:T(8,128)(2,1)S(1)}, bf16[448,128]{1,0:T(8,128)(2,1)S(1)}, u32[]{:S(2)}, u32[]{:S(2)}) collective-permute-start(bf16[448,128]{1,0:T(8,128)(2,1)S(1)} %added.3.after_ref.refs_0_), channel_id=1, source_target_pairs={{0,4},{4,0},{1,5},{5,1},{2,6},{6,2},{3,7},{7,3},{8,12},{12,8},{9,1... | collective-permute-start | bytes 344072 | tf_op jit(solution)/shard_map/ppermute | solution.py:27
  74.7 3.4 %collective-permute-start.21 = (bf16[448,128]{1,0:T(8,128)(2,1)S(1)}, bf16[448,128]{1,0:T(8,128)(2,1)S(1)}, u32[]{:S(2)}, u32[]{:S(2)}) collective-permute-start(bf16[448,128]{1,0:T(8,128)(2,1)S(1)} %collective-permute-done.17.refs_3_), channel_id=1, source_target_pairs={{0,4},{4,0},{1,5},{5,1},{2,6},{6,2},{3,7},{7,3},{8,12},{12,8},{9,1... | collective-permute-start | bytes 344072 | tf_op jit(solution)/shard_map/ppermute | solution.py:27
  75.5 2.5 %collective-permute-start.20 = (bf16[448,128]{1,0:T(8,128)(2,1)S(1)}, bf16[448,128]{1,0:T(8,128)(2,1)S(1)}, u32[]{:S(2)}, u32[]{:S(2)}) collective-permute-start(bf16[448,128]{1,0:T(8,128)(2,1)S(1)} %collective-permute-done.16.refs_2_), channel_id=1, source_target_pairs={{0,4},{4,0},{1,5},{5,1},{2,6},{6,2},{3,7},{7,3},{8,12},{12,8},{9,1... | collective-permute-start | bytes 344072 | tf_op jit(solution)/shard_map/ppermute | solution.py:27
  75.6 2.5 %collective-permute-start.19 = (bf16[448,128]{1,0:T(8,128)(2,1)S(1)}, bf16[448,128]{1,0:T(8,128)(2,1)S(1)}, u32[]{:S(2)}, u32[]{:S(2)}) collective-permute-start(bf16[448,128]{1,0:T(8,128)(2,1)S(1)} %collective-permute-done.15.refs_1_), channel_id=1, source_target_pairs={{0,4},{4,0},{1,5},{5,1},{2,6},{6,2},{3,7},{7,3},{8,12},{12,8},{9,1... | collective-permute-start | bytes 344072 | tf_op jit(solution)/shard_map/ppermute | solution.py:27

commit v6 on v5

--- a/solution.py
+++ b/solution.py
@@ -56,8 +56,20 @@
     return count, total, mean, squares
 
 
+def ends_kernel(video_hbm, low_ref, high_ref, sems):
+    rows = video_hbm.shape[2]
+    copies = [
+        pltpu.make_async_copy(video_hbm.at[0, :, row], ref, sems.at[n])
+        for n, (row, ref) in enumerate(((rows - 1, low_ref), (0, high_ref)))
+    ]
+    for copy in copies:
+        copy.start()
+    for copy in copies:
+        copy.wait()
+
+
 def stats_kernel(per, before, info_ref, video_hbm, cot_hbm, *refs):
-    out_ref, video_ref, cot_ref, tail_ref, ends_ref, early_ref, sems = refs
+    out_ref, video_ref, cot_ref, tail_ref, sems = refs
     frames, rows, cols, chans = video_ref.shape[1:]
     parts_n = 2 * frames
     some = rows // 2
@@ -65,18 +77,10 @@
     copies = []
     for n in range(parts_n):
         at = (0, n // 2, pl.ds(n % 2 * some, some))
-        copies.append((video_hbm.at[at], video_ref.at[at]))
-    copies.append((video_hbm.at[:, first:], tail_ref))
-    for side, row in enumerate((rows - 1, 0)):
-        copies.append((video_hbm.at[0, :, row], ends_ref.at[side]))
-        copies.append((video_hbm.at[0, first:, row], early_ref.at[side]))
-    copies.append((cot_hbm, cot_ref))
-    copies = [
-        pltpu.make_async_copy(source, target, sems.at[n])
-        for n, (source, target) in enumerate(copies)
-    ]
-    for copy in copies:
-        copy.start()
+        copies.append(pltpu.make_async_copy(video_hbm.at[at], video_ref.at[at], sems.at[n]))
+        copies[-1].start()
+    later = [pltpu.make_async_copy(cot_hbm, cot_ref, sems.at[parts_n])]
+    later[0].start()
     size = float(some * cols * per)
     lanes = 4
     split = (cols // (8 * lanes), lanes, 8, chans)
@@ -85,6 +89,10 @@
     for n in range(parts_n):
         copies[n].wait()
         f, y0 = n // 2, n % 2 * some
+        if n % 2 and f >= first:
+            sem = sems.at[parts_n + 1 + f - first]
+            later.append(pltpu.make_async_copy(video_ref.at[0, f], tail_ref.at[0, f - first], sem))
+            later[-1].start()
 
         def add(y, acc, f=f, y0=y0):
             return acc + jnp.sum(video_ref[0, f, y0 + y].astype(F32).reshape(split), axis=0)
@@ -107,20 +115,15 @@
     out_ref[...] = jnp.concatenate(
         [count, total, deviations, jnp.zeros((5, chans), F32)], axis=0
     )
-    for copy in copies[parts_n:]:
+    for copy in later:
         copy.wait()
 
 
-def merge_kernel(parts_n, ends_ref, early_ref, *refs):
-    parts, (out_ref, low_ref, high_ref) = refs[:parts_n], refs[parts_n:]
-    count, total, _, deviations = merged([ref[...] for ref in parts])
-    out_ref[...] = jnp.concatenate(
+def merge_kernel(*refs):
+    count, total, _, deviations = merged([ref[...] for ref in refs[:-1]])
+    refs[-1][...] = jnp.concatenate(
         [count, total, deviations, jnp.zeros((5, count.shape[1]), F32)], axis=0
     )
-    before = early_ref.shape[1]
-    for side, ref in enumerate((low_ref, high_ref)):
-        ref[0:before] = early_ref[side]
-        ref[before:] = ends_ref[side]
 
 
 def cotangent_kernel(info_ref, cot_ref, turned_ref, bias_ref, wide):
@@ -147,8 +150,9 @@
 
 
 def activate_kernel(
-    parts_n, info_ref, video_ref, early_ref, low_ref, high_ref, gain_ref, shift_ref, *refs
+    parts_n, info_ref, video_ref, early_ref, low_ref, high_ref, low_early_ref, high_early_ref, *refs
 ):
+    gain_ref, shift_ref, *refs = refs
     parts, out_ref, wide = refs[:parts_n], refs[parts_n], refs[parts_n + 1]
     frames, rows, cols, chans = video_ref.shape[1:]
     before = early_ref.shape[1]
@@ -178,8 +182,10 @@
             return carry
 
         lax.fori_loop(0, rows, inner, 0, unroll=4)
-        row(low_ref[f], keep * has_low.astype(F32), 0, f, 0)
-        row(high_ref[f], keep * has_high.astype(F32), 1, f, rows + 1)
+        low = low_early_ref[frames + local] if local < 0 else low_ref[local]
+        high = high_early_ref[frames + local] if local < 0 else high_ref[local]
+        row(low, keep * has_low.astype(F32), 0, f, 0)
+        row(high, keep * has_high.astype(F32), 1, f, rows + 1)
 
 
 def packed(value):
@@ -334,43 +340,47 @@
         ]
     ).astype(jnp.int32)
 
-    both = 2 * frames + 6
-    stats, local, masked_in, tail, ends, ends_tail = pl.pallas_call(
+    source = pltpu.with_memory_space_constraint(video, pltpu.HBM)
+    border = jax.ShapeDtypeStruct((frames, cols, chans), BF16)
+    edge_low, edge_high = pl.pallas_call(
+        ends_kernel,
+        in_specs=[ANY],
+        out_specs=[VMEM, VMEM],
+        out_shape=[border, border],
+        scratch_shapes=[pltpu.SemaphoreType.DMA((2,))],
+        compiler_params=params(1),
+        name="ends",
+    )(source)
+    low = shifted(edge_low, "space", 1)
+    high = shifted(edge_high, "space", -1)
+    stats, local, masked_in, tail = pl.pallas_call(
         functools.partial(stats_kernel, per, before),
         in_specs=[SMEM, ANY, ANY],
-        out_specs=[VMEM] * 6,
+        out_specs=[VMEM] * 4,
         out_shape=[
             jax.ShapeDtypeStruct((8, chans), F32),
             jax.ShapeDtypeStruct(video.shape, BF16),
             jax.ShapeDtypeStruct(cotangent.shape, BF16),
             jax.ShapeDtypeStruct((1, before, rows, cols, chans), BF16),
-            jax.ShapeDtypeStruct((2, frames, cols, chans), BF16),
-            jax.ShapeDtypeStruct((2, before, cols, chans), BF16),
         ],
-        scratch_shapes=[pltpu.SemaphoreType.DMA((both,))],
+        scratch_shapes=[pltpu.SemaphoreType.DMA((2 * frames + 1 + before,))],
         compiler_params=params(2),
         name="stats",
-    )(
-        info,
-        pltpu.with_memory_space_constraint(video, pltpu.HBM),
-        pltpu.with_memory_space_constraint(cotangent, pltpu.HBM),
-    )
+    )(info, source, pltpu.with_memory_space_constraint(cotangent, pltpu.HBM))
+    following = [(i, (i + 1) % tms) for i in range(tms)]
     gathered = [stats] + [swap(stats, "tm", r) for r in range(1, tms)]
-    following = [(i, (i + 1) % tms) for i in range(tms)]
-    early_ends = lax.ppermute(ends_tail, "tm", following)
     early = lax.ppermute(tail, "tm", following)
-    border = jax.ShapeDtypeStruct((before + frames, cols, chans), BF16)
-    stats, edge_low, edge_high = pl.pallas_call(
-        functools.partial(merge_kernel, tms),
-        in_specs=[VMEM] * (2 + tms),
-        out_specs=[VMEM] * 3,
-        out_shape=[jax.ShapeDtypeStruct((8, chans), F32), border, border],
-        compiler_params=params(2),
+    stats = pl.pallas_call(
+        merge_kernel,
+        in_specs=[VMEM] * tms,
+        out_specs=VMEM,
+        out_shape=jax.ShapeDtypeStruct((8, chans), F32),
+        compiler_params=params(1),
         name="merge",
-    )(ends, early_ends, *gathered)
+    )(*gathered)
     parts = [stats] + [swap(stats, "space", r) for r in range(1, spaces)]
-    low = shifted(edge_low, "space", 1)
-    high = shifted(edge_high, "space", -1)
+    low_early = lax.ppermute(low, "tm", following)
+    high_early = lax.ppermute(high, "tm", following)
     pair = 2
     taps = pl.pallas_call(
         taps_kernel,
@@ -381,7 +391,7 @@
         ),
         compiler_params=params(2),
         name="taps",
-    )(ends, kernel)
+    )(stats, kernel)
 
     turned, bias = pl.pallas_call(
         cotangent_kernel,
@@ -398,7 +408,7 @@
 
     act = pl.pallas_call(
         functools.partial(activate_kernel, spaces),
-        in_specs=[SMEM] + [VMEM] * (6 + spaces),
+        in_specs=[SMEM] + [VMEM] * (8 + spaces),
         out_specs=VMEM,
         out_shape=jax.ShapeDtypeStruct(
             (frames + before, rows + 2, step + 2, TILE, chans), BF16
@@ -412,6 +422,8 @@
         early,
         low,
         high,
+        low_early,
+        high_early,
         norm_gain.reshape(1, chans),
         norm_shift.reshape(1, chans),
         *parts,

time: 81 us -> 82.8 us (1.022)
  waiting for transfers between devices: 13.9 us -> 16.9 us
  starting transfers between devices: 24 us -> 21.9 us
  Pallas kernels: 40.8 us -> 41.8 us
    ppermute x2, waiting for transfers between devices: 0.01 us -> 6.2 us  [shifted(): lax.ppermute(array, axis, [(i, i + by) for i in range(length) if 0 <= i +...]
    ppermute x18, waiting for transfers between devices: 13.9 us -> 10.7 us  [swap(): return lax.ppermute(array, axis, [(i, i ^ by) for i in range(length)])]
    ppermute x18, starting transfers between devices: 17.3 us -> 15.5 us  [swap(): return lax.ppermute(array, axis, [(i, i ^ by) for i in range(length)])]
    pallas_call x1 -> x2, Pallas kernels: 0.03 us -> 1 us  [the longest x1 0.98 us: step_of(): pl.pallas_call(ends_kernel, in_specs=[ANY], out_specs=[VMEM, VMEM], out_s...]
  transfers between devices with their start and end apart: 22 -> 23, of which waited for: 7 -> 9; matrix products, arithmetic and copies ran while one was open for 0% -> 0% of each run, Pallas kernels for 24% -> 24%
where the time goes in v6:
time: 82.8 us; the launch traced here: 82.6 us
  Pallas kernels  41.8 us (50%)
  starting transfers between devices  21.9 us (26%)
  waiting for transfers between devices  16.9 us (20%)
  between operations  1.74 us (2%)
    pallas_call x8, Pallas kernels, cover(): pl.pallas_call(functools.partial(conv_kernel, pieces[n], where(n - 1) if...  16.4 us
    ppermute x18, starting transfers between devices, swap(): return lax.ppermute(array, axis, [(i, i ^ by) for i in range(length)])  15.5 us
    ppermute x18, waiting for transfers between devices, swap(): return lax.ppermute(array, axis, [(i, i ^ by) for i in range(length)])  10.7 us
    pallas_call x1, Pallas kernels, step_of(): pl.pallas_call(weights_kernel, in_specs=[SMEM, VMEM, VMEM, VMEM], out_spe...  9.96 us
    ppermute x2, waiting for transfers between devices, shifted(): lax.ppermute(array, axis, [(i, i + by) for i in range(length) if 0 <= i +...  6.2 us
    ppermute x2, starting transfers between devices, shifted(): lax.ppermute(array, axis, [(i, i + by) for i in range(length) if 0 <= i +...  5.78 us
    pallas_call x1, Pallas kernels, step_of(): pl.pallas_call(functools.partial(stats_kernel, per, before), in_specs=[SM...  5.05 us
    pallas_call x1, Pallas kernels, step_of(): pl.pallas_call(functools.partial(activate_kernel, spaces), in_specs=[SMEM...  3.25 us
  transfers between devices with their start and end apart: 23, of which 9 were waited for; matrix products, arithmetic and copies ran while one was open for 0% of the time, Pallas kernels for 24%

profile of v6, /device:TPU:0, one launch (start us, length us, event | category | flops | bytes accessed | tf_op | source)
XLA Modules:
  0.0 82.6 jit_solution(4226789526560675831)
XLA Ops:
  1.3 0.1 stack.35.info_ref
  1.4 5.1 %stats.1 = (f32[8,128]{1,0:T(8,128)S(1)}, bf16[1,4,16,128,128]{4,3,2,1,0:T(8,128)(2,1)S(1)}, bf16[1,4,16,128,128]{4,3,2,1,0:T(8,128)(2,1)S(1)}, bf16[1,2,16,128,128]{4,3,2,1,0:T(8,128)(2,1)S(1)}) custom-call(s32[6]{0:T(128)S(1)} %stack.35.info_ref, bf16[1,4,16,128,128]{4,3,2,1,0:T(8,128)(2,1)} %video_hbm.3, bf16[1,4,16,128,128]{4,3,2,1,0:T(8,128)(2,1)} %cot_hbm.1), custom_call_target="tpu_custom_call" | custom-call | tf_op jit(solution)/shard_map/stats/pallas_call | solution.py:356
  6.4 0.0 copy-start.2
  6.4 0.0 copy-start.3
  6.5 0.6 collective-permute-start
  7.0 1.0 %ends.1 = (bf16[4,128,128]{2,1,0:T(8,128)(2,1)S(1)}, bf16[4,128,128]{2,1,0:T(8,128)(2,1)S(1)}) custom-call(bf16[1,4,16,128,128]{4,3,2,1,0:T(8,128)(2,1)} %video_hbm.3), custom_call_target="tpu_custom_call" | custom-call | tf_op jit(solution)/shard_map/ends/pallas_call | solution.py:345
  8.0 4.5 %collective-permute-start.1 = (bf16[4,128,128]{2,1,0:T(8,128)(2,1)S(1)}, bf16[4,128,128]{2,1,0:T(8,128)(2,1)S(1)}, u32[]{:S(2)}, u32[]{:S(2)}) collective-permute-start(bf16[4,128,128]{2,1,0:T(8,128)(2,1)S(1)} %get-tuple-element.40), channel_id=1, source_target_pairs={{0,1},{1,2},{2,3},{4,5},{5,6},{6,7},{8,9},{9,10},{10,11},{12,13},{... | collective-permute-start | bytes 393224 | tf_op jit(solution)/shard_map/ppermute | solution.py:32
  12.5 1.3 %collective-permute-start.2 = (bf16[4,128,128]{2,1,0:T(8,128)(2,1)S(1)}, bf16[4,128,128]{2,1,0:T(8,128)(2,1)S(1)}, u32[]{:S(2)}, u32[]{:S(2)}) collective-permute-start(bf16[4,128,128]{2,1,0:T(8,128)(2,1)S(1)} %get-tuple-element.41), channel_id=1, source_target_pairs={{1,0},{2,1},{3,2},{5,4},{6,5},{7,6},{9,8},{10,9},{11,10},{13,12},{... | collective-permute-start | bytes 393224 | tf_op jit(solution)/shard_map/ppermute | solution.py:32
  13.8 2.1 %collective-permute-done.1.low_ref = bf16[4,128,128]{2,1,0:T(8,128)(2,1)S(1)} collective-permute-done((bf16[4,128,128]{2,1,0:T(8,128)(2,1)S(1)}, bf16[4,128,128]{2,1,0:T(8,128)(2,1)S(1)}, u32[]{:S(2)}, u32[]{:S(2)}) %collective-permute-start.1) | collective-permute-done | bytes 131104 | tf_op jit(solution)/shard_map/ppermute | solution.py:32
  15.9 4.1 %collective-permute-done.2.high_ref = bf16[4,128,128]{2,1,0:T(8,128)(2,1)S(1)} collective-permute-done((bf16[4,128,128]{2,1,0:T(8,128)(2,1)S(1)}, bf16[4,128,128]{2,1,0:T(8,128)(2,1)S(1)}, u32[]{:S(2)}, u32[]{:S(2)}) %collective-permute-start.2) | collective-permute-done | bytes 131104 | tf_op jit(solution)/shard_map/ppermute | solution.py:32
  20.0 0.5 collective-permute-start.5
  20.5 0.8 %collective-permute-done.5.refs_1_ = f32[8,128]{1,0:T(8,128)S(1)} collective-permute-done((f32[8,128]{1,0:T(8,128)S(1)}, f32[8,128]{1,0:T(8,128)S(1)}, u32[]{:S(2)}, u32[]{:S(2)}) %collective-permute-start.5) | collective-permute-done | bytes 4128 | tf_op jit(solution)/shard_map/ppermute | solution.py:27
  21.4 1.6 %collective-permute-start.8 = (f32[8,128]{1,0:T(8,128)S(1)}, f32[8,128]{1,0:T(8,128)S(1)}, u32[]{:S(2)}, u32[]{:S(2)}) collective-permute-start(f32[8,128]{1,0:T(8,128)S(1)} %merge.1.refs_2_.after_ref), channel_id=1, source_target_pairs={{0,3},{1,2},{2,1},{3,0},{4,7},{5,6},{6,5},{7,4},{8,11},{9,10},{10,... | collective-permute-start | bytes 12296 | tf_op jit(solution)/shard_map/ppermute | solution.py:27
  23.0 1.5 %collective-permute-start.7 = (f32[8,128]{1,0:T(8,128)S(1)}, f32[8,128]{1,0:T(8,128)S(1)}, u32[]{:S(2)}, u32[]{:S(2)}) collective-permute-start(f32[8,128]{1,0:T(8,128)S(1)} %merge.1.refs_2_.after_ref), channel_id=1, source_target_pairs={{0,2},{1,3},{2,0},{3,1},{4,6},{5,7},{6,4},{7,5},{8,10},{9,11},{10,... | collective-permute-start | bytes 12296 | tf_op jit(solution)/shard_map/ppermute | solution.py:27
  24.5 2.4 %collective-permute-done.8.refs_5_ = f32[8,128]{1,0:T(8,128)S(1)} collective-permute-done((f32[8,128]{1,0:T(8,128)S(1)}, f32[8,128]{1,0:T(8,128)S(1)}, u32[]{:S(2)}, u32[]{:S(2)}) %collective-permute-start.8) | collective-permute-done | bytes 4128 | tf_op jit(solution)/shard_map/ppermute | solution.py:27
  26.9 2.5 %cotangent.1 = (bf16[4,16,128,128]{3,2,1,0:T(8,128)(2,1)S(1)}, f32[8,128]{1,0:T(8,128)S(1)}) custom-call(s32[6]{0:T(128)S(1)} %stack.35.info_ref, bf16[1,4,16,128,128]{4,3,2,1,0:T(8,128)(2,1)S(1)} %get-tuple-element.36.cot_ref), custom_call_target="tpu_custom_call" | custom-call | tf_op jit(solution)/shard_map/cotangent/pallas_call | solution.py:396
  29.4 1.1 %collective-permute-done.6.refs_3_ = f32[8,128]{1,0:T(8,128)S(1)} collective-permute-done((f32[8,128]{1,0:T(8,128)S(1)}, f32[8,128]{1,0:T(8,128)S(1)}, u32[]{:S(2)}, u32[]{:S(2)}) %collective-permute-start.6) | collective-permute-done | bytes 4128 | tf_op jit(solution)/shard_map/ppermute | solution.py:27
  30.5 3.2 %activate.1.act_ref = bf16[6,18,10,16,128]{4,3,2,1,0:T(8,128)(2,1)S(1)} custom-call(s32[6]{0:T(128)S(1)} %stack.35.info_ref, bf16[1,4,16,128,128]{4,3,2,1,0:T(8,128)(2,1)S(1)} %get-tuple-element.38.video_ref, bf16[1,2,16,128,128]{4,3,2,1,0:T(8,128)(2,1)S(1)} %collective-permute-done.early_ref, bf16[4,128,128]{2,1,0:T(8,128)(2,1)S(1)} %collective-permute-done.1.low_ref, ...), custom_call_target="tpu_custom_call" | custom-call | tf_op jit(solution)/shard_map/activate/pallas_call | solution.py:409
  33.8 10.0 %weights.1 = (f32[4,448,128]{2,1,0:T(8,128)S(1)}, f32[4,448,128]{2,1,0:T(8,128)S(1)}) custom-call(s32[6]{0:T(128)S(1)} %stack.35.info_ref, bf16[4,16,128,128]{3,2,1,0:T(8,128)(2,1)S(1)} %get-tuple-element.37.turned_ref, bf16[6,18,10,16,128]{4,3,2,1,0:T(8,128)(2,1)S(1)} %activate.1.act_ref, f32[8,128]{1,0:T(8,128)S(1)} %get-tuple-element.43.bias_ref), custom_call_target="tpu_custom_call" | custom-call | tf_op jit(solution)/shard_map/weights/pallas_call | solution.py:437
  43.7 0.1 collective-permute-start.9
  43.8 0.4 taps.1.taps_ref
  44.2 0.2 copy-done.1
  44.4 2.0 %conv.8 = (bf16[2,4,128,128]{3,2,1,0:T(8,128)(2,1)S(1)}, bf16[1,4,16,128,128]{4,3,2,1,0:T(8,128)(2,1)}) custom-call(s32[6]{0:T(128)S(1)} %stack.35.info_ref, f32[4,448,128]{2,1,0:T(8,128)S(1)} %get-tuple-element.44.after_ref.keep_ref, bf16[6,18,10,16,128]{4,3,2,1,0:T(8,128)(2,1)S(1)} %activate.1.act_ref, bf16[4608,256]{1,0:T(8,128)(2,1)S(1)} %taps.1.taps_ref, ...), custom_call_target="tpu_custom_call" | custom-call | tf_op jit(solution)/shard_map/conv/pallas_call | solution.py:464
  46.4 0.6 spread.1
  47.0 1.6 %collective-permute-start.10 = (bf16[448,128]{1,0:T(8,128)(2,1)S(1)}, bf16[448,128]{1,0:T(8,128)(2,1)S(1)}, u32[]{:S(2)}, u32[]{:S(2)}) collective-permute-start(bf16[448,128]{1,0:T(8,128)(2,1)S(1)} %get-tuple-element.54), channel_id=1, source_target_pairs={{0,8},{8,0},{16,24},{24,16},{1,9},{9,1},{17,25},{25,17},{2,10},{10... | collective-permute-start | bytes 344072 | tf_op jit(solution)/shard_map/ppermute | solution.py:27
  48.6 1.5 %collective-permute-start.11 = (bf16[448,128]{1,0:T(8,128)(2,1)S(1)}, bf16[448,128]{1,0:T(8,128)(2,1)S(1)}, u32[]{:S(2)}, u32[]{:S(2)}) collective-permute-start(bf16[448,128]{1,0:T(8,128)(2,1)S(1)} %get-tuple-element.55), channel_id=1, source_target_pairs={{0,16},{8,24},{16,0},{24,8},{1,17},{9,25},{17,1},{25,9},{2,18},{10... | collective-permute-start | bytes 344072 | tf_op jit(solution)/shard_map/ppermute | solution.py:27
  50.1 0.5 collective-permute-start.12
  50.6 2.5 %conv.9 = (bf16[2,4,128,128]{3,2,1,0:T(8,128)(2,1)S(1)}, bf16[1,4,16,128,128]{4,3,2,1,0:T(8,128)(2,1)}) custom-call(s32[6]{0:T(128)S(1)} %stack.35.info_ref, f32[448,128]{1,0:T(8,128)S(1)} %get-tuple-element.47.after_ref.refs_0_, bf16[6,18,10,16,128]{4,3,2,1,0:T(8,128)(2,1)S(1)} %activate.1.act_ref, ...), custom_call_target="tpu_custom_call", output_to_operand_aliasing={{1}: (7, {})} | custom-call | tf_op jit(solution)/shard_map/conv/pallas_call | solution.py:464
  53.1 2.0 %conv.10 = (bf16[2,4,128,128]{3,2,1,0:T(8,128)(2,1)S(1)}, bf16[1,4,16,128,128]{4,3,2,1,0:T(8,128)(2,1)}) custom-call(s32[6]{0:T(128)S(1)} %stack.35.info_ref, bf16[2,4,128,128]{3,2,1,0:T(8,128)(2,1)S(1)} %get-tuple-element.49.after_ref.refs_0_, bf16[6,18,10,16,128]{4,3,2,1,0:T(8,128)(2,1)S(1)} %activate.1.act_ref, ...), custom_call_target="tpu_custom_call", output_to_operand_aliasing={{1}: (7, {})} | custom-call | tf_op jit(solution)/shard_map/conv/pallas_call | solution.py:464
  55.1 2.0 %conv.11 = (bf16[2,4,128,128]{3,2,1,0:T(8,128)(2,1)S(1)}, bf16[1,4,16,128,128]{4,3,2,1,0:T(8,128)(2,1)}) custom-call(s32[6]{0:T(128)S(1)} %stack.35.info_ref, bf16[2,4,128,128]{3,2,1,0:T(8,128)(2,1)S(1)} %get-tuple-element.51.after_ref.refs_0_, bf16[6,18,10,16,128]{4,3,2,1,0:T(8,128)(2,1)S(1)} %activate.1.act_ref, ...), custom_call_target="tpu_custom_call", output_to_operand_aliasing={{1}: (7, {})} | custom-call | tf_op jit(solution)/shard_map/conv/pallas_call | solution.py:464
  57.1 0.1 added.2.after_ref.refs_0_
  57.2 1.6 %collective-permute-start.15 = (bf16[448,128]{1,0:T(8,128)(2,1)S(1)}, bf16[448,128]{1,0:T(8,128)(2,1)S(1)}, u32[]{:S(2)}, u32[]{:S(2)}) collective-permute-start(bf16[448,128]{1,0:T(8,128)(2,1)S(1)} %added.2.after_ref.refs_0_), channel_id=1, source_target_pairs={{0,3},{1,2},{2,1},{3,0},{4,7},{5,6},{6,5},{7,4},{8,11},{9,10},{10,... | collective-permute-start | bytes 344072 | tf_op jit(solution)/shard_map/ppermute | solution.py:27
  58.8 0.8 collective-permute-start.14
  59.6 2.0 %collective-permute-start.13 = (bf16[448,128]{1,0:T(8,128)(2,1)S(1)}, bf16[448,128]{1,0:T(8,128)(2,1)S(1)}, u32[]{:S(2)}, u32[]{:S(2)}) collective-permute-start(bf16[448,128]{1,0:T(8,128)(2,1)S(1)} %added.2.after_ref.refs_0_), channel_id=1, source_target_pairs={{0,1},{1,0},{2,3},{3,2},{4,5},{5,4},{6,7},{7,6},{8,9},{9,8},{10,11... | collective-permute-start | bytes 344072 | tf_op jit(solution)/shard_map/ppermute | solution.py:27
  61.6 2.0 %conv.12 = (bf16[2,4,128,128]{3,2,1,0:T(8,128)(2,1)S(1)}, bf16[1,4,16,128,128]{4,3,2,1,0:T(8,128)(2,1)}) custom-call(s32[6]{0:T(128)S(1)} %stack.35.info_ref, bf16[448,128]{1,0:T(8,128)(2,1)S(1)} %added.2.after_ref.refs_0_, bf16[6,18,10,16,128]{4,3,2,1,0:T(8,128)(2,1)S(1)} %activate.1.act_ref, ...), custom_call_target="tpu_custom_call", output_to_operand_aliasing={{1}: (7, {})} | custom-call | tf_op jit(solution)/shard_map/conv/pallas_call | solution.py:464
  63.6 2.0 %conv.13 = (bf16[2,4,128,128]{3,2,1,0:T(8,128)(2,1)S(1)}, bf16[1,4,16,128,128]{4,3,2,1,0:T(8,128)(2,1)}) custom-call(s32[6]{0:T(128)S(1)} %stack.35.info_ref, bf16[2,4,128,128]{3,2,1,0:T(8,128)(2,1)S(1)} %get-tuple-element.58.after_ref.refs_0_, bf16[6,18,10,16,128]{4,3,2,1,0:T(8,128)(2,1)S(1)} %activate.1.act_ref, ...), custom_call_target="tpu_custom_call", output_to_operand_aliasing={{1}: (7, {})} | custom-call | tf_op jit(solution)/shard_map/conv/pallas_call | solution.py:464
  65.6 2.0 %conv.14 = (bf16[2,4,128,128]{3,2,1,0:T(8,128)(2,1)S(1)}, bf16[1,4,16,128,128]{4,3,2,1,0:T(8,128)(2,1)}) custom-call(s32[6]{0:T(128)S(1)} %stack.35.info_ref, bf16[2,4,128,128]{3,2,1,0:T(8,128)(2,1)S(1)} %get-tuple-element.60.after_ref.refs_0_, bf16[6,18,10,16,128]{4,3,2,1,0:T(8,128)(2,1)S(1)} %activate.1.act_ref, ...), custom_call_target="tpu_custom_call", output_to_operand_aliasing={{1}: (7, {})} | custom-call | tf_op jit(solution)/shard_map/conv/pallas_call | solution.py:464
  67.6 2.1 %collective-permute-done.14.refs_2_ = bf16[448,128]{1,0:T(8,128)(2,1)S(1)} collective-permute-done((bf16[448,128]{1,0:T(8,128)(2,1)S(1)}, bf16[448,128]{1,0:T(8,128)(2,1)S(1)}, u32[]{:S(2)}, u32[]{:S(2)}) %collective-permute-start.14) | collective-permute-done | bytes 114720 | tf_op jit(solution)/shard_map/ppermute | solution.py:27
  69.7 0.1 added.3.after_ref.refs_0_
  69.8 2.5 %collective-permute-start.18 = (bf16[448,128]{1,0:T(8,128)(2,1)S(1)}, bf16[448,128]{1,0:T(8,128)(2,1)S(1)}, u32[]{:S(2)}, u32[]{:S(2)}) collective-permute-start(bf16[448,128]{1,0:T(8,128)(2,1)S(1)} %added.3.after_ref.refs_0_), channel_id=1, source_target_pairs={{0,24},{8,16},{16,8},{24,0},{1,25},{9,17},{17,9},{25,1},{2,26},{10... | collective-permute-start | bytes 344072 | tf_op jit(solution)/shard_map/ppermute | solution.py:27
  72.3 0.5 collective-permute-start.17
  72.8 0.5 collective-permute-start.16
  73.3 3.0 %collective-permute-done.18.refs_3_ = bf16[448,128]{1,0:T(8,128)(2,1)S(1)} collective-permute-done((bf16[448,128]{1,0:T(8,128)(2,1)S(1)}, bf16[448,128]{1,0:T(8,128)(2,1)S(1)}, u32[]{:S(2)}, u32[]{:S(2)}) %collective-permute-start.18) | collective-permute-done | bytes 114720 | tf_op jit(solution)/shard_map/ppermute | solution.py:27
  76.4 1.0 %collective-permute-done.17.refs_2_ = bf16[448,128]{1,0:T(8,128)(2,1)S(1)} collective-permute-done((bf16[448,128]{1,0:T(8,128)(2,1)S(1)}, bf16[448,128]{1,0:T(8,128)(2,1)S(1)}, u32[]{:S(2)}, u32[]{:S(2)}) %collective-permute-start.17) | collective-permute-done | bytes 114720 | tf_op jit(solution)/shard_map/ppermute | solution.py:27
  77.4 0.2 collective-permute-done.16.refs_1_
  77.6 0.3 collective-permute-start.20
  77.9 2.0 %conv.15 = (bf16[2,4,128,128]{3,2,1,0:T(8,128)(2,1)S(1)}, bf16[1,4,16,128,128]{4,3,2,1,0:T(8,128)(2,1)}) custom-call(s32[6]{0:T(128)S(1)} %stack.35.info_ref, bf16[448,128]{1,0:T(8,128)(2,1)S(1)} %added.3.after_ref.refs_0_, bf16[6,18,10,16,128]{4,3,2,1,0:T(8,128)(2,1)S(1)} %activate.1.act_ref, ...), custom_call_target="tpu_custom_call", output_to_operand_aliasing={{1}: (7, {})} | custom-call | tf_op jit(solution)/shard_map/conv/pallas_call | solution.py:464
  79.9 2.5 %collect.1 = (f32[8,432,128]{2,1,0:T(8,128)}, f32[1,128]{1,0:T(1,128)}, bf16[1,4,16,128,128]{4,3,2,1,0:T(8,128)(2,1)}) custom-call(s32[6]{0:T(128)S(1)} %stack.35.info_ref, bf16[448,128]{1,0:T(8,128)(2,1)S(1)} %added.3.after_ref.refs_0_, bf16[448,128]{1,0:T(8,128)(2,1)S(1)} %collective-permute-done.16.refs_1_, ...), custom_call_target="tpu_custom_call", output_to_operand_aliasing={{2}: (10, {})} | custom-call | tf_op jit(solution)/shard_map/collect/pallas_call | solution.py:529
  (26 shorter events, 0.1 us)
Async XLA Ops:
  6.4 24.0 %copy-start.2 = (f32[128]{0:T(128)S(1)}, f32[128]{0:T(128)}, u32[]{:S(2)}) copy-start(f32[128]{0:T(128)} %param.9) | copy-start | bytes 1540
  6.4 24.0 %copy-start.3 = (f32[128]{0:T(128)S(1)}, f32[128]{0:T(128)}, u32[]{:S(2)}) copy-start(f32[128]{0:T(128)} %param.10) | copy-start | bytes 1540
  6.5 24.0 %collective-permute-start = (bf16[1,2,16,128,128]{4,3,2,1,0:T(8,128)(2,1)S(1)}, bf16[1,2,16,128,128]{4,3,2,1,0:T(8,128)(2,1)S(1)}, u32[]{:S(2)}, u32[]{:S(2)}) collective-permute-start(bf16[1,2,16,128,128]{4,3,2,1,0:T(8,128)(2,1)S(1)} %get-tuple-element.39), channel_id=1, source_target_pairs={{0,4},{4,0},{1,5},{5,1},{2,6},{6,2},{3,7},{7,3},{8,12},{12,8},{9,1... | collective-permute-start | bytes 3145736 | tf_op jit(solution)/shard_map/ppermute | solution.py:372
  8.0 7.9 %collective-permute-start.1 = (bf16[4,128,128]{2,1,0:T(8,128)(2,1)S(1)}, bf16[4,128,128]{2,1,0:T(8,128)(2,1)S(1)}, u32[]{:S(2)}, u32[]{:S(2)}) collective-permute-start(bf16[4,128,128]{2,1,0:T(8,128)(2,1)S(1)} %get-tuple-element.40), channel_id=1, source_target_pairs={{0,1},{1,2},{2,3},{4,5},{5,6},{6,7},{8,9},{9,10},{10,11},{12,13},{... | collective-permute-start | bytes 393224 | tf_op jit(solution)/shard_map/ppermute | solution.py:32
  12.5 7.5 %collective-permute-start.2 = (bf16[4,128,128]{2,1,0:T(8,128)(2,1)S(1)}, bf16[4,128,128]{2,1,0:T(8,128)(2,1)S(1)}, u32[]{:S(2)}, u32[]{:S(2)}) collective-permute-start(bf16[4,128,128]{2,1,0:T(8,128)(2,1)S(1)} %get-tuple-element.41), channel_id=1, source_target_pairs={{1,0},{2,1},{3,2},{5,4},{6,5},{7,6},{9,8},{10,9},{11,10},{13,12},{... | collective-permute-start | bytes 393224 | tf_op jit(solution)/shard_map/ppermute | solution.py:32
  15.9 14.6 %collective-permute-start.3 = (bf16[4,128,128]{2,1,0:T(8,128)(2,1)S(1)}, bf16[4,128,128]{2,1,0:T(8,128)(2,1)S(1)}, u32[]{:S(2)}, u32[]{:S(2)}) collective-permute-start(bf16[4,128,128]{2,1,0:T(8,128)(2,1)S(1)} %collective-permute-done.1.low_ref), channel_id=1, source_target_pairs={{0,4},{4,0},{1,5},{5,1},{2,6},{6,2},{3,7},{7,3},{8,12},{12,8},{9,1... | collective-permute-start | bytes 393224 | tf_op jit(solution)/shard_map/ppermute | solution.py:382
  20.0 10.5 %collective-permute-start.4 = (bf16[4,128,128]{2,1,0:T(8,128)(2,1)S(1)}, bf16[4,128,128]{2,1,0:T(8,128)(2,1)S(1)}, u32[]{:S(2)}, u32[]{:S(2)}) collective-permute-start(bf16[4,128,128]{2,1,0:T(8,128)(2,1)S(1)} %collective-permute-done.2.high_ref), channel_id=1, source_target_pairs={{0,4},{4,0},{1,5},{5,1},{2,6},{6,2},{3,7},{7,3},{8,12},{12,8},{9,1... | collective-permute-start | bytes 393224 | tf_op jit(solution)/shard_map/ppermute | solution.py:383
  20.0 1.4 %collective-permute-start.5 = (f32[8,128]{1,0:T(8,128)S(1)}, f32[8,128]{1,0:T(8,128)S(1)}, u32[]{:S(2)}, u32[]{:S(2)}) collective-permute-start(f32[8,128]{1,0:T(8,128)S(1)} %get-tuple-element.42.refs_0_), channel_id=1, source_target_pairs={{0,4},{4,0},{1,5},{5,1},{2,6},{6,2},{3,7},{7,3},{8,12},{12,8},{9,1... | collective-permute-start | bytes 12296 | tf_op jit(solution)/shard_map/ppermute | solution.py:27
  21.4 5.5 %collective-permute-start.8 = (f32[8,128]{1,0:T(8,128)S(1)}, f32[8,128]{1,0:T(8,128)S(1)}, u32[]{:S(2)}, u32[]{:S(2)}) collective-permute-start(f32[8,128]{1,0:T(8,128)S(1)} %merge.1.refs_2_.after_ref), channel_id=1, source_target_pairs={{0,3},{1,2},{2,1},{3,0},{4,7},{5,6},{6,5},{7,4},{8,11},{9,10},{10,... | collective-permute-start | bytes 12296 | tf_op jit(solution)/shard_map/ppermute | solution.py:27
  23.0 6.3 %collective-permute-start.7 = (f32[8,128]{1,0:T(8,128)S(1)}, f32[8,128]{1,0:T(8,128)S(1)}, u32[]{:S(2)}, u32[]{:S(2)}) collective-permute-start(f32[8,128]{1,0:T(8,128)S(1)} %merge.1.refs_2_.after_ref), channel_id=1, source_target_pairs={{0,2},{1,3},{2,0},{3,1},{4,6},{5,7},{6,4},{7,5},{8,10},{9,11},{10,... | collective-permute-start | bytes 12296 | tf_op jit(solution)/shard_map/ppermute | solution.py:27
  26.9 3.6 %collective-permute-start.6 = (f32[8,128]{1,0:T(8,128)S(1)}, f32[8,128]{1,0:T(8,128)S(1)}, u32[]{:S(2)}, u32[]{:S(2)}) collective-permute-start(f32[8,128]{1,0:T(8,128)S(1)} %merge.1.refs_2_.after_ref), channel_id=1, source_target_pairs={{0,1},{1,0},{2,3},{3,2},{4,5},{5,4},{6,7},{7,6},{8,9},{9,8},{10,11... | collective-permute-start | bytes 12296 | tf_op jit(solution)/shard_map/ppermute | solution.py:27
  33.8 10.1 %copy-start = (bf16[3,3,3,128,128]{4,3,2,1,0:T(8,128)(2,1)S(1)}, bf16[3,3,3,128,128]{4,3,2,1,0:T(8,128)(2,1)}, u32[]{:S(2)}) copy-start(bf16[3,3,3,128,128]{4,3,2,1,0:T(8,128)(2,1)} %kernel_ref.1) | copy-start | bytes 2654212
  43.7 0.7 copy-start.1
  43.7 2.6 %collective-permute-start.9 = (f32[4,448,128]{2,1,0:T(8,128)S(1)}, f32[4,448,128]{2,1,0:T(8,128)S(1)}, u32[]{:S(2)}, u32[]{:S(2)}) collective-permute-start(f32[4,448,128]{2,1,0:T(8,128)S(1)} %get-tuple-element.46), channel_id=1, source_target_pairs={{0,4},{4,0},{1,5},{5,1},{2,6},{6,2},{3,7},{7,3},{8,12},{12,8},{9,1... | collective-permute-start | bytes 2752520 | tf_op jit(solution)/shard_map/ppermute | solution.py:27
  47.0 10.0 %collective-permute-start.10 = (bf16[448,128]{1,0:T(8,128)(2,1)S(1)}, bf16[448,128]{1,0:T(8,128)(2,1)S(1)}, u32[]{:S(2)}, u32[]{:S(2)}) collective-permute-start(bf16[448,128]{1,0:T(8,128)(2,1)S(1)} %get-tuple-element.54), channel_id=1, source_target_pairs={{0,8},{8,0},{16,24},{24,16},{1,9},{9,1},{17,25},{25,17},{2,10},{10... | collective-permute-start | bytes 344072 | tf_op jit(solution)/shard_map/ppermute | solution.py:27
  48.6 8.5 %collective-permute-start.11 = (bf16[448,128]{1,0:T(8,128)(2,1)S(1)}, bf16[448,128]{1,0:T(8,128)(2,1)S(1)}, u32[]{:S(2)}, u32[]{:S(2)}) collective-permute-start(bf16[448,128]{1,0:T(8,128)(2,1)S(1)} %get-tuple-element.55), channel_id=1, source_target_pairs={{0,16},{8,24},{16,0},{24,8},{1,17},{9,25},{17,1},{25,9},{2,18},{10... | collective-permute-start | bytes 344072 | tf_op jit(solution)/shard_map/ppermute | solution.py:27
  50.1 7.0 %collective-permute-start.12 = (bf16[448,128]{1,0:T(8,128)(2,1)S(1)}, bf16[448,128]{1,0:T(8,128)(2,1)S(1)}, u32[]{:S(2)}, u32[]{:S(2)}) collective-permute-start(bf16[448,128]{1,0:T(8,128)(2,1)S(1)} %get-tuple-element.56), channel_id=1, source_target_pairs={{0,24},{8,16},{16,8},{24,0},{1,25},{9,17},{17,9},{25,1},{2,26},{10... | collective-permute-start | bytes 344072 | tf_op jit(solution)/shard_map/ppermute | solution.py:27
  57.2 10.4 %collective-permute-start.15 = (bf16[448,128]{1,0:T(8,128)(2,1)S(1)}, bf16[448,128]{1,0:T(8,128)(2,1)S(1)}, u32[]{:S(2)}, u32[]{:S(2)}) collective-permute-start(bf16[448,128]{1,0:T(8,128)(2,1)S(1)} %added.2.after_ref.refs_0_), channel_id=1, source_target_pairs={{0,3},{1,2},{2,1},{3,0},{4,7},{5,6},{6,5},{7,4},{8,11},{9,10},{10,... | collective-permute-start | bytes 344072 | tf_op jit(solution)/shard_map/ppermute | solution.py:27
  58.8 10.9 %collective-permute-start.14 = (bf16[448,128]{1,0:T(8,128)(2,1)S(1)}, bf16[448,128]{1,0:T(8,128)(2,1)S(1)}, u32[]{:S(2)}, u32[]{:S(2)}) collective-permute-start(bf16[448,128]{1,0:T(8,128)(2,1)S(1)} %added.2.after_ref.refs_0_), channel_id=1, source_target_pairs={{0,2},{1,3},{2,0},{3,1},{4,6},{5,7},{6,4},{7,5},{8,10},{9,11},{10,... | collective-permute-start | bytes 344072 | tf_op jit(solution)/shard_map/ppermute | solution.py:27
  59.6 10.1 %collective-permute-start.13 = (bf16[448,128]{1,0:T(8,128)(2,1)S(1)}, bf16[448,128]{1,0:T(8,128)(2,1)S(1)}, u32[]{:S(2)}, u32[]{:S(2)}) collective-permute-start(bf16[448,128]{1,0:T(8,128)(2,1)S(1)} %added.2.after_ref.refs_0_), channel_id=1, source_target_pairs={{0,1},{1,0},{2,3},{3,2},{4,5},{5,4},{6,7},{7,6},{8,9},{9,8},{10,11... | collective-permute-start | bytes 344072 | tf_op jit(solution)/shard_map/ppermute | solution.py:27
  69.8 6.6 %collective-permute-start.18 = (bf16[448,128]{1,0:T(8,128)(2,1)S(1)}, bf16[448,128]{1,0:T(8,128)(2,1)S(1)}, u32[]{:S(2)}, u32[]{:S(2)}) collective-permute-start(bf16[448,128]{1,0:T(8,128)(2,1)S(1)} %added.3.after_ref.refs_0_), channel_id=1, source_target_pairs={{0,24},{8,16},{16,8},{24,0},{1,25},{9,17},{17,9},{25,1},{2,26},{10... | collective-permute-start | bytes 344072 | tf_op jit(solution)/shard_map/ppermute | solution.py:27
  72.3 5.0 %collective-permute-start.17 = (bf16[448,128]{1,0:T(8,128)(2,1)S(1)}, bf16[448,128]{1,0:T(8,128)(2,1)S(1)}, u32[]{:S(2)}, u32[]{:S(2)}) collective-permute-start(bf16[448,128]{1,0:T(8,128)(2,1)S(1)} %added.3.after_ref.refs_0_), channel_id=1, source_target_pairs={{0,16},{8,24},{16,0},{24,8},{1,17},{9,25},{17,1},{25,9},{2,18},{10... | collective-permute-start | bytes 344072 | tf_op jit(solution)/shard_map/ppermute | solution.py:27
  72.8 4.8 %collective-permute-start.16 = (bf16[448,128]{1,0:T(8,128)(2,1)S(1)}, bf16[448,128]{1,0:T(8,128)(2,1)S(1)}, u32[]{:S(2)}, u32[]{:S(2)}) collective-permute-start(bf16[448,128]{1,0:T(8,128)(2,1)S(1)} %added.3.after_ref.refs_0_), channel_id=1, source_target_pairs={{0,8},{8,0},{16,24},{24,16},{1,9},{9,1},{17,25},{25,17},{2,10},{10... | collective-permute-start | bytes 344072 | tf_op jit(solution)/shard_map/ppermute | solution.py:27
  73.3 6.5 %collective-permute-start.19 = (bf16[448,128]{1,0:T(8,128)(2,1)S(1)}, bf16[448,128]{1,0:T(8,128)(2,1)S(1)}, u32[]{:S(2)}, u32[]{:S(2)}) collective-permute-start(bf16[448,128]{1,0:T(8,128)(2,1)S(1)} %added.3.after_ref.refs_0_), channel_id=1, source_target_pairs={{0,4},{4,0},{1,5},{5,1},{2,6},{6,2},{3,7},{7,3},{8,12},{12,8},{9,1... | collective-permute-start | bytes 344072 | tf_op jit(solution)/shard_map/ppermute | solution.py:27
  76.4 3.5 %collective-permute-start.22 = (bf16[448,128]{1,0:T(8,128)(2,1)S(1)}, bf16[448,128]{1,0:T(8,128)(2,1)S(1)}, u32[]{:S(2)}, u32[]{:S(2)}) collective-permute-start(bf16[448,128]{1,0:T(8,128)(2,1)S(1)} %collective-permute-done.18.refs_3_), channel_id=1, source_target_pairs={{0,4},{4,0},{1,5},{5,1},{2,6},{6,2},{3,7},{7,3},{8,12},{12,8},{9,1... | collective-permute-start | bytes 344072 | tf_op jit(solution)/shard_map/ppermute | solution.py:27
  77.3 2.5 %collective-permute-start.21 = (bf16[448,128]{1,0:T(8,128)(2,1)S(1)}, bf16[448,128]{1,0:T(8,128)(2,1)S(1)}, u32[]{:S(2)}, u32[]{:S(2)}) collective-permute-start(bf16[448,128]{1,0:T(8,128)(2,1)S(1)} %collective-permute-done.17.refs_2_), channel_id=1, source_target_pairs={{0,4},{4,0},{1,5},{5,1},{2,6},{6,2},{3,7},{7,3},{8,12},{12,8},{9,1... | collective-permute-start | bytes 344072 | tf_op jit(solution)/shard_map/ppermute | solution.py:27
  77.6 2.3 %collective-permute-start.20 = (bf16[448,128]{1,0:T(8,128)(2,1)S(1)}, bf16[448,128]{1,0:T(8,128)(2,1)S(1)}, u32[]{:S(2)}, u32[]{:S(2)}) collective-permute-start(bf16[448,128]{1,0:T(8,128)(2,1)S(1)} %collective-permute-done.16.refs_1_), channel_id=1, source_target_pairs={{0,4},{4,0},{1,5},{5,1},{2,6},{6,2},{3,7},{7,3},{8,12},{12,8},{9,1... | collective-permute-start | bytes 344072 | tf_op jit(solution)/shard_map/ppermute | solution.py:27

commit v7 on v6

--- a/solution.py
+++ b/solution.py
@@ -25,11 +25,6 @@
     length = lax.axis_size(axis)
     assert length & (length - 1) == 0
     return lax.ppermute(array, axis, [(i, i ^ by) for i in range(length)])
-
-
-def shifted(array, axis, by):
-    length = lax.axis_size(axis)
-    return lax.ppermute(array, axis, [(i, i + by) for i in range(length) if 0 <= i + by < length])
 
 
 def group_sum(row, per):
@@ -46,21 +41,24 @@
 
 
 def merged(parts):
-    count = sum(part[0:1] for part in parts)
-    total = sum(part[1:2] for part in parts)
+    count = sum(part[0] for part in parts)
+    total = sum(part[1] for part in parts)
     mean = total / jnp.maximum(count, 1.0)
     squares = jnp.zeros_like(mean)
     for part in parts:
-        away = part[1:2] / jnp.maximum(part[0:1], 1.0) - mean
-        squares = squares + (part[2:3] + part[0:1] * (away * away))
-    return count, total, mean, squares
-
-
-def ends_kernel(video_hbm, low_ref, high_ref, sems):
+        away = part[1] / jnp.maximum(part[0], 1.0) - mean
+        squares = squares + (part[2] + part[0] * (away * away))
+    return count, total, squares
+
+
+def ends_kernel(info_ref, video_hbm, near_ref, far_ref, sems):
     rows = video_hbm.shape[2]
+    odd = info_ref[6]
     copies = [
         pltpu.make_async_copy(video_hbm.at[0, :, row], ref, sems.at[n])
-        for n, (row, ref) in enumerate(((rows - 1, low_ref), (0, high_ref)))
+        for n, (row, ref) in enumerate(
+            (((1 - odd) * (rows - 1), near_ref), (odd * (rows - 1), far_ref))
+        )
     ]
     for copy in copies:
         copy.start()
@@ -68,7 +66,7 @@
         copy.wait()
 
 
-def stats_kernel(per, before, info_ref, video_hbm, cot_hbm, *refs):
+def stats_kernel(before, info_ref, video_hbm, cot_hbm, *refs):
     out_ref, video_ref, cot_ref, tail_ref, sems = refs
     frames, rows, cols, chans = video_ref.shape[1:]
     parts_n = 2 * frames
@@ -81,7 +79,7 @@
         copies[-1].start()
     later = [pltpu.make_async_copy(cot_hbm, cot_ref, sems.at[parts_n])]
     later[0].start()
-    size = float(some * cols * per)
+    size = float(some * cols // 8)
     lanes = 4
     split = (cols // (8 * lanes), lanes, 8, chans)
     start = jnp.zeros((lanes, 8, chans), F32)
@@ -97,33 +95,25 @@
         def add(y, acc, f=f, y0=y0):
             return acc + jnp.sum(video_ref[0, f, y0 + y].astype(F32).reshape(split), axis=0)
 
-        acc = jnp.sum(lax.fori_loop(0, some, add, start, unroll=4), axis=0)
-        total = group_sum(jnp.sum(acc, axis=0, keepdims=True), per)
+        total = jnp.sum(lax.fori_loop(0, some, add, start, unroll=8), axis=0)
         mean = total / size
 
         def deviate(y, acc, f=f, y0=y0, mean=mean):
             away = video_ref[0, f, y0 + y].astype(F32).reshape(split) - mean
             return acc + jnp.sum(away * away, axis=0)
 
-        acc = jnp.sum(lax.fori_loop(0, some, deviate, start, unroll=4), axis=0)
-        squares = group_sum(jnp.sum(acc, axis=0, keepdims=True), per)
+        squares = jnp.sum(lax.fori_loop(0, some, deviate, start, unroll=8), axis=0)
         keep = (f < info_ref[0]).astype(F32)
-        parts.append(
-            jnp.concatenate([jnp.full((1, chans), size, F32), total, squares], axis=0) * keep
-        )
-    count, total, _, deviations = merged(parts)
-    out_ref[...] = jnp.concatenate(
-        [count, total, deviations, jnp.zeros((5, chans), F32)], axis=0
-    )
+        parts.append((jnp.full((8, chans), size, F32) * keep, total * keep, squares * keep))
+    for n, value in enumerate(merged(parts)):
+        out_ref[n] = value
     for copy in later:
         copy.wait()
 
 
 def merge_kernel(*refs):
-    count, total, _, deviations = merged([ref[...] for ref in refs[:-1]])
-    refs[-1][...] = jnp.concatenate(
-        [count, total, deviations, jnp.zeros((5, count.shape[1]), F32)], axis=0
-    )
+    for n, value in enumerate(merged([ref[...] for ref in refs[:-1]])):
+        refs[-1][n] = value
 
 
 def cotangent_kernel(info_ref, cot_ref, turned_ref, bias_ref, wide):
@@ -150,16 +140,22 @@
 
 
 def activate_kernel(
-    parts_n, info_ref, video_ref, early_ref, low_ref, high_ref, low_early_ref, high_early_ref, *refs
+    parts_n, per, info_ref, video_ref, early_ref, near_ref, far_ref, near_early_ref, *refs
 ):
-    gain_ref, shift_ref, *refs = refs
+    far_early_ref, gain_ref, shift_ref, *refs = refs
     parts, out_ref, wide = refs[:parts_n], refs[parts_n], refs[parts_n + 1]
     frames, rows, cols, chans = video_ref.shape[1:]
     before = early_ref.shape[1]
     step = cols // TILE
     inside, first, has_low, has_high = info_ref[0], info_ref[1], info_ref[2], info_ref[3]
-    count, _, mean, squares = merged([ref[...] for ref in parts])
-    scale = 0.5 * lax.rsqrt(squares / count + 1e-05) * gain_ref[...]
+    count, total, squares = merged([ref[...] for ref in parts])
+    every = jnp.sum(count, axis=0, keepdims=True) * per
+    mean = group_sum(jnp.sum(total, axis=0, keepdims=True), per) / every
+    away = total / jnp.maximum(count, 1.0) - mean
+    squares = jnp.sum(squares + count * (away * away), axis=0, keepdims=True)
+    squares = group_sum(squares, per)
+    odd = info_ref[6] == 1
+    scale = 0.5 * lax.rsqrt(squares / every + 1e-05) * gain_ref[...]
     offset = 0.5 * shift_ref[...] - mean * scale
     slots = wide.shape[0]
     wide[:, 0:8, :] = jnp.zeros((slots, 8, chans), F32)
@@ -182,8 +178,10 @@
             return carry
 
         lax.fori_loop(0, rows, inner, 0, unroll=4)
-        low = low_early_ref[frames + local] if local < 0 else low_ref[local]
-        high = high_early_ref[frames + local] if local < 0 else high_ref[local]
+        near = near_early_ref[frames + local] if local < 0 else near_ref[local]
+        far = far_early_ref[frames + local] if local < 0 else far_ref[local]
+        near, far = near.astype(F32), far.astype(F32)
+        low, high = jnp.where(odd, near, far), jnp.where(odd, far, near)
         row(low, keep * has_low.astype(F32), 0, f, 0)
         row(high, keep * has_high.astype(F32), 1, f, rows + 1)
 
@@ -337,28 +335,30 @@
             (space < spaces - 1).astype(jnp.int32),
             tm,
             dp,
+            space % 2,
         ]
     ).astype(jnp.int32)
 
     source = pltpu.with_memory_space_constraint(video, pltpu.HBM)
     border = jax.ShapeDtypeStruct((frames, cols, chans), BF16)
-    edge_low, edge_high = pl.pallas_call(
+    near, far = pl.pallas_call(
         ends_kernel,
-        in_specs=[ANY],
+        in_specs=[SMEM, ANY],
         out_specs=[VMEM, VMEM],
         out_shape=[border, border],
         scratch_shapes=[pltpu.SemaphoreType.DMA((2,))],
         compiler_params=params(1),
         name="ends",
-    )(source)
-    low = shifted(edge_low, "space", 1)
-    high = shifted(edge_high, "space", -1)
+    )(info, source)
+    near = swap(near, "space", 1)
+    between = [(i, i + 1) for i in range(1, spaces - 1, 2)]
+    far = lax.ppermute(far, "space", between + [(j, i) for i, j in between])
     stats, local, masked_in, tail = pl.pallas_call(
-        functools.partial(stats_kernel, per, before),
+        functools.partial(stats_kernel, before),
         in_specs=[SMEM, ANY, ANY],
         out_specs=[VMEM] * 4,
         out_shape=[
-            jax.ShapeDtypeStruct((8, chans), F32),
+            jax.ShapeDtypeStruct((3, 8, chans), F32),
             jax.ShapeDtypeStruct(video.shape, BF16),
             jax.ShapeDtypeStruct(cotangent.shape, BF16),
             jax.ShapeDtypeStruct((1, before, rows, cols, chans), BF16),
@@ -374,13 +374,13 @@
         merge_kernel,
         in_specs=[VMEM] * tms,
         out_specs=VMEM,
-        out_shape=jax.ShapeDtypeStruct((8, chans), F32),
+        out_shape=jax.ShapeDtypeStruct((3, 8, chans), F32),
         compiler_params=params(1),
         name="merge",
     )(*gathered)
     parts = [stats] + [swap(stats, "space", r) for r in range(1, spaces)]
-    low_early = lax.ppermute(low, "tm", following)
-    high_early = lax.ppermute(high, "tm", following)
+    near_early = lax.ppermute(near, "tm", following)
+    far_early = lax.ppermute(far, "tm", following)
     pair = 2
     taps = pl.pallas_call(
         taps_kernel,
@@ -407,7 +407,7 @@
     )(info, masked_in)
 
     act = pl.pallas_call(
-        functools.partial(activate_kernel, spaces),
+        functools.partial(activate_kernel, spaces, per),
         in_specs=[SMEM] + [VMEM] * (8 + spaces),
         out_specs=VMEM,
         out_shape=jax.ShapeDtypeStruct(
@@ -420,10 +420,10 @@
         info,
         local,
         early,
-        low,
-        high,
-        low_early,
-        high_early,
+        near,
+        far,
+        near_early,
+        far_early,
         norm_gain.reshape(1, chans),
         norm_shift.reshape(1, chans),
         *parts,

time: 82.8 us -> 78.2 us (0.944)
  waiting for transfers between devices: 16.9 us -> 11.1 us
  starting transfers between devices: 21.9 us -> 24.4 us
  Pallas kernels: 41.8 us -> 40.5 us
    ppermute x18 -> x19, starting transfers between devices: 15.5 us -> 22.7 us  [swap(): return lax.ppermute(array, axis, [(i, i ^ by) for i in range(length)])]
    ppermute x4 -> x3, waiting for transfers between devices: 6.21 us -> 0.01 us  [the longest x1 0.01 us: step_of(): near_early = lax.ppermute(near, 'tm', following)]
    ppermute x4 -> x3, starting transfers between devices: 5.79 us -> 1.17 us  [the longest x1 0.66 us: step_of(): far = lax.ppermute(far, 'space', between + [(j, i) for i, j in between])]
    pallas_call x3, Pallas kernels: 9.28 us -> 7.96 us  [the longest x1 3.55 us: step_of(): pl.pallas_call(functools.partial(activate_kernel, spaces, per), in_specs=...]
    ppermute x18 -> x19, waiting for transfers between devices: 10.7 us -> 11.1 us  [swap(): return lax.ppermute(array, axis, [(i, i ^ by) for i in range(length)])]
  transfers between devices with their start and end apart: 23 -> 23, of which waited for: 9 -> 6; matrix products, arithmetic and copies ran while one was open for 0% -> 0% of each run, Pallas kernels for 24% -> 27%
where the time goes in v7:
time: 78.2 us; the launch traced here: 78.1 us
  Pallas kernels  40.5 us (52%)
  starting transfers between devices  24.4 us (31%)
  waiting for transfers between devices  11.1 us (14%)
  between operations  1.77 us (2%)
    ppermute x19, starting transfers between devices, swap(): return lax.ppermute(array, axis, [(i, i ^ by) for i in range(length)])  22.7 us
    pallas_call x8, Pallas kernels, cover(): pl.pallas_call(functools.partial(conv_kernel, pieces[n], where(n - 1) if...  16.4 us
    ppermute x19, waiting for transfers between devices, swap(): return lax.ppermute(array, axis, [(i, i ^ by) for i in range(length)])  11.1 us
    pallas_call x1, Pallas kernels, step_of(): pl.pallas_call(weights_kernel, in_specs=[SMEM, VMEM, VMEM, VMEM], out_spe...  9.95 us
    pallas_call x1, Pallas kernels, step_of(): pl.pallas_call(functools.partial(activate_kernel, spaces, per), in_specs=...  3.55 us
    pallas_call x1, Pallas kernels, step_of(): pl.pallas_call(functools.partial(stats_kernel, before), in_specs=[SMEM, A...  2.89 us
    pallas_call x1, Pallas kernels, step_of(): pl.pallas_call(collect, in_specs=[SMEM] + [VMEM] * (len(order) + 1) + [AN...  2.54 us
    pallas_call x1, Pallas kernels, step_of(): pl.pallas_call(cotangent_kernel, in_specs=[SMEM, VMEM], out_specs=[VMEM,...  2.47 us
  transfers between devices with their start and end apart: 23, of which 6 were waited for; matrix products, arithmetic and copies ran while one was open for 0% of the time, Pallas kernels for 27%

profile of v7, /device:TPU:0, one launch (start us, length us, event | category | flops | bytes accessed | tf_op | source)
XLA Modules:
  0.0 78.1 jit_solution(13910492456533845061)
XLA Ops:
  1.3 0.1 stack.39.info_ref
  1.4 2.9 %stats.1 = (f32[3,8,128]{2,1,0:T(8,128)S(1)}, bf16[1,4,16,128,128]{4,3,2,1,0:T(8,128)(2,1)S(1)}, bf16[1,4,16,128,128]{4,3,2,1,0:T(8,128)(2,1)S(1)}, bf16[1,2,16,128,128]{4,3,2,1,0:T(8,128)(2,1)S(1)}) custom-call(s32[7]{0:T(128)S(1)} %stack.39.info_ref, bf16[1,4,16,128,128]{4,3,2,1,0:T(8,128)(2,1)} %video_hbm.3, bf16[1,4,16,128,128]{4,3,2,1,0:T(8,128)(2,1)} %cot_hbm.1), custom_call_target="tpu_custom_call" | custom-call | tf_op jit(solution)/shard_map/stats/pallas_call | solution.py:356
  4.3 0.0 copy-start.2
  4.3 0.0 copy-start.3
  4.3 0.6 collective-permute-start
  4.9 1.5 %ends.1 = (bf16[4,128,128]{2,1,0:T(8,128)(2,1)S(1)}, bf16[4,128,128]{2,1,0:T(8,128)(2,1)S(1)}) custom-call(s32[7]{0:T(128)S(1)} %stack.39.info_ref, bf16[1,4,16,128,128]{4,3,2,1,0:T(8,128)(2,1)} %video_hbm.3), custom_call_target="tpu_custom_call" | custom-call | tf_op jit(solution)/shard_map/ends/pallas_call | solution.py:344
  6.4 2.6 %collective-permute-start.1 = (bf16[4,128,128]{2,1,0:T(8,128)(2,1)S(1)}, bf16[4,128,128]{2,1,0:T(8,128)(2,1)S(1)}, u32[]{:S(2)}, u32[]{:S(2)}) collective-permute-start(bf16[4,128,128]{2,1,0:T(8,128)(2,1)S(1)} %get-tuple-element.40), channel_id=1, source_target_pairs={{0,1},{1,0},{2,3},{3,2},{4,5},{5,4},{6,7},{7,6},{8,9},{9,8},{10,11... | collective-permute-start | bytes 393224 | tf_op jit(solution)/shard_map/ppermute | solution.py:27
  9.0 0.7 collective-permute-start.2
  9.7 3.5 %collective-permute-done.1.near_ref = bf16[4,128,128]{2,1,0:T(8,128)(2,1)S(1)} collective-permute-done((bf16[4,128,128]{2,1,0:T(8,128)(2,1)S(1)}, bf16[4,128,128]{2,1,0:T(8,128)(2,1)S(1)}, u32[]{:S(2)}, u32[]{:S(2)}) %collective-permute-start.1) | collective-permute-done | bytes 131104 | tf_op jit(solution)/shard_map/ppermute | solution.py:27
  13.2 0.5 collective-permute-start.4
  13.7 1.2 %collective-permute-done.5.refs_1_ = f32[3,8,128]{2,1,0:T(8,128)S(1)} collective-permute-done((f32[3,8,128]{2,1,0:T(8,128)S(1)}, f32[3,8,128]{2,1,0:T(8,128)S(1)}, u32[]{:S(2)}, u32[]{:S(2)}) %collective-permute-start.5) | collective-permute-done | bytes 12320 | tf_op jit(solution)/shard_map/ppermute | solution.py:27
  14.9 3.8 %collective-permute-start.8 = (f32[3,8,128]{2,1,0:T(8,128)S(1)}, f32[3,8,128]{2,1,0:T(8,128)S(1)}, u32[]{:S(2)}, u32[]{:S(2)}) collective-permute-start(f32[3,8,128]{2,1,0:T(8,128)S(1)} %merge.1.refs_3_.after_ref), channel_id=1, source_target_pairs={{0,3},{1,2},{2,1},{3,0},{4,7},{5,6},{6,5},{7,4},{8,11},{9,10},{10,... | collective-permute-start | bytes 36872 | tf_op jit(solution)/shard_map/ppermute | solution.py:27
  18.7 2.1 %collective-permute-start.7 = (f32[3,8,128]{2,1,0:T(8,128)S(1)}, f32[3,8,128]{2,1,0:T(8,128)S(1)}, u32[]{:S(2)}, u32[]{:S(2)}) collective-permute-start(f32[3,8,128]{2,1,0:T(8,128)S(1)} %merge.1.refs_3_.after_ref), channel_id=1, source_target_pairs={{0,2},{1,3},{2,0},{3,1},{4,6},{5,7},{6,4},{7,5},{8,10},{9,11},{10,... | collective-permute-start | bytes 36872 | tf_op jit(solution)/shard_map/ppermute | solution.py:27
  20.9 2.2 %collective-permute-start.6 = (f32[3,8,128]{2,1,0:T(8,128)S(1)}, f32[3,8,128]{2,1,0:T(8,128)S(1)}, u32[]{:S(2)}, u32[]{:S(2)}) collective-permute-start(f32[3,8,128]{2,1,0:T(8,128)S(1)} %merge.1.refs_3_.after_ref), channel_id=1, source_target_pairs={{0,1},{1,0},{2,3},{3,2},{4,5},{5,4},{6,7},{7,6},{8,9},{9,8},{10,11... | collective-permute-start | bytes 36872 | tf_op jit(solution)/shard_map/ppermute | solution.py:27
  23.1 2.5 %cotangent.1 = (bf16[4,16,128,128]{3,2,1,0:T(8,128)(2,1)S(1)}, f32[8,128]{1,0:T(8,128)S(1)}) custom-call(s32[7]{0:T(128)S(1)} %stack.39.info_ref, bf16[1,4,16,128,128]{4,3,2,1,0:T(8,128)(2,1)S(1)} %get-tuple-element.36.cot_ref), custom_call_target="tpu_custom_call" | custom-call | tf_op jit(solution)/shard_map/cotangent/pallas_call | solution.py:396
  25.6 3.5 %activate.1.act_ref = bf16[6,18,10,16,128]{4,3,2,1,0:T(8,128)(2,1)S(1)} custom-call(s32[7]{0:T(128)S(1)} %stack.39.info_ref, bf16[1,4,16,128,128]{4,3,2,1,0:T(8,128)(2,1)S(1)} %get-tuple-element.38.video_ref, bf16[1,2,16,128,128]{4,3,2,1,0:T(8,128)(2,1)S(1)} %collective-permute-done.early_ref, bf16[4,128,128]{2,1,0:T(8,128)(2,1)S(1)} %collective-permute-done.1.near_ref, ...), custom_call_target="tpu_custom_call" | custom-call | tf_op jit(solution)/shard_map/activate/pallas_call | solution.py:409
  29.2 0.0 copy-start
  29.2 10.0 %weights.1 = (f32[4,448,128]{2,1,0:T(8,128)S(1)}, f32[4,448,128]{2,1,0:T(8,128)S(1)}) custom-call(s32[7]{0:T(128)S(1)} %stack.39.info_ref, bf16[4,16,128,128]{3,2,1,0:T(8,128)(2,1)S(1)} %get-tuple-element.37.turned_ref, bf16[6,18,10,16,128]{4,3,2,1,0:T(8,128)(2,1)S(1)} %activate.1.act_ref, f32[8,128]{1,0:T(8,128)S(1)} %get-tuple-element.43.bias_ref), custom_call_target="tpu_custom_call" | custom-call | tf_op jit(solution)/shard_map/weights/pallas_call | solution.py:437
  39.2 0.0 copy-start.1
  39.2 0.1 collective-permute-start.9
  39.3 0.4 taps.1.taps_ref
  39.7 0.2 copy-done.1
  39.8 2.0 %conv.8 = (bf16[2,4,128,128]{3,2,1,0:T(8,128)(2,1)S(1)}, bf16[1,4,16,128,128]{4,3,2,1,0:T(8,128)(2,1)}) custom-call(s32[7]{0:T(128)S(1)} %stack.39.info_ref, f32[4,448,128]{2,1,0:T(8,128)S(1)} %get-tuple-element.44.after_ref.keep_ref, bf16[6,18,10,16,128]{4,3,2,1,0:T(8,128)(2,1)S(1)} %activate.1.act_ref, bf16[4608,256]{1,0:T(8,128)(2,1)S(1)} %taps.1.taps_ref, ...), custom_call_target="tpu_custom_call" | custom-call | tf_op jit(solution)/shard_map/conv/pallas_call | solution.py:464
  41.8 0.6 spread.1
  42.5 1.6 %collective-permute-start.10 = (bf16[448,128]{1,0:T(8,128)(2,1)S(1)}, bf16[448,128]{1,0:T(8,128)(2,1)S(1)}, u32[]{:S(2)}, u32[]{:S(2)}) collective-permute-start(bf16[448,128]{1,0:T(8,128)(2,1)S(1)} %get-tuple-element.54), channel_id=1, source_target_pairs={{0,8},{8,0},{16,24},{24,16},{1,9},{9,1},{17,25},{25,17},{2,10},{10... | collective-permute-start | bytes 344072 | tf_op jit(solution)/shard_map/ppermute | solution.py:27
  44.0 1.5 %collective-permute-start.11 = (bf16[448,128]{1,0:T(8,128)(2,1)S(1)}, bf16[448,128]{1,0:T(8,128)(2,1)S(1)}, u32[]{:S(2)}, u32[]{:S(2)}) collective-permute-start(bf16[448,128]{1,0:T(8,128)(2,1)S(1)} %get-tuple-element.55), channel_id=1, source_target_pairs={{0,16},{8,24},{16,0},{24,8},{1,17},{9,25},{17,1},{25,9},{2,18},{10... | collective-permute-start | bytes 344072 | tf_op jit(solution)/shard_map/ppermute | solution.py:27
  45.6 0.5 collective-permute-start.12
  46.0 2.5 %conv.9 = (bf16[2,4,128,128]{3,2,1,0:T(8,128)(2,1)S(1)}, bf16[1,4,16,128,128]{4,3,2,1,0:T(8,128)(2,1)}) custom-call(s32[7]{0:T(128)S(1)} %stack.39.info_ref, f32[448,128]{1,0:T(8,128)S(1)} %get-tuple-element.47.after_ref.refs_0_, bf16[6,18,10,16,128]{4,3,2,1,0:T(8,128)(2,1)S(1)} %activate.1.act_ref, ...), custom_call_target="tpu_custom_call", output_to_operand_aliasing={{1}: (7, {})} | custom-call | tf_op jit(solution)/shard_map/conv/pallas_call | solution.py:464
  48.5 2.0 %conv.10 = (bf16[2,4,128,128]{3,2,1,0:T(8,128)(2,1)S(1)}, bf16[1,4,16,128,128]{4,3,2,1,0:T(8,128)(2,1)}) custom-call(s32[7]{0:T(128)S(1)} %stack.39.info_ref, bf16[2,4,128,128]{3,2,1,0:T(8,128)(2,1)S(1)} %get-tuple-element.49.after_ref.refs_0_, bf16[6,18,10,16,128]{4,3,2,1,0:T(8,128)(2,1)S(1)} %activate.1.act_ref, ...), custom_call_target="tpu_custom_call", output_to_operand_aliasing={{1}: (7, {})} | custom-call | tf_op jit(solution)/shard_map/conv/pallas_call | solution.py:464
  50.5 2.0 %conv.11 = (bf16[2,4,128,128]{3,2,1,0:T(8,128)(2,1)S(1)}, bf16[1,4,16,128,128]{4,3,2,1,0:T(8,128)(2,1)}) custom-call(s32[7]{0:T(128)S(1)} %stack.39.info_ref, bf16[2,4,128,128]{3,2,1,0:T(8,128)(2,1)S(1)} %get-tuple-element.51.after_ref.refs_0_, bf16[6,18,10,16,128]{4,3,2,1,0:T(8,128)(2,1)S(1)} %activate.1.act_ref, ...), custom_call_target="tpu_custom_call", output_to_operand_aliasing={{1}: (7, {})} | custom-call | tf_op jit(solution)/shard_map/conv/pallas_call | solution.py:464
  52.6 0.1 added.2.after_ref.refs_0_
  52.6 2.7 %collective-permute-start.15 = (bf16[448,128]{1,0:T(8,128)(2,1)S(1)}, bf16[448,128]{1,0:T(8,128)(2,1)S(1)}, u32[]{:S(2)}, u32[]{:S(2)}) collective-permute-start(bf16[448,128]{1,0:T(8,128)(2,1)S(1)} %added.2.after_ref.refs_0_), channel_id=1, source_target_pairs={{0,3},{1,2},{2,1},{3,0},{4,7},{5,6},{6,5},{7,4},{8,11},{9,10},{10,... | collective-permute-start | bytes 344072 | tf_op jit(solution)/shard_map/ppermute | solution.py:27
  55.3 0.0 collective-permute-start.14
  55.3 1.8 %collective-permute-start.13 = (bf16[448,128]{1,0:T(8,128)(2,1)S(1)}, bf16[448,128]{1,0:T(8,128)(2,1)S(1)}, u32[]{:S(2)}, u32[]{:S(2)}) collective-permute-start(bf16[448,128]{1,0:T(8,128)(2,1)S(1)} %added.2.after_ref.refs_0_), channel_id=1, source_target_pairs={{0,1},{1,0},{2,3},{3,2},{4,5},{5,4},{6,7},{7,6},{8,9},{9,8},{10,11... | collective-permute-start | bytes 344072 | tf_op jit(solution)/shard_map/ppermute | solution.py:27
  57.1 2.0 %conv.12 = (bf16[2,4,128,128]{3,2,1,0:T(8,128)(2,1)S(1)}, bf16[1,4,16,128,128]{4,3,2,1,0:T(8,128)(2,1)}) custom-call(s32[7]{0:T(128)S(1)} %stack.39.info_ref, bf16[448,128]{1,0:T(8,128)(2,1)S(1)} %added.2.after_ref.refs_0_, bf16[6,18,10,16,128]{4,3,2,1,0:T(8,128)(2,1)S(1)} %activate.1.act_ref, ...), custom_call_target="tpu_custom_call", output_to_operand_aliasing={{1}: (7, {})} | custom-call | tf_op jit(solution)/shard_map/conv/pallas_call | solution.py:464
  59.1 2.0 %conv.13 = (bf16[2,4,128,128]{3,2,1,0:T(8,128)(2,1)S(1)}, bf16[1,4,16,128,128]{4,3,2,1,0:T(8,128)(2,1)}) custom-call(s32[7]{0:T(128)S(1)} %stack.39.info_ref, bf16[2,4,128,128]{3,2,1,0:T(8,128)(2,1)S(1)} %get-tuple-element.58.after_ref.refs_0_, bf16[6,18,10,16,128]{4,3,2,1,0:T(8,128)(2,1)S(1)} %activate.1.act_ref, ...), custom_call_target="tpu_custom_call", output_to_operand_aliasing={{1}: (7, {})} | custom-call | tf_op jit(solution)/shard_map/conv/pallas_call | solution.py:464
  61.1 2.0 %conv.14 = (bf16[2,4,128,128]{3,2,1,0:T(8,128)(2,1)S(1)}, bf16[1,4,16,128,128]{4,3,2,1,0:T(8,128)(2,1)}) custom-call(s32[7]{0:T(128)S(1)} %stack.39.info_ref, bf16[2,4,128,128]{3,2,1,0:T(8,128)(2,1)S(1)} %get-tuple-element.60.after_ref.refs_0_, bf16[6,18,10,16,128]{4,3,2,1,0:T(8,128)(2,1)S(1)} %activate.1.act_ref, ...), custom_call_target="tpu_custom_call", output_to_operand_aliasing={{1}: (7, {})} | custom-call | tf_op jit(solution)/shard_map/conv/pallas_call | solution.py:464
  63.1 2.1 %collective-permute-done.14.refs_2_ = bf16[448,128]{1,0:T(8,128)(2,1)S(1)} collective-permute-done((bf16[448,128]{1,0:T(8,128)(2,1)S(1)}, bf16[448,128]{1,0:T(8,128)(2,1)S(1)}, u32[]{:S(2)}, u32[]{:S(2)}) %collective-permute-start.14) | collective-permute-done | bytes 114720 | tf_op jit(solution)/shard_map/ppermute | solution.py:27
  65.2 0.1 added.3.after_ref.refs_0_
  65.3 2.5 %collective-permute-start.18 = (bf16[448,128]{1,0:T(8,128)(2,1)S(1)}, bf16[448,128]{1,0:T(8,128)(2,1)S(1)}, u32[]{:S(2)}, u32[]{:S(2)}) collective-permute-start(bf16[448,128]{1,0:T(8,128)(2,1)S(1)} %added.3.after_ref.refs_0_), channel_id=1, source_target_pairs={{0,24},{8,16},{16,8},{24,0},{1,25},{9,17},{17,9},{25,1},{2,26},{10... | collective-permute-start | bytes 344072 | tf_op jit(solution)/shard_map/ppermute | solution.py:27
  67.8 0.5 collective-permute-start.17
  68.3 0.5 collective-permute-start.16
  68.8 3.0 %collective-permute-done.18.refs_3_ = bf16[448,128]{1,0:T(8,128)(2,1)S(1)} collective-permute-done((bf16[448,128]{1,0:T(8,128)(2,1)S(1)}, bf16[448,128]{1,0:T(8,128)(2,1)S(1)}, u32[]{:S(2)}, u32[]{:S(2)}) %collective-permute-start.18) | collective-permute-done | bytes 114720 | tf_op jit(solution)/shard_map/ppermute | solution.py:27
  71.8 1.0 %collective-permute-done.17.refs_2_ = bf16[448,128]{1,0:T(8,128)(2,1)S(1)} collective-permute-done((bf16[448,128]{1,0:T(8,128)(2,1)S(1)}, bf16[448,128]{1,0:T(8,128)(2,1)S(1)}, u32[]{:S(2)}, u32[]{:S(2)}) %collective-permute-start.17) | collective-permute-done | bytes 114720 | tf_op jit(solution)/shard_map/ppermute | solution.py:27
  72.8 0.3 collective-permute-done.16.refs_1_
  73.1 0.3 collective-permute-start.20
  73.3 2.0 %conv.15 = (bf16[2,4,128,128]{3,2,1,0:T(8,128)(2,1)S(1)}, bf16[1,4,16,128,128]{4,3,2,1,0:T(8,128)(2,1)}) custom-call(s32[7]{0:T(128)S(1)} %stack.39.info_ref, bf16[448,128]{1,0:T(8,128)(2,1)S(1)} %added.3.after_ref.refs_0_, bf16[6,18,10,16,128]{4,3,2,1,0:T(8,128)(2,1)S(1)} %activate.1.act_ref, ...), custom_call_target="tpu_custom_call", output_to_operand_aliasing={{1}: (7, {})} | custom-call | tf_op jit(solution)/shard_map/conv/pallas_call | solution.py:464
  75.4 2.5 %collect.1 = (f32[8,432,128]{2,1,0:T(8,128)}, f32[1,128]{1,0:T(1,128)}, bf16[1,4,16,128,128]{4,3,2,1,0:T(8,128)(2,1)}) custom-call(s32[7]{0:T(128)S(1)} %stack.39.info_ref, bf16[448,128]{1,0:T(8,128)(2,1)S(1)} %added.3.after_ref.refs_0_, bf16[448,128]{1,0:T(8,128)(2,1)S(1)} %collective-permute-done.16.refs_1_, ...), custom_call_target="tpu_custom_call", output_to_operand_aliasing={{2}: (10, {})} | custom-call | tf_op jit(solution)/shard_map/collect/pallas_call | solution.py:529
  (26 shorter events, 0.1 us)
Async XLA Ops:
  4.3 21.4 %copy-start.2 = (f32[128]{0:T(128)S(1)}, f32[128]{0:T(128)}, u32[]{:S(2)}) copy-start(f32[128]{0:T(128)} %param.9) | copy-start | bytes 1540
  4.3 21.4 %copy-start.3 = (f32[128]{0:T(128)S(1)}, f32[128]{0:T(128)}, u32[]{:S(2)}) copy-start(f32[128]{0:T(128)} %param.10) | copy-start | bytes 1540
  4.3 21.3 %collective-permute-start = (bf16[1,2,16,128,128]{4,3,2,1,0:T(8,128)(2,1)S(1)}, bf16[1,2,16,128,128]{4,3,2,1,0:T(8,128)(2,1)S(1)}, u32[]{:S(2)}, u32[]{:S(2)}) collective-permute-start(bf16[1,2,16,128,128]{4,3,2,1,0:T(8,128)(2,1)S(1)} %get-tuple-element.39), channel_id=1, source_target_pairs={{0,4},{4,0},{1,5},{5,1},{2,6},{6,2},{3,7},{7,3},{8,12},{12,8},{9,1... | collective-permute-start | bytes 3145736 | tf_op jit(solution)/shard_map/ppermute | solution.py:372
  6.4 6.8 %collective-permute-start.1 = (bf16[4,128,128]{2,1,0:T(8,128)(2,1)S(1)}, bf16[4,128,128]{2,1,0:T(8,128)(2,1)S(1)}, u32[]{:S(2)}, u32[]{:S(2)}) collective-permute-start(bf16[4,128,128]{2,1,0:T(8,128)(2,1)S(1)} %get-tuple-element.40), channel_id=1, source_target_pairs={{0,1},{1,0},{2,3},{3,2},{4,5},{5,4},{6,7},{7,6},{8,9},{9,8},{10,11... | collective-permute-start | bytes 393224 | tf_op jit(solution)/shard_map/ppermute | solution.py:27
  9.0 4.2 %collective-permute-start.2 = (bf16[4,128,128]{2,1,0:T(8,128)(2,1)S(1)}, bf16[4,128,128]{2,1,0:T(8,128)(2,1)S(1)}, u32[]{:S(2)}, u32[]{:S(2)}) collective-permute-start(bf16[4,128,128]{2,1,0:T(8,128)(2,1)S(1)} %get-tuple-element.41), channel_id=1, source_target_pairs={{1,2},{2,1},{5,6},{6,5},{9,10},{10,9},{13,14},{14,13},{17,18},{18,... | collective-permute-start | bytes 393224 | tf_op jit(solution)/shard_map/ppermute | solution.py:355
  13.2 12.4 %collective-permute-start.3 = (bf16[4,128,128]{2,1,0:T(8,128)(2,1)S(1)}, bf16[4,128,128]{2,1,0:T(8,128)(2,1)S(1)}, u32[]{:S(2)}, u32[]{:S(2)}) collective-permute-start(bf16[4,128,128]{2,1,0:T(8,128)(2,1)S(1)} %collective-permute-done.1.near_ref), channel_id=1, source_target_pairs={{0,4},{4,0},{1,5},{5,1},{2,6},{6,2},{3,7},{7,3},{8,12},{12,8},{9,1... | collective-permute-start | bytes 393224 | tf_op jit(solution)/shard_map/ppermute | solution.py:382
  13.2 12.4 %collective-permute-start.4 = (bf16[4,128,128]{2,1,0:T(8,128)(2,1)S(1)}, bf16[4,128,128]{2,1,0:T(8,128)(2,1)S(1)}, u32[]{:S(2)}, u32[]{:S(2)}) collective-permute-start(bf16[4,128,128]{2,1,0:T(8,128)(2,1)S(1)} %collective-permute-done.2.far_ref), channel_id=1, source_target_pairs={{0,4},{4,0},{1,5},{5,1},{2,6},{6,2},{3,7},{7,3},{8,12},{12,8},{9,1... | collective-permute-start | bytes 393224 | tf_op jit(solution)/shard_map/ppermute | solution.py:383
  13.7 1.2 %collective-permute-start.5 = (f32[3,8,128]{2,1,0:T(8,128)S(1)}, f32[3,8,128]{2,1,0:T(8,128)S(1)}, u32[]{:S(2)}, u32[]{:S(2)}) collective-permute-start(f32[3,8,128]{2,1,0:T(8,128)S(1)} %get-tuple-element.42.refs_0_), channel_id=1, source_target_pairs={{0,4},{4,0},{1,5},{5,1},{2,6},{6,2},{3,7},{7,3},{8,12},{12,8},{9,1... | collective-permute-start | bytes 36872 | tf_op jit(solution)/shard_map/ppermute | solution.py:27
  14.9 6.0 %collective-permute-start.8 = (f32[3,8,128]{2,1,0:T(8,128)S(1)}, f32[3,8,128]{2,1,0:T(8,128)S(1)}, u32[]{:S(2)}, u32[]{:S(2)}) collective-permute-start(f32[3,8,128]{2,1,0:T(8,128)S(1)} %merge.1.refs_3_.after_ref), channel_id=1, source_target_pairs={{0,3},{1,2},{2,1},{3,0},{4,7},{5,6},{6,5},{7,4},{8,11},{9,10},{10,... | collective-permute-start | bytes 36872 | tf_op jit(solution)/shard_map/ppermute | solution.py:27
  18.7 6.8 %collective-permute-start.7 = (f32[3,8,128]{2,1,0:T(8,128)S(1)}, f32[3,8,128]{2,1,0:T(8,128)S(1)}, u32[]{:S(2)}, u32[]{:S(2)}) collective-permute-start(f32[3,8,128]{2,1,0:T(8,128)S(1)} %merge.1.refs_3_.after_ref), channel_id=1, source_target_pairs={{0,2},{1,3},{2,0},{3,1},{4,6},{5,7},{6,4},{7,5},{8,10},{9,11},{10,... | collective-permute-start | bytes 36872 | tf_op jit(solution)/shard_map/ppermute | solution.py:27
  20.9 4.7 %collective-permute-start.6 = (f32[3,8,128]{2,1,0:T(8,128)S(1)}, f32[3,8,128]{2,1,0:T(8,128)S(1)}, u32[]{:S(2)}, u32[]{:S(2)}) collective-permute-start(f32[3,8,128]{2,1,0:T(8,128)S(1)} %merge.1.refs_3_.after_ref), channel_id=1, source_target_pairs={{0,1},{1,0},{2,3},{3,2},{4,5},{5,4},{6,7},{7,6},{8,9},{9,8},{10,11... | collective-permute-start | bytes 36872 | tf_op jit(solution)/shard_map/ppermute | solution.py:27
  29.2 10.1 %copy-start = (bf16[3,3,3,128,128]{4,3,2,1,0:T(8,128)(2,1)S(1)}, bf16[3,3,3,128,128]{4,3,2,1,0:T(8,128)(2,1)}, u32[]{:S(2)}) copy-start(bf16[3,3,3,128,128]{4,3,2,1,0:T(8,128)(2,1)} %kernel_ref.1) | copy-start | bytes 2654212
  39.2 0.7 copy-start.1
  39.2 2.6 %collective-permute-start.9 = (f32[4,448,128]{2,1,0:T(8,128)S(1)}, f32[4,448,128]{2,1,0:T(8,128)S(1)}, u32[]{:S(2)}, u32[]{:S(2)}) collective-permute-start(f32[4,448,128]{2,1,0:T(8,128)S(1)} %get-tuple-element.46), channel_id=1, source_target_pairs={{0,4},{4,0},{1,5},{5,1},{2,6},{6,2},{3,7},{7,3},{8,12},{12,8},{9,1... | collective-permute-start | bytes 2752520 | tf_op jit(solution)/shard_map/ppermute | solution.py:27
  42.5 10.1 %collective-permute-start.10 = (bf16[448,128]{1,0:T(8,128)(2,1)S(1)}, bf16[448,128]{1,0:T(8,128)(2,1)S(1)}, u32[]{:S(2)}, u32[]{:S(2)}) collective-permute-start(bf16[448,128]{1,0:T(8,128)(2,1)S(1)} %get-tuple-element.54), channel_id=1, source_target_pairs={{0,8},{8,0},{16,24},{24,16},{1,9},{9,1},{17,25},{25,17},{2,10},{10... | collective-permute-start | bytes 344072 | tf_op jit(solution)/shard_map/ppermute | solution.py:27
  44.0 8.5 %collective-permute-start.11 = (bf16[448,128]{1,0:T(8,128)(2,1)S(1)}, bf16[448,128]{1,0:T(8,128)(2,1)S(1)}, u32[]{:S(2)}, u32[]{:S(2)}) collective-permute-start(bf16[448,128]{1,0:T(8,128)(2,1)S(1)} %get-tuple-element.55), channel_id=1, source_target_pairs={{0,16},{8,24},{16,0},{24,8},{1,17},{9,25},{17,1},{25,9},{2,18},{10... | collective-permute-start | bytes 344072 | tf_op jit(solution)/shard_map/ppermute | solution.py:27
  45.6 7.0 %collective-permute-start.12 = (bf16[448,128]{1,0:T(8,128)(2,1)S(1)}, bf16[448,128]{1,0:T(8,128)(2,1)S(1)}, u32[]{:S(2)}, u32[]{:S(2)}) collective-permute-start(bf16[448,128]{1,0:T(8,128)(2,1)S(1)} %get-tuple-element.56), channel_id=1, source_target_pairs={{0,24},{8,16},{16,8},{24,0},{1,25},{9,17},{17,9},{25,1},{2,26},{10... | collective-permute-start | bytes 344072 | tf_op jit(solution)/shard_map/ppermute | solution.py:27
  52.6 10.4 %collective-permute-start.15 = (bf16[448,128]{1,0:T(8,128)(2,1)S(1)}, bf16[448,128]{1,0:T(8,128)(2,1)S(1)}, u32[]{:S(2)}, u32[]{:S(2)}) collective-permute-start(bf16[448,128]{1,0:T(8,128)(2,1)S(1)} %added.2.after_ref.refs_0_), channel_id=1, source_target_pairs={{0,3},{1,2},{2,1},{3,0},{4,7},{5,6},{6,5},{7,4},{8,11},{9,10},{10,... | collective-permute-start | bytes 344072 | tf_op jit(solution)/shard_map/ppermute | solution.py:27
  55.3 9.9 %collective-permute-start.14 = (bf16[448,128]{1,0:T(8,128)(2,1)S(1)}, bf16[448,128]{1,0:T(8,128)(2,1)S(1)}, u32[]{:S(2)}, u32[]{:S(2)}) collective-permute-start(bf16[448,128]{1,0:T(8,128)(2,1)S(1)} %added.2.after_ref.refs_0_), channel_id=1, source_target_pairs={{0,2},{1,3},{2,0},{3,1},{4,6},{5,7},{6,4},{7,5},{8,10},{9,11},{10,... | collective-permute-start | bytes 344072 | tf_op jit(solution)/shard_map/ppermute | solution.py:27
  55.3 9.9 %collective-permute-start.13 = (bf16[448,128]{1,0:T(8,128)(2,1)S(1)}, bf16[448,128]{1,0:T(8,128)(2,1)S(1)}, u32[]{:S(2)}, u32[]{:S(2)}) collective-permute-start(bf16[448,128]{1,0:T(8,128)(2,1)S(1)} %added.2.after_ref.refs_0_), channel_id=1, source_target_pairs={{0,1},{1,0},{2,3},{3,2},{4,5},{5,4},{6,7},{7,6},{8,9},{9,8},{10,11... | collective-permute-start | bytes 344072 | tf_op jit(solution)/shard_map/ppermute | solution.py:27
  65.3 6.6 %collective-permute-start.18 = (bf16[448,128]{1,0:T(8,128)(2,1)S(1)}, bf16[448,128]{1,0:T(8,128)(2,1)S(1)}, u32[]{:S(2)}, u32[]{:S(2)}) collective-permute-start(bf16[448,128]{1,0:T(8,128)(2,1)S(1)} %added.3.after_ref.refs_0_), channel_id=1, source_target_pairs={{0,24},{8,16},{16,8},{24,0},{1,25},{9,17},{17,9},{25,1},{2,26},{10... | collective-permute-start | bytes 344072 | tf_op jit(solution)/shard_map/ppermute | solution.py:27
  67.8 5.0 %collective-permute-start.17 = (bf16[448,128]{1,0:T(8,128)(2,1)S(1)}, bf16[448,128]{1,0:T(8,128)(2,1)S(1)}, u32[]{:S(2)}, u32[]{:S(2)}) collective-permute-start(bf16[448,128]{1,0:T(8,128)(2,1)S(1)} %added.3.after_ref.refs_0_), channel_id=1, source_target_pairs={{0,16},{8,24},{16,0},{24,8},{1,17},{9,25},{17,1},{25,9},{2,18},{10... | collective-permute-start | bytes 344072 | tf_op jit(solution)/shard_map/ppermute | solution.py:27
  68.3 4.8 %collective-permute-start.16 = (bf16[448,128]{1,0:T(8,128)(2,1)S(1)}, bf16[448,128]{1,0:T(8,128)(2,1)S(1)}, u32[]{:S(2)}, u32[]{:S(2)}) collective-permute-start(bf16[448,128]{1,0:T(8,128)(2,1)S(1)} %added.3.after_ref.refs_0_), channel_id=1, source_target_pairs={{0,8},{8,0},{16,24},{24,16},{1,9},{9,1},{17,25},{25,17},{2,10},{10... | collective-permute-start | bytes 344072 | tf_op jit(solution)/shard_map/ppermute | solution.py:27
  68.8 6.5 %collective-permute-start.19 = (bf16[448,128]{1,0:T(8,128)(2,1)S(1)}, bf16[448,128]{1,0:T(8,128)(2,1)S(1)}, u32[]{:S(2)}, u32[]{:S(2)}) collective-permute-start(bf16[448,128]{1,0:T(8,128)(2,1)S(1)} %added.3.after_ref.refs_0_), channel_id=1, source_target_pairs={{0,4},{4,0},{1,5},{5,1},{2,6},{6,2},{3,7},{7,3},{8,12},{12,8},{9,1... | collective-permute-start | bytes 344072 | tf_op jit(solution)/shard_map/ppermute | solution.py:27
  71.8 3.5 %collective-permute-start.22 = (bf16[448,128]{1,0:T(8,128)(2,1)S(1)}, bf16[448,128]{1,0:T(8,128)(2,1)S(1)}, u32[]{:S(2)}, u32[]{:S(2)}) collective-permute-start(bf16[448,128]{1,0:T(8,128)(2,1)S(1)} %collective-permute-done.18.refs_3_), channel_id=1, source_target_pairs={{0,4},{4,0},{1,5},{5,1},{2,6},{6,2},{3,7},{7,3},{8,12},{12,8},{9,1... | collective-permute-start | bytes 344072 | tf_op jit(solution)/shard_map/ppermute | solution.py:27
  72.8 2.5 %collective-permute-start.21 = (bf16[448,128]{1,0:T(8,128)(2,1)S(1)}, bf16[448,128]{1,0:T(8,128)(2,1)S(1)}, u32[]{:S(2)}, u32[]{:S(2)}) collective-permute-start(bf16[448,128]{1,0:T(8,128)(2,1)S(1)} %collective-permute-done.17.refs_2_), channel_id=1, source_target_pairs={{0,4},{4,0},{1,5},{5,1},{2,6},{6,2},{3,7},{7,3},{8,12},{12,8},{9,1... | collective-permute-start | bytes 344072 | tf_op jit(solution)/shard_map/ppermute | solution.py:27
  73.1 2.3 %collective-permute-start.20 = (bf16[448,128]{1,0:T(8,128)(2,1)S(1)}, bf16[448,128]{1,0:T(8,128)(2,1)S(1)}, u32[]{:S(2)}, u32[]{:S(2)}) collective-permute-start(bf16[448,128]{1,0:T(8,128)(2,1)S(1)} %collective-permute-done.16.refs_1_), channel_id=1, source_target_pairs={{0,4},{4,0},{1,5},{5,1},{2,6},{6,2},{3,7},{7,3},{8,12},{12,8},{9,1... | collective-permute-start | bytes 344072 | tf_op jit(solution)/shard_map/ppermute | solution.py:27

commit v8 on v7

--- a/solution.py
+++ b/solution.py
@@ -139,14 +139,26 @@
     bias_ref[...] = jnp.broadcast_to(total, bias_ref.shape)
 
 
-def activate_kernel(
-    parts_n, per, info_ref, video_ref, early_ref, near_ref, far_ref, near_early_ref, *refs
+def packed(value):
+    per = value.shape[0] - TILE
+    total = value[per : per + 1] + value[per + 1 : per + 2] + value[per + 2 : per + 3]
+    top = total.astype(BF16).astype(F32)
+    mid = (total - top).astype(BF16).astype(F32)
+    rest = total - top - mid
+    tail = jnp.concatenate([top, mid, rest, jnp.zeros((TILE - 3, value.shape[1]), F32)], axis=0)
+    return jnp.concatenate([value[:per].astype(BF16), tail.astype(BF16)], axis=0)
+
+
+def weights_kernel(
+    parts_n, per, info_ref, turned_ref, bias_ref, video_ref, early_ref, near_ref, far_ref, *refs
 ):
-    far_early_ref, gain_ref, shift_ref, *refs = refs
-    parts, out_ref, wide = refs[:parts_n], refs[parts_n], refs[parts_n + 1]
+    near_early_ref, far_early_ref, gain_ref, shift_ref, *refs = refs
+    parts, (act_ref, keep_ref, *send_refs) = refs[:parts_n], refs[parts_n:-3]
+    wide, acc, shards = refs[-3:]
     frames, rows, cols, chans = video_ref.shape[1:]
     before = early_ref.shape[1]
     step = cols // TILE
+    slots = wide.shape[0]
     inside, first, has_low, has_high = info_ref[0], info_ref[1], info_ref[2], info_ref[3]
     count, total, squares = merged([ref[...] for ref in parts])
     every = jnp.sum(count, axis=0, keepdims=True) * per
@@ -157,7 +169,6 @@
     odd = info_ref[6] == 1
     scale = 0.5 * lax.rsqrt(squares / every + 1e-05) * gain_ref[...]
     offset = 0.5 * shift_ref[...] - mean * scale
-    slots = wide.shape[0]
     wide[:, 0:8, :] = jnp.zeros((slots, 8, chans), F32)
     wide[:, 8 + cols : 16 + cols, :] = jnp.zeros((slots, 8, chans), F32)
 
@@ -165,51 +176,62 @@
         half = values.astype(F32) * (scale * keep) + offset * keep
         wide[slot, 8 : 8 + cols, :] = half + half * jnp.tanh(half)
         for r in range(-1, step + 1):
-            out_ref[f, y, r + 1] = wide[slot, pl.ds(8 + r, TILE, stride=step), :].astype(BF16)
-
-    for f in range(frames + before):
+            act_ref[f, y, r + 1] = wide[slot, pl.ds(8 + r, TILE, stride=step), :].astype(BF16)
+
+    def kept(f):
         local = f - before
-        ok = (local < inside) & (first + local >= 0)
-        keep = ok.astype(F32)
+        return ((local < inside) & (first + local >= 0)).astype(F32)
+
+    def inner(f, y, slot):
+        local = f - before
         source = early_ref.at[0, f] if local < 0 else video_ref.at[0, local]
-
-        def inner(y, carry, source=source, keep=keep, f=f):
-            row(source[y], keep, y % slots, f, y + 1)
-            return carry
-
-        lax.fori_loop(0, rows, inner, 0, unroll=4)
+        row(source[y], kept(f), slot, f, y + 1)
+
+    def border(f, side, slot):
+        local = f - before
         near = near_early_ref[frames + local] if local < 0 else near_ref[local]
         far = far_early_ref[frames + local] if local < 0 else far_ref[local]
         near, far = near.astype(F32), far.astype(F32)
-        low, high = jnp.where(odd, near, far), jnp.where(odd, far, near)
-        row(low, keep * has_low.astype(F32), 0, f, 0)
-        row(high, keep * has_high.astype(F32), 1, f, rows + 1)
-
-
-def packed(value):
-    per = value.shape[0] - TILE
-    total = value[per : per + 1] + value[per + 1 : per + 2] + value[per + 2 : per + 3]
-    top = total.astype(BF16).astype(F32)
-    mid = (total - top).astype(BF16).astype(F32)
-    rest = total - top - mid
-    tail = jnp.concatenate([top, mid, rest, jnp.zeros((TILE - 3, value.shape[1]), F32)], axis=0)
-    return jnp.concatenate([value[:per].astype(BF16), tail.astype(BF16)], axis=0)
-
-
-def weights_kernel(info_ref, turned_ref, act_ref, bias_ref, keep_ref, *refs):
-    send_refs, acc = refs[:-2], refs[-2:]
-    acc, shards = acc
-    frames, rows = turned_ref.shape[:2]
-    chans = turned_ref.shape[2]
-    k = turned_ref.shape[3]
-    step = act_ref.shape[2] - 2
+        if side:
+            value, has = jnp.where(odd, far, near), has_high
+        else:
+            value, has = jnp.where(odd, near, far), has_low
+        row(value, kept(f) * has.astype(F32), slot, f, side * (rows + 1))
+
+    for f in range(before + 1):
+
+        def many(y, carry, f=f):
+            inner(f, y, y % slots)
+            return carry
+
+        lax.fori_loop(0, rows, many, 0, unroll=4)
+        border(f, 0, 0)
+        border(f, 1, 1)
+
     taps = [(kt, ky, kx) for kt in range(3) for ky in range(3) for kx in range(3)]
     pair = 2
-
-    def frame(t, carry):
+    k = turned_ref.shape[3]
+    tms, dps, full = shards.shape[:3]
+    size = full - TILE
+
+    def place(tap):
+        block = acc[:, tap * chans : (tap + 1) * chans].T
+        done = 0
+        while done < chans:
+            shard, at = divmod(tap * chans + done, size)
+            take = min(chans - done, size - at)
+            shards[shard // dps, shard % dps, at : at + take, :] = block[done : done + take]
+            done += take
+
+    groups = [taps[j : j + pair] for j in range(0, len(taps), pair)]
+    for t in range(frames):
+        f = t + before + 1
+        work = []
+        if f < frames + before:
+            work = [functools.partial(border, f, side, side) for side in range(2)]
+            work += [functools.partial(inner, f, y, y % slots) for y in range(rows)]
         left = jnp.concatenate([turned_ref[t, y] for y in range(rows)], axis=1)
-        for j in range(0, len(taps), pair):
-            chosen = taps[j : j + pair]
+        for j, chosen in enumerate(groups):
             right = jnp.concatenate(
                 [
                     act_ref[t + kt, ky : ky + rows, kx : kx + step].reshape(rows * k, chans)
@@ -218,25 +240,17 @@
                 axis=1,
             )
             product = jnp.dot(left, right, preferred_element_type=F32)
-            where = slice(j * chans, (j + len(chosen)) * chans)
-            acc[:, where] = jnp.where(t == 0, product, acc[:, where] + product)
-        return carry
-
-    lax.fori_loop(0, frames, frame, 0)
-    tms, dps, per = shards.shape[:3]
-    per -= TILE
-    for tap in range(len(taps)):
-        block = acc[:, tap * chans : (tap + 1) * chans].T
-        done = 0
-        while done < chans:
-            shard, at = divmod(tap * chans + done, per)
-            take = min(chans - done, per - at)
-            shards[shard // dps, shard % dps, at : at + take, :] = block[done : done + take]
-            done += take
+            where = slice(j * pair * chans, (j * pair + len(chosen)) * chans)
+            acc[:, where] = product if t == 0 else acc[:, where] + product
+            for task in work[j * len(work) // len(groups) : (j + 1) * len(work) // len(groups)]:
+                task()
+            if t == frames - 1:
+                for n in range(len(chosen)):
+                    place(j * pair + n)
     tail = jnp.concatenate([bias_ref[0:1], jnp.zeros((TILE - 1, chans), F32)], axis=0)
     for i in range(tms):
         for j in range(dps):
-            shards[i, j, per : per + TILE, :] = tail
+            shards[i, j, size:full, :] = tail
     me = info_ref[4]
     keep_ref[...] = shards[me]
     for r in range(1, tms):
@@ -406,18 +420,30 @@
         name="cotangent",
     )(info, masked_in)
 
-    act = pl.pallas_call(
-        functools.partial(activate_kernel, spaces, per),
-        in_specs=[SMEM] + [VMEM] * (8 + spaces),
-        out_specs=VMEM,
-        out_shape=jax.ShapeDtypeStruct(
-            (frames + before, rows + 2, step + 2, TILE, chans), BF16
-        ),
-        scratch_shapes=[pltpu.VMEM((4, cols + 16, chans), F32)],
-        compiler_params=params(8),
-        name="activate",
+    count = kernel.shape[0] * kernel.shape[1] * kernel.shape[2] * chans
+    shards_n = tms * dps
+    assert count % shards_n == 0
+    shard = count // shards_n
+    full = shard + TILE
+    act, keep, *sends = pl.pallas_call(
+        functools.partial(weights_kernel, spaces, per),
+        in_specs=[SMEM] + [VMEM] * (10 + spaces),
+        out_specs=[VMEM] * (1 + tms),
+        out_shape=[
+            jax.ShapeDtypeStruct((frames + before, rows + 2, step + 2, TILE, chans), BF16)
+        ]
+        + [jax.ShapeDtypeStruct((dps, full, chans), F32)] * tms,
+        scratch_shapes=[
+            pltpu.VMEM((8, cols + 16, chans), F32),
+            pltpu.VMEM((chans, count), F32),
+            pltpu.VMEM((tms, dps, full, chans), F32),
+        ],
+        compiler_params=params(16),
+        name="weights",
     )(
         info,
+        turned,
+        bias,
         local,
         early,
         near,
@@ -428,24 +454,6 @@
         norm_shift.reshape(1, chans),
         *parts,
     )
-
-    count = kernel.shape[0] * kernel.shape[1] * kernel.shape[2] * chans
-    shards_n = tms * dps
-    assert count % shards_n == 0
-    shard = count // shards_n
-    full = shard + TILE
-    keep, *sends = pl.pallas_call(
-        weights_kernel,
-        in_specs=[SMEM, VMEM, VMEM, VMEM],
-        out_specs=[VMEM] * tms,
-        out_shape=[jax.ShapeDtypeStruct((dps, full, chans), F32)] * tms,
-        scratch_shapes=[
-            pltpu.VMEM((chans, count), F32),
-            pltpu.VMEM((tms, dps, full, chans), F32),
-        ],
-        compiler_params=params(16),
-        name="weights",
-    )(info, turned, act, bias)
 
     block = 4
     pieces = [(t0, y0) for t0 in range(0, frames, pair) for y0 in range(0, rows, block)]
@@ -501,10 +509,10 @@
         )(after, *arrays)
 
     incoming = [swap(send, "dp", r + 1) for r, send in enumerate(sends)]
-    token = cover(own, 3)
+    token = cover(own, 2)
     total = added(BF16, token, own, *incoming)
     others = [swap(total, "space", r) for r in range(1, spaces)]
-    token = cover(total, 3)
+    token = cover(total, 4)
     total = added(BF16, token, total, *others)
     mine = [total] + [swap(total, "dp", r) for r in range(1, dps)]
     cover(total, len(pieces))

time: 78.2 us -> 75.6 us (0.967)
  Pallas kernels: 40.5 us -> 38.2 us
    pallas_call x2 -> x1, Pallas kernels: 13.5 us -> 10.8 us  [step_of(): pl.pallas_call(functools.partial(weights_kernel, spaces, per), in_specs=[...]
  transfers between devices with their start and end apart: 23 -> 23, of which waited for: 6 -> 8; matrix products, arithmetic and copies ran while one was open for 0% -> 0% of each run, Pallas kernels for 27% -> 28%
where the time goes in v8:
time: 75.6 us; the launch traced here: 75.4 us
  Pallas kernels  38.2 us (51%)
  starting transfers between devices  24.5 us (32%)
  waiting for transfers between devices  10.6 us (14%)
  between operations  1.75 us (2%)
    ppermute x19, starting transfers between devices, swap(): return lax.ppermute(array, axis, [(i, i ^ by) for i in range(length)])  22.8 us
    pallas_call x8, Pallas kernels, cover(): pl.pallas_call(functools.partial(conv_kernel, pieces[n], where(n - 1) if...  16.7 us
    pallas_call x1, Pallas kernels, step_of(): pl.pallas_call(functools.partial(weights_kernel, spaces, per), in_specs=[...  10.8 us
    ppermute x19, waiting for transfers between devices, swap(): return lax.ppermute(array, axis, [(i, i ^ by) for i in range(length)])  10.6 us
    pallas_call x1, Pallas kernels, step_of(): pl.pallas_call(functools.partial(stats_kernel, before), in_specs=[SMEM, A...  2.89 us
    pallas_call x1, Pallas kernels, step_of(): pl.pallas_call(collect, in_specs=[SMEM] + [VMEM] * (len(order) + 1) + [AN...  2.54 us
    pallas_call x1, Pallas kernels, step_of(): pl.pallas_call(cotangent_kernel, in_specs=[SMEM, VMEM], out_specs=[VMEM,...  2.47 us
    pallas_call x1, Pallas kernels, step_of(): pl.pallas_call(ends_kernel, in_specs=[SMEM, ANY], out_specs=[VMEM, VMEM],...  1.53 us
  transfers between devices with their start and end apart: 23, of which 8 were waited for; matrix products, arithmetic and copies ran while one was open for 0% of the time, Pallas kernels for 28%

profile of v8, /device:TPU:0, one launch (start us, length us, event | category | flops | bytes accessed | tf_op | source)
XLA Modules:
  0.0 75.4 jit_solution(1463443620997053239)
XLA Ops:
  1.3 0.1 stack.39.info_ref
  1.4 2.9 %stats.1 = (f32[3,8,128]{2,1,0:T(8,128)S(1)}, bf16[1,4,16,128,128]{4,3,2,1,0:T(8,128)(2,1)S(1)}, bf16[1,4,16,128,128]{4,3,2,1,0:T(8,128)(2,1)S(1)}, bf16[1,2,16,128,128]{4,3,2,1,0:T(8,128)(2,1)S(1)}) custom-call(s32[7]{0:T(128)S(1)} %stack.39.info_ref, bf16[1,4,16,128,128]{4,3,2,1,0:T(8,128)(2,1)} %video_hbm.3, bf16[1,4,16,128,128]{4,3,2,1,0:T(8,128)(2,1)} %cot_hbm.1), custom_call_target="tpu_custom_call" | custom-call | tf_op jit(solution)/shard_map/stats/pallas_call | solution.py:370
  4.3 0.0 copy-start.3
  4.3 0.6 collective-permute-start
  4.9 1.5 %ends.1 = (bf16[4,128,128]{2,1,0:T(8,128)(2,1)S(1)}, bf16[4,128,128]{2,1,0:T(8,128)(2,1)S(1)}) custom-call(s32[7]{0:T(128)S(1)} %stack.39.info_ref, bf16[1,4,16,128,128]{4,3,2,1,0:T(8,128)(2,1)} %video_hbm.3), custom_call_target="tpu_custom_call" | custom-call | tf_op jit(solution)/shard_map/ends/pallas_call | solution.py:358
  6.4 2.6 %collective-permute-start.1 = (bf16[4,128,128]{2,1,0:T(8,128)(2,1)S(1)}, bf16[4,128,128]{2,1,0:T(8,128)(2,1)S(1)}, u32[]{:S(2)}, u32[]{:S(2)}) collective-permute-start(bf16[4,128,128]{2,1,0:T(8,128)(2,1)S(1)} %get-tuple-element.42), channel_id=1, source_target_pairs={{0,1},{1,0},{2,3},{3,2},{4,5},{5,4},{6,7},{7,6},{8,9},{9,8},{10,11... | collective-permute-start | bytes 393224 | tf_op jit(solution)/shard_map/ppermute | solution.py:27
  9.0 0.7 collective-permute-start.2
  9.7 3.5 %collective-permute-done.1.near_ref = bf16[4,128,128]{2,1,0:T(8,128)(2,1)S(1)} collective-permute-done((bf16[4,128,128]{2,1,0:T(8,128)(2,1)S(1)}, bf16[4,128,128]{2,1,0:T(8,128)(2,1)S(1)}, u32[]{:S(2)}, u32[]{:S(2)}) %collective-permute-start.1) | collective-permute-done | bytes 131104 | tf_op jit(solution)/shard_map/ppermute | solution.py:27
  13.2 0.5 collective-permute-start.4
  13.7 1.2 %collective-permute-done.5.refs_1_ = f32[3,8,128]{2,1,0:T(8,128)S(1)} collective-permute-done((f32[3,8,128]{2,1,0:T(8,128)S(1)}, f32[3,8,128]{2,1,0:T(8,128)S(1)}, u32[]{:S(2)}, u32[]{:S(2)}) %collective-permute-start.5) | collective-permute-done | bytes 12320 | tf_op jit(solution)/shard_map/ppermute | solution.py:27
  14.9 4.5 %collective-permute-start.6 = (f32[3,8,128]{2,1,0:T(8,128)S(1)}, f32[3,8,128]{2,1,0:T(8,128)S(1)}, u32[]{:S(2)}, u32[]{:S(2)}) collective-permute-start(f32[3,8,128]{2,1,0:T(8,128)S(1)} %merge.1.refs_4_.after_ref), channel_id=1, source_target_pairs={{0,1},{1,0},{2,3},{3,2},{4,5},{5,4},{6,7},{7,6},{8,9},{9,8},{10,11... | collective-permute-start | bytes 36872 | tf_op jit(solution)/shard_map/ppermute | solution.py:27
  19.4 1.2 %collective-permute-start.7 = (f32[3,8,128]{2,1,0:T(8,128)S(1)}, f32[3,8,128]{2,1,0:T(8,128)S(1)}, u32[]{:S(2)}, u32[]{:S(2)}) collective-permute-start(f32[3,8,128]{2,1,0:T(8,128)S(1)} %merge.1.refs_4_.after_ref), channel_id=1, source_target_pairs={{0,2},{1,3},{2,0},{3,1},{4,6},{5,7},{6,4},{7,5},{8,10},{9,11},{10,... | collective-permute-start | bytes 36872 | tf_op jit(solution)/shard_map/ppermute | solution.py:27
  20.6 0.4 collective-permute-done.6.refs_5_
  21.1 2.6 %collective-permute-start.8 = (f32[3,8,128]{2,1,0:T(8,128)S(1)}, f32[3,8,128]{2,1,0:T(8,128)S(1)}, u32[]{:S(2)}, u32[]{:S(2)}) collective-permute-start(f32[3,8,128]{2,1,0:T(8,128)S(1)} %merge.1.refs_4_.after_ref), channel_id=1, source_target_pairs={{0,3},{1,2},{2,1},{3,0},{4,7},{5,6},{6,5},{7,4},{8,11},{9,10},{10,... | collective-permute-start | bytes 36872 | tf_op jit(solution)/shard_map/ppermute | solution.py:27
  23.7 2.5 %cotangent.1 = (bf16[4,16,128,128]{3,2,1,0:T(8,128)(2,1)S(1)}, f32[8,128]{1,0:T(8,128)S(1)}) custom-call(s32[7]{0:T(128)S(1)} %stack.39.info_ref, bf16[1,4,16,128,128]{4,3,2,1,0:T(8,128)(2,1)S(1)} %get-tuple-element.37.cot_ref), custom_call_target="tpu_custom_call" | custom-call | tf_op jit(solution)/shard_map/cotangent/pallas_call | solution.py:410
  26.2 0.4 collective-permute-done.8.refs_7_
  26.6 0.0 copy-start
  26.6 10.8 %weights.1 = (bf16[6,18,10,16,128]{4,3,2,1,0:T(8,128)(2,1)S(1)}, f32[4,448,128]{2,1,0:T(8,128)S(1)}, f32[4,448,128]{2,1,0:T(8,128)S(1)}) custom-call(s32[7]{0:T(128)S(1)} %stack.39.info_ref, bf16[4,16,128,128]{3,2,1,0:T(8,128)(2,1)S(1)} %get-tuple-element.38.turned_ref, f32[8,128]{1,0:T(8,128)S(1)} %get-tuple-element.39.bias_ref, ...), custom_call_target="tpu_custom_call" | custom-call | tf_op jit(solution)/shard_map/weights/pallas_call | solution.py:428
  37.5 0.0 copy-start.1
  37.5 0.1 collective-permute-start.9
  37.6 0.4 taps.1.taps_ref
  37.9 0.2 copy-done.1
  38.1 2.0 %conv.8 = (bf16[2,4,128,128]{3,2,1,0:T(8,128)(2,1)S(1)}, bf16[1,4,16,128,128]{4,3,2,1,0:T(8,128)(2,1)}) custom-call(s32[7]{0:T(128)S(1)} %stack.39.info_ref, f32[4,448,128]{2,1,0:T(8,128)S(1)} %get-tuple-element.45.after_ref.keep_ref, bf16[6,18,10,16,128]{4,3,2,1,0:T(8,128)(2,1)S(1)} %get-tuple-element.46.act_ref, bf16[4608,256]{1,0:T(8,128)(2,1)S(1)} %taps.1.taps_ref, ...), custom_call_target="tpu_custom_call" | custom-call | tf_op jit(solution)/shard_map/conv/pallas_call | solution.py:472
  40.1 0.7 spread.1
  40.8 1.6 %collective-permute-start.10 = (bf16[448,128]{1,0:T(8,128)(2,1)S(1)}, bf16[448,128]{1,0:T(8,128)(2,1)S(1)}, u32[]{:S(2)}, u32[]{:S(2)}) collective-permute-start(bf16[448,128]{1,0:T(8,128)(2,1)S(1)} %get-tuple-element.54), channel_id=1, source_target_pairs={{0,8},{8,0},{16,24},{24,16},{1,9},{9,1},{17,25},{25,17},{2,10},{10... | collective-permute-start | bytes 344072 | tf_op jit(solution)/shard_map/ppermute | solution.py:27
  42.4 1.5 %collective-permute-start.11 = (bf16[448,128]{1,0:T(8,128)(2,1)S(1)}, bf16[448,128]{1,0:T(8,128)(2,1)S(1)}, u32[]{:S(2)}, u32[]{:S(2)}) collective-permute-start(bf16[448,128]{1,0:T(8,128)(2,1)S(1)} %get-tuple-element.55), channel_id=1, source_target_pairs={{0,16},{8,24},{16,0},{24,8},{1,17},{9,25},{17,1},{25,9},{2,18},{10... | collective-permute-start | bytes 344072 | tf_op jit(solution)/shard_map/ppermute | solution.py:27
  43.9 0.5 collective-permute-start.12
  44.4 2.5 %conv.9 = (bf16[2,4,128,128]{3,2,1,0:T(8,128)(2,1)S(1)}, bf16[1,4,16,128,128]{4,3,2,1,0:T(8,128)(2,1)}) custom-call(s32[7]{0:T(128)S(1)} %stack.39.info_ref, f32[448,128]{1,0:T(8,128)S(1)} %get-tuple-element.49.after_ref.refs_0_, bf16[6,18,10,16,128]{4,3,2,1,0:T(8,128)(2,1)S(1)} %get-tuple-element.46.act_ref, ...), custom_call_target="tpu_custom_call", output_to_operand_aliasing={{1}: (7, {})} | custom-call | tf_op jit(solution)/shard_map/conv/pallas_call | solution.py:472
  46.9 2.0 %conv.10 = (bf16[2,4,128,128]{3,2,1,0:T(8,128)(2,1)S(1)}, bf16[1,4,16,128,128]{4,3,2,1,0:T(8,128)(2,1)}) custom-call(s32[7]{0:T(128)S(1)} %stack.39.info_ref, bf16[2,4,128,128]{3,2,1,0:T(8,128)(2,1)S(1)} %get-tuple-element.51.after_ref.refs_0_, bf16[6,18,10,16,128]{4,3,2,1,0:T(8,128)(2,1)S(1)} %get-tuple-element.46.act_ref, ...), custom_call_target="tpu_custom_call", output_to_operand_aliasing={{1}: (7, {})} | custom-call | tf_op jit(solution)/shard_map/conv/pallas_call | solution.py:472
  48.9 1.0 %collective-permute-done.11.refs_2_ = bf16[448,128]{1,0:T(8,128)(2,1)S(1)} collective-permute-done((bf16[448,128]{1,0:T(8,128)(2,1)S(1)}, bf16[448,128]{1,0:T(8,128)(2,1)S(1)}, u32[]{:S(2)}, u32[]{:S(2)}) %collective-permute-start.11) | collective-permute-done | bytes 114720 | tf_op jit(solution)/shard_map/ppermute | solution.py:27
  50.0 0.1 added.2.after_ref.refs_0_
  50.0 0.8 %collective-permute-start.13 = (bf16[448,128]{1,0:T(8,128)(2,1)S(1)}, bf16[448,128]{1,0:T(8,128)(2,1)S(1)}, u32[]{:S(2)}, u32[]{:S(2)}) collective-permute-start(bf16[448,128]{1,0:T(8,128)(2,1)S(1)} %added.2.after_ref.refs_0_), channel_id=1, source_target_pairs={{0,1},{1,0},{2,3},{3,2},{4,5},{5,4},{6,7},{7,6},{8,9},{9,8},{10,11... | collective-permute-start | bytes 344072 | tf_op jit(solution)/shard_map/ppermute | solution.py:27
  50.9 2.4 %collective-permute-start.14 = (bf16[448,128]{1,0:T(8,128)(2,1)S(1)}, bf16[448,128]{1,0:T(8,128)(2,1)S(1)}, u32[]{:S(2)}, u32[]{:S(2)}) collective-permute-start(bf16[448,128]{1,0:T(8,128)(2,1)S(1)} %added.2.after_ref.refs_0_), channel_id=1, source_target_pairs={{0,2},{1,3},{2,0},{3,1},{4,6},{5,7},{6,4},{7,5},{8,10},{9,11},{10,... | collective-permute-start | bytes 344072 | tf_op jit(solution)/shard_map/ppermute | solution.py:27
  53.3 1.2 %collective-permute-start.15 = (bf16[448,128]{1,0:T(8,128)(2,1)S(1)}, bf16[448,128]{1,0:T(8,128)(2,1)S(1)}, u32[]{:S(2)}, u32[]{:S(2)}) collective-permute-start(bf16[448,128]{1,0:T(8,128)(2,1)S(1)} %added.2.after_ref.refs_0_), channel_id=1, source_target_pairs={{0,3},{1,2},{2,1},{3,0},{4,7},{5,6},{6,5},{7,4},{8,11},{9,10},{10,... | collective-permute-start | bytes 344072 | tf_op jit(solution)/shard_map/ppermute | solution.py:27
  54.5 2.2 %conv.11 = (bf16[2,4,128,128]{3,2,1,0:T(8,128)(2,1)S(1)}, bf16[1,4,16,128,128]{4,3,2,1,0:T(8,128)(2,1)}) custom-call(s32[7]{0:T(128)S(1)} %stack.39.info_ref, bf16[448,128]{1,0:T(8,128)(2,1)S(1)} %added.2.after_ref.refs_0_, bf16[6,18,10,16,128]{4,3,2,1,0:T(8,128)(2,1)S(1)} %get-tuple-element.46.act_ref, ...), custom_call_target="tpu_custom_call", output_to_operand_aliasing={{1}: (7, {})} | custom-call | tf_op jit(solution)/shard_map/conv/pallas_call | solution.py:472
  56.7 2.0 %conv.12 = (bf16[2,4,128,128]{3,2,1,0:T(8,128)(2,1)S(1)}, bf16[1,4,16,128,128]{4,3,2,1,0:T(8,128)(2,1)}) custom-call(s32[7]{0:T(128)S(1)} %stack.39.info_ref, bf16[2,4,128,128]{3,2,1,0:T(8,128)(2,1)S(1)} %get-tuple-element.58.after_ref.refs_0_, bf16[6,18,10,16,128]{4,3,2,1,0:T(8,128)(2,1)S(1)} %get-tuple-element.46.act_ref, ...), custom_call_target="tpu_custom_call", output_to_operand_aliasing={{1}: (7, {})} | custom-call | tf_op jit(solution)/shard_map/conv/pallas_call | solution.py:472
  58.7 2.0 %conv.13 = (bf16[2,4,128,128]{3,2,1,0:T(8,128)(2,1)S(1)}, bf16[1,4,16,128,128]{4,3,2,1,0:T(8,128)(2,1)}) custom-call(s32[7]{0:T(128)S(1)} %stack.39.info_ref, bf16[2,4,128,128]{3,2,1,0:T(8,128)(2,1)S(1)} %get-tuple-element.60.after_ref.refs_0_, bf16[6,18,10,16,128]{4,3,2,1,0:T(8,128)(2,1)S(1)} %get-tuple-element.46.act_ref, ...), custom_call_target="tpu_custom_call", output_to_operand_aliasing={{1}: (7, {})} | custom-call | tf_op jit(solution)/shard_map/conv/pallas_call | solution.py:472
  60.7 2.0 %conv.14 = (bf16[2,4,128,128]{3,2,1,0:T(8,128)(2,1)S(1)}, bf16[1,4,16,128,128]{4,3,2,1,0:T(8,128)(2,1)}) custom-call(s32[7]{0:T(128)S(1)} %stack.39.info_ref, bf16[2,4,128,128]{3,2,1,0:T(8,128)(2,1)S(1)} %get-tuple-element.62.after_ref.refs_0_, bf16[6,18,10,16,128]{4,3,2,1,0:T(8,128)(2,1)S(1)} %get-tuple-element.46.act_ref, ...), custom_call_target="tpu_custom_call", output_to_operand_aliasing={{1}: (7, {})} | custom-call | tf_op jit(solution)/shard_map/conv/pallas_call | solution.py:472
  62.8 0.1 added.3.after_ref.refs_0_
  62.8 1.3 %collective-permute-start.16 = (bf16[448,128]{1,0:T(8,128)(2,1)S(1)}, bf16[448,128]{1,0:T(8,128)(2,1)S(1)}, u32[]{:S(2)}, u32[]{:S(2)}) collective-permute-start(bf16[448,128]{1,0:T(8,128)(2,1)S(1)} %added.3.after_ref.refs_0_), channel_id=1, source_target_pairs={{0,8},{8,0},{16,24},{24,16},{1,9},{9,1},{17,25},{25,17},{2,10},{10... | collective-permute-start | bytes 344072 | tf_op jit(solution)/shard_map/ppermute | solution.py:27
  64.1 0.8 %collective-permute-start.17 = (bf16[448,128]{1,0:T(8,128)(2,1)S(1)}, bf16[448,128]{1,0:T(8,128)(2,1)S(1)}, u32[]{:S(2)}, u32[]{:S(2)}) collective-permute-start(bf16[448,128]{1,0:T(8,128)(2,1)S(1)} %added.3.after_ref.refs_0_), channel_id=1, source_target_pairs={{0,16},{8,24},{16,0},{24,8},{1,17},{9,25},{17,1},{25,9},{2,18},{10... | collective-permute-start | bytes 344072 | tf_op jit(solution)/shard_map/ppermute | solution.py:27
  64.9 1.4 %collective-permute-start.18 = (bf16[448,128]{1,0:T(8,128)(2,1)S(1)}, bf16[448,128]{1,0:T(8,128)(2,1)S(1)}, u32[]{:S(2)}, u32[]{:S(2)}) collective-permute-start(bf16[448,128]{1,0:T(8,128)(2,1)S(1)} %added.3.after_ref.refs_0_), channel_id=1, source_target_pairs={{0,24},{8,16},{16,8},{24,0},{1,25},{9,17},{17,9},{25,1},{2,26},{10... | collective-permute-start | bytes 344072 | tf_op jit(solution)/shard_map/ppermute | solution.py:27
  66.4 2.3 %collective-permute-done.16.refs_1_ = bf16[448,128]{1,0:T(8,128)(2,1)S(1)} collective-permute-done((bf16[448,128]{1,0:T(8,128)(2,1)S(1)}, bf16[448,128]{1,0:T(8,128)(2,1)S(1)}, u32[]{:S(2)}, u32[]{:S(2)}) %collective-permute-start.16) | collective-permute-done | bytes 114720 | tf_op jit(solution)/shard_map/ppermute | solution.py:27
  68.7 0.4 collective-permute-done.17.refs_2_
  69.1 0.1 collective-permute-start.21
  69.2 1.4 %collective-permute-done.18.refs_3_ = bf16[448,128]{1,0:T(8,128)(2,1)S(1)} collective-permute-done((bf16[448,128]{1,0:T(8,128)(2,1)S(1)}, bf16[448,128]{1,0:T(8,128)(2,1)S(1)}, u32[]{:S(2)}, u32[]{:S(2)}) %collective-permute-start.18) | collective-permute-done | bytes 114720 | tf_op jit(solution)/shard_map/ppermute | solution.py:27
  70.6 2.0 %conv.15 = (bf16[2,4,128,128]{3,2,1,0:T(8,128)(2,1)S(1)}, bf16[1,4,16,128,128]{4,3,2,1,0:T(8,128)(2,1)}) custom-call(s32[7]{0:T(128)S(1)} %stack.39.info_ref, bf16[448,128]{1,0:T(8,128)(2,1)S(1)} %added.3.after_ref.refs_0_, bf16[6,18,10,16,128]{4,3,2,1,0:T(8,128)(2,1)S(1)} %get-tuple-element.46.act_ref, ...), custom_call_target="tpu_custom_call", output_to_operand_aliasing={{1}: (7, {})} | custom-call | tf_op jit(solution)/shard_map/conv/pallas_call | solution.py:472
  72.7 2.5 %collect.1 = (f32[8,432,128]{2,1,0:T(8,128)}, f32[1,128]{1,0:T(1,128)}, bf16[1,4,16,128,128]{4,3,2,1,0:T(8,128)(2,1)}) custom-call(s32[7]{0:T(128)S(1)} %stack.39.info_ref, bf16[448,128]{1,0:T(8,128)(2,1)S(1)} %added.3.after_ref.refs_0_, bf16[448,128]{1,0:T(8,128)(2,1)S(1)} %collective-permute-done.16.refs_1_, ...), custom_call_target="tpu_custom_call", output_to_operand_aliasing={{2}: (10, {})} | custom-call | tf_op jit(solution)/shard_map/collect/pallas_call | solution.py:537
  (25 shorter events, 0.1 us)
Async XLA Ops:
  4.3 22.3 %copy-start.2 = (f32[128]{0:T(128)S(1)}, f32[128]{0:T(128)}, u32[]{:S(2)}) copy-start(f32[128]{0:T(128)} %param.9) | copy-start | bytes 1540
  4.3 22.3 %copy-start.3 = (f32[128]{0:T(128)S(1)}, f32[128]{0:T(128)}, u32[]{:S(2)}) copy-start(f32[128]{0:T(128)} %param.10) | copy-start | bytes 1540
  4.3 22.3 %collective-permute-start = (bf16[1,2,16,128,128]{4,3,2,1,0:T(8,128)(2,1)S(1)}, bf16[1,2,16,128,128]{4,3,2,1,0:T(8,128)(2,1)S(1)}, u32[]{:S(2)}, u32[]{:S(2)}) collective-permute-start(bf16[1,2,16,128,128]{4,3,2,1,0:T(8,128)(2,1)S(1)} %get-tuple-element.41), channel_id=1, source_target_pairs={{0,4},{4,0},{1,5},{5,1},{2,6},{6,2},{3,7},{7,3},{8,12},{12,8},{9,1... | collective-permute-start | bytes 3145736 | tf_op jit(solution)/shard_map/ppermute | solution.py:386
  6.4 6.8 %collective-permute-start.1 = (bf16[4,128,128]{2,1,0:T(8,128)(2,1)S(1)}, bf16[4,128,128]{2,1,0:T(8,128)(2,1)S(1)}, u32[]{:S(2)}, u32[]{:S(2)}) collective-permute-start(bf16[4,128,128]{2,1,0:T(8,128)(2,1)S(1)} %get-tuple-element.42), channel_id=1, source_target_pairs={{0,1},{1,0},{2,3},{3,2},{4,5},{5,4},{6,7},{7,6},{8,9},{9,8},{10,11... | collective-permute-start | bytes 393224 | tf_op jit(solution)/shard_map/ppermute | solution.py:27
  9.0 4.2 %collective-permute-start.2 = (bf16[4,128,128]{2,1,0:T(8,128)(2,1)S(1)}, bf16[4,128,128]{2,1,0:T(8,128)(2,1)S(1)}, u32[]{:S(2)}, u32[]{:S(2)}) collective-permute-start(bf16[4,128,128]{2,1,0:T(8,128)(2,1)S(1)} %get-tuple-element.43), channel_id=1, source_target_pairs={{1,2},{2,1},{5,6},{6,5},{9,10},{10,9},{13,14},{14,13},{17,18},{18,... | collective-permute-start | bytes 393224 | tf_op jit(solution)/shard_map/ppermute | solution.py:369
  13.2 13.4 %collective-permute-start.3 = (bf16[4,128,128]{2,1,0:T(8,128)(2,1)S(1)}, bf16[4,128,128]{2,1,0:T(8,128)(2,1)S(1)}, u32[]{:S(2)}, u32[]{:S(2)}) collective-permute-start(bf16[4,128,128]{2,1,0:T(8,128)(2,1)S(1)} %collective-permute-done.1.near_ref), channel_id=1, source_target_pairs={{0,4},{4,0},{1,5},{5,1},{2,6},{6,2},{3,7},{7,3},{8,12},{12,8},{9,1... | collective-permute-start | bytes 393224 | tf_op jit(solution)/shard_map/ppermute | solution.py:396
  13.2 13.4 %collective-permute-start.4 = (bf16[4,128,128]{2,1,0:T(8,128)(2,1)S(1)}, bf16[4,128,128]{2,1,0:T(8,128)(2,1)S(1)}, u32[]{:S(2)}, u32[]{:S(2)}) collective-permute-start(bf16[4,128,128]{2,1,0:T(8,128)(2,1)S(1)} %collective-permute-done.2.far_ref), channel_id=1, source_target_pairs={{0,4},{4,0},{1,5},{5,1},{2,6},{6,2},{3,7},{7,3},{8,12},{12,8},{9,1... | collective-permute-start | bytes 393224 | tf_op jit(solution)/shard_map/ppermute | solution.py:397
  13.7 1.2 %collective-permute-start.5 = (f32[3,8,128]{2,1,0:T(8,128)S(1)}, f32[3,8,128]{2,1,0:T(8,128)S(1)}, u32[]{:S(2)}, u32[]{:S(2)}) collective-permute-start(f32[3,8,128]{2,1,0:T(8,128)S(1)} %get-tuple-element.44.refs_0_), channel_id=1, source_target_pairs={{0,4},{4,0},{1,5},{5,1},{2,6},{6,2},{3,7},{7,3},{8,12},{12,8},{9,1... | collective-permute-start | bytes 36872 | tf_op jit(solution)/shard_map/ppermute | solution.py:27
  14.9 6.2 %collective-permute-start.6 = (f32[3,8,128]{2,1,0:T(8,128)S(1)}, f32[3,8,128]{2,1,0:T(8,128)S(1)}, u32[]{:S(2)}, u32[]{:S(2)}) collective-permute-start(f32[3,8,128]{2,1,0:T(8,128)S(1)} %merge.1.refs_4_.after_ref), channel_id=1, source_target_pairs={{0,1},{1,0},{2,3},{3,2},{4,5},{5,4},{6,7},{7,6},{8,9},{9,8},{10,11... | collective-permute-start | bytes 36872 | tf_op jit(solution)/shard_map/ppermute | solution.py:27
  19.4 6.8 %collective-permute-start.7 = (f32[3,8,128]{2,1,0:T(8,128)S(1)}, f32[3,8,128]{2,1,0:T(8,128)S(1)}, u32[]{:S(2)}, u32[]{:S(2)}) collective-permute-start(f32[3,8,128]{2,1,0:T(8,128)S(1)} %merge.1.refs_4_.after_ref), channel_id=1, source_target_pairs={{0,2},{1,3},{2,0},{3,1},{4,6},{5,7},{6,4},{7,5},{8,10},{9,11},{10,... | collective-permute-start | bytes 36872 | tf_op jit(solution)/shard_map/ppermute | solution.py:27
  21.1 5.5 %collective-permute-start.8 = (f32[3,8,128]{2,1,0:T(8,128)S(1)}, f32[3,8,128]{2,1,0:T(8,128)S(1)}, u32[]{:S(2)}, u32[]{:S(2)}) collective-permute-start(f32[3,8,128]{2,1,0:T(8,128)S(1)} %merge.1.refs_4_.after_ref), channel_id=1, source_target_pairs={{0,3},{1,2},{2,1},{3,0},{4,7},{5,6},{6,5},{7,4},{8,11},{9,10},{10,... | collective-permute-start | bytes 36872 | tf_op jit(solution)/shard_map/ppermute | solution.py:27
  26.6 11.0 %copy-start = (bf16[3,3,3,128,128]{4,3,2,1,0:T(8,128)(2,1)S(1)}, bf16[3,3,3,128,128]{4,3,2,1,0:T(8,128)(2,1)}, u32[]{:S(2)}) copy-start(bf16[3,3,3,128,128]{4,3,2,1,0:T(8,128)(2,1)} %kernel_ref.1) | copy-start | bytes 2654212
  37.5 0.7 copy-start.1
  37.5 2.6 %collective-permute-start.9 = (f32[4,448,128]{2,1,0:T(8,128)S(1)}, f32[4,448,128]{2,1,0:T(8,128)S(1)}, u32[]{:S(2)}, u32[]{:S(2)}) collective-permute-start(f32[4,448,128]{2,1,0:T(8,128)S(1)} %get-tuple-element.48), channel_id=1, source_target_pairs={{0,4},{4,0},{1,5},{5,1},{2,6},{6,2},{3,7},{7,3},{8,12},{12,8},{9,1... | collective-permute-start | bytes 2752520 | tf_op jit(solution)/shard_map/ppermute | solution.py:27
  40.8 8.1 %collective-permute-start.10 = (bf16[448,128]{1,0:T(8,128)(2,1)S(1)}, bf16[448,128]{1,0:T(8,128)(2,1)S(1)}, u32[]{:S(2)}, u32[]{:S(2)}) collective-permute-start(bf16[448,128]{1,0:T(8,128)(2,1)S(1)} %get-tuple-element.54), channel_id=1, source_target_pairs={{0,8},{8,0},{16,24},{24,16},{1,9},{9,1},{17,25},{25,17},{2,10},{10... | collective-permute-start | bytes 344072 | tf_op jit(solution)/shard_map/ppermute | solution.py:27
  42.4 7.5 %collective-permute-start.11 = (bf16[448,128]{1,0:T(8,128)(2,1)S(1)}, bf16[448,128]{1,0:T(8,128)(2,1)S(1)}, u32[]{:S(2)}, u32[]{:S(2)}) collective-permute-start(bf16[448,128]{1,0:T(8,128)(2,1)S(1)} %get-tuple-element.55), channel_id=1, source_target_pairs={{0,16},{8,24},{16,0},{24,8},{1,17},{9,25},{17,1},{25,9},{2,18},{10... | collective-permute-start | bytes 344072 | tf_op jit(solution)/shard_map/ppermute | solution.py:27
  43.9 6.0 %collective-permute-start.12 = (bf16[448,128]{1,0:T(8,128)(2,1)S(1)}, bf16[448,128]{1,0:T(8,128)(2,1)S(1)}, u32[]{:S(2)}, u32[]{:S(2)}) collective-permute-start(bf16[448,128]{1,0:T(8,128)(2,1)S(1)} %get-tuple-element.56), channel_id=1, source_target_pairs={{0,24},{8,16},{16,8},{24,0},{1,25},{9,17},{17,9},{25,1},{2,26},{10... | collective-permute-start | bytes 344072 | tf_op jit(solution)/shard_map/ppermute | solution.py:27
  50.0 12.7 %collective-permute-start.13 = (bf16[448,128]{1,0:T(8,128)(2,1)S(1)}, bf16[448,128]{1,0:T(8,128)(2,1)S(1)}, u32[]{:S(2)}, u32[]{:S(2)}) collective-permute-start(bf16[448,128]{1,0:T(8,128)(2,1)S(1)} %added.2.after_ref.refs_0_), channel_id=1, source_target_pairs={{0,1},{1,0},{2,3},{3,2},{4,5},{5,4},{6,7},{7,6},{8,9},{9,8},{10,11... | collective-permute-start | bytes 344072 | tf_op jit(solution)/shard_map/ppermute | solution.py:27
  50.9 11.9 %collective-permute-start.14 = (bf16[448,128]{1,0:T(8,128)(2,1)S(1)}, bf16[448,128]{1,0:T(8,128)(2,1)S(1)}, u32[]{:S(2)}, u32[]{:S(2)}) collective-permute-start(bf16[448,128]{1,0:T(8,128)(2,1)S(1)} %added.2.after_ref.refs_0_), channel_id=1, source_target_pairs={{0,2},{1,3},{2,0},{3,1},{4,6},{5,7},{6,4},{7,5},{8,10},{9,11},{10,... | collective-permute-start | bytes 344072 | tf_op jit(solution)/shard_map/ppermute | solution.py:27
  53.3 9.5 %collective-permute-start.15 = (bf16[448,128]{1,0:T(8,128)(2,1)S(1)}, bf16[448,128]{1,0:T(8,128)(2,1)S(1)}, u32[]{:S(2)}, u32[]{:S(2)}) collective-permute-start(bf16[448,128]{1,0:T(8,128)(2,1)S(1)} %added.2.after_ref.refs_0_), channel_id=1, source_target_pairs={{0,3},{1,2},{2,1},{3,0},{4,7},{5,6},{6,5},{7,4},{8,11},{9,10},{10,... | collective-permute-start | bytes 344072 | tf_op jit(solution)/shard_map/ppermute | solution.py:27
  62.8 5.9 %collective-permute-start.16 = (bf16[448,128]{1,0:T(8,128)(2,1)S(1)}, bf16[448,128]{1,0:T(8,128)(2,1)S(1)}, u32[]{:S(2)}, u32[]{:S(2)}) collective-permute-start(bf16[448,128]{1,0:T(8,128)(2,1)S(1)} %added.3.after_ref.refs_0_), channel_id=1, source_target_pairs={{0,8},{8,0},{16,24},{24,16},{1,9},{9,1},{17,25},{25,17},{2,10},{10... | collective-permute-start | bytes 344072 | tf_op jit(solution)/shard_map/ppermute | solution.py:27
  64.1 5.0 %collective-permute-start.17 = (bf16[448,128]{1,0:T(8,128)(2,1)S(1)}, bf16[448,128]{1,0:T(8,128)(2,1)S(1)}, u32[]{:S(2)}, u32[]{:S(2)}) collective-permute-start(bf16[448,128]{1,0:T(8,128)(2,1)S(1)} %added.3.after_ref.refs_0_), channel_id=1, source_target_pairs={{0,16},{8,24},{16,0},{24,8},{1,17},{9,25},{17,1},{25,9},{2,18},{10... | collective-permute-start | bytes 344072 | tf_op jit(solution)/shard_map/ppermute | solution.py:27
  64.9 5.7 %collective-permute-start.18 = (bf16[448,128]{1,0:T(8,128)(2,1)S(1)}, bf16[448,128]{1,0:T(8,128)(2,1)S(1)}, u32[]{:S(2)}, u32[]{:S(2)}) collective-permute-start(bf16[448,128]{1,0:T(8,128)(2,1)S(1)} %added.3.after_ref.refs_0_), channel_id=1, source_target_pairs={{0,24},{8,16},{16,8},{24,0},{1,25},{9,17},{17,9},{25,1},{2,26},{10... | collective-permute-start | bytes 344072 | tf_op jit(solution)/shard_map/ppermute | solution.py:27
  66.4 6.3 %collective-permute-start.19 = (bf16[448,128]{1,0:T(8,128)(2,1)S(1)}, bf16[448,128]{1,0:T(8,128)(2,1)S(1)}, u32[]{:S(2)}, u32[]{:S(2)}) collective-permute-start(bf16[448,128]{1,0:T(8,128)(2,1)S(1)} %added.3.after_ref.refs_0_), channel_id=1, source_target_pairs={{0,4},{4,0},{1,5},{5,1},{2,6},{6,2},{3,7},{7,3},{8,12},{12,8},{9,1... | collective-permute-start | bytes 344072 | tf_op jit(solution)/shard_map/ppermute | solution.py:27
  68.7 4.0 %collective-permute-start.20 = (bf16[448,128]{1,0:T(8,128)(2,1)S(1)}, bf16[448,128]{1,0:T(8,128)(2,1)S(1)}, u32[]{:S(2)}, u32[]{:S(2)}) collective-permute-start(bf16[448,128]{1,0:T(8,128)(2,1)S(1)} %collective-permute-done.16.refs_1_), channel_id=1, source_target_pairs={{0,4},{4,0},{1,5},{5,1},{2,6},{6,2},{3,7},{7,3},{8,12},{12,8},{9,1... | collective-permute-start | bytes 344072 | tf_op jit(solution)/shard_map/ppermute | solution.py:27
  69.1 3.6 %collective-permute-start.21 = (bf16[448,128]{1,0:T(8,128)(2,1)S(1)}, bf16[448,128]{1,0:T(8,128)(2,1)S(1)}, u32[]{:S(2)}, u32[]{:S(2)}) collective-permute-start(bf16[448,128]{1,0:T(8,128)(2,1)S(1)} %collective-permute-done.17.refs_2_), channel_id=1, source_target_pairs={{0,4},{4,0},{1,5},{5,1},{2,6},{6,2},{3,7},{7,3},{8,12},{12,8},{9,1... | collective-permute-start | bytes 344072 | tf_op jit(solution)/shard_map/ppermute | solution.py:27
  70.6 2.0 %collective-permute-start.22 = (bf16[448,128]{1,0:T(8,128)(2,1)S(1)}, bf16[448,128]{1,0:T(8,128)(2,1)S(1)}, u32[]{:S(2)}, u32[]{:S(2)}) collective-permute-start(bf16[448,128]{1,0:T(8,128)(2,1)S(1)} %collective-permute-done.18.refs_3_), channel_id=1, source_target_pairs={{0,4},{4,0},{1,5},{5,1},{2,6},{6,2},{3,7},{7,3},{8,12},{12,8},{9,1... | collective-permute-start | bytes 344072 | tf_op jit(solution)/shard_map/ppermute | solution.py:27

commit v9 on v8

--- a/solution.py
+++ b/solution.py
@@ -117,11 +117,11 @@
 
 
 def cotangent_kernel(info_ref, cot_ref, turned_ref, bias_ref, wide):
-    frames, rows, cols, chans = cot_ref.shape[1:]
+    rows, cols, chans = cot_ref.shape[2:]
     step = cols // TILE
     lanes = 4
     bias = jnp.zeros((lanes, 8, chans), F32)
-    for t in range(frames):
+    for t in range(turned_ref.shape[0]):
         keep = (t < info_ref[0]).astype(F32)
 
         def row(y, acc, t=t, keep=keep):
@@ -135,8 +135,7 @@
             return acc + jnp.sum(value.reshape(cols // (8 * lanes), lanes, 8, chans), axis=0)
 
         bias = lax.fori_loop(0, rows, row, bias, unroll=8)
-    total = jnp.sum(jnp.sum(bias, axis=0), axis=0, keepdims=True)
-    bias_ref[...] = jnp.broadcast_to(total, bias_ref.shape)
+    bias_ref[...] = jnp.sum(bias, axis=0)
 
 
 def packed(value):
@@ -150,11 +149,13 @@
 
 
 def weights_kernel(
-    parts_n, per, info_ref, turned_ref, bias_ref, video_ref, early_ref, near_ref, far_ref, *refs
+    parts_n, per, info_ref, turned_ref, bias_ref, cot_ref, video_ref, early_ref, near_ref, *refs
 ):
-    near_early_ref, far_early_ref, gain_ref, shift_ref, *refs = refs
-    parts, (act_ref, keep_ref, *send_refs) = refs[:parts_n], refs[parts_n:-3]
-    wide, acc, shards = refs[-3:]
+    far_ref, near_early_ref, far_early_ref, gain_ref, shift_ref, *refs = refs
+    parts, (act_ref, keep_ref, *send_refs) = refs[:parts_n], refs[parts_n:-6]
+    wide, acc, shards, late, plain, bias_acc = refs[-6:]
+    ahead = turned_ref.shape[0]
+    bias_acc[...] = bias_ref[...]
     frames, rows, cols, chans = video_ref.shape[1:]
     before = early_ref.shape[1]
     step = cols // TILE
@@ -198,15 +199,26 @@
             value, has = jnp.where(odd, near, far), has_low
         row(value, kept(f) * has.astype(F32), slot, f, side * (rows + 1))
 
-    for f in range(before + 1):
-
-        def many(y, carry, f=f):
-            inner(f, y, y % slots)
-            return carry
-
-        lax.fori_loop(0, rows, many, 0, unroll=4)
-        border(f, 0, 0)
-        border(f, 1, 1)
+    def turn(t, y, slot):
+        value = cot_ref[0, t, y].astype(F32) * (t < inside).astype(F32)
+        plain[slot] = value
+        order = jnp.concatenate(
+            [plain[slot, pl.ds(r, TILE, stride=step), :] for r in range(step)], axis=0
+        )
+        late[t - ahead, y] = order.astype(BF16).T
+        bias_acc[...] += jnp.sum(value.reshape(cols // 8, 8, chans), axis=0)
+
+    def all_rows(f):
+        work = [functools.partial(border, f, side, side) for side in range(2)]
+        return work + [functools.partial(inner, f, y, y % slots) for y in range(rows)]
+
+    def many(y, carry):
+        inner(0, y, y % slots)
+        return carry
+
+    lax.fori_loop(0, rows, many, 0, unroll=4)
+    border(0, 0, 0)
+    border(0, 1, 1)
 
     taps = [(kt, ky, kx) for kt in range(3) for ky in range(3) for kx in range(3)]
     pair = 2
@@ -225,12 +237,25 @@
 
     groups = [taps[j : j + pair] for j in range(0, len(taps), pair)]
     for t in range(frames):
-        f = t + before + 1
         work = []
-        if f < frames + before:
-            work = [functools.partial(border, f, side, side) for side in range(2)]
-            work += [functools.partial(inner, f, y, y % slots) for y in range(rows)]
-        left = jnp.concatenate([turned_ref[t, y] for y in range(rows)], axis=1)
+        if t == 0:
+            for f in range(1, before + 1):
+                work.append((f * 9 // pair, all_rows(f)))
+        if t + before + 1 < frames + before:
+            tasks = all_rows(t + before + 1)
+            if ahead <= t + 1 < frames:
+                tasks += [
+                    functools.partial(turn, t + 1, y, y % plain.shape[0]) for y in range(rows)
+                ]
+            work.append((len(groups), tasks))
+        slots_of = [[] for _ in groups]
+        begin = 0
+        for end, tasks in work:
+            for n, task in enumerate(tasks):
+                slots_of[begin + n * (end - begin) // len(tasks)].append(task)
+            begin = end
+        source = turned_ref.at[t] if t < ahead else late.at[t - ahead]
+        left = jnp.concatenate([source[y] for y in range(rows)], axis=1)
         for j, chosen in enumerate(groups):
             right = jnp.concatenate(
                 [
@@ -242,12 +267,13 @@
             product = jnp.dot(left, right, preferred_element_type=F32)
             where = slice(j * pair * chans, (j * pair + len(chosen)) * chans)
             acc[:, where] = product if t == 0 else acc[:, where] + product
-            for task in work[j * len(work) // len(groups) : (j + 1) * len(work) // len(groups)]:
+            for task in slots_of[j]:
                 task()
             if t == frames - 1:
                 for n in range(len(chosen)):
                     place(j * pair + n)
-    tail = jnp.concatenate([bias_ref[0:1], jnp.zeros((TILE - 1, chans), F32)], axis=0)
+    bias = jnp.sum(bias_acc[...], axis=0, keepdims=True)
+    tail = jnp.concatenate([bias, jnp.zeros((TILE - 1, chans), F32)], axis=0)
     for i in range(tms):
         for j in range(dps):
             shards[i, j, size:full, :] = tail
@@ -407,12 +433,13 @@
         name="taps",
     )(stats, kernel)
 
+    ahead = frames // 2
     turned, bias = pl.pallas_call(
         cotangent_kernel,
         in_specs=[SMEM, VMEM],
         out_specs=[VMEM, VMEM],
         out_shape=[
-            jax.ShapeDtypeStruct((frames, rows, chans, cols), BF16),
+            jax.ShapeDtypeStruct((ahead, rows, chans, cols), BF16),
             jax.ShapeDtypeStruct((8, chans), F32),
         ],
         scratch_shapes=[pltpu.VMEM((8, cols, chans), F32)],
@@ -427,7 +454,7 @@
     full = shard + TILE
     act, keep, *sends = pl.pallas_call(
         functools.partial(weights_kernel, spaces, per),
-        in_specs=[SMEM] + [VMEM] * (10 + spaces),
+        in_specs=[SMEM] + [VMEM] * (11 + spaces),
         out_specs=[VMEM] * (1 + tms),
         out_shape=[
             jax.ShapeDtypeStruct((frames + before, rows + 2, step + 2, TILE, chans), BF16)
@@ -437,6 +464,9 @@
             pltpu.VMEM((8, cols + 16, chans), F32),
             pltpu.VMEM((chans, count), F32),
             pltpu.VMEM((tms, dps, full, chans), F32),
+            pltpu.VMEM((frames - ahead, rows, chans, cols), BF16),
+            pltpu.VMEM((8, cols, chans), F32),
+            pltpu.VMEM((8, chans), F32),
         ],
         compiler_params=params(16),
         name="weights",
@@ -444,6 +474,7 @@
         info,
         turned,
         bias,
+        masked_in,
         local,
         early,
         near,
@@ -486,6 +517,12 @@
             after = piece
         return after
 
+    def exchanged(arrays, axis):
+        result = []
+        for n, array in enumerate(arrays):
+            result.append(swap(array, axis, n + 1))
+        return result
+
     incoming = [swap(send, "tm", r + 1) for r, send in enumerate(sends)]
     token = cover(keep, 1)
     own, *sends = pl.pallas_call(
@@ -508,46 +545,67 @@
             name="added",
         )(after, *arrays)
 
-    incoming = [swap(send, "dp", r + 1) for r, send in enumerate(sends)]
+    incoming = exchanged(sends, "dp")
     token = cover(own, 2)
     total = added(BF16, token, own, *incoming)
-    others = [swap(total, "space", r) for r in range(1, spaces)]
+    others = exchanged([total] * (spaces - 1), "space")
     token = cover(total, 4)
     total = added(BF16, token, total, *others)
-    mine = [total] + [swap(total, "dp", r) for r in range(1, dps)]
+    mine = [total] + exchanged([total] * (dps - 1), "dp")
     cover(total, len(pieces))
     shards = {(0, r): array for r, array in enumerate(mine)}
     for q in range(1, tms):
         for r, array in enumerate(mine):
             shards[q, r] = swap(array, "tm", q)
-    order = list(shards)
-
-    def collect(info_ref, *refs):
-        shard_refs, piece_ref = refs[: len(order)], refs[len(order)]
-        out_ref, sum_ref, whole_ref, sem = refs[-4:]
-        copy = pltpu.make_async_copy(piece_ref, whole_ref.at[where(len(pieces) - 1)], sem)
-        copy.start()
-        for (q, r), ref in zip(order, shard_refs):
+    final = 1 % dps
+    late = [key for key in shards if key[1] == final]
+    order = [key for key in shards if key[1] != final]
+
+    def collect(keys, info_ref, *refs):
+        shard_refs, out_ref = refs[: len(keys)], refs[-3]
+        wide, sems = refs[-2:]
+        copies = []
+        if keys is order:
+            target = refs[-4].at[where(len(pieces) - 1)]
+            copies.append(pltpu.make_async_copy(refs[len(keys)], target, sems.at[len(keys)]))
+            copies[-1].start()
+            tail = shard_refs[0][shard : shard + TILE, :].astype(F32)
+            refs[-5][...] = tail[0:1] + tail[1:2] + tail[2:3]
+        for n, ((q, r), ref) in enumerate(zip(keys, shard_refs)):
             at = (info_ref[4] ^ q) * dps + (info_ref[5] ^ r)
-            out_ref[at] = ref[0:shard, :].astype(F32)
-        tail = shard_refs[0][shard : shard + TILE, :].astype(F32)
-        sum_ref[...] = tail[0:1] + tail[1:2] + tail[2:3]
-        copy.wait()
-
-    grad_kernel, grad_bias, output = pl.pallas_call(
-        collect,
+            wide[n] = ref[0:shard, :].astype(F32)
+            copies.append(pltpu.make_async_copy(wide.at[n], out_ref.at[at], sems.at[n]))
+            copies[-1].start()
+        for copy in copies:
+            copy.wait()
+
+    gradient = jax.ShapeDtypeStruct((shards_n, shard, chans), F32)
+    grad_bias, output, grad_kernel = pl.pallas_call(
+        functools.partial(collect, order),
         in_specs=[SMEM] + [VMEM] * (len(order) + 1) + [ANY],
-        out_specs=[VMEM, VMEM, ANY],
-        out_shape=[
-            jax.ShapeDtypeStruct((shards_n, shard, chans), F32),
-            jax.ShapeDtypeStruct((1, chans), F32),
-            whole,
+        out_specs=[VMEM, ANY, ANY],
+        out_shape=[jax.ShapeDtypeStruct((1, chans), F32), whole, gradient],
+        scratch_shapes=[
+            pltpu.VMEM((len(order), shard, chans), F32),
+            pltpu.SemaphoreType.DMA((len(order) + 1,)),
         ],
-        scratch_shapes=[pltpu.SemaphoreType.DMA],
-        input_output_aliases={len(order) + 2: 2},
-        compiler_params=params(4),
-        name="collect",
+        input_output_aliases={len(order) + 2: 1},
+        compiler_params=params(8),
+        name="collect_most",
     )(info, *[shards[key] for key in order], *done[-1])
+    grad_kernel = pl.pallas_call(
+        functools.partial(collect, late),
+        in_specs=[SMEM] + [VMEM] * len(late) + [ANY],
+        out_specs=ANY,
+        out_shape=gradient,
+        scratch_shapes=[
+            pltpu.VMEM((len(late), shard, chans), F32),
+            pltpu.SemaphoreType.DMA((len(late),)),
+        ],
+        input_output_aliases={len(late) + 1: 0},
+        compiler_params=params(8),
+        name="collect_rest",
+    )(info, *[shards[key] for key in late], grad_kernel)
 
     return output, grad_kernel.reshape(kernel.shape), grad_bias.reshape(chans)
 

time: 75.6 us -> 75.8 us (level)
    pallas_call x1 -> x2, Pallas kernels: 2.54 us -> 3.59 us  [the longest x1 2.25 us: step_of(): pl.pallas_call(functools.partial(collect, order), in_specs=[SMEM] + [VMEM...]
    pallas_call x1, Pallas kernels: 2.47 us -> 1.51 us  [step_of(): pl.pallas_call(cotangent_kernel, in_specs=[SMEM, VMEM], out_specs=[VMEM,...]
  transfers between devices with their start and end apart: 23 -> 23, of which waited for: 8 -> 8; matrix products, arithmetic and copies ran while one was open for 0% -> 0% of each run, Pallas kernels for 28% -> 30%
where the time goes in v9:
time: 75.8 us; the launch traced here: 75.6 us
  Pallas kernels  38.3 us (51%)
  starting transfers between devices  24.2 us (32%)
  waiting for transfers between devices  11 us (15%)
  between operations  1.74 us (2%)
    ppermute x19, starting transfers between devices, swap(): return lax.ppermute(array, axis, [(i, i ^ by) for i in range(length)])  22.5 us
    pallas_call x8, Pallas kernels, cover(): pl.pallas_call(functools.partial(conv_kernel, pieces[n], where(n - 1) if...  16.7 us
    ppermute x19, waiting for transfers between devices, swap(): return lax.ppermute(array, axis, [(i, i ^ by) for i in range(length)])  11 us
    pallas_call x1, Pallas kernels, step_of(): pl.pallas_call(functools.partial(weights_kernel, spaces, per), in_specs=[...  10.9 us
    pallas_call x1, Pallas kernels, step_of(): pl.pallas_call(functools.partial(stats_kernel, before), in_specs=[SMEM, A...  2.89 us
    pallas_call x1, Pallas kernels, step_of(): pl.pallas_call(functools.partial(collect, order), in_specs=[SMEM] + [VMEM...  2.25 us
    pallas_call x1, Pallas kernels, step_of(): pl.pallas_call(ends_kernel, in_specs=[SMEM, ANY], out_specs=[VMEM, VMEM],...  1.53 us
  transfers between devices with their start and end apart: 23, of which 8 were waited for; matrix products, arithmetic and copies ran while one was open for 0% of the time, Pallas kernels for 30%

profile of v9, /device:TPU:0, one launch (start us, length us, event | category | flops | bytes accessed | tf_op | source)
XLA Modules:
  0.0 75.6 jit_solution(17962238593173916321)
XLA Ops:
  1.3 0.1 stack.39.info_ref
  1.4 2.9 %stats.1 = (f32[3,8,128]{2,1,0:T(8,128)S(1)}, bf16[1,4,16,128,128]{4,3,2,1,0:T(8,128)(2,1)S(1)}, bf16[1,4,16,128,128]{4,3,2,1,0:T(8,128)(2,1)S(1)}, bf16[1,2,16,128,128]{4,3,2,1,0:T(8,128)(2,1)S(1)}) custom-call(s32[7]{0:T(128)S(1)} %stack.39.info_ref, bf16[1,4,16,128,128]{4,3,2,1,0:T(8,128)(2,1)} %video_hbm.3, bf16[1,4,16,128,128]{4,3,2,1,0:T(8,128)(2,1)} %cot_hbm.1), custom_call_target="tpu_custom_call" | custom-call | tf_op jit(solution)/shard_map/stats/pallas_call | solution.py:396
  4.3 0.0 copy-start.3
  4.3 0.6 collective-permute-start
  4.9 1.5 %ends.1 = (bf16[4,128,128]{2,1,0:T(8,128)(2,1)S(1)}, bf16[4,128,128]{2,1,0:T(8,128)(2,1)S(1)}) custom-call(s32[7]{0:T(128)S(1)} %stack.39.info_ref, bf16[1,4,16,128,128]{4,3,2,1,0:T(8,128)(2,1)} %video_hbm.3), custom_call_target="tpu_custom_call" | custom-call | tf_op jit(solution)/shard_map/ends/pallas_call | solution.py:384
  6.4 2.6 %collective-permute-start.1 = (bf16[4,128,128]{2,1,0:T(8,128)(2,1)S(1)}, bf16[4,128,128]{2,1,0:T(8,128)(2,1)S(1)}, u32[]{:S(2)}, u32[]{:S(2)}) collective-permute-start(bf16[4,128,128]{2,1,0:T(8,128)(2,1)S(1)} %get-tuple-element.42), channel_id=1, source_target_pairs={{0,1},{1,0},{2,3},{3,2},{4,5},{5,4},{6,7},{7,6},{8,9},{9,8},{10,11... | collective-permute-start | bytes 393224 | tf_op jit(solution)/shard_map/ppermute | solution.py:27
  9.0 0.7 collective-permute-start.2
  9.7 3.5 %collective-permute-done.1.near_ref = bf16[4,128,128]{2,1,0:T(8,128)(2,1)S(1)} collective-permute-done((bf16[4,128,128]{2,1,0:T(8,128)(2,1)S(1)}, bf16[4,128,128]{2,1,0:T(8,128)(2,1)S(1)}, u32[]{:S(2)}, u32[]{:S(2)}) %collective-permute-start.1) | collective-permute-done | bytes 131104 | tf_op jit(solution)/shard_map/ppermute | solution.py:27
  13.2 0.5 collective-permute-start.4
  13.7 1.2 %collective-permute-done.5.refs_1_ = f32[3,8,128]{2,1,0:T(8,128)S(1)} collective-permute-done((f32[3,8,128]{2,1,0:T(8,128)S(1)}, f32[3,8,128]{2,1,0:T(8,128)S(1)}, u32[]{:S(2)}, u32[]{:S(2)}) %collective-permute-start.5) | collective-permute-done | bytes 12320 | tf_op jit(solution)/shard_map/ppermute | solution.py:27
  14.9 3.8 %collective-permute-start.8 = (f32[3,8,128]{2,1,0:T(8,128)S(1)}, f32[3,8,128]{2,1,0:T(8,128)S(1)}, u32[]{:S(2)}, u32[]{:S(2)}) collective-permute-start(f32[3,8,128]{2,1,0:T(8,128)S(1)} %merge.1.refs_5_.after_ref), channel_id=1, source_target_pairs={{0,3},{1,2},{2,1},{3,0},{4,7},{5,6},{6,5},{7,4},{8,11},{9,10},{10,... | collective-permute-start | bytes 36872 | tf_op jit(solution)/shard_map/ppermute | solution.py:27
  18.7 2.1 %collective-permute-start.7 = (f32[3,8,128]{2,1,0:T(8,128)S(1)}, f32[3,8,128]{2,1,0:T(8,128)S(1)}, u32[]{:S(2)}, u32[]{:S(2)}) collective-permute-start(f32[3,8,128]{2,1,0:T(8,128)S(1)} %merge.1.refs_5_.after_ref), channel_id=1, source_target_pairs={{0,2},{1,3},{2,0},{3,1},{4,6},{5,7},{6,4},{7,5},{8,10},{9,11},{10,... | collective-permute-start | bytes 36872 | tf_op jit(solution)/shard_map/ppermute | solution.py:27
  20.9 2.2 %collective-permute-start.6 = (f32[3,8,128]{2,1,0:T(8,128)S(1)}, f32[3,8,128]{2,1,0:T(8,128)S(1)}, u32[]{:S(2)}, u32[]{:S(2)}) collective-permute-start(f32[3,8,128]{2,1,0:T(8,128)S(1)} %merge.1.refs_5_.after_ref), channel_id=1, source_target_pairs={{0,1},{1,0},{2,3},{3,2},{4,5},{5,4},{6,7},{7,6},{8,9},{9,8},{10,11... | collective-permute-start | bytes 36872 | tf_op jit(solution)/shard_map/ppermute | solution.py:27
  23.1 1.5 %cotangent.1 = (bf16[2,16,128,128]{3,2,1,0:T(8,128)(2,1)S(1)}, f32[8,128]{1,0:T(8,128)S(1)}) custom-call(s32[7]{0:T(128)S(1)} %stack.39.info_ref, bf16[1,4,16,128,128]{4,3,2,1,0:T(8,128)(2,1)S(1)} %get-tuple-element.37.cot_ref), custom_call_target="tpu_custom_call" | custom-call | tf_op jit(solution)/shard_map/cotangent/pallas_call | solution.py:437
  24.6 0.1 collective-permute-done.6.refs_6_
  24.8 0.0 copy-start
  24.8 10.9 %weights.1 = (bf16[6,18,10,16,128]{4,3,2,1,0:T(8,128)(2,1)S(1)}, f32[4,448,128]{2,1,0:T(8,128)S(1)}, f32[4,448,128]{2,1,0:T(8,128)S(1)}) custom-call(s32[7]{0:T(128)S(1)} %stack.39.info_ref, bf16[2,16,128,128]{3,2,1,0:T(8,128)(2,1)S(1)} %get-tuple-element.38.turned_ref, f32[8,128]{1,0:T(8,128)S(1)} %get-tuple-element.39.bias_ref, ...), custom_call_target="tpu_custom_call" | custom-call | tf_op jit(solution)/shard_map/weights/pallas_call | solution.py:455
  35.7 0.0 copy-start.1
  35.7 0.1 collective-permute-start.9
  35.8 0.4 taps.1.taps_ref
  36.2 0.2 copy-done.1
  36.4 2.0 %conv.8 = (bf16[2,4,128,128]{3,2,1,0:T(8,128)(2,1)S(1)}, bf16[1,4,16,128,128]{4,3,2,1,0:T(8,128)(2,1)}) custom-call(s32[7]{0:T(128)S(1)} %stack.39.info_ref, f32[4,448,128]{2,1,0:T(8,128)S(1)} %get-tuple-element.45.after_ref.keep_ref, bf16[6,18,10,16,128]{4,3,2,1,0:T(8,128)(2,1)S(1)} %get-tuple-element.46.act_ref, bf16[4608,256]{1,0:T(8,128)(2,1)S(1)} %taps.1.taps_ref, ...), custom_call_target="tpu_custom_call" | custom-call | tf_op jit(solution)/shard_map/conv/pallas_call | solution.py:503
  38.4 0.7 spread.1
  39.1 1.6 %collective-permute-start.10 = (bf16[448,128]{1,0:T(8,128)(2,1)S(1)}, bf16[448,128]{1,0:T(8,128)(2,1)S(1)}, u32[]{:S(2)}, u32[]{:S(2)}) collective-permute-start(bf16[448,128]{1,0:T(8,128)(2,1)S(1)} %get-tuple-element.54), channel_id=1, source_target_pairs={{0,8},{8,0},{16,24},{24,16},{1,9},{9,1},{17,25},{25,17},{2,10},{10... | collective-permute-start | bytes 344072 | tf_op jit(solution)/shard_map/ppermute | solution.py:27
  40.7 1.5 %collective-permute-start.11 = (bf16[448,128]{1,0:T(8,128)(2,1)S(1)}, bf16[448,128]{1,0:T(8,128)(2,1)S(1)}, u32[]{:S(2)}, u32[]{:S(2)}) collective-permute-start(bf16[448,128]{1,0:T(8,128)(2,1)S(1)} %get-tuple-element.55), channel_id=1, source_target_pairs={{0,16},{8,24},{16,0},{24,8},{1,17},{9,25},{17,1},{25,9},{2,18},{10... | collective-permute-start | bytes 344072 | tf_op jit(solution)/shard_map/ppermute | solution.py:27
  42.2 0.5 collective-permute-start.12
  42.7 2.5 %conv.9 = (bf16[2,4,128,128]{3,2,1,0:T(8,128)(2,1)S(1)}, bf16[1,4,16,128,128]{4,3,2,1,0:T(8,128)(2,1)}) custom-call(s32[7]{0:T(128)S(1)} %stack.39.info_ref, f32[448,128]{1,0:T(8,128)S(1)} %get-tuple-element.49.after_ref.refs_0_, bf16[6,18,10,16,128]{4,3,2,1,0:T(8,128)(2,1)S(1)} %get-tuple-element.46.act_ref, ...), custom_call_target="tpu_custom_call", output_to_operand_aliasing={{1}: (7, {})} | custom-call | tf_op jit(solution)/shard_map/conv/pallas_call | solution.py:503
  45.2 2.2 %conv.10 = (bf16[2,4,128,128]{3,2,1,0:T(8,128)(2,1)S(1)}, bf16[1,4,16,128,128]{4,3,2,1,0:T(8,128)(2,1)}) custom-call(s32[7]{0:T(128)S(1)} %stack.39.info_ref, bf16[2,4,128,128]{3,2,1,0:T(8,128)(2,1)S(1)} %get-tuple-element.51.after_ref.refs_0_, bf16[6,18,10,16,128]{4,3,2,1,0:T(8,128)(2,1)S(1)} %get-tuple-element.46.act_ref, ...), custom_call_target="tpu_custom_call", output_to_operand_aliasing={{1}: (7, {})} | custom-call | tf_op jit(solution)/shard_map/conv/pallas_call | solution.py:503
  47.4 0.8 %collective-permute-done.11.refs_2_ = bf16[448,128]{1,0:T(8,128)(2,1)S(1)} collective-permute-done((bf16[448,128]{1,0:T(8,128)(2,1)S(1)}, bf16[448,128]{1,0:T(8,128)(2,1)S(1)}, u32[]{:S(2)}, u32[]{:S(2)}) %collective-permute-start.11) | collective-permute-done | bytes 114720 | tf_op jit(solution)/shard_map/ppermute | solution.py:27
  48.2 0.1 added.2.after_ref.refs_0_
  48.3 3.2 %collective-permute-start.15 = (bf16[448,128]{1,0:T(8,128)(2,1)S(1)}, bf16[448,128]{1,0:T(8,128)(2,1)S(1)}, u32[]{:S(2)}, u32[]{:S(2)}) collective-permute-start(bf16[448,128]{1,0:T(8,128)(2,1)S(1)} %added.2.after_ref.refs_0_), channel_id=1, source_target_pairs={{0,3},{1,2},{2,1},{3,0},{4,7},{5,6},{6,5},{7,4},{8,11},{9,10},{10,... | collective-permute-start | bytes 344072 | tf_op jit(solution)/shard_map/ppermute | solution.py:27
  51.5 0.3 collective-permute-start.14
  51.8 0.9 %collective-permute-start.13 = (bf16[448,128]{1,0:T(8,128)(2,1)S(1)}, bf16[448,128]{1,0:T(8,128)(2,1)S(1)}, u32[]{:S(2)}, u32[]{:S(2)}) collective-permute-start(bf16[448,128]{1,0:T(8,128)(2,1)S(1)} %added.2.after_ref.refs_0_), channel_id=1, source_target_pairs={{0,1},{1,0},{2,3},{3,2},{4,5},{5,4},{6,7},{7,6},{8,9},{9,8},{10,11... | collective-permute-start | bytes 344072 | tf_op jit(solution)/shard_map/ppermute | solution.py:27
  52.7 2.0 %conv.11 = (bf16[2,4,128,128]{3,2,1,0:T(8,128)(2,1)S(1)}, bf16[1,4,16,128,128]{4,3,2,1,0:T(8,128)(2,1)}) custom-call(s32[7]{0:T(128)S(1)} %stack.39.info_ref, bf16[448,128]{1,0:T(8,128)(2,1)S(1)} %added.2.after_ref.refs_0_, bf16[6,18,10,16,128]{4,3,2,1,0:T(8,128)(2,1)S(1)} %get-tuple-element.46.act_ref, ...), custom_call_target="tpu_custom_call", output_to_operand_aliasing={{1}: (7, {})} | custom-call | tf_op jit(solution)/shard_map/conv/pallas_call | solution.py:503
  54.7 2.0 %conv.12 = (bf16[2,4,128,128]{3,2,1,0:T(8,128)(2,1)S(1)}, bf16[1,4,16,128,128]{4,3,2,1,0:T(8,128)(2,1)}) custom-call(s32[7]{0:T(128)S(1)} %stack.39.info_ref, bf16[2,4,128,128]{3,2,1,0:T(8,128)(2,1)S(1)} %get-tuple-element.58.after_ref.refs_0_, bf16[6,18,10,16,128]{4,3,2,1,0:T(8,128)(2,1)S(1)} %get-tuple-element.46.act_ref, ...), custom_call_target="tpu_custom_call", output_to_operand_aliasing={{1}: (7, {})} | custom-call | tf_op jit(solution)/shard_map/conv/pallas_call | solution.py:503
  56.7 2.0 %conv.13 = (bf16[2,4,128,128]{3,2,1,0:T(8,128)(2,1)S(1)}, bf16[1,4,16,128,128]{4,3,2,1,0:T(8,128)(2,1)}) custom-call(s32[7]{0:T(128)S(1)} %stack.39.info_ref, bf16[2,4,128,128]{3,2,1,0:T(8,128)(2,1)S(1)} %get-tuple-element.60.after_ref.refs_0_, bf16[6,18,10,16,128]{4,3,2,1,0:T(8,128)(2,1)S(1)} %get-tuple-element.46.act_ref, ...), custom_call_target="tpu_custom_call", output_to_operand_aliasing={{1}: (7, {})} | custom-call | tf_op jit(solution)/shard_map/conv/pallas_call | solution.py:503
  58.7 2.0 %conv.14 = (bf16[2,4,128,128]{3,2,1,0:T(8,128)(2,1)S(1)}, bf16[1,4,16,128,128]{4,3,2,1,0:T(8,128)(2,1)}) custom-call(s32[7]{0:T(128)S(1)} %stack.39.info_ref, bf16[2,4,128,128]{3,2,1,0:T(8,128)(2,1)S(1)} %get-tuple-element.62.after_ref.refs_0_, bf16[6,18,10,16,128]{4,3,2,1,0:T(8,128)(2,1)S(1)} %get-tuple-element.46.act_ref, ...), custom_call_target="tpu_custom_call", output_to_operand_aliasing={{1}: (7, {})} | custom-call | tf_op jit(solution)/shard_map/conv/pallas_call | solution.py:503
  60.8 0.3 collective-permute-done.14.refs_2_
  61.0 0.1 added.3.after_ref.refs_0_
  61.1 2.4 %collective-permute-start.17 = (bf16[448,128]{1,0:T(8,128)(2,1)S(1)}, bf16[448,128]{1,0:T(8,128)(2,1)S(1)}, u32[]{:S(2)}, u32[]{:S(2)}) collective-permute-start(bf16[448,128]{1,0:T(8,128)(2,1)S(1)} %added.3.after_ref.refs_0_), channel_id=1, source_target_pairs={{0,24},{8,16},{16,8},{24,0},{1,25},{9,17},{17,9},{25,1},{2,26},{10... | collective-permute-start | bytes 344072 | tf_op jit(solution)/shard_map/ppermute | solution.py:27
  63.5 1.0 %collective-permute-start.16 = (bf16[448,128]{1,0:T(8,128)(2,1)S(1)}, bf16[448,128]{1,0:T(8,128)(2,1)S(1)}, u32[]{:S(2)}, u32[]{:S(2)}) collective-permute-start(bf16[448,128]{1,0:T(8,128)(2,1)S(1)} %added.3.after_ref.refs_0_), channel_id=1, source_target_pairs={{0,16},{8,24},{16,0},{24,8},{1,17},{9,25},{17,1},{25,9},{2,18},{10... | collective-permute-start | bytes 344072 | tf_op jit(solution)/shard_map/ppermute | solution.py:27
  64.5 0.1 collective-permute-start.21
  64.7 2.5 %collective-permute-done.17.refs_2_ = bf16[448,128]{1,0:T(8,128)(2,1)S(1)} collective-permute-done((bf16[448,128]{1,0:T(8,128)(2,1)S(1)}, bf16[448,128]{1,0:T(8,128)(2,1)S(1)}, u32[]{:S(2)}, u32[]{:S(2)}) %collective-permute-start.17) | collective-permute-done | bytes 114720 | tf_op jit(solution)/shard_map/ppermute | solution.py:27
  67.1 2.0 %collective-permute-done.16.refs_1_ = bf16[448,128]{1,0:T(8,128)(2,1)S(1)} collective-permute-done((bf16[448,128]{1,0:T(8,128)(2,1)S(1)}, bf16[448,128]{1,0:T(8,128)(2,1)S(1)}, u32[]{:S(2)}, u32[]{:S(2)}) %collective-permute-start.16) | collective-permute-done | bytes 114720 | tf_op jit(solution)/shard_map/ppermute | solution.py:27
  69.2 0.6 collective-permute-done.21.refs_0_
  69.8 2.0 %conv.15 = (bf16[2,4,128,128]{3,2,1,0:T(8,128)(2,1)S(1)}, bf16[1,4,16,128,128]{4,3,2,1,0:T(8,128)(2,1)}) custom-call(s32[7]{0:T(128)S(1)} %stack.39.info_ref, bf16[448,128]{1,0:T(8,128)(2,1)S(1)} %added.3.after_ref.refs_0_, bf16[6,18,10,16,128]{4,3,2,1,0:T(8,128)(2,1)S(1)} %get-tuple-element.46.act_ref, ...), custom_call_target="tpu_custom_call", output_to_operand_aliasing={{1}: (7, {})} | custom-call | tf_op jit(solution)/shard_map/conv/pallas_call | solution.py:503
  71.8 2.3 %collect_most.1 = (f32[1,128]{1,0:T(1,128)}, bf16[1,4,16,128,128]{4,3,2,1,0:T(8,128)(2,1)}, f32[8,432,128]{2,1,0:T(8,128)}) custom-call(s32[7]{0:T(128)S(1)} %stack.39.info_ref, bf16[448,128]{1,0:T(8,128)(2,1)S(1)} %added.3.after_ref.refs_0_, bf16[448,128]{1,0:T(8,128)(2,1)S(1)} %collective-permute-done.16.refs_1_, ...), custom_call_target="tpu_custom_call", output_to_operand_aliasing={{1}: (8, {})} | custom-call | tf_op jit(solution)/shard_map/collect_most/pallas_call | solution.py:583
  74.1 1.3 %collect_rest.1 = f32[8,432,128]{2,1,0:T(8,128)} custom-call(s32[7]{0:T(128)S(1)} %stack.39.info_ref, bf16[448,128]{1,0:T(8,128)(2,1)S(1)} %collective-permute-done.21.refs_0_, bf16[448,128]{1,0:T(8,128)(2,1)S(1)} %collective-permute-done.22.refs_1_, f32[8,432,128]{2,1,0:T(8,128)} %get-tuple-element.69.refs_2_), custom_call_target="tpu_custom_call", output_to_operand_aliasing={{}: (3, {})} | custom-call | tf_op jit(solution)/shard_map/collect_rest/pallas_call | solution.py:596
  (26 shorter events, 0.1 us)
Async XLA Ops:
  4.3 20.5 %copy-start.2 = (f32[128]{0:T(128)S(1)}, f32[128]{0:T(128)}, u32[]{:S(2)}) copy-start(f32[128]{0:T(128)} %param.9) | copy-start | bytes 1540
  4.3 20.5 %copy-start.3 = (f32[128]{0:T(128)S(1)}, f32[128]{0:T(128)}, u32[]{:S(2)}) copy-start(f32[128]{0:T(128)} %param.10) | copy-start | bytes 1540
  4.3 20.5 %collective-permute-start = (bf16[1,2,16,128,128]{4,3,2,1,0:T(8,128)(2,1)S(1)}, bf16[1,2,16,128,128]{4,3,2,1,0:T(8,128)(2,1)S(1)}, u32[]{:S(2)}, u32[]{:S(2)}) collective-permute-start(bf16[1,2,16,128,128]{4,3,2,1,0:T(8,128)(2,1)S(1)} %get-tuple-element.41), channel_id=1, source_target_pairs={{0,4},{4,0},{1,5},{5,1},{2,6},{6,2},{3,7},{7,3},{8,12},{12,8},{9,1... | collective-permute-start | bytes 3145736 | tf_op jit(solution)/shard_map/ppermute | solution.py:412
  6.4 6.8 %collective-permute-start.1 = (bf16[4,128,128]{2,1,0:T(8,128)(2,1)S(1)}, bf16[4,128,128]{2,1,0:T(8,128)(2,1)S(1)}, u32[]{:S(2)}, u32[]{:S(2)}) collective-permute-start(bf16[4,128,128]{2,1,0:T(8,128)(2,1)S(1)} %get-tuple-element.42), channel_id=1, source_target_pairs={{0,1},{1,0},{2,3},{3,2},{4,5},{5,4},{6,7},{7,6},{8,9},{9,8},{10,11... | collective-permute-start | bytes 393224 | tf_op jit(solution)/shard_map/ppermute | solution.py:27
  9.0 4.2 %collective-permute-start.2 = (bf16[4,128,128]{2,1,0:T(8,128)(2,1)S(1)}, bf16[4,128,128]{2,1,0:T(8,128)(2,1)S(1)}, u32[]{:S(2)}, u32[]{:S(2)}) collective-permute-start(bf16[4,128,128]{2,1,0:T(8,128)(2,1)S(1)} %get-tuple-element.43), channel_id=1, source_target_pairs={{1,2},{2,1},{5,6},{6,5},{9,10},{10,9},{13,14},{14,13},{17,18},{18,... | collective-permute-start | bytes 393224 | tf_op jit(solution)/shard_map/ppermute | solution.py:395
  13.2 11.6 %collective-permute-start.3 = (bf16[4,128,128]{2,1,0:T(8,128)(2,1)S(1)}, bf16[4,128,128]{2,1,0:T(8,128)(2,1)S(1)}, u32[]{:S(2)}, u32[]{:S(2)}) collective-permute-start(bf16[4,128,128]{2,1,0:T(8,128)(2,1)S(1)} %collective-permute-done.1.near_ref), channel_id=1, source_target_pairs={{0,4},{4,0},{1,5},{5,1},{2,6},{6,2},{3,7},{7,3},{8,12},{12,8},{9,1... | collective-permute-start | bytes 393224 | tf_op jit(solution)/shard_map/ppermute | solution.py:422
  13.2 11.6 %collective-permute-start.4 = (bf16[4,128,128]{2,1,0:T(8,128)(2,1)S(1)}, bf16[4,128,128]{2,1,0:T(8,128)(2,1)S(1)}, u32[]{:S(2)}, u32[]{:S(2)}) collective-permute-start(bf16[4,128,128]{2,1,0:T(8,128)(2,1)S(1)} %collective-permute-done.2.refs_0_), channel_id=1, source_target_pairs={{0,4},{4,0},{1,5},{5,1},{2,6},{6,2},{3,7},{7,3},{8,12},{12,8},{9,1... | collective-permute-start | bytes 393224 | tf_op jit(solution)/shard_map/ppermute | solution.py:423
  13.7 1.2 %collective-permute-start.5 = (f32[3,8,128]{2,1,0:T(8,128)S(1)}, f32[3,8,128]{2,1,0:T(8,128)S(1)}, u32[]{:S(2)}, u32[]{:S(2)}) collective-permute-start(f32[3,8,128]{2,1,0:T(8,128)S(1)} %get-tuple-element.44.refs_0_), channel_id=1, source_target_pairs={{0,4},{4,0},{1,5},{5,1},{2,6},{6,2},{3,7},{7,3},{8,12},{12,8},{9,1... | collective-permute-start | bytes 36872 | tf_op jit(solution)/shard_map/ppermute | solution.py:27
  14.9 6.0 %collective-permute-start.8 = (f32[3,8,128]{2,1,0:T(8,128)S(1)}, f32[3,8,128]{2,1,0:T(8,128)S(1)}, u32[]{:S(2)}, u32[]{:S(2)}) collective-permute-start(f32[3,8,128]{2,1,0:T(8,128)S(1)} %merge.1.refs_5_.after_ref), channel_id=1, source_target_pairs={{0,3},{1,2},{2,1},{3,0},{4,7},{5,6},{6,5},{7,4},{8,11},{9,10},{10,... | collective-permute-start | bytes 36872 | tf_op jit(solution)/shard_map/ppermute | solution.py:27
  18.7 5.9 %collective-permute-start.7 = (f32[3,8,128]{2,1,0:T(8,128)S(1)}, f32[3,8,128]{2,1,0:T(8,128)S(1)}, u32[]{:S(2)}, u32[]{:S(2)}) collective-permute-start(f32[3,8,128]{2,1,0:T(8,128)S(1)} %merge.1.refs_5_.after_ref), channel_id=1, source_target_pairs={{0,2},{1,3},{2,0},{3,1},{4,6},{5,7},{6,4},{7,5},{8,10},{9,11},{10,... | collective-permute-start | bytes 36872 | tf_op jit(solution)/shard_map/ppermute | solution.py:27
  20.9 3.9 %collective-permute-start.6 = (f32[3,8,128]{2,1,0:T(8,128)S(1)}, f32[3,8,128]{2,1,0:T(8,128)S(1)}, u32[]{:S(2)}, u32[]{:S(2)}) collective-permute-start(f32[3,8,128]{2,1,0:T(8,128)S(1)} %merge.1.refs_5_.after_ref), channel_id=1, source_target_pairs={{0,1},{1,0},{2,3},{3,2},{4,5},{5,4},{6,7},{7,6},{8,9},{9,8},{10,11... | collective-permute-start | bytes 36872 | tf_op jit(solution)/shard_map/ppermute | solution.py:27
  24.8 11.0 %copy-start = (bf16[3,3,3,128,128]{4,3,2,1,0:T(8,128)(2,1)S(1)}, bf16[3,3,3,128,128]{4,3,2,1,0:T(8,128)(2,1)}, u32[]{:S(2)}) copy-start(bf16[3,3,3,128,128]{4,3,2,1,0:T(8,128)(2,1)} %kernel_ref.1) | copy-start | bytes 2654212
  35.7 0.7 copy-start.1
  35.7 2.6 %collective-permute-start.9 = (f32[4,448,128]{2,1,0:T(8,128)S(1)}, f32[4,448,128]{2,1,0:T(8,128)S(1)}, u32[]{:S(2)}, u32[]{:S(2)}) collective-permute-start(f32[4,448,128]{2,1,0:T(8,128)S(1)} %get-tuple-element.48), channel_id=1, source_target_pairs={{0,4},{4,0},{1,5},{5,1},{2,6},{6,2},{3,7},{7,3},{8,12},{12,8},{9,1... | collective-permute-start | bytes 2752520 | tf_op jit(solution)/shard_map/ppermute | solution.py:27
  39.1 8.3 %collective-permute-start.10 = (bf16[448,128]{1,0:T(8,128)(2,1)S(1)}, bf16[448,128]{1,0:T(8,128)(2,1)S(1)}, u32[]{:S(2)}, u32[]{:S(2)}) collective-permute-start(bf16[448,128]{1,0:T(8,128)(2,1)S(1)} %get-tuple-element.54), channel_id=1, source_target_pairs={{0,8},{8,0},{16,24},{24,16},{1,9},{9,1},{17,25},{25,17},{2,10},{10... | collective-permute-start | bytes 344072 | tf_op jit(solution)/shard_map/ppermute | solution.py:27
  40.7 7.5 %collective-permute-start.11 = (bf16[448,128]{1,0:T(8,128)(2,1)S(1)}, bf16[448,128]{1,0:T(8,128)(2,1)S(1)}, u32[]{:S(2)}, u32[]{:S(2)}) collective-permute-start(bf16[448,128]{1,0:T(8,128)(2,1)S(1)} %get-tuple-element.55), channel_id=1, source_target_pairs={{0,16},{8,24},{16,0},{24,8},{1,17},{9,25},{17,1},{25,9},{2,18},{10... | collective-permute-start | bytes 344072 | tf_op jit(solution)/shard_map/ppermute | solution.py:27
  42.2 6.0 %collective-permute-start.12 = (bf16[448,128]{1,0:T(8,128)(2,1)S(1)}, bf16[448,128]{1,0:T(8,128)(2,1)S(1)}, u32[]{:S(2)}, u32[]{:S(2)}) collective-permute-start(bf16[448,128]{1,0:T(8,128)(2,1)S(1)} %get-tuple-element.56), channel_id=1, source_target_pairs={{0,24},{8,16},{16,8},{24,0},{1,25},{9,17},{17,9},{25,1},{2,26},{10... | collective-permute-start | bytes 344072 | tf_op jit(solution)/shard_map/ppermute | solution.py:27
  48.3 12.5 %collective-permute-start.15 = (bf16[448,128]{1,0:T(8,128)(2,1)S(1)}, bf16[448,128]{1,0:T(8,128)(2,1)S(1)}, u32[]{:S(2)}, u32[]{:S(2)}) collective-permute-start(bf16[448,128]{1,0:T(8,128)(2,1)S(1)} %added.2.after_ref.refs_0_), channel_id=1, source_target_pairs={{0,3},{1,2},{2,1},{3,0},{4,7},{5,6},{6,5},{7,4},{8,11},{9,10},{10,... | collective-permute-start | bytes 344072 | tf_op jit(solution)/shard_map/ppermute | solution.py:27
  51.5 9.5 %collective-permute-start.14 = (bf16[448,128]{1,0:T(8,128)(2,1)S(1)}, bf16[448,128]{1,0:T(8,128)(2,1)S(1)}, u32[]{:S(2)}, u32[]{:S(2)}) collective-permute-start(bf16[448,128]{1,0:T(8,128)(2,1)S(1)} %added.2.after_ref.refs_0_), channel_id=1, source_target_pairs={{0,2},{1,3},{2,0},{3,1},{4,6},{5,7},{6,4},{7,5},{8,10},{9,11},{10,... | collective-permute-start | bytes 344072 | tf_op jit(solution)/shard_map/ppermute | solution.py:27
  51.8 9.2 %collective-permute-start.13 = (bf16[448,128]{1,0:T(8,128)(2,1)S(1)}, bf16[448,128]{1,0:T(8,128)(2,1)S(1)}, u32[]{:S(2)}, u32[]{:S(2)}) collective-permute-start(bf16[448,128]{1,0:T(8,128)(2,1)S(1)} %added.2.after_ref.refs_0_), channel_id=1, source_target_pairs={{0,1},{1,0},{2,3},{3,2},{4,5},{5,4},{6,7},{7,6},{8,9},{9,8},{10,11... | collective-permute-start | bytes 344072 | tf_op jit(solution)/shard_map/ppermute | solution.py:27
  61.1 6.0 %collective-permute-start.17 = (bf16[448,128]{1,0:T(8,128)(2,1)S(1)}, bf16[448,128]{1,0:T(8,128)(2,1)S(1)}, u32[]{:S(2)}, u32[]{:S(2)}) collective-permute-start(bf16[448,128]{1,0:T(8,128)(2,1)S(1)} %added.3.after_ref.refs_0_), channel_id=1, source_target_pairs={{0,24},{8,16},{16,8},{24,0},{1,25},{9,17},{17,9},{25,1},{2,26},{10... | collective-permute-start | bytes 344072 | tf_op jit(solution)/shard_map/ppermute | solution.py:27
  63.5 5.7 %collective-permute-start.16 = (bf16[448,128]{1,0:T(8,128)(2,1)S(1)}, bf16[448,128]{1,0:T(8,128)(2,1)S(1)}, u32[]{:S(2)}, u32[]{:S(2)}) collective-permute-start(bf16[448,128]{1,0:T(8,128)(2,1)S(1)} %added.3.after_ref.refs_0_), channel_id=1, source_target_pairs={{0,16},{8,24},{16,0},{24,8},{1,17},{9,25},{17,1},{25,9},{2,18},{10... | collective-permute-start | bytes 344072 | tf_op jit(solution)/shard_map/ppermute | solution.py:27
  64.5 5.2 %collective-permute-start.21 = (bf16[448,128]{1,0:T(8,128)(2,1)S(1)}, bf16[448,128]{1,0:T(8,128)(2,1)S(1)}, u32[]{:S(2)}, u32[]{:S(2)}) collective-permute-start(bf16[448,128]{1,0:T(8,128)(2,1)S(1)} %added.3.after_ref.refs_0_), channel_id=1, source_target_pairs={{0,8},{8,0},{16,24},{24,16},{1,9},{9,1},{17,25},{25,17},{2,10},{10... | collective-permute-start | bytes 344072 | tf_op jit(solution)/shard_map/ppermute | solution.py:27
  64.7 7.1 %collective-permute-start.18 = (bf16[448,128]{1,0:T(8,128)(2,1)S(1)}, bf16[448,128]{1,0:T(8,128)(2,1)S(1)}, u32[]{:S(2)}, u32[]{:S(2)}) collective-permute-start(bf16[448,128]{1,0:T(8,128)(2,1)S(1)} %added.3.after_ref.refs_0_), channel_id=1, source_target_pairs={{0,4},{4,0},{1,5},{5,1},{2,6},{6,2},{3,7},{7,3},{8,12},{12,8},{9,1... | collective-permute-start | bytes 344072 | tf_op jit(solution)/shard_map/ppermute | solution.py:27
  67.1 4.6 %collective-permute-start.20 = (bf16[448,128]{1,0:T(8,128)(2,1)S(1)}, bf16[448,128]{1,0:T(8,128)(2,1)S(1)}, u32[]{:S(2)}, u32[]{:S(2)}) collective-permute-start(bf16[448,128]{1,0:T(8,128)(2,1)S(1)} %collective-permute-done.17.refs_2_), channel_id=1, source_target_pairs={{0,4},{4,0},{1,5},{5,1},{2,6},{6,2},{3,7},{7,3},{8,12},{12,8},{9,1... | collective-permute-start | bytes 344072 | tf_op jit(solution)/shard_map/ppermute | solution.py:27
  69.2 2.6 %collective-permute-start.19 = (bf16[448,128]{1,0:T(8,128)(2,1)S(1)}, bf16[448,128]{1,0:T(8,128)(2,1)S(1)}, u32[]{:S(2)}, u32[]{:S(2)}) collective-permute-start(bf16[448,128]{1,0:T(8,128)(2,1)S(1)} %collective-permute-done.16.refs_1_), channel_id=1, source_target_pairs={{0,4},{4,0},{1,5},{5,1},{2,6},{6,2},{3,7},{7,3},{8,12},{12,8},{9,1... | collective-permute-start | bytes 344072 | tf_op jit(solution)/shard_map/ppermute | solution.py:27
  69.8 4.3 %collective-permute-start.22 = (bf16[448,128]{1,0:T(8,128)(2,1)S(1)}, bf16[448,128]{1,0:T(8,128)(2,1)S(1)}, u32[]{:S(2)}, u32[]{:S(2)}) collective-permute-start(bf16[448,128]{1,0:T(8,128)(2,1)S(1)} %collective-permute-done.21.refs_0_), channel_id=1, source_target_pairs={{0,4},{4,0},{1,5},{5,1},{2,6},{6,2},{3,7},{7,3},{8,12},{12,8},{9,1... | collective-permute-start | bytes 344072 | tf_op jit(solution)/shard_map/ppermute | solution.py:27

commit v10 on v9

--- a/solution.py
+++ b/solution.py
@@ -116,16 +116,16 @@
         refs[-1][n] = value
 
 
-def cotangent_kernel(info_ref, cot_ref, turned_ref, bias_ref, wide):
+def cotangent_kernel(t0, info_ref, cot_ref, turned_ref, bias_ref, wide):
     rows, cols, chans = cot_ref.shape[2:]
     step = cols // TILE
     lanes = 4
     bias = jnp.zeros((lanes, 8, chans), F32)
     for t in range(turned_ref.shape[0]):
-        keep = (t < info_ref[0]).astype(F32)
+        keep = (t0 + t < info_ref[0]).astype(F32)
 
         def row(y, acc, t=t, keep=keep):
-            value = cot_ref[0, t, y].astype(F32) * keep
+            value = cot_ref[0, t0 + t, y].astype(F32) * keep
             slot = wide.at[y % wide.shape[0]]
             slot[...] = value
             order = jnp.concatenate(
@@ -149,19 +149,18 @@
 
 
 def weights_kernel(
-    parts_n, per, info_ref, turned_ref, bias_ref, cot_ref, video_ref, early_ref, near_ref, *refs
+    per, info_ref, turned_0, turned_1, bias_0, bias_1, video_ref, early_ref, near_ref, *refs
 ):
     far_ref, near_early_ref, far_early_ref, gain_ref, shift_ref, *refs = refs
-    parts, (act_ref, keep_ref, *send_refs) = refs[:parts_n], refs[parts_n:-6]
-    wide, acc, shards, late, plain, bias_acc = refs[-6:]
-    ahead = turned_ref.shape[0]
-    bias_acc[...] = bias_ref[...]
+    stats_ref, act_ref, keep_ref, *send_refs = refs[:-3]
+    wide, acc, shards = refs[-3:]
+    ahead = turned_0.shape[0]
     frames, rows, cols, chans = video_ref.shape[1:]
     before = early_ref.shape[1]
     step = cols // TILE
     slots = wide.shape[0]
     inside, first, has_low, has_high = info_ref[0], info_ref[1], info_ref[2], info_ref[3]
-    count, total, squares = merged([ref[...] for ref in parts])
+    count, total, squares = stats_ref[0], stats_ref[1], stats_ref[2]
     every = jnp.sum(count, axis=0, keepdims=True) * per
     mean = group_sum(jnp.sum(total, axis=0, keepdims=True), per) / every
     away = total / jnp.maximum(count, 1.0) - mean
@@ -199,15 +198,6 @@
             value, has = jnp.where(odd, near, far), has_low
         row(value, kept(f) * has.astype(F32), slot, f, side * (rows + 1))
 
-    def turn(t, y, slot):
-        value = cot_ref[0, t, y].astype(F32) * (t < inside).astype(F32)
-        plain[slot] = value
-        order = jnp.concatenate(
-            [plain[slot, pl.ds(r, TILE, stride=step), :] for r in range(step)], axis=0
-        )
-        late[t - ahead, y] = order.astype(BF16).T
-        bias_acc[...] += jnp.sum(value.reshape(cols // 8, 8, chans), axis=0)
-
     def all_rows(f):
         work = [functools.partial(border, f, side, side) for side in range(2)]
         return work + [functools.partial(inner, f, y, y % slots) for y in range(rows)]
@@ -222,7 +212,7 @@
 
     taps = [(kt, ky, kx) for kt in range(3) for ky in range(3) for kx in range(3)]
     pair = 2
-    k = turned_ref.shape[3]
+    k = turned_0.shape[3]
     tms, dps, full = shards.shape[:3]
     size = full - TILE
 
@@ -243,10 +233,6 @@
                 work.append((f * 9 // pair, all_rows(f)))
         if t + before + 1 < frames + before:
             tasks = all_rows(t + before + 1)
-            if ahead <= t + 1 < frames:
-                tasks += [
-                    functools.partial(turn, t + 1, y, y % plain.shape[0]) for y in range(rows)
-                ]
             work.append((len(groups), tasks))
         slots_of = [[] for _ in groups]
         begin = 0
@@ -254,7 +240,7 @@
             for n, task in enumerate(tasks):
                 slots_of[begin + n * (end - begin) // len(tasks)].append(task)
             begin = end
-        source = turned_ref.at[t] if t < ahead else late.at[t - ahead]
+        source = (turned_0 if t < ahead else turned_1).at[t % ahead]
         left = jnp.concatenate([source[y] for y in range(rows)], axis=1)
         for j, chosen in enumerate(groups):
             right = jnp.concatenate(
@@ -272,7 +258,7 @@
             if t == frames - 1:
                 for n in range(len(chosen)):
                     place(j * pair + n)
-    bias = jnp.sum(bias_acc[...], axis=0, keepdims=True)
+    bias = jnp.sum(bias_0[...] + bias_1[...], axis=0, keepdims=True)
     tail = jnp.concatenate([bias, jnp.zeros((TILE - 1, chans), F32)], axis=0)
     for i in range(tms):
         for j in range(dps):
@@ -410,15 +396,23 @@
     following = [(i, (i + 1) % tms) for i in range(tms)]
     gathered = [stats] + [swap(stats, "tm", r) for r in range(1, tms)]
     early = lax.ppermute(tail, "tm", following)
-    stats = pl.pallas_call(
-        merge_kernel,
-        in_specs=[VMEM] * tms,
-        out_specs=VMEM,
-        out_shape=jax.ShapeDtypeStruct((3, 8, chans), F32),
-        compiler_params=params(1),
-        name="merge",
-    )(*gathered)
-    parts = [stats] + [swap(stats, "space", r) for r in range(1, spaces)]
+
+    def together(arrays):
+        return pl.pallas_call(
+            merge_kernel,
+            in_specs=[VMEM] * len(arrays),
+            out_specs=VMEM,
+            out_shape=jax.ShapeDtypeStruct((3, 8, chans), F32),
+            compiler_params=params(1),
+            name="merge",
+        )(*arrays)
+
+    stats = core_stats = together(gathered)
+    by = 1
+    while by < spaces:
+        other = swap(stats, "space", by)
+        stats = together([stats, other])
+        by *= 2
     near_early = lax.ppermute(near, "tm", following)
     far_early = lax.ppermute(far, "tm", following)
     pair = 2
@@ -431,21 +425,25 @@
         ),
         compiler_params=params(2),
         name="taps",
-    )(stats, kernel)
+    )(core_stats, kernel)
 
     ahead = frames // 2
-    turned, bias = pl.pallas_call(
-        cotangent_kernel,
-        in_specs=[SMEM, VMEM],
-        out_specs=[VMEM, VMEM],
-        out_shape=[
-            jax.ShapeDtypeStruct((ahead, rows, chans, cols), BF16),
-            jax.ShapeDtypeStruct((8, chans), F32),
-        ],
-        scratch_shapes=[pltpu.VMEM((8, cols, chans), F32)],
-        compiler_params=params(4),
-        name="cotangent",
-    )(info, masked_in)
+    turned, bias = [], []
+    for n in range(2):
+        some, part = pl.pallas_call(
+            functools.partial(cotangent_kernel, n * ahead),
+            in_specs=[SMEM, VMEM],
+            out_specs=[VMEM, VMEM],
+            out_shape=[
+                jax.ShapeDtypeStruct((ahead, rows, chans, cols), BF16),
+                jax.ShapeDtypeStruct((8, chans), F32),
+            ],
+            scratch_shapes=[pltpu.VMEM((8, cols, chans), F32)],
+            compiler_params=params(2),
+            name="cotangent",
+        )(info, masked_in)
+        turned.append(some)
+        bias.append(part)
 
     count = kernel.shape[0] * kernel.shape[1] * kernel.shape[2] * chans
     shards_n = tms * dps
@@ -453,8 +451,8 @@
     shard = count // shards_n
     full = shard + TILE
     act, keep, *sends = pl.pallas_call(
-        functools.partial(weights_kernel, spaces, per),
-        in_specs=[SMEM] + [VMEM] * (11 + spaces),
+        functools.partial(weights_kernel, per),
+        in_specs=[SMEM] + [VMEM] * 13,
         out_specs=[VMEM] * (1 + tms),
         out_shape=[
             jax.ShapeDtypeStruct((frames + before, rows + 2, step + 2, TILE, chans), BF16)
@@ -464,17 +462,13 @@
             pltpu.VMEM((8, cols + 16, chans), F32),
             pltpu.VMEM((chans, count), F32),
             pltpu.VMEM((tms, dps, full, chans), F32),
-            pltpu.VMEM((frames - ahead, rows, chans, cols), BF16),
-            pltpu.VMEM((8, cols, chans), F32),
-            pltpu.VMEM((8, chans), F32),
         ],
         compiler_params=params(16),
         name="weights",
     )(
         info,
-        turned,
-        bias,
-        masked_in,
+        *turned,
+        *bias,
         local,
         early,
         near,
@@ -483,7 +477,7 @@
         far_early,
         norm_gain.reshape(1, chans),
         norm_shift.reshape(1, chans),
-        *parts,
+        stats,
     )
 
     block = 4
@@ -558,54 +552,42 @@
         for r, array in enumerate(mine):
             shards[q, r] = swap(array, "tm", q)
     final = 1 % dps
-    late = [key for key in shards if key[1] == final]
-    order = [key for key in shards if key[1] != final]
-
-    def collect(keys, info_ref, *refs):
-        shard_refs, out_ref = refs[: len(keys)], refs[-3]
-        wide, sems = refs[-2:]
+    order = sorted(shards, key=lambda key: key[1] == final)
+
+    def collect(info_ref, *refs):
+        shard_refs, piece_ref = refs[: len(order)], refs[len(order)]
+        bias_ref, output_ref, out_ref, wide, sems = refs[-5:]
         copies = []
-        if keys is order:
-            target = refs[-4].at[where(len(pieces) - 1)]
-            copies.append(pltpu.make_async_copy(refs[len(keys)], target, sems.at[len(keys)]))
-            copies[-1].start()
-            tail = shard_refs[0][shard : shard + TILE, :].astype(F32)
-            refs[-5][...] = tail[0:1] + tail[1:2] + tail[2:3]
-        for n, ((q, r), ref) in enumerate(zip(keys, shard_refs)):
+        for n, ((q, r), ref) in enumerate(zip(order, shard_refs)):
             at = (info_ref[4] ^ q) * dps + (info_ref[5] ^ r)
             wide[n] = ref[0:shard, :].astype(F32)
             copies.append(pltpu.make_async_copy(wide.at[n], out_ref.at[at], sems.at[n]))
             copies[-1].start()
+        target = output_ref.at[where(len(pieces) - 1)]
+        copies.append(pltpu.make_async_copy(piece_ref, target, sems.at[len(order)]))
+        copies[-1].start()
+        tail = shard_refs[0][shard : shard + TILE, :].astype(F32)
+        bias_ref[...] = tail[0:1] + tail[1:2] + tail[2:3]
         for copy in copies:
             copy.wait()
 
-    gradient = jax.ShapeDtypeStruct((shards_n, shard, chans), F32)
     grad_bias, output, grad_kernel = pl.pallas_call(
-        functools.partial(collect, order),
+        collect,
         in_specs=[SMEM] + [VMEM] * (len(order) + 1) + [ANY],
         out_specs=[VMEM, ANY, ANY],
-        out_shape=[jax.ShapeDtypeStruct((1, chans), F32), whole, gradient],
+        out_shape=[
+            jax.ShapeDtypeStruct((1, chans), F32),
+            whole,
+            jax.ShapeDtypeStruct((shards_n, shard, chans), F32),
+        ],
         scratch_shapes=[
             pltpu.VMEM((len(order), shard, chans), F32),
             pltpu.SemaphoreType.DMA((len(order) + 1,)),
         ],
         input_output_aliases={len(order) + 2: 1},
-        compiler_params=params(8),
-        name="collect_most",
+        compiler_params=params(4),
+        name="collect",
     )(info, *[shards[key] for key in order], *done[-1])
-    grad_kernel = pl.pallas_call(
-        functools.partial(collect, late),
-        in_specs=[SMEM] + [VMEM] * len(late) + [ANY],
-        out_specs=ANY,
-        out_shape=gradient,
-        scratch_shapes=[
-            pltpu.VMEM((len(late), shard, chans), F32),
-            pltpu.SemaphoreType.DMA((len(late),)),
-        ],
-        input_output_aliases={len(late) + 1: 0},
-        compiler_params=params(8),
-        name="collect_rest",
-    )(info, *[shards[key] for key in late], grad_kernel)
 
     return output, grad_kernel.reshape(kernel.shape), grad_bias.reshape(chans)
 

time: 75.8 us -> 75.7 us (level)
    ppermute x19 -> x18, starting transfers between devices: 22.5 us -> 22 us  [swap(): return lax.ppermute(array, axis, [(i, i ^ by) for i in range(length)])]
    ppermute x19 -> x18, waiting for transfers between devices: 11 us -> 11.4 us  [swap(): return lax.ppermute(array, axis, [(i, i ^ by) for i in range(length)])]
    pallas_call x5 -> x7, Pallas kernels: 16 us -> 16 us  [the longest x1 10.5 us: step_of(): pl.pallas_call(functools.partial(weights_kernel, per), in_specs=[SMEM] +...]
  transfers between devices with their start and end apart: 23 -> 22, of which waited for: 8 -> 8; matrix products, arithmetic and copies ran while one was open for 0% -> 0% of each run, Pallas kernels for 30% -> 28%
where the time goes in v10:
time: 75.7 us; the launch traced here: 75.6 us
  Pallas kernels  38.1 us (50%)
  starting transfers between devices  23.8 us (31%)
  waiting for transfers between devices  11.4 us (15%)
  between operations  1.99 us (3%)
    ppermute x18, starting transfers between devices, swap(): return lax.ppermute(array, axis, [(i, i ^ by) for i in range(length)])  22 us
    pallas_call x8, Pallas kernels, cover(): pl.pallas_call(functools.partial(conv_kernel, pieces[n], where(n - 1) if...  16.5 us
    ppermute x18, waiting for transfers between devices, swap(): return lax.ppermute(array, axis, [(i, i ^ by) for i in range(length)])  11.4 us
    pallas_call x1, Pallas kernels, step_of(): pl.pallas_call(functools.partial(weights_kernel, per), in_specs=[SMEM] +...  10.5 us
    pallas_call x2, Pallas kernels, step_of(): pl.pallas_call(functools.partial(cotangent_kernel, n * ahead), in_specs=[...  3.01 us
    pallas_call x1, Pallas kernels, step_of(): pl.pallas_call(functools.partial(stats_kernel, before), in_specs=[SMEM, A...  2.89 us
    pallas_call x1, Pallas kernels, step_of(): pl.pallas_call(collect, in_specs=[SMEM] + [VMEM] * (len(order) + 1) + [AN...  2.43 us
    pallas_call x1, Pallas kernels, step_of(): pl.pallas_call(ends_kernel, in_specs=[SMEM, ANY], out_specs=[VMEM, VMEM],...  1.53 us
  transfers between devices with their start and end apart: 22, of which 8 were waited for; matrix products, arithmetic and copies ran while one was open for 0% of the time, Pallas kernels for 28%

profile of v10, /device:TPU:0, one launch (start us, length us, event | category | flops | bytes accessed | tf_op | source)
XLA Modules:
  0.0 75.6 jit_solution(5939520794360711895)
XLA Ops:
  1.3 0.1 stack.39.info_ref
  1.4 2.9 %stats.1 = (f32[3,8,128]{2,1,0:T(8,128)S(1)}, bf16[1,4,16,128,128]{4,3,2,1,0:T(8,128)(2,1)S(1)}, bf16[1,4,16,128,128]{4,3,2,1,0:T(8,128)(2,1)S(1)}, bf16[1,2,16,128,128]{4,3,2,1,0:T(8,128)(2,1)S(1)}) custom-call(s32[7]{0:T(128)S(1)} %stack.39.info_ref, bf16[1,4,16,128,128]{4,3,2,1,0:T(8,128)(2,1)} %video_hbm.3, bf16[1,4,16,128,128]{4,3,2,1,0:T(8,128)(2,1)} %cot_hbm.1), custom_call_target="tpu_custom_call" | custom-call | tf_op jit(solution)/shard_map/stats/pallas_call | solution.py:382
  4.3 0.6 collective-permute-start
  4.8 1.5 %ends.1 = (bf16[4,128,128]{2,1,0:T(8,128)(2,1)S(1)}, bf16[4,128,128]{2,1,0:T(8,128)(2,1)S(1)}) custom-call(s32[7]{0:T(128)S(1)} %stack.39.info_ref, bf16[1,4,16,128,128]{4,3,2,1,0:T(8,128)(2,1)} %video_hbm.3), custom_call_target="tpu_custom_call" | custom-call | tf_op jit(solution)/shard_map/ends/pallas_call | solution.py:370
  6.4 2.6 %collective-permute-start.1 = (bf16[4,128,128]{2,1,0:T(8,128)(2,1)S(1)}, bf16[4,128,128]{2,1,0:T(8,128)(2,1)S(1)}, u32[]{:S(2)}, u32[]{:S(2)}) collective-permute-start(bf16[4,128,128]{2,1,0:T(8,128)(2,1)S(1)} %get-tuple-element.46), channel_id=1, source_target_pairs={{0,1},{1,0},{2,3},{3,2},{4,5},{5,4},{6,7},{7,6},{8,9},{9,8},{10,11... | collective-permute-start | bytes 393224 | tf_op jit(solution)/shard_map/ppermute | solution.py:27
  9.0 0.7 collective-permute-start.2
  9.7 3.5 %collective-permute-done.1.near_ref = bf16[4,128,128]{2,1,0:T(8,128)(2,1)S(1)} collective-permute-done((bf16[4,128,128]{2,1,0:T(8,128)(2,1)S(1)}, bf16[4,128,128]{2,1,0:T(8,128)(2,1)S(1)}, u32[]{:S(2)}, u32[]{:S(2)}) %collective-permute-start.1) | collective-permute-done | bytes 131104 | tf_op jit(solution)/shard_map/ppermute | solution.py:27
  13.2 0.0 collective-permute-start.3
  13.2 0.5 collective-permute-start.4
  13.7 0.0 collective-permute-start.5
  13.7 1.2 %collective-permute-done.5.refs_1_ = f32[3,8,128]{2,1,0:T(8,128)S(1)} collective-permute-done((f32[3,8,128]{2,1,0:T(8,128)S(1)}, f32[3,8,128]{2,1,0:T(8,128)S(1)}, u32[]{:S(2)}, u32[]{:S(2)}) %collective-permute-start.5) | collective-permute-done | bytes 12320 | tf_op jit(solution)/shard_map/ppermute | solution.py:27
  14.9 4.5 %collective-permute-start.6 = (f32[3,8,128]{2,1,0:T(8,128)S(1)}, f32[3,8,128]{2,1,0:T(8,128)S(1)}, u32[]{:S(2)}, u32[]{:S(2)}) collective-permute-start(f32[3,8,128]{2,1,0:T(8,128)S(1)} %merge.3.refs_0_.after_ref), channel_id=1, source_target_pairs={{0,1},{1,0},{2,3},{3,2},{4,5},{5,4},{6,7},{7,6},{8,9},{9,8},{10,11... | collective-permute-start | bytes 36872 | tf_op jit(solution)/shard_map/ppermute | solution.py:27
  19.4 1.7 %collective-permute-done.6.refs_1_ = f32[3,8,128]{2,1,0:T(8,128)S(1)} collective-permute-done((f32[3,8,128]{2,1,0:T(8,128)S(1)}, f32[3,8,128]{2,1,0:T(8,128)S(1)}, u32[]{:S(2)}, u32[]{:S(2)}) %collective-permute-start.6) | collective-permute-done | bytes 12320 | tf_op jit(solution)/shard_map/ppermute | solution.py:27
  21.1 3.3 %collective-permute-start.7 = (f32[3,8,128]{2,1,0:T(8,128)S(1)}, f32[3,8,128]{2,1,0:T(8,128)S(1)}, u32[]{:S(2)}, u32[]{:S(2)}) collective-permute-start(f32[3,8,128]{2,1,0:T(8,128)S(1)} %merge.4.refs_0_), channel_id=1, source_target_pairs={{0,2},{1,3},{2,0},{3,1},{4,6},{5,7},{6,4},{7,5},{8,10},{9,11},{10,... | collective-permute-start | bytes 36872 | tf_op jit(solution)/shard_map/ppermute | solution.py:27
  24.3 1.5 %cotangent.3 = (bf16[2,16,128,128]{3,2,1,0:T(8,128)(2,1)S(1)}, f32[8,128]{1,0:T(8,128)S(1)}) custom-call(s32[7]{0:T(128)S(1)} %stack.39.info_ref, bf16[1,4,16,128,128]{4,3,2,1,0:T(8,128)(2,1)S(1)} %get-tuple-element.39.cot_ref), custom_call_target="tpu_custom_call" | custom-call | tf_op jit(solution)/shard_map/cotangent/pallas_call | solution.py:433
  25.8 1.5 %cotangent.2 = (bf16[2,16,128,128]{3,2,1,0:T(8,128)(2,1)S(1)}, f32[8,128]{1,0:T(8,128)S(1)}) custom-call(s32[7]{0:T(128)S(1)} %stack.39.info_ref, bf16[1,4,16,128,128]{4,3,2,1,0:T(8,128)(2,1)S(1)} %get-tuple-element.39.cot_ref), custom_call_target="tpu_custom_call" | custom-call | tf_op jit(solution)/shard_map/cotangent/pallas_call | solution.py:433
  27.4 0.0 copy-start
  27.4 10.5 %weights.1 = (bf16[6,18,10,16,128]{4,3,2,1,0:T(8,128)(2,1)S(1)}, f32[4,448,128]{2,1,0:T(8,128)S(1)}, f32[4,448,128]{2,1,0:T(8,128)S(1)}) custom-call(s32[7]{0:T(128)S(1)} %stack.39.info_ref, bf16[2,16,128,128]{3,2,1,0:T(8,128)(2,1)S(1)} %get-tuple-element.40.turned_0, bf16[2,16,128,128]{3,2,1,0:T(8,128)(2,1)S(1)} %get-tuple-element.41.turned_1, ...), custom_call_target="tpu_custom_call" | custom-call | tf_op jit(solution)/shard_map/weights/pallas_call | solution.py:453
  38.0 0.0 copy-start.1
  38.0 0.1 collective-permute-start.8
  38.1 0.4 taps.1.taps_ref
  38.4 0.2 copy-done.1
  38.6 2.0 %conv.8 = (bf16[2,4,128,128]{3,2,1,0:T(8,128)(2,1)S(1)}, bf16[1,4,16,128,128]{4,3,2,1,0:T(8,128)(2,1)}) custom-call(s32[7]{0:T(128)S(1)} %stack.39.info_ref, f32[4,448,128]{2,1,0:T(8,128)S(1)} %get-tuple-element.49.after_ref.keep_ref, bf16[6,18,10,16,128]{4,3,2,1,0:T(8,128)(2,1)S(1)} %get-tuple-element.50.act_ref, bf16[4608,256]{1,0:T(8,128)(2,1)S(1)} %taps.1.taps_ref, ...), custom_call_target="tpu_custom_call" | custom-call | tf_op jit(solution)/shard_map/conv/pallas_call | solution.py:497
  40.6 0.7 spread.1
  41.3 1.6 %collective-permute-start.10 = (bf16[448,128]{1,0:T(8,128)(2,1)S(1)}, bf16[448,128]{1,0:T(8,128)(2,1)S(1)}, u32[]{:S(2)}, u32[]{:S(2)}) collective-permute-start(bf16[448,128]{1,0:T(8,128)(2,1)S(1)} %get-tuple-element.59), channel_id=1, source_target_pairs={{0,16},{8,24},{16,0},{24,8},{1,17},{9,25},{17,1},{25,9},{2,18},{10... | collective-permute-start | bytes 344072 | tf_op jit(solution)/shard_map/ppermute | solution.py:27
  42.9 1.4 %collective-permute-start.11 = (bf16[448,128]{1,0:T(8,128)(2,1)S(1)}, bf16[448,128]{1,0:T(8,128)(2,1)S(1)}, u32[]{:S(2)}, u32[]{:S(2)}) collective-permute-start(bf16[448,128]{1,0:T(8,128)(2,1)S(1)} %get-tuple-element.60), channel_id=1, source_target_pairs={{0,24},{8,16},{16,8},{24,0},{1,25},{9,17},{17,9},{25,1},{2,26},{10... | collective-permute-start | bytes 344072 | tf_op jit(solution)/shard_map/ppermute | solution.py:27
  44.4 0.5 collective-permute-start.9
  44.9 2.5 %conv.9 = (bf16[2,4,128,128]{3,2,1,0:T(8,128)(2,1)S(1)}, bf16[1,4,16,128,128]{4,3,2,1,0:T(8,128)(2,1)}) custom-call(s32[7]{0:T(128)S(1)} %stack.39.info_ref, f32[448,128]{1,0:T(8,128)S(1)} %get-tuple-element.53.after_ref.refs_0_, bf16[6,18,10,16,128]{4,3,2,1,0:T(8,128)(2,1)S(1)} %get-tuple-element.50.act_ref, ...), custom_call_target="tpu_custom_call", output_to_operand_aliasing={{1}: (7, {})} | custom-call | tf_op jit(solution)/shard_map/conv/pallas_call | solution.py:497
  47.4 2.0 %conv.10 = (bf16[2,4,128,128]{3,2,1,0:T(8,128)(2,1)S(1)}, bf16[1,4,16,128,128]{4,3,2,1,0:T(8,128)(2,1)}) custom-call(s32[7]{0:T(128)S(1)} %stack.39.info_ref, bf16[2,4,128,128]{3,2,1,0:T(8,128)(2,1)S(1)} %get-tuple-element.55.after_ref.refs_0_, bf16[6,18,10,16,128]{4,3,2,1,0:T(8,128)(2,1)S(1)} %get-tuple-element.50.act_ref, ...), custom_call_target="tpu_custom_call", output_to_operand_aliasing={{1}: (7, {})} | custom-call | tf_op jit(solution)/shard_map/conv/pallas_call | solution.py:497
  49.6 0.2 collective-permute-done.11.refs_3_
  49.9 0.6 collective-permute-done.9.refs_1_
  50.5 0.1 added.2.after_ref.refs_0_
  50.5 0.4 collective-permute-start.12
  51.0 1.4 %collective-permute-start.13 = (bf16[448,128]{1,0:T(8,128)(2,1)S(1)}, bf16[448,128]{1,0:T(8,128)(2,1)S(1)}, u32[]{:S(2)}, u32[]{:S(2)}) collective-permute-start(bf16[448,128]{1,0:T(8,128)(2,1)S(1)} %added.2.after_ref.refs_0_), channel_id=1, source_target_pairs={{0,2},{1,3},{2,0},{3,1},{4,6},{5,7},{6,4},{7,5},{8,10},{9,11},{10,... | collective-permute-start | bytes 344072 | tf_op jit(solution)/shard_map/ppermute | solution.py:27
  52.3 2.6 %collective-permute-start.14 = (bf16[448,128]{1,0:T(8,128)(2,1)S(1)}, bf16[448,128]{1,0:T(8,128)(2,1)S(1)}, u32[]{:S(2)}, u32[]{:S(2)}) collective-permute-start(bf16[448,128]{1,0:T(8,128)(2,1)S(1)} %added.2.after_ref.refs_0_), channel_id=1, source_target_pairs={{0,3},{1,2},{2,1},{3,0},{4,7},{5,6},{6,5},{7,4},{8,11},{9,10},{10,... | collective-permute-start | bytes 344072 | tf_op jit(solution)/shard_map/ppermute | solution.py:27
  55.0 2.0 %conv.11 = (bf16[2,4,128,128]{3,2,1,0:T(8,128)(2,1)S(1)}, bf16[1,4,16,128,128]{4,3,2,1,0:T(8,128)(2,1)}) custom-call(s32[7]{0:T(128)S(1)} %stack.39.info_ref, bf16[448,128]{1,0:T(8,128)(2,1)S(1)} %added.2.after_ref.refs_0_, bf16[6,18,10,16,128]{4,3,2,1,0:T(8,128)(2,1)S(1)} %get-tuple-element.50.act_ref, ...), custom_call_target="tpu_custom_call", output_to_operand_aliasing={{1}: (7, {})} | custom-call | tf_op jit(solution)/shard_map/conv/pallas_call | solution.py:497
  57.0 2.0 %conv.12 = (bf16[2,4,128,128]{3,2,1,0:T(8,128)(2,1)S(1)}, bf16[1,4,16,128,128]{4,3,2,1,0:T(8,128)(2,1)}) custom-call(s32[7]{0:T(128)S(1)} %stack.39.info_ref, bf16[2,4,128,128]{3,2,1,0:T(8,128)(2,1)S(1)} %get-tuple-element.62.after_ref.refs_0_, bf16[6,18,10,16,128]{4,3,2,1,0:T(8,128)(2,1)S(1)} %get-tuple-element.50.act_ref, ...), custom_call_target="tpu_custom_call", output_to_operand_aliasing={{1}: (7, {})} | custom-call | tf_op jit(solution)/shard_map/conv/pallas_call | solution.py:497
  59.0 2.0 %conv.13 = (bf16[2,4,128,128]{3,2,1,0:T(8,128)(2,1)S(1)}, bf16[1,4,16,128,128]{4,3,2,1,0:T(8,128)(2,1)}) custom-call(s32[7]{0:T(128)S(1)} %stack.39.info_ref, bf16[2,4,128,128]{3,2,1,0:T(8,128)(2,1)S(1)} %get-tuple-element.64.after_ref.refs_0_, bf16[6,18,10,16,128]{4,3,2,1,0:T(8,128)(2,1)S(1)} %get-tuple-element.50.act_ref, ...), custom_call_target="tpu_custom_call", output_to_operand_aliasing={{1}: (7, {})} | custom-call | tf_op jit(solution)/shard_map/conv/pallas_call | solution.py:497
  61.0 2.0 %conv.14 = (bf16[2,4,128,128]{3,2,1,0:T(8,128)(2,1)S(1)}, bf16[1,4,16,128,128]{4,3,2,1,0:T(8,128)(2,1)}) custom-call(s32[7]{0:T(128)S(1)} %stack.39.info_ref, bf16[2,4,128,128]{3,2,1,0:T(8,128)(2,1)S(1)} %get-tuple-element.66.after_ref.refs_0_, bf16[6,18,10,16,128]{4,3,2,1,0:T(8,128)(2,1)S(1)} %get-tuple-element.50.act_ref, ...), custom_call_target="tpu_custom_call", output_to_operand_aliasing={{1}: (7, {})} | custom-call | tf_op jit(solution)/shard_map/conv/pallas_call | solution.py:497
  63.0 0.1 added.3.after_ref.refs_0_
  63.1 1.6 %collective-permute-start.15 = (bf16[448,128]{1,0:T(8,128)(2,1)S(1)}, bf16[448,128]{1,0:T(8,128)(2,1)S(1)}, u32[]{:S(2)}, u32[]{:S(2)}) collective-permute-start(bf16[448,128]{1,0:T(8,128)(2,1)S(1)} %added.3.after_ref.refs_0_), channel_id=1, source_target_pairs={{0,16},{8,24},{16,0},{24,8},{1,17},{9,25},{17,1},{25,9},{2,18},{10... | collective-permute-start | bytes 344072 | tf_op jit(solution)/shard_map/ppermute | solution.py:27
  64.7 1.4 %collective-permute-start.16 = (bf16[448,128]{1,0:T(8,128)(2,1)S(1)}, bf16[448,128]{1,0:T(8,128)(2,1)S(1)}, u32[]{:S(2)}, u32[]{:S(2)}) collective-permute-start(bf16[448,128]{1,0:T(8,128)(2,1)S(1)} %added.3.after_ref.refs_0_), channel_id=1, source_target_pairs={{0,24},{8,16},{16,8},{24,0},{1,25},{9,17},{17,9},{25,1},{2,26},{10... | collective-permute-start | bytes 344072 | tf_op jit(solution)/shard_map/ppermute | solution.py:27
  66.1 0.6 collective-permute-start.20
  66.7 2.0 %collective-permute-done.15.refs_1_ = bf16[448,128]{1,0:T(8,128)(2,1)S(1)} collective-permute-done((bf16[448,128]{1,0:T(8,128)(2,1)S(1)}, bf16[448,128]{1,0:T(8,128)(2,1)S(1)}, u32[]{:S(2)}, u32[]{:S(2)}) %collective-permute-start.15) | collective-permute-done | bytes 114720 | tf_op jit(solution)/shard_map/ppermute | solution.py:27
  68.7 1.7 %collective-permute-done.16.refs_2_ = bf16[448,128]{1,0:T(8,128)(2,1)S(1)} collective-permute-done((bf16[448,128]{1,0:T(8,128)(2,1)S(1)}, bf16[448,128]{1,0:T(8,128)(2,1)S(1)}, u32[]{:S(2)}, u32[]{:S(2)}) %collective-permute-start.16) | collective-permute-done | bytes 114720 | tf_op jit(solution)/shard_map/ppermute | solution.py:27
  70.4 0.5 collective-permute-done.20.refs_6_
  70.9 2.0 %conv.15 = (bf16[2,4,128,128]{3,2,1,0:T(8,128)(2,1)S(1)}, bf16[1,4,16,128,128]{4,3,2,1,0:T(8,128)(2,1)}) custom-call(s32[7]{0:T(128)S(1)} %stack.39.info_ref, bf16[448,128]{1,0:T(8,128)(2,1)S(1)} %added.3.after_ref.refs_0_, bf16[6,18,10,16,128]{4,3,2,1,0:T(8,128)(2,1)S(1)} %get-tuple-element.50.act_ref, ...), custom_call_target="tpu_custom_call", output_to_operand_aliasing={{1}: (7, {})} | custom-call | tf_op jit(solution)/shard_map/conv/pallas_call | solution.py:497
  72.9 2.4 %collect.1 = (f32[1,128]{1,0:T(1,128)}, bf16[1,4,16,128,128]{4,3,2,1,0:T(8,128)(2,1)}, f32[8,432,128]{2,1,0:T(8,128)}) custom-call(s32[7]{0:T(128)S(1)} %stack.39.info_ref, bf16[448,128]{1,0:T(8,128)(2,1)S(1)} %added.3.after_ref.refs_0_, bf16[448,128]{1,0:T(8,128)(2,1)S(1)} %collective-permute-done.15.refs_1_, ...), custom_call_target="tpu_custom_call", output_to_operand_aliasing={{1}: (10, {})} | custom-call | tf_op jit(solution)/shard_map/collect/pallas_call | solution.py:574
  (26 shorter events, 0.1 us)
Async XLA Ops:
  4.3 23.1 %collective-permute-start = (bf16[1,2,16,128,128]{4,3,2,1,0:T(8,128)(2,1)S(1)}, bf16[1,2,16,128,128]{4,3,2,1,0:T(8,128)(2,1)S(1)}, u32[]{:S(2)}, u32[]{:S(2)}) collective-permute-start(bf16[1,2,16,128,128]{4,3,2,1,0:T(8,128)(2,1)S(1)} %get-tuple-element.45), channel_id=1, source_target_pairs={{0,4},{4,0},{1,5},{5,1},{2,6},{6,2},{3,7},{7,3},{8,12},{12,8},{9,1... | collective-permute-start | bytes 3145736 | tf_op jit(solution)/shard_map/ppermute | solution.py:398
  6.4 6.8 %collective-permute-start.1 = (bf16[4,128,128]{2,1,0:T(8,128)(2,1)S(1)}, bf16[4,128,128]{2,1,0:T(8,128)(2,1)S(1)}, u32[]{:S(2)}, u32[]{:S(2)}) collective-permute-start(bf16[4,128,128]{2,1,0:T(8,128)(2,1)S(1)} %get-tuple-element.46), channel_id=1, source_target_pairs={{0,1},{1,0},{2,3},{3,2},{4,5},{5,4},{6,7},{7,6},{8,9},{9,8},{10,11... | collective-permute-start | bytes 393224 | tf_op jit(solution)/shard_map/ppermute | solution.py:27
  9.0 4.2 %collective-permute-start.2 = (bf16[4,128,128]{2,1,0:T(8,128)(2,1)S(1)}, bf16[4,128,128]{2,1,0:T(8,128)(2,1)S(1)}, u32[]{:S(2)}, u32[]{:S(2)}) collective-permute-start(bf16[4,128,128]{2,1,0:T(8,128)(2,1)S(1)} %get-tuple-element.47), channel_id=1, source_target_pairs={{1,2},{2,1},{5,6},{6,5},{9,10},{10,9},{13,14},{14,13},{17,18},{18,... | collective-permute-start | bytes 393224 | tf_op jit(solution)/shard_map/ppermute | solution.py:381
  13.2 14.2 %collective-permute-start.3 = (bf16[4,128,128]{2,1,0:T(8,128)(2,1)S(1)}, bf16[4,128,128]{2,1,0:T(8,128)(2,1)S(1)}, u32[]{:S(2)}, u32[]{:S(2)}) collective-permute-start(bf16[4,128,128]{2,1,0:T(8,128)(2,1)S(1)} %collective-permute-done.1.near_ref), channel_id=1, source_target_pairs={{0,4},{4,0},{1,5},{5,1},{2,6},{6,2},{3,7},{7,3},{8,12},{12,8},{9,1... | collective-permute-start | bytes 393224 | tf_op jit(solution)/shard_map/ppermute | solution.py:416
  13.2 14.2 %collective-permute-start.4 = (bf16[4,128,128]{2,1,0:T(8,128)(2,1)S(1)}, bf16[4,128,128]{2,1,0:T(8,128)(2,1)S(1)}, u32[]{:S(2)}, u32[]{:S(2)}) collective-permute-start(bf16[4,128,128]{2,1,0:T(8,128)(2,1)S(1)} %collective-permute-done.2.refs_0_), channel_id=1, source_target_pairs={{0,4},{4,0},{1,5},{5,1},{2,6},{6,2},{3,7},{7,3},{8,12},{12,8},{9,1... | collective-permute-start | bytes 393224 | tf_op jit(solution)/shard_map/ppermute | solution.py:417
  13.7 1.2 %collective-permute-start.5 = (f32[3,8,128]{2,1,0:T(8,128)S(1)}, f32[3,8,128]{2,1,0:T(8,128)S(1)}, u32[]{:S(2)}, u32[]{:S(2)}) collective-permute-start(f32[3,8,128]{2,1,0:T(8,128)S(1)} %get-tuple-element.48.refs_0_), channel_id=1, source_target_pairs={{0,4},{4,0},{1,5},{5,1},{2,6},{6,2},{3,7},{7,3},{8,12},{12,8},{9,1... | collective-permute-start | bytes 36872 | tf_op jit(solution)/shard_map/ppermute | solution.py:27
  14.9 6.2 %collective-permute-start.6 = (f32[3,8,128]{2,1,0:T(8,128)S(1)}, f32[3,8,128]{2,1,0:T(8,128)S(1)}, u32[]{:S(2)}, u32[]{:S(2)}) collective-permute-start(f32[3,8,128]{2,1,0:T(8,128)S(1)} %merge.3.refs_0_.after_ref), channel_id=1, source_target_pairs={{0,1},{1,0},{2,3},{3,2},{4,5},{5,4},{6,7},{7,6},{8,9},{9,8},{10,11... | collective-permute-start | bytes 36872 | tf_op jit(solution)/shard_map/ppermute | solution.py:27
  21.1 6.3 %collective-permute-start.7 = (f32[3,8,128]{2,1,0:T(8,128)S(1)}, f32[3,8,128]{2,1,0:T(8,128)S(1)}, u32[]{:S(2)}, u32[]{:S(2)}) collective-permute-start(f32[3,8,128]{2,1,0:T(8,128)S(1)} %merge.4.refs_0_), channel_id=1, source_target_pairs={{0,2},{1,3},{2,0},{3,1},{4,6},{5,7},{6,4},{7,5},{8,10},{9,11},{10,... | collective-permute-start | bytes 36872 | tf_op jit(solution)/shard_map/ppermute | solution.py:27
  24.3 3.1 %copy-start.2 = (f32[128]{0:T(128)S(1)}, f32[128]{0:T(128)}, u32[]{:S(2)}) copy-start(f32[128]{0:T(128)} %param.9) | copy-start | bytes 1540
  24.3 3.1 %copy-start.3 = (f32[128]{0:T(128)S(1)}, f32[128]{0:T(128)}, u32[]{:S(2)}) copy-start(f32[128]{0:T(128)} %param.10) | copy-start | bytes 1540
  27.4 10.6 %copy-start = (bf16[3,3,3,128,128]{4,3,2,1,0:T(8,128)(2,1)S(1)}, bf16[3,3,3,128,128]{4,3,2,1,0:T(8,128)(2,1)}, u32[]{:S(2)}) copy-start(bf16[3,3,3,128,128]{4,3,2,1,0:T(8,128)(2,1)} %kernel_ref.1) | copy-start | bytes 2654212
  38.0 0.7 copy-start.1
  38.0 2.6 %collective-permute-start.8 = (f32[4,448,128]{2,1,0:T(8,128)S(1)}, f32[4,448,128]{2,1,0:T(8,128)S(1)}, u32[]{:S(2)}, u32[]{:S(2)}) collective-permute-start(f32[4,448,128]{2,1,0:T(8,128)S(1)} %get-tuple-element.52), channel_id=1, source_target_pairs={{0,4},{4,0},{1,5},{5,1},{2,6},{6,2},{3,7},{7,3},{8,12},{12,8},{9,1... | collective-permute-start | bytes 2752520 | tf_op jit(solution)/shard_map/ppermute | solution.py:27
  41.3 8.1 %collective-permute-start.10 = (bf16[448,128]{1,0:T(8,128)(2,1)S(1)}, bf16[448,128]{1,0:T(8,128)(2,1)S(1)}, u32[]{:S(2)}, u32[]{:S(2)}) collective-permute-start(bf16[448,128]{1,0:T(8,128)(2,1)S(1)} %get-tuple-element.59), channel_id=1, source_target_pairs={{0,16},{8,24},{16,0},{24,8},{1,17},{9,25},{17,1},{25,9},{2,18},{10... | collective-permute-start | bytes 344072 | tf_op jit(solution)/shard_map/ppermute | solution.py:27
  42.9 7.0 %collective-permute-start.11 = (bf16[448,128]{1,0:T(8,128)(2,1)S(1)}, bf16[448,128]{1,0:T(8,128)(2,1)S(1)}, u32[]{:S(2)}, u32[]{:S(2)}) collective-permute-start(bf16[448,128]{1,0:T(8,128)(2,1)S(1)} %get-tuple-element.60), channel_id=1, source_target_pairs={{0,24},{8,16},{16,8},{24,0},{1,25},{9,17},{17,9},{25,1},{2,26},{10... | collective-permute-start | bytes 344072 | tf_op jit(solution)/shard_map/ppermute | solution.py:27
  44.4 6.1 %collective-permute-start.9 = (bf16[448,128]{1,0:T(8,128)(2,1)S(1)}, bf16[448,128]{1,0:T(8,128)(2,1)S(1)}, u32[]{:S(2)}, u32[]{:S(2)}) collective-permute-start(bf16[448,128]{1,0:T(8,128)(2,1)S(1)} %get-tuple-element.58), channel_id=1, source_target_pairs={{0,8},{8,0},{16,24},{24,16},{1,9},{9,1},{17,25},{25,17},{2,10},{10... | collective-permute-start | bytes 344072 | tf_op jit(solution)/shard_map/ppermute | solution.py:27
  50.5 12.5 %collective-permute-start.12 = (bf16[448,128]{1,0:T(8,128)(2,1)S(1)}, bf16[448,128]{1,0:T(8,128)(2,1)S(1)}, u32[]{:S(2)}, u32[]{:S(2)}) collective-permute-start(bf16[448,128]{1,0:T(8,128)(2,1)S(1)} %added.2.after_ref.refs_0_), channel_id=1, source_target_pairs={{0,1},{1,0},{2,3},{3,2},{4,5},{5,4},{6,7},{7,6},{8,9},{9,8},{10,11... | collective-permute-start | bytes 344072 | tf_op jit(solution)/shard_map/ppermute | solution.py:27
  51.0 12.0 %collective-permute-start.13 = (bf16[448,128]{1,0:T(8,128)(2,1)S(1)}, bf16[448,128]{1,0:T(8,128)(2,1)S(1)}, u32[]{:S(2)}, u32[]{:S(2)}) collective-permute-start(bf16[448,128]{1,0:T(8,128)(2,1)S(1)} %added.2.after_ref.refs_0_), channel_id=1, source_target_pairs={{0,2},{1,3},{2,0},{3,1},{4,6},{5,7},{6,4},{7,5},{8,10},{9,11},{10,... | collective-permute-start | bytes 344072 | tf_op jit(solution)/shard_map/ppermute | solution.py:27
  52.3 10.7 %collective-permute-start.14 = (bf16[448,128]{1,0:T(8,128)(2,1)S(1)}, bf16[448,128]{1,0:T(8,128)(2,1)S(1)}, u32[]{:S(2)}, u32[]{:S(2)}) collective-permute-start(bf16[448,128]{1,0:T(8,128)(2,1)S(1)} %added.2.after_ref.refs_0_), channel_id=1, source_target_pairs={{0,3},{1,2},{2,1},{3,0},{4,7},{5,6},{6,5},{7,4},{8,11},{9,10},{10,... | collective-permute-start | bytes 344072 | tf_op jit(solution)/shard_map/ppermute | solution.py:27
  63.1 5.6 %collective-permute-start.15 = (bf16[448,128]{1,0:T(8,128)(2,1)S(1)}, bf16[448,128]{1,0:T(8,128)(2,1)S(1)}, u32[]{:S(2)}, u32[]{:S(2)}) collective-permute-start(bf16[448,128]{1,0:T(8,128)(2,1)S(1)} %added.3.after_ref.refs_0_), channel_id=1, source_target_pairs={{0,16},{8,24},{16,0},{24,8},{1,17},{9,25},{17,1},{25,9},{2,18},{10... | collective-permute-start | bytes 344072 | tf_op jit(solution)/shard_map/ppermute | solution.py:27
  64.7 5.7 %collective-permute-start.16 = (bf16[448,128]{1,0:T(8,128)(2,1)S(1)}, bf16[448,128]{1,0:T(8,128)(2,1)S(1)}, u32[]{:S(2)}, u32[]{:S(2)}) collective-permute-start(bf16[448,128]{1,0:T(8,128)(2,1)S(1)} %added.3.after_ref.refs_0_), channel_id=1, source_target_pairs={{0,24},{8,16},{16,8},{24,0},{1,25},{9,17},{17,9},{25,1},{2,26},{10... | collective-permute-start | bytes 344072 | tf_op jit(solution)/shard_map/ppermute | solution.py:27
  66.1 4.8 %collective-permute-start.20 = (bf16[448,128]{1,0:T(8,128)(2,1)S(1)}, bf16[448,128]{1,0:T(8,128)(2,1)S(1)}, u32[]{:S(2)}, u32[]{:S(2)}) collective-permute-start(bf16[448,128]{1,0:T(8,128)(2,1)S(1)} %added.3.after_ref.refs_0_), channel_id=1, source_target_pairs={{0,8},{8,0},{16,24},{24,16},{1,9},{9,1},{17,25},{25,17},{2,10},{10... | collective-permute-start | bytes 344072 | tf_op jit(solution)/shard_map/ppermute | solution.py:27
  66.7 6.2 %collective-permute-start.17 = (bf16[448,128]{1,0:T(8,128)(2,1)S(1)}, bf16[448,128]{1,0:T(8,128)(2,1)S(1)}, u32[]{:S(2)}, u32[]{:S(2)}) collective-permute-start(bf16[448,128]{1,0:T(8,128)(2,1)S(1)} %added.3.after_ref.refs_0_), channel_id=1, source_target_pairs={{0,4},{4,0},{1,5},{5,1},{2,6},{6,2},{3,7},{7,3},{8,12},{12,8},{9,1... | collective-permute-start | bytes 344072 | tf_op jit(solution)/shard_map/ppermute | solution.py:27
  68.7 4.2 %collective-permute-start.18 = (bf16[448,128]{1,0:T(8,128)(2,1)S(1)}, bf16[448,128]{1,0:T(8,128)(2,1)S(1)}, u32[]{:S(2)}, u32[]{:S(2)}) collective-permute-start(bf16[448,128]{1,0:T(8,128)(2,1)S(1)} %collective-permute-done.15.refs_1_), channel_id=1, source_target_pairs={{0,4},{4,0},{1,5},{5,1},{2,6},{6,2},{3,7},{7,3},{8,12},{12,8},{9,1... | collective-permute-start | bytes 344072 | tf_op jit(solution)/shard_map/ppermute | solution.py:27
  70.4 2.6 %collective-permute-start.19 = (bf16[448,128]{1,0:T(8,128)(2,1)S(1)}, bf16[448,128]{1,0:T(8,128)(2,1)S(1)}, u32[]{:S(2)}, u32[]{:S(2)}) collective-permute-start(bf16[448,128]{1,0:T(8,128)(2,1)S(1)} %collective-permute-done.16.refs_2_), channel_id=1, source_target_pairs={{0,4},{4,0},{1,5},{5,1},{2,6},{6,2},{3,7},{7,3},{8,12},{12,8},{9,1... | collective-permute-start | bytes 344072 | tf_op jit(solution)/shard_map/ppermute | solution.py:27
  70.9 2.0 %collective-permute-start.21 = (bf16[448,128]{1,0:T(8,128)(2,1)S(1)}, bf16[448,128]{1,0:T(8,128)(2,1)S(1)}, u32[]{:S(2)}, u32[]{:S(2)}) collective-permute-start(bf16[448,128]{1,0:T(8,128)(2,1)S(1)} %collective-permute-done.20.refs_6_), channel_id=1, source_target_pairs={{0,4},{4,0},{1,5},{5,1},{2,6},{6,2},{3,7},{7,3},{8,12},{12,8},{9,1... | collective-permute-start | bytes 344072 | tf_op jit(solution)/shard_map/ppermute | solution.py:27

commit v11 on v10

--- a/solution.py
+++ b/solution.py
@@ -149,10 +149,10 @@
 
 
 def weights_kernel(
-    per, info_ref, turned_0, turned_1, bias_0, bias_1, video_ref, early_ref, near_ref, *refs
+    parts_n, per, info_ref, turned_0, turned_1, bias_0, bias_1, video_ref, early_ref, near_ref, *refs
 ):
     far_ref, near_early_ref, far_early_ref, gain_ref, shift_ref, *refs = refs
-    stats_ref, act_ref, keep_ref, *send_refs = refs[:-3]
+    parts, (act_ref, keep_ref, *send_refs) = refs[:parts_n], refs[parts_n:-3]
     wide, acc, shards = refs[-3:]
     ahead = turned_0.shape[0]
     frames, rows, cols, chans = video_ref.shape[1:]
@@ -160,7 +160,7 @@
     step = cols // TILE
     slots = wide.shape[0]
     inside, first, has_low, has_high = info_ref[0], info_ref[1], info_ref[2], info_ref[3]
-    count, total, squares = stats_ref[0], stats_ref[1], stats_ref[2]
+    count, total, squares = merged([ref[...] for ref in parts])
     every = jnp.sum(count, axis=0, keepdims=True) * per
     mean = group_sum(jnp.sum(total, axis=0, keepdims=True), per) / every
     away = total / jnp.maximum(count, 1.0) - mean
@@ -407,12 +407,8 @@
             name="merge",
         )(*arrays)
 
-    stats = core_stats = together(gathered)
-    by = 1
-    while by < spaces:
-        other = swap(stats, "space", by)
-        stats = together([stats, other])
-        by *= 2
+    stats = together(gathered)
+    parts = [stats] + [swap(stats, "space", r) for r in range(1, spaces)]
     near_early = lax.ppermute(near, "tm", following)
     far_early = lax.ppermute(far, "tm", following)
     pair = 2
@@ -425,7 +421,7 @@
         ),
         compiler_params=params(2),
         name="taps",
-    )(core_stats, kernel)
+    )(stats, kernel)
 
     ahead = frames // 2
     turned, bias = [], []
@@ -451,8 +447,8 @@
     shard = count // shards_n
     full = shard + TILE
     act, keep, *sends = pl.pallas_call(
-        functools.partial(weights_kernel, per),
-        in_specs=[SMEM] + [VMEM] * 13,
+        functools.partial(weights_kernel, spaces, per),
+        in_specs=[SMEM] + [VMEM] * (12 + spaces),
         out_specs=[VMEM] * (1 + tms),
         out_shape=[
             jax.ShapeDtypeStruct((frames + before, rows + 2, step + 2, TILE, chans), BF16)
@@ -477,7 +473,7 @@
         far_early,
         norm_gain.reshape(1, chans),
         norm_shift.reshape(1, chans),
-        stats,
+        *parts,
     )
 
     block = 4

time: 75.7 us -> 74.9 us (0.989)
  waiting for transfers between devices: 11.4 us -> 9.94 us
  starting transfers between devices: 23.8 us -> 24.6 us
    ppermute x18 -> x19, waiting for transfers between devices: 11.4 us -> 9.93 us  [swap(): return lax.ppermute(array, axis, [(i, i ^ by) for i in range(length)])]
    ppermute x18 -> x19, starting transfers between devices: 22 us -> 22.9 us  [swap(): return lax.ppermute(array, axis, [(i, i ^ by) for i in range(length)])]
  transfers between devices with their start and end apart: 22 -> 23, of which waited for: 8 -> 7; matrix products, arithmetic and copies ran while one was open for 0% -> 0% of each run, Pallas kernels for 28% -> 29%
where the time goes in v11:
time: 74.9 us; the launch traced here: 74.7 us
  Pallas kernels  37.8 us (50%)
  starting transfers between devices  24.6 us (33%)
  waiting for transfers between devices  9.94 us (13%)
  between operations  1.99 us (3%)
    ppermute x19, starting transfers between devices, swap(): return lax.ppermute(array, axis, [(i, i ^ by) for i in range(length)])  22.9 us
    pallas_call x8, Pallas kernels, cover(): pl.pallas_call(functools.partial(conv_kernel, pieces[n], where(n - 1) if...  16.4 us
    pallas_call x1, Pallas kernels, step_of(): pl.pallas_call(functools.partial(weights_kernel, spaces, per), in_specs=[...  10.4 us
    ppermute x19, waiting for transfers between devices, swap(): return lax.ppermute(array, axis, [(i, i ^ by) for i in range(length)])  9.93 us
    pallas_call x2, Pallas kernels, step_of(): pl.pallas_call(functools.partial(cotangent_kernel, n * ahead), in_specs=[...  3.01 us
    pallas_call x1, Pallas kernels, step_of(): pl.pallas_call(functools.partial(stats_kernel, before), in_specs=[SMEM, A...  2.89 us
    pallas_call x1, Pallas kernels, step_of(): pl.pallas_call(collect, in_specs=[SMEM] + [VMEM] * (len(order) + 1) + [AN...  2.43 us
    pallas_call x1, Pallas kernels, step_of(): pl.pallas_call(ends_kernel, in_specs=[SMEM, ANY], out_specs=[VMEM, VMEM],...  1.53 us
  transfers between devices with their start and end apart: 23, of which 7 were waited for; matrix products, arithmetic and copies ran while one was open for 0% of the time, Pallas kernels for 29%

profile of v11, /device:TPU:0, one launch (start us, length us, event | category | flops | bytes accessed | tf_op | source)
XLA Modules:
  0.0 74.7 jit_solution(16435215692921295983)
XLA Ops:
  1.3 0.1 stack.39.info_ref
  1.4 2.9 %stats.1 = (f32[3,8,128]{2,1,0:T(8,128)S(1)}, bf16[1,4,16,128,128]{4,3,2,1,0:T(8,128)(2,1)S(1)}, bf16[1,4,16,128,128]{4,3,2,1,0:T(8,128)(2,1)S(1)}, bf16[1,2,16,128,128]{4,3,2,1,0:T(8,128)(2,1)S(1)}) custom-call(s32[7]{0:T(128)S(1)} %stack.39.info_ref, bf16[1,4,16,128,128]{4,3,2,1,0:T(8,128)(2,1)} %video_hbm.3, bf16[1,4,16,128,128]{4,3,2,1,0:T(8,128)(2,1)} %cot_hbm.1), custom_call_target="tpu_custom_call" | custom-call | tf_op jit(solution)/shard_map/stats/pallas_call | solution.py:382
  4.3 0.6 collective-permute-start
  4.8 1.5 %ends.1 = (bf16[4,128,128]{2,1,0:T(8,128)(2,1)S(1)}, bf16[4,128,128]{2,1,0:T(8,128)(2,1)S(1)}) custom-call(s32[7]{0:T(128)S(1)} %stack.39.info_ref, bf16[1,4,16,128,128]{4,3,2,1,0:T(8,128)(2,1)} %video_hbm.3), custom_call_target="tpu_custom_call" | custom-call | tf_op jit(solution)/shard_map/ends/pallas_call | solution.py:370
  6.4 2.6 %collective-permute-start.1 = (bf16[4,128,128]{2,1,0:T(8,128)(2,1)S(1)}, bf16[4,128,128]{2,1,0:T(8,128)(2,1)S(1)}, u32[]{:S(2)}, u32[]{:S(2)}) collective-permute-start(bf16[4,128,128]{2,1,0:T(8,128)(2,1)S(1)} %get-tuple-element.46), channel_id=1, source_target_pairs={{0,1},{1,0},{2,3},{3,2},{4,5},{5,4},{6,7},{7,6},{8,9},{9,8},{10,11... | collective-permute-start | bytes 393224 | tf_op jit(solution)/shard_map/ppermute | solution.py:27
  9.0 0.7 collective-permute-start.2
  9.7 3.5 %collective-permute-done.1.near_ref = bf16[4,128,128]{2,1,0:T(8,128)(2,1)S(1)} collective-permute-done((bf16[4,128,128]{2,1,0:T(8,128)(2,1)S(1)}, bf16[4,128,128]{2,1,0:T(8,128)(2,1)S(1)}, u32[]{:S(2)}, u32[]{:S(2)}) %collective-permute-start.1) | collective-permute-done | bytes 131104 | tf_op jit(solution)/shard_map/ppermute | solution.py:27
  13.2 0.5 collective-permute-start.4
  13.7 0.0 collective-permute-start.5
  13.7 1.2 %collective-permute-done.5.refs_1_ = f32[3,8,128]{2,1,0:T(8,128)S(1)} collective-permute-done((f32[3,8,128]{2,1,0:T(8,128)S(1)}, f32[3,8,128]{2,1,0:T(8,128)S(1)}, u32[]{:S(2)}, u32[]{:S(2)}) %collective-permute-start.5) | collective-permute-done | bytes 12320 | tf_op jit(solution)/shard_map/ppermute | solution.py:27
  14.9 4.5 %collective-permute-start.6 = (f32[3,8,128]{2,1,0:T(8,128)S(1)}, f32[3,8,128]{2,1,0:T(8,128)S(1)}, u32[]{:S(2)}, u32[]{:S(2)}) collective-permute-start(f32[3,8,128]{2,1,0:T(8,128)S(1)} %merge.1.refs_5_.after_ref), channel_id=1, source_target_pairs={{0,1},{1,0},{2,3},{3,2},{4,5},{5,4},{6,7},{7,6},{8,9},{9,8},{10,11... | collective-permute-start | bytes 36872 | tf_op jit(solution)/shard_map/ppermute | solution.py:27
  19.4 1.2 %collective-permute-start.7 = (f32[3,8,128]{2,1,0:T(8,128)S(1)}, f32[3,8,128]{2,1,0:T(8,128)S(1)}, u32[]{:S(2)}, u32[]{:S(2)}) collective-permute-start(f32[3,8,128]{2,1,0:T(8,128)S(1)} %merge.1.refs_5_.after_ref), channel_id=1, source_target_pairs={{0,2},{1,3},{2,0},{3,1},{4,6},{5,7},{6,4},{7,5},{8,10},{9,11},{10,... | collective-permute-start | bytes 36872 | tf_op jit(solution)/shard_map/ppermute | solution.py:27
  20.6 0.4 collective-permute-done.6.refs_6_
  21.0 2.6 %collective-permute-start.8 = (f32[3,8,128]{2,1,0:T(8,128)S(1)}, f32[3,8,128]{2,1,0:T(8,128)S(1)}, u32[]{:S(2)}, u32[]{:S(2)}) collective-permute-start(f32[3,8,128]{2,1,0:T(8,128)S(1)} %merge.1.refs_5_.after_ref), channel_id=1, source_target_pairs={{0,3},{1,2},{2,1},{3,0},{4,7},{5,6},{6,5},{7,4},{8,11},{9,10},{10,... | collective-permute-start | bytes 36872 | tf_op jit(solution)/shard_map/ppermute | solution.py:27
  23.7 1.5 %cotangent.3 = (bf16[2,16,128,128]{3,2,1,0:T(8,128)(2,1)S(1)}, f32[8,128]{1,0:T(8,128)S(1)}) custom-call(s32[7]{0:T(128)S(1)} %stack.39.info_ref, bf16[1,4,16,128,128]{4,3,2,1,0:T(8,128)(2,1)S(1)} %get-tuple-element.39.cot_ref), custom_call_target="tpu_custom_call" | custom-call | tf_op jit(solution)/shard_map/cotangent/pallas_call | solution.py:429
  25.2 1.5 %cotangent.2 = (bf16[2,16,128,128]{3,2,1,0:T(8,128)(2,1)S(1)}, f32[8,128]{1,0:T(8,128)S(1)}) custom-call(s32[7]{0:T(128)S(1)} %stack.39.info_ref, bf16[1,4,16,128,128]{4,3,2,1,0:T(8,128)(2,1)S(1)} %get-tuple-element.39.cot_ref), custom_call_target="tpu_custom_call" | custom-call | tf_op jit(solution)/shard_map/cotangent/pallas_call | solution.py:429
  26.8 0.0 copy-start
  26.8 10.4 %weights.1 = (bf16[6,18,10,16,128]{4,3,2,1,0:T(8,128)(2,1)S(1)}, f32[4,448,128]{2,1,0:T(8,128)S(1)}, f32[4,448,128]{2,1,0:T(8,128)S(1)}) custom-call(s32[7]{0:T(128)S(1)} %stack.39.info_ref, bf16[2,16,128,128]{3,2,1,0:T(8,128)(2,1)S(1)} %get-tuple-element.40.turned_0, bf16[2,16,128,128]{3,2,1,0:T(8,128)(2,1)S(1)} %get-tuple-element.41.turned_1, ...), custom_call_target="tpu_custom_call" | custom-call | tf_op jit(solution)/shard_map/weights/pallas_call | solution.py:449
  37.2 0.0 copy-start.1
  37.2 0.1 collective-permute-start.9
  37.3 0.4 taps.1.taps_ref
  37.7 0.2 copy-done.1
  37.9 2.0 %conv.8 = (bf16[2,4,128,128]{3,2,1,0:T(8,128)(2,1)S(1)}, bf16[1,4,16,128,128]{4,3,2,1,0:T(8,128)(2,1)}) custom-call(s32[7]{0:T(128)S(1)} %stack.39.info_ref, f32[4,448,128]{2,1,0:T(8,128)S(1)} %get-tuple-element.49.after_ref.keep_ref, bf16[6,18,10,16,128]{4,3,2,1,0:T(8,128)(2,1)S(1)} %get-tuple-element.50.act_ref, bf16[4608,256]{1,0:T(8,128)(2,1)S(1)} %taps.1.taps_ref, ...), custom_call_target="tpu_custom_call" | custom-call | tf_op jit(solution)/shard_map/conv/pallas_call | solution.py:493
  39.9 0.6 spread.1
  40.5 1.6 %collective-permute-start.10 = (bf16[448,128]{1,0:T(8,128)(2,1)S(1)}, bf16[448,128]{1,0:T(8,128)(2,1)S(1)}, u32[]{:S(2)}, u32[]{:S(2)}) collective-permute-start(bf16[448,128]{1,0:T(8,128)(2,1)S(1)} %get-tuple-element.58), channel_id=1, source_target_pairs={{0,8},{8,0},{16,24},{24,16},{1,9},{9,1},{17,25},{25,17},{2,10},{10... | collective-permute-start | bytes 344072 | tf_op jit(solution)/shard_map/ppermute | solution.py:27
  42.1 1.5 %collective-permute-start.11 = (bf16[448,128]{1,0:T(8,128)(2,1)S(1)}, bf16[448,128]{1,0:T(8,128)(2,1)S(1)}, u32[]{:S(2)}, u32[]{:S(2)}) collective-permute-start(bf16[448,128]{1,0:T(8,128)(2,1)S(1)} %get-tuple-element.59), channel_id=1, source_target_pairs={{0,16},{8,24},{16,0},{24,8},{1,17},{9,25},{17,1},{25,9},{2,18},{10... | collective-permute-start | bytes 344072 | tf_op jit(solution)/shard_map/ppermute | solution.py:27
  43.6 0.5 collective-permute-start.12
  44.1 2.5 %conv.9 = (bf16[2,4,128,128]{3,2,1,0:T(8,128)(2,1)S(1)}, bf16[1,4,16,128,128]{4,3,2,1,0:T(8,128)(2,1)}) custom-call(s32[7]{0:T(128)S(1)} %stack.39.info_ref, f32[448,128]{1,0:T(8,128)S(1)} %get-tuple-element.53.after_ref.refs_0_, bf16[6,18,10,16,128]{4,3,2,1,0:T(8,128)(2,1)S(1)} %get-tuple-element.50.act_ref, ...), custom_call_target="tpu_custom_call", output_to_operand_aliasing={{1}: (7, {})} | custom-call | tf_op jit(solution)/shard_map/conv/pallas_call | solution.py:493
  46.6 2.0 %conv.10 = (bf16[2,4,128,128]{3,2,1,0:T(8,128)(2,1)S(1)}, bf16[1,4,16,128,128]{4,3,2,1,0:T(8,128)(2,1)}) custom-call(s32[7]{0:T(128)S(1)} %stack.39.info_ref, bf16[2,4,128,128]{3,2,1,0:T(8,128)(2,1)S(1)} %get-tuple-element.55.after_ref.refs_0_, bf16[6,18,10,16,128]{4,3,2,1,0:T(8,128)(2,1)S(1)} %get-tuple-element.50.act_ref, ...), custom_call_target="tpu_custom_call", output_to_operand_aliasing={{1}: (7, {})} | custom-call | tf_op jit(solution)/shard_map/conv/pallas_call | solution.py:493
  48.8 0.8 %collective-permute-done.11.refs_2_ = bf16[448,128]{1,0:T(8,128)(2,1)S(1)} collective-permute-done((bf16[448,128]{1,0:T(8,128)(2,1)S(1)}, bf16[448,128]{1,0:T(8,128)(2,1)S(1)}, u32[]{:S(2)}, u32[]{:S(2)}) %collective-permute-start.11) | collective-permute-done | bytes 114720 | tf_op jit(solution)/shard_map/ppermute | solution.py:27
  49.6 0.1 added.2.after_ref.refs_0_
  49.7 1.2 %collective-permute-start.13 = (bf16[448,128]{1,0:T(8,128)(2,1)S(1)}, bf16[448,128]{1,0:T(8,128)(2,1)S(1)}, u32[]{:S(2)}, u32[]{:S(2)}) collective-permute-start(bf16[448,128]{1,0:T(8,128)(2,1)S(1)} %added.2.after_ref.refs_0_), channel_id=1, source_target_pairs={{0,1},{1,0},{2,3},{3,2},{4,5},{5,4},{6,7},{7,6},{8,9},{9,8},{10,11... | collective-permute-start | bytes 344072 | tf_op jit(solution)/shard_map/ppermute | solution.py:27
  50.9 1.9 %collective-permute-start.14 = (bf16[448,128]{1,0:T(8,128)(2,1)S(1)}, bf16[448,128]{1,0:T(8,128)(2,1)S(1)}, u32[]{:S(2)}, u32[]{:S(2)}) collective-permute-start(bf16[448,128]{1,0:T(8,128)(2,1)S(1)} %added.2.after_ref.refs_0_), channel_id=1, source_target_pairs={{0,2},{1,3},{2,0},{3,1},{4,6},{5,7},{6,4},{7,5},{8,10},{9,11},{10,... | collective-permute-start | bytes 344072 | tf_op jit(solution)/shard_map/ppermute | solution.py:27
  52.8 1.4 %collective-permute-start.15 = (bf16[448,128]{1,0:T(8,128)(2,1)S(1)}, bf16[448,128]{1,0:T(8,128)(2,1)S(1)}, u32[]{:S(2)}, u32[]{:S(2)}) collective-permute-start(bf16[448,128]{1,0:T(8,128)(2,1)S(1)} %added.2.after_ref.refs_0_), channel_id=1, source_target_pairs={{0,3},{1,2},{2,1},{3,0},{4,7},{5,6},{6,5},{7,4},{8,11},{9,10},{10,... | collective-permute-start | bytes 344072 | tf_op jit(solution)/shard_map/ppermute | solution.py:27
  54.2 2.0 %conv.11 = (bf16[2,4,128,128]{3,2,1,0:T(8,128)(2,1)S(1)}, bf16[1,4,16,128,128]{4,3,2,1,0:T(8,128)(2,1)}) custom-call(s32[7]{0:T(128)S(1)} %stack.39.info_ref, bf16[448,128]{1,0:T(8,128)(2,1)S(1)} %added.2.after_ref.refs_0_, bf16[6,18,10,16,128]{4,3,2,1,0:T(8,128)(2,1)S(1)} %get-tuple-element.50.act_ref, ...), custom_call_target="tpu_custom_call", output_to_operand_aliasing={{1}: (7, {})} | custom-call | tf_op jit(solution)/shard_map/conv/pallas_call | solution.py:493
  56.1 2.0 %conv.12 = (bf16[2,4,128,128]{3,2,1,0:T(8,128)(2,1)S(1)}, bf16[1,4,16,128,128]{4,3,2,1,0:T(8,128)(2,1)}) custom-call(s32[7]{0:T(128)S(1)} %stack.39.info_ref, bf16[2,4,128,128]{3,2,1,0:T(8,128)(2,1)S(1)} %get-tuple-element.62.after_ref.refs_0_, bf16[6,18,10,16,128]{4,3,2,1,0:T(8,128)(2,1)S(1)} %get-tuple-element.50.act_ref, ...), custom_call_target="tpu_custom_call", output_to_operand_aliasing={{1}: (7, {})} | custom-call | tf_op jit(solution)/shard_map/conv/pallas_call | solution.py:493
  58.1 2.0 %conv.13 = (bf16[2,4,128,128]{3,2,1,0:T(8,128)(2,1)S(1)}, bf16[1,4,16,128,128]{4,3,2,1,0:T(8,128)(2,1)}) custom-call(s32[7]{0:T(128)S(1)} %stack.39.info_ref, bf16[2,4,128,128]{3,2,1,0:T(8,128)(2,1)S(1)} %get-tuple-element.64.after_ref.refs_0_, bf16[6,18,10,16,128]{4,3,2,1,0:T(8,128)(2,1)S(1)} %get-tuple-element.50.act_ref, ...), custom_call_target="tpu_custom_call", output_to_operand_aliasing={{1}: (7, {})} | custom-call | tf_op jit(solution)/shard_map/conv/pallas_call | solution.py:493
  60.1 2.0 %conv.14 = (bf16[2,4,128,128]{3,2,1,0:T(8,128)(2,1)S(1)}, bf16[1,4,16,128,128]{4,3,2,1,0:T(8,128)(2,1)}) custom-call(s32[7]{0:T(128)S(1)} %stack.39.info_ref, bf16[2,4,128,128]{3,2,1,0:T(8,128)(2,1)S(1)} %get-tuple-element.66.after_ref.refs_0_, bf16[6,18,10,16,128]{4,3,2,1,0:T(8,128)(2,1)S(1)} %get-tuple-element.50.act_ref, ...), custom_call_target="tpu_custom_call", output_to_operand_aliasing={{1}: (7, {})} | custom-call | tf_op jit(solution)/shard_map/conv/pallas_call | solution.py:493
  62.2 0.1 added.3.after_ref.refs_0_
  62.2 1.6 %collective-permute-start.16 = (bf16[448,128]{1,0:T(8,128)(2,1)S(1)}, bf16[448,128]{1,0:T(8,128)(2,1)S(1)}, u32[]{:S(2)}, u32[]{:S(2)}) collective-permute-start(bf16[448,128]{1,0:T(8,128)(2,1)S(1)} %added.3.after_ref.refs_0_), channel_id=1, source_target_pairs={{0,16},{8,24},{16,0},{24,8},{1,17},{9,25},{17,1},{25,9},{2,18},{10... | collective-permute-start | bytes 344072 | tf_op jit(solution)/shard_map/ppermute | solution.py:27
  63.8 1.2 %collective-permute-start.17 = (bf16[448,128]{1,0:T(8,128)(2,1)S(1)}, bf16[448,128]{1,0:T(8,128)(2,1)S(1)}, u32[]{:S(2)}, u32[]{:S(2)}) collective-permute-start(bf16[448,128]{1,0:T(8,128)(2,1)S(1)} %added.3.after_ref.refs_0_), channel_id=1, source_target_pairs={{0,24},{8,16},{16,8},{24,0},{1,25},{9,17},{17,9},{25,1},{2,26},{10... | collective-permute-start | bytes 344072 | tf_op jit(solution)/shard_map/ppermute | solution.py:27
  65.0 0.8 %collective-permute-start.21 = (bf16[448,128]{1,0:T(8,128)(2,1)S(1)}, bf16[448,128]{1,0:T(8,128)(2,1)S(1)}, u32[]{:S(2)}, u32[]{:S(2)}) collective-permute-start(bf16[448,128]{1,0:T(8,128)(2,1)S(1)} %added.3.after_ref.refs_0_), channel_id=1, source_target_pairs={{0,8},{8,0},{16,24},{24,16},{1,9},{9,1},{17,25},{25,17},{2,10},{10... | collective-permute-start | bytes 344072 | tf_op jit(solution)/shard_map/ppermute | solution.py:27
  65.8 2.0 %collective-permute-done.16.refs_1_ = bf16[448,128]{1,0:T(8,128)(2,1)S(1)} collective-permute-done((bf16[448,128]{1,0:T(8,128)(2,1)S(1)}, bf16[448,128]{1,0:T(8,128)(2,1)S(1)}, u32[]{:S(2)}, u32[]{:S(2)}) %collective-permute-start.16) | collective-permute-done | bytes 114720 | tf_op jit(solution)/shard_map/ppermute | solution.py:27
  67.8 1.7 %collective-permute-done.17.refs_2_ = bf16[448,128]{1,0:T(8,128)(2,1)S(1)} collective-permute-done((bf16[448,128]{1,0:T(8,128)(2,1)S(1)}, bf16[448,128]{1,0:T(8,128)(2,1)S(1)}, u32[]{:S(2)}, u32[]{:S(2)}) %collective-permute-start.17) | collective-permute-done | bytes 114720 | tf_op jit(solution)/shard_map/ppermute | solution.py:27
  69.5 0.3 collective-permute-done.21.refs_6_
  69.8 0.2 collective-permute-start.22
  70.0 2.0 %conv.15 = (bf16[2,4,128,128]{3,2,1,0:T(8,128)(2,1)S(1)}, bf16[1,4,16,128,128]{4,3,2,1,0:T(8,128)(2,1)}) custom-call(s32[7]{0:T(128)S(1)} %stack.39.info_ref, bf16[448,128]{1,0:T(8,128)(2,1)S(1)} %added.3.after_ref.refs_0_, bf16[6,18,10,16,128]{4,3,2,1,0:T(8,128)(2,1)S(1)} %get-tuple-element.50.act_ref, ...), custom_call_target="tpu_custom_call", output_to_operand_aliasing={{1}: (7, {})} | custom-call | tf_op jit(solution)/shard_map/conv/pallas_call | solution.py:493
  72.1 2.4 %collect.1 = (f32[1,128]{1,0:T(1,128)}, bf16[1,4,16,128,128]{4,3,2,1,0:T(8,128)(2,1)}, f32[8,432,128]{2,1,0:T(8,128)}) custom-call(s32[7]{0:T(128)S(1)} %stack.39.info_ref, bf16[448,128]{1,0:T(8,128)(2,1)S(1)} %added.3.after_ref.refs_0_, bf16[448,128]{1,0:T(8,128)(2,1)S(1)} %collective-permute-done.16.refs_1_, ...), custom_call_target="tpu_custom_call", output_to_operand_aliasing={{1}: (10, {})} | custom-call | tf_op jit(solution)/shard_map/collect/pallas_call | solution.py:570
  (26 shorter events, 0.1 us)
Async XLA Ops:
  4.3 22.5 %collective-permute-start = (bf16[1,2,16,128,128]{4,3,2,1,0:T(8,128)(2,1)S(1)}, bf16[1,2,16,128,128]{4,3,2,1,0:T(8,128)(2,1)S(1)}, u32[]{:S(2)}, u32[]{:S(2)}) collective-permute-start(bf16[1,2,16,128,128]{4,3,2,1,0:T(8,128)(2,1)S(1)} %get-tuple-element.45), channel_id=1, source_target_pairs={{0,4},{4,0},{1,5},{5,1},{2,6},{6,2},{3,7},{7,3},{8,12},{12,8},{9,1... | collective-permute-start | bytes 3145736 | tf_op jit(solution)/shard_map/ppermute | solution.py:398
  6.4 6.8 %collective-permute-start.1 = (bf16[4,128,128]{2,1,0:T(8,128)(2,1)S(1)}, bf16[4,128,128]{2,1,0:T(8,128)(2,1)S(1)}, u32[]{:S(2)}, u32[]{:S(2)}) collective-permute-start(bf16[4,128,128]{2,1,0:T(8,128)(2,1)S(1)} %get-tuple-element.46), channel_id=1, source_target_pairs={{0,1},{1,0},{2,3},{3,2},{4,5},{5,4},{6,7},{7,6},{8,9},{9,8},{10,11... | collective-permute-start | bytes 393224 | tf_op jit(solution)/shard_map/ppermute | solution.py:27
  9.0 4.2 %collective-permute-start.2 = (bf16[4,128,128]{2,1,0:T(8,128)(2,1)S(1)}, bf16[4,128,128]{2,1,0:T(8,128)(2,1)S(1)}, u32[]{:S(2)}, u32[]{:S(2)}) collective-permute-start(bf16[4,128,128]{2,1,0:T(8,128)(2,1)S(1)} %get-tuple-element.47), channel_id=1, source_target_pairs={{1,2},{2,1},{5,6},{6,5},{9,10},{10,9},{13,14},{14,13},{17,18},{18,... | collective-permute-start | bytes 393224 | tf_op jit(solution)/shard_map/ppermute | solution.py:381
  13.2 13.6 %collective-permute-start.3 = (bf16[4,128,128]{2,1,0:T(8,128)(2,1)S(1)}, bf16[4,128,128]{2,1,0:T(8,128)(2,1)S(1)}, u32[]{:S(2)}, u32[]{:S(2)}) collective-permute-start(bf16[4,128,128]{2,1,0:T(8,128)(2,1)S(1)} %collective-permute-done.1.near_ref), channel_id=1, source_target_pairs={{0,4},{4,0},{1,5},{5,1},{2,6},{6,2},{3,7},{7,3},{8,12},{12,8},{9,1... | collective-permute-start | bytes 393224 | tf_op jit(solution)/shard_map/ppermute | solution.py:412
  13.2 13.6 %collective-permute-start.4 = (bf16[4,128,128]{2,1,0:T(8,128)(2,1)S(1)}, bf16[4,128,128]{2,1,0:T(8,128)(2,1)S(1)}, u32[]{:S(2)}, u32[]{:S(2)}) collective-permute-start(bf16[4,128,128]{2,1,0:T(8,128)(2,1)S(1)} %collective-permute-done.2.refs_0_), channel_id=1, source_target_pairs={{0,4},{4,0},{1,5},{5,1},{2,6},{6,2},{3,7},{7,3},{8,12},{12,8},{9,1... | collective-permute-start | bytes 393224 | tf_op jit(solution)/shard_map/ppermute | solution.py:413
  13.7 1.2 %collective-permute-start.5 = (f32[3,8,128]{2,1,0:T(8,128)S(1)}, f32[3,8,128]{2,1,0:T(8,128)S(1)}, u32[]{:S(2)}, u32[]{:S(2)}) collective-permute-start(f32[3,8,128]{2,1,0:T(8,128)S(1)} %get-tuple-element.48.refs_0_), channel_id=1, source_target_pairs={{0,4},{4,0},{1,5},{5,1},{2,6},{6,2},{3,7},{7,3},{8,12},{12,8},{9,1... | collective-permute-start | bytes 36872 | tf_op jit(solution)/shard_map/ppermute | solution.py:27
  14.9 6.2 %collective-permute-start.6 = (f32[3,8,128]{2,1,0:T(8,128)S(1)}, f32[3,8,128]{2,1,0:T(8,128)S(1)}, u32[]{:S(2)}, u32[]{:S(2)}) collective-permute-start(f32[3,8,128]{2,1,0:T(8,128)S(1)} %merge.1.refs_5_.after_ref), channel_id=1, source_target_pairs={{0,1},{1,0},{2,3},{3,2},{4,5},{5,4},{6,7},{7,6},{8,9},{9,8},{10,11... | collective-permute-start | bytes 36872 | tf_op jit(solution)/shard_map/ppermute | solution.py:27
  19.4 7.3 %collective-permute-start.7 = (f32[3,8,128]{2,1,0:T(8,128)S(1)}, f32[3,8,128]{2,1,0:T(8,128)S(1)}, u32[]{:S(2)}, u32[]{:S(2)}) collective-permute-start(f32[3,8,128]{2,1,0:T(8,128)S(1)} %merge.1.refs_5_.after_ref), channel_id=1, source_target_pairs={{0,2},{1,3},{2,0},{3,1},{4,6},{5,7},{6,4},{7,5},{8,10},{9,11},{10,... | collective-permute-start | bytes 36872 | tf_op jit(solution)/shard_map/ppermute | solution.py:27
  21.0 5.7 %collective-permute-start.8 = (f32[3,8,128]{2,1,0:T(8,128)S(1)}, f32[3,8,128]{2,1,0:T(8,128)S(1)}, u32[]{:S(2)}, u32[]{:S(2)}) collective-permute-start(f32[3,8,128]{2,1,0:T(8,128)S(1)} %merge.1.refs_5_.after_ref), channel_id=1, source_target_pairs={{0,3},{1,2},{2,1},{3,0},{4,7},{5,6},{6,5},{7,4},{8,11},{9,10},{10,... | collective-permute-start | bytes 36872 | tf_op jit(solution)/shard_map/ppermute | solution.py:27
  23.7 3.1 %copy-start.2 = (f32[128]{0:T(128)S(1)}, f32[128]{0:T(128)}, u32[]{:S(2)}) copy-start(f32[128]{0:T(128)} %param.9) | copy-start | bytes 1540
  23.7 3.1 %copy-start.3 = (f32[128]{0:T(128)S(1)}, f32[128]{0:T(128)}, u32[]{:S(2)}) copy-start(f32[128]{0:T(128)} %param.10) | copy-start | bytes 1540
  26.8 10.5 %copy-start = (bf16[3,3,3,128,128]{4,3,2,1,0:T(8,128)(2,1)S(1)}, bf16[3,3,3,128,128]{4,3,2,1,0:T(8,128)(2,1)}, u32[]{:S(2)}) copy-start(bf16[3,3,3,128,128]{4,3,2,1,0:T(8,128)(2,1)} %kernel_ref.1) | copy-start | bytes 2654212
  37.2 0.7 copy-start.1
  37.2 2.6 %collective-permute-start.9 = (f32[4,448,128]{2,1,0:T(8,128)S(1)}, f32[4,448,128]{2,1,0:T(8,128)S(1)}, u32[]{:S(2)}, u32[]{:S(2)}) collective-permute-start(f32[4,448,128]{2,1,0:T(8,128)S(1)} %get-tuple-element.52), channel_id=1, source_target_pairs={{0,4},{4,0},{1,5},{5,1},{2,6},{6,2},{3,7},{7,3},{8,12},{12,8},{9,1... | collective-permute-start | bytes 2752520 | tf_op jit(solution)/shard_map/ppermute | solution.py:27
  40.5 8.1 %collective-permute-start.10 = (bf16[448,128]{1,0:T(8,128)(2,1)S(1)}, bf16[448,128]{1,0:T(8,128)(2,1)S(1)}, u32[]{:S(2)}, u32[]{:S(2)}) collective-permute-start(bf16[448,128]{1,0:T(8,128)(2,1)S(1)} %get-tuple-element.58), channel_id=1, source_target_pairs={{0,8},{8,0},{16,24},{24,16},{1,9},{9,1},{17,25},{25,17},{2,10},{10... | collective-permute-start | bytes 344072 | tf_op jit(solution)/shard_map/ppermute | solution.py:27
  42.1 7.5 %collective-permute-start.11 = (bf16[448,128]{1,0:T(8,128)(2,1)S(1)}, bf16[448,128]{1,0:T(8,128)(2,1)S(1)}, u32[]{:S(2)}, u32[]{:S(2)}) collective-permute-start(bf16[448,128]{1,0:T(8,128)(2,1)S(1)} %get-tuple-element.59), channel_id=1, source_target_pairs={{0,16},{8,24},{16,0},{24,8},{1,17},{9,25},{17,1},{25,9},{2,18},{10... | collective-permute-start | bytes 344072 | tf_op jit(solution)/shard_map/ppermute | solution.py:27
  43.6 6.0 %collective-permute-start.12 = (bf16[448,128]{1,0:T(8,128)(2,1)S(1)}, bf16[448,128]{1,0:T(8,128)(2,1)S(1)}, u32[]{:S(2)}, u32[]{:S(2)}) collective-permute-start(bf16[448,128]{1,0:T(8,128)(2,1)S(1)} %get-tuple-element.60), channel_id=1, source_target_pairs={{0,24},{8,16},{16,8},{24,0},{1,25},{9,17},{17,9},{25,1},{2,26},{10... | collective-permute-start | bytes 344072 | tf_op jit(solution)/shard_map/ppermute | solution.py:27
  49.7 12.4 %collective-permute-start.13 = (bf16[448,128]{1,0:T(8,128)(2,1)S(1)}, bf16[448,128]{1,0:T(8,128)(2,1)S(1)}, u32[]{:S(2)}, u32[]{:S(2)}) collective-permute-start(bf16[448,128]{1,0:T(8,128)(2,1)S(1)} %added.2.after_ref.refs_0_), channel_id=1, source_target_pairs={{0,1},{1,0},{2,3},{3,2},{4,5},{5,4},{6,7},{7,6},{8,9},{9,8},{10,11... | collective-permute-start | bytes 344072 | tf_op jit(solution)/shard_map/ppermute | solution.py:27
  50.9 11.2 %collective-permute-start.14 = (bf16[448,128]{1,0:T(8,128)(2,1)S(1)}, bf16[448,128]{1,0:T(8,128)(2,1)S(1)}, u32[]{:S(2)}, u32[]{:S(2)}) collective-permute-start(bf16[448,128]{1,0:T(8,128)(2,1)S(1)} %added.2.after_ref.refs_0_), channel_id=1, source_target_pairs={{0,2},{1,3},{2,0},{3,1},{4,6},{5,7},{6,4},{7,5},{8,10},{9,11},{10,... | collective-permute-start | bytes 344072 | tf_op jit(solution)/shard_map/ppermute | solution.py:27
  52.8 9.4 %collective-permute-start.15 = (bf16[448,128]{1,0:T(8,128)(2,1)S(1)}, bf16[448,128]{1,0:T(8,128)(2,1)S(1)}, u32[]{:S(2)}, u32[]{:S(2)}) collective-permute-start(bf16[448,128]{1,0:T(8,128)(2,1)S(1)} %added.2.after_ref.refs_0_), channel_id=1, source_target_pairs={{0,3},{1,2},{2,1},{3,0},{4,7},{5,6},{6,5},{7,4},{8,11},{9,10},{10,... | collective-permute-start | bytes 344072 | tf_op jit(solution)/shard_map/ppermute | solution.py:27
  62.2 5.6 %collective-permute-start.16 = (bf16[448,128]{1,0:T(8,128)(2,1)S(1)}, bf16[448,128]{1,0:T(8,128)(2,1)S(1)}, u32[]{:S(2)}, u32[]{:S(2)}) collective-permute-start(bf16[448,128]{1,0:T(8,128)(2,1)S(1)} %added.3.after_ref.refs_0_), channel_id=1, source_target_pairs={{0,16},{8,24},{16,0},{24,8},{1,17},{9,25},{17,1},{25,9},{2,18},{10... | collective-permute-start | bytes 344072 | tf_op jit(solution)/shard_map/ppermute | solution.py:27
  63.8 5.7 %collective-permute-start.17 = (bf16[448,128]{1,0:T(8,128)(2,1)S(1)}, bf16[448,128]{1,0:T(8,128)(2,1)S(1)}, u32[]{:S(2)}, u32[]{:S(2)}) collective-permute-start(bf16[448,128]{1,0:T(8,128)(2,1)S(1)} %added.3.after_ref.refs_0_), channel_id=1, source_target_pairs={{0,24},{8,16},{16,8},{24,0},{1,25},{9,17},{17,9},{25,1},{2,26},{10... | collective-permute-start | bytes 344072 | tf_op jit(solution)/shard_map/ppermute | solution.py:27
  65.0 4.8 %collective-permute-start.21 = (bf16[448,128]{1,0:T(8,128)(2,1)S(1)}, bf16[448,128]{1,0:T(8,128)(2,1)S(1)}, u32[]{:S(2)}, u32[]{:S(2)}) collective-permute-start(bf16[448,128]{1,0:T(8,128)(2,1)S(1)} %added.3.after_ref.refs_0_), channel_id=1, source_target_pairs={{0,8},{8,0},{16,24},{24,16},{1,9},{9,1},{17,25},{25,17},{2,10},{10... | collective-permute-start | bytes 344072 | tf_op jit(solution)/shard_map/ppermute | solution.py:27
  65.8 6.2 %collective-permute-start.18 = (bf16[448,128]{1,0:T(8,128)(2,1)S(1)}, bf16[448,128]{1,0:T(8,128)(2,1)S(1)}, u32[]{:S(2)}, u32[]{:S(2)}) collective-permute-start(bf16[448,128]{1,0:T(8,128)(2,1)S(1)} %added.3.after_ref.refs_0_), channel_id=1, source_target_pairs={{0,4},{4,0},{1,5},{5,1},{2,6},{6,2},{3,7},{7,3},{8,12},{12,8},{9,1... | collective-permute-start | bytes 344072 | tf_op jit(solution)/shard_map/ppermute | solution.py:27
  67.8 4.2 %collective-permute-start.19 = (bf16[448,128]{1,0:T(8,128)(2,1)S(1)}, bf16[448,128]{1,0:T(8,128)(2,1)S(1)}, u32[]{:S(2)}, u32[]{:S(2)}) collective-permute-start(bf16[448,128]{1,0:T(8,128)(2,1)S(1)} %collective-permute-done.16.refs_1_), channel_id=1, source_target_pairs={{0,4},{4,0},{1,5},{5,1},{2,6},{6,2},{3,7},{7,3},{8,12},{12,8},{9,1... | collective-permute-start | bytes 344072 | tf_op jit(solution)/shard_map/ppermute | solution.py:27
  69.5 2.5 %collective-permute-start.20 = (bf16[448,128]{1,0:T(8,128)(2,1)S(1)}, bf16[448,128]{1,0:T(8,128)(2,1)S(1)}, u32[]{:S(2)}, u32[]{:S(2)}) collective-permute-start(bf16[448,128]{1,0:T(8,128)(2,1)S(1)} %collective-permute-done.17.refs_2_), channel_id=1, source_target_pairs={{0,4},{4,0},{1,5},{5,1},{2,6},{6,2},{3,7},{7,3},{8,12},{12,8},{9,1... | collective-permute-start | bytes 344072 | tf_op jit(solution)/shard_map/ppermute | solution.py:27
  69.8 2.3 %collective-permute-start.22 = (bf16[448,128]{1,0:T(8,128)(2,1)S(1)}, bf16[448,128]{1,0:T(8,128)(2,1)S(1)}, u32[]{:S(2)}, u32[]{:S(2)}) collective-permute-start(bf16[448,128]{1,0:T(8,128)(2,1)S(1)} %collective-permute-done.21.refs_6_), channel_id=1, source_target_pairs={{0,4},{4,0},{1,5},{5,1},{2,6},{6,2},{3,7},{7,3},{8,12},{12,8},{9,1... | collective-permute-start | bytes 344072 | tf_op jit(solution)/shard_map/ppermute | solution.py:27

commit v12 on v11

--- a/solution.py
+++ b/solution.py
@@ -25,6 +25,13 @@
     length = lax.axis_size(axis)
     assert length & (length - 1) == 0
     return lax.ppermute(array, axis, [(i, i ^ by) for i in range(length)])
+
+
+def exchanged(arrays, axis):
+    result = []
+    for n, array in enumerate(arrays):
+        result.append(swap(array, axis, n + 1))
+    return result
 
 
 def group_sum(row, per):
@@ -51,9 +58,9 @@
     return count, total, squares
 
 
-def ends_kernel(info_ref, video_hbm, near_ref, far_ref, sems):
+def ends_kernel(video_hbm, near_ref, far_ref, sems):
     rows = video_hbm.shape[2]
-    odd = info_ref[6]
+    odd = lax.axis_index("space") % 2
     copies = [
         pltpu.make_async_copy(video_hbm.at[0, :, row], ref, sems.at[n])
         for n, (row, ref) in enumerate(
@@ -369,13 +376,13 @@
     border = jax.ShapeDtypeStruct((frames, cols, chans), BF16)
     near, far = pl.pallas_call(
         ends_kernel,
-        in_specs=[SMEM, ANY],
+        in_specs=[ANY],
         out_specs=[VMEM, VMEM],
         out_shape=[border, border],
         scratch_shapes=[pltpu.SemaphoreType.DMA((2,))],
         compiler_params=params(1),
         name="ends",
-    )(info, source)
+    )(source)
     near = swap(near, "space", 1)
     between = [(i, i + 1) for i in range(1, spaces - 1, 2)]
     far = lax.ppermute(far, "space", between + [(j, i) for i, j in between])
@@ -408,7 +415,7 @@
         )(*arrays)
 
     stats = together(gathered)
-    parts = [stats] + [swap(stats, "space", r) for r in range(1, spaces)]
+    parts = [stats] + exchanged([stats] * (spaces - 1), "space")
     near_early = lax.ppermute(near, "tm", following)
     far_early = lax.ppermute(far, "tm", following)
     pair = 2
@@ -507,12 +514,6 @@
             after = piece
         return after
 
-    def exchanged(arrays, axis):
-        result = []
-        for n, array in enumerate(arrays):
-            result.append(swap(array, axis, n + 1))
-        return result
-
     incoming = [swap(send, "tm", r + 1) for r, send in enumerate(sends)]
     token = cover(keep, 1)
     own, *sends = pl.pallas_call(

time: 74.9 us -> 74.3 us (level)
  transfers between devices with their start and end apart: 23 -> 23, of which waited for: 7 -> 7; matrix products, arithmetic and copies ran while one was open for 0% -> 0% of each run, Pallas kernels for 29% -> 28%
where the time goes in v12:
time: 74.3 us; the launch traced here: 74.1 us
  Pallas kernels  37.3 us (50%)
  starting transfers between devices  24.6 us (33%)
  waiting for transfers between devices  9.94 us (13%)
  between operations  1.99 us (3%)
    ppermute x19, starting transfers between devices, swap(): return lax.ppermute(array, axis, [(i, i ^ by) for i in range(length)])  22.9 us
    pallas_call x8, Pallas kernels, cover(): pl.pallas_call(functools.partial(conv_kernel, pieces[n], where(n - 1) if...  16.4 us
    pallas_call x1, Pallas kernels, step_of(): pl.pallas_call(functools.partial(weights_kernel, spaces, per), in_specs=[...  10.4 us
    ppermute x19, waiting for transfers between devices, swap(): return lax.ppermute(array, axis, [(i, i ^ by) for i in range(length)])  9.92 us
    pallas_call x2, Pallas kernels, step_of(): pl.pallas_call(functools.partial(cotangent_kernel, n * ahead), in_specs=[...  3.01 us
    pallas_call x1, Pallas kernels, step_of(): pl.pallas_call(functools.partial(stats_kernel, before), in_specs=[SMEM, A...  2.89 us
    pallas_call x1, Pallas kernels, step_of(): pl.pallas_call(collect, in_specs=[SMEM] + [VMEM] * (len(order) + 1) + [AN...  2.43 us
  transfers between devices with their start and end apart: 23, of which 7 were waited for; matrix products, arithmetic and copies ran while one was open for 0% of the time, Pallas kernels for 28%

profile of v12, /device:TPU:0, one launch (start us, length us, event | category | flops | bytes accessed | tf_op | source)
XLA Modules:
  0.0 74.1 jit_solution(2208250051687482594)
XLA Ops:
  1.3 0.1 stack.39.info_ref
  1.4 2.9 %stats.1 = (f32[3,8,128]{2,1,0:T(8,128)S(1)}, bf16[1,4,16,128,128]{4,3,2,1,0:T(8,128)(2,1)S(1)}, bf16[1,4,16,128,128]{4,3,2,1,0:T(8,128)(2,1)S(1)}, bf16[1,2,16,128,128]{4,3,2,1,0:T(8,128)(2,1)S(1)}) custom-call(s32[7]{0:T(128)S(1)} %stack.39.info_ref, bf16[1,4,16,128,128]{4,3,2,1,0:T(8,128)(2,1)} %video_hbm.3, bf16[1,4,16,128,128]{4,3,2,1,0:T(8,128)(2,1)} %cot_hbm.1), custom_call_target="tpu_custom_call" | custom-call | tf_op jit(solution)/shard_map/stats/pallas_call | solution.py:389
  4.3 0.6 collective-permute-start
  4.8 1.0 %ends.1 = (bf16[4,128,128]{2,1,0:T(8,128)(2,1)S(1)}, bf16[4,128,128]{2,1,0:T(8,128)(2,1)S(1)}) custom-call(bf16[1,4,16,128,128]{4,3,2,1,0:T(8,128)(2,1)} %video_hbm.3), custom_call_target="tpu_custom_call" | custom-call | tf_op jit(solution)/shard_map/ends/pallas_call | solution.py:377
  5.8 2.7 %collective-permute-start.1 = (bf16[4,128,128]{2,1,0:T(8,128)(2,1)S(1)}, bf16[4,128,128]{2,1,0:T(8,128)(2,1)S(1)}, u32[]{:S(2)}, u32[]{:S(2)}) collective-permute-start(bf16[4,128,128]{2,1,0:T(8,128)(2,1)S(1)} %get-tuple-element.46), channel_id=1, source_target_pairs={{0,1},{1,0},{2,3},{3,2},{4,5},{5,4},{6,7},{7,6},{8,9},{9,8},{10,11... | collective-permute-start | bytes 393224 | tf_op jit(solution)/shard_map/ppermute | solution.py:27
  8.5 0.7 collective-permute-start.2
  9.1 3.5 %collective-permute-done.1.near_ref = bf16[4,128,128]{2,1,0:T(8,128)(2,1)S(1)} collective-permute-done((bf16[4,128,128]{2,1,0:T(8,128)(2,1)S(1)}, bf16[4,128,128]{2,1,0:T(8,128)(2,1)S(1)}, u32[]{:S(2)}, u32[]{:S(2)}) %collective-permute-start.1) | collective-permute-done | bytes 131104 | tf_op jit(solution)/shard_map/ppermute | solution.py:27
  12.6 0.5 collective-permute-start.4
  13.1 0.0 collective-permute-start.5
  13.1 1.2 %collective-permute-done.5.refs_1_ = f32[3,8,128]{2,1,0:T(8,128)S(1)} collective-permute-done((f32[3,8,128]{2,1,0:T(8,128)S(1)}, f32[3,8,128]{2,1,0:T(8,128)S(1)}, u32[]{:S(2)}, u32[]{:S(2)}) %collective-permute-start.5) | collective-permute-done | bytes 12320 | tf_op jit(solution)/shard_map/ppermute | solution.py:27
  14.3 4.5 %collective-permute-start.6 = (f32[3,8,128]{2,1,0:T(8,128)S(1)}, f32[3,8,128]{2,1,0:T(8,128)S(1)}, u32[]{:S(2)}, u32[]{:S(2)}) collective-permute-start(f32[3,8,128]{2,1,0:T(8,128)S(1)} %merge.1.refs_5_.after_ref), channel_id=1, source_target_pairs={{0,1},{1,0},{2,3},{3,2},{4,5},{5,4},{6,7},{7,6},{8,9},{9,8},{10,11... | collective-permute-start | bytes 36872 | tf_op jit(solution)/shard_map/ppermute | solution.py:27
  18.8 1.2 %collective-permute-start.7 = (f32[3,8,128]{2,1,0:T(8,128)S(1)}, f32[3,8,128]{2,1,0:T(8,128)S(1)}, u32[]{:S(2)}, u32[]{:S(2)}) collective-permute-start(f32[3,8,128]{2,1,0:T(8,128)S(1)} %merge.1.refs_5_.after_ref), channel_id=1, source_target_pairs={{0,2},{1,3},{2,0},{3,1},{4,6},{5,7},{6,4},{7,5},{8,10},{9,11},{10,... | collective-permute-start | bytes 36872 | tf_op jit(solution)/shard_map/ppermute | solution.py:27
  20.1 0.4 collective-permute-done.6.refs_6_
  20.5 2.6 %collective-permute-start.8 = (f32[3,8,128]{2,1,0:T(8,128)S(1)}, f32[3,8,128]{2,1,0:T(8,128)S(1)}, u32[]{:S(2)}, u32[]{:S(2)}) collective-permute-start(f32[3,8,128]{2,1,0:T(8,128)S(1)} %merge.1.refs_5_.after_ref), channel_id=1, source_target_pairs={{0,3},{1,2},{2,1},{3,0},{4,7},{5,6},{6,5},{7,4},{8,11},{9,10},{10,... | collective-permute-start | bytes 36872 | tf_op jit(solution)/shard_map/ppermute | solution.py:27
  23.1 1.5 %cotangent.3 = (bf16[2,16,128,128]{3,2,1,0:T(8,128)(2,1)S(1)}, f32[8,128]{1,0:T(8,128)S(1)}) custom-call(s32[7]{0:T(128)S(1)} %stack.39.info_ref, bf16[1,4,16,128,128]{4,3,2,1,0:T(8,128)(2,1)S(1)} %get-tuple-element.39.cot_ref), custom_call_target="tpu_custom_call" | custom-call | tf_op jit(solution)/shard_map/cotangent/pallas_call | solution.py:436
  24.7 1.5 %cotangent.2 = (bf16[2,16,128,128]{3,2,1,0:T(8,128)(2,1)S(1)}, f32[8,128]{1,0:T(8,128)S(1)}) custom-call(s32[7]{0:T(128)S(1)} %stack.39.info_ref, bf16[1,4,16,128,128]{4,3,2,1,0:T(8,128)(2,1)S(1)} %get-tuple-element.39.cot_ref), custom_call_target="tpu_custom_call" | custom-call | tf_op jit(solution)/shard_map/cotangent/pallas_call | solution.py:436
  26.2 0.0 copy-start
  26.2 10.4 %weights.1 = (bf16[6,18,10,16,128]{4,3,2,1,0:T(8,128)(2,1)S(1)}, f32[4,448,128]{2,1,0:T(8,128)S(1)}, f32[4,448,128]{2,1,0:T(8,128)S(1)}) custom-call(s32[7]{0:T(128)S(1)} %stack.39.info_ref, bf16[2,16,128,128]{3,2,1,0:T(8,128)(2,1)S(1)} %get-tuple-element.40.turned_0, bf16[2,16,128,128]{3,2,1,0:T(8,128)(2,1)S(1)} %get-tuple-element.41.turned_1, ...), custom_call_target="tpu_custom_call" | custom-call | tf_op jit(solution)/shard_map/weights/pallas_call | solution.py:456
  36.7 0.0 copy-start.1
  36.7 0.1 collective-permute-start.9
  36.8 0.4 taps.1.taps_ref
  37.2 0.2 copy-done.1
  37.3 2.0 %conv.8 = (bf16[2,4,128,128]{3,2,1,0:T(8,128)(2,1)S(1)}, bf16[1,4,16,128,128]{4,3,2,1,0:T(8,128)(2,1)}) custom-call(s32[7]{0:T(128)S(1)} %stack.39.info_ref, f32[4,448,128]{2,1,0:T(8,128)S(1)} %get-tuple-element.49.after_ref.keep_ref, bf16[6,18,10,16,128]{4,3,2,1,0:T(8,128)(2,1)S(1)} %get-tuple-element.50.act_ref, bf16[4608,256]{1,0:T(8,128)(2,1)S(1)} %taps.1.taps_ref, ...), custom_call_target="tpu_custom_call" | custom-call | tf_op jit(solution)/shard_map/conv/pallas_call | solution.py:500
  39.3 0.6 spread.1
  40.0 1.6 %collective-permute-start.10 = (bf16[448,128]{1,0:T(8,128)(2,1)S(1)}, bf16[448,128]{1,0:T(8,128)(2,1)S(1)}, u32[]{:S(2)}, u32[]{:S(2)}) collective-permute-start(bf16[448,128]{1,0:T(8,128)(2,1)S(1)} %get-tuple-element.58), channel_id=1, source_target_pairs={{0,8},{8,0},{16,24},{24,16},{1,9},{9,1},{17,25},{25,17},{2,10},{10... | collective-permute-start | bytes 344072 | tf_op jit(solution)/shard_map/ppermute | solution.py:27
  41.5 1.5 %collective-permute-start.11 = (bf16[448,128]{1,0:T(8,128)(2,1)S(1)}, bf16[448,128]{1,0:T(8,128)(2,1)S(1)}, u32[]{:S(2)}, u32[]{:S(2)}) collective-permute-start(bf16[448,128]{1,0:T(8,128)(2,1)S(1)} %get-tuple-element.59), channel_id=1, source_target_pairs={{0,16},{8,24},{16,0},{24,8},{1,17},{9,25},{17,1},{25,9},{2,18},{10... | collective-permute-start | bytes 344072 | tf_op jit(solution)/shard_map/ppermute | solution.py:27
  43.1 0.5 collective-permute-start.12
  43.5 2.5 %conv.9 = (bf16[2,4,128,128]{3,2,1,0:T(8,128)(2,1)S(1)}, bf16[1,4,16,128,128]{4,3,2,1,0:T(8,128)(2,1)}) custom-call(s32[7]{0:T(128)S(1)} %stack.39.info_ref, f32[448,128]{1,0:T(8,128)S(1)} %get-tuple-element.53.after_ref.refs_0_, bf16[6,18,10,16,128]{4,3,2,1,0:T(8,128)(2,1)S(1)} %get-tuple-element.50.act_ref, ...), custom_call_target="tpu_custom_call", output_to_operand_aliasing={{1}: (7, {})} | custom-call | tf_op jit(solution)/shard_map/conv/pallas_call | solution.py:500
  46.0 2.0 %conv.10 = (bf16[2,4,128,128]{3,2,1,0:T(8,128)(2,1)S(1)}, bf16[1,4,16,128,128]{4,3,2,1,0:T(8,128)(2,1)}) custom-call(s32[7]{0:T(128)S(1)} %stack.39.info_ref, bf16[2,4,128,128]{3,2,1,0:T(8,128)(2,1)S(1)} %get-tuple-element.55.after_ref.refs_0_, bf16[6,18,10,16,128]{4,3,2,1,0:T(8,128)(2,1)S(1)} %get-tuple-element.50.act_ref, ...), custom_call_target="tpu_custom_call", output_to_operand_aliasing={{1}: (7, {})} | custom-call | tf_op jit(solution)/shard_map/conv/pallas_call | solution.py:500
  48.3 0.8 %collective-permute-done.11.refs_2_ = bf16[448,128]{1,0:T(8,128)(2,1)S(1)} collective-permute-done((bf16[448,128]{1,0:T(8,128)(2,1)S(1)}, bf16[448,128]{1,0:T(8,128)(2,1)S(1)}, u32[]{:S(2)}, u32[]{:S(2)}) %collective-permute-start.11) | collective-permute-done | bytes 114720 | tf_op jit(solution)/shard_map/ppermute | solution.py:27
  49.1 0.1 added.2.after_ref.refs_0_
  49.2 1.2 %collective-permute-start.13 = (bf16[448,128]{1,0:T(8,128)(2,1)S(1)}, bf16[448,128]{1,0:T(8,128)(2,1)S(1)}, u32[]{:S(2)}, u32[]{:S(2)}) collective-permute-start(bf16[448,128]{1,0:T(8,128)(2,1)S(1)} %added.2.after_ref.refs_0_), channel_id=1, source_target_pairs={{0,1},{1,0},{2,3},{3,2},{4,5},{5,4},{6,7},{7,6},{8,9},{9,8},{10,11... | collective-permute-start | bytes 344072 | tf_op jit(solution)/shard_map/ppermute | solution.py:27
  50.4 1.9 %collective-permute-start.14 = (bf16[448,128]{1,0:T(8,128)(2,1)S(1)}, bf16[448,128]{1,0:T(8,128)(2,1)S(1)}, u32[]{:S(2)}, u32[]{:S(2)}) collective-permute-start(bf16[448,128]{1,0:T(8,128)(2,1)S(1)} %added.2.after_ref.refs_0_), channel_id=1, source_target_pairs={{0,2},{1,3},{2,0},{3,1},{4,6},{5,7},{6,4},{7,5},{8,10},{9,11},{10,... | collective-permute-start | bytes 344072 | tf_op jit(solution)/shard_map/ppermute | solution.py:27
  52.2 1.4 %collective-permute-start.15 = (bf16[448,128]{1,0:T(8,128)(2,1)S(1)}, bf16[448,128]{1,0:T(8,128)(2,1)S(1)}, u32[]{:S(2)}, u32[]{:S(2)}) collective-permute-start(bf16[448,128]{1,0:T(8,128)(2,1)S(1)} %added.2.after_ref.refs_0_), channel_id=1, source_target_pairs={{0,3},{1,2},{2,1},{3,0},{4,7},{5,6},{6,5},{7,4},{8,11},{9,10},{10,... | collective-permute-start | bytes 344072 | tf_op jit(solution)/shard_map/ppermute | solution.py:27
  53.6 2.0 %conv.11 = (bf16[2,4,128,128]{3,2,1,0:T(8,128)(2,1)S(1)}, bf16[1,4,16,128,128]{4,3,2,1,0:T(8,128)(2,1)}) custom-call(s32[7]{0:T(128)S(1)} %stack.39.info_ref, bf16[448,128]{1,0:T(8,128)(2,1)S(1)} %added.2.after_ref.refs_0_, bf16[6,18,10,16,128]{4,3,2,1,0:T(8,128)(2,1)S(1)} %get-tuple-element.50.act_ref, ...), custom_call_target="tpu_custom_call", output_to_operand_aliasing={{1}: (7, {})} | custom-call | tf_op jit(solution)/shard_map/conv/pallas_call | solution.py:500
  55.6 2.0 %conv.12 = (bf16[2,4,128,128]{3,2,1,0:T(8,128)(2,1)S(1)}, bf16[1,4,16,128,128]{4,3,2,1,0:T(8,128)(2,1)}) custom-call(s32[7]{0:T(128)S(1)} %stack.39.info_ref, bf16[2,4,128,128]{3,2,1,0:T(8,128)(2,1)S(1)} %get-tuple-element.62.after_ref.refs_0_, bf16[6,18,10,16,128]{4,3,2,1,0:T(8,128)(2,1)S(1)} %get-tuple-element.50.act_ref, ...), custom_call_target="tpu_custom_call", output_to_operand_aliasing={{1}: (7, {})} | custom-call | tf_op jit(solution)/shard_map/conv/pallas_call | solution.py:500
  57.6 2.0 %conv.13 = (bf16[2,4,128,128]{3,2,1,0:T(8,128)(2,1)S(1)}, bf16[1,4,16,128,128]{4,3,2,1,0:T(8,128)(2,1)}) custom-call(s32[7]{0:T(128)S(1)} %stack.39.info_ref, bf16[2,4,128,128]{3,2,1,0:T(8,128)(2,1)S(1)} %get-tuple-element.64.after_ref.refs_0_, bf16[6,18,10,16,128]{4,3,2,1,0:T(8,128)(2,1)S(1)} %get-tuple-element.50.act_ref, ...), custom_call_target="tpu_custom_call", output_to_operand_aliasing={{1}: (7, {})} | custom-call | tf_op jit(solution)/shard_map/conv/pallas_call | solution.py:500
  59.6 2.0 %conv.14 = (bf16[2,4,128,128]{3,2,1,0:T(8,128)(2,1)S(1)}, bf16[1,4,16,128,128]{4,3,2,1,0:T(8,128)(2,1)}) custom-call(s32[7]{0:T(128)S(1)} %stack.39.info_ref, bf16[2,4,128,128]{3,2,1,0:T(8,128)(2,1)S(1)} %get-tuple-element.66.after_ref.refs_0_, bf16[6,18,10,16,128]{4,3,2,1,0:T(8,128)(2,1)S(1)} %get-tuple-element.50.act_ref, ...), custom_call_target="tpu_custom_call", output_to_operand_aliasing={{1}: (7, {})} | custom-call | tf_op jit(solution)/shard_map/conv/pallas_call | solution.py:500
  61.6 0.1 added.3.after_ref.refs_0_
  61.7 1.6 %collective-permute-start.16 = (bf16[448,128]{1,0:T(8,128)(2,1)S(1)}, bf16[448,128]{1,0:T(8,128)(2,1)S(1)}, u32[]{:S(2)}, u32[]{:S(2)}) collective-permute-start(bf16[448,128]{1,0:T(8,128)(2,1)S(1)} %added.3.after_ref.refs_0_), channel_id=1, source_target_pairs={{0,16},{8,24},{16,0},{24,8},{1,17},{9,25},{17,1},{25,9},{2,18},{10... | collective-permute-start | bytes 344072 | tf_op jit(solution)/shard_map/ppermute | solution.py:27
  63.3 1.2 %collective-permute-start.17 = (bf16[448,128]{1,0:T(8,128)(2,1)S(1)}, bf16[448,128]{1,0:T(8,128)(2,1)S(1)}, u32[]{:S(2)}, u32[]{:S(2)}) collective-permute-start(bf16[448,128]{1,0:T(8,128)(2,1)S(1)} %added.3.after_ref.refs_0_), channel_id=1, source_target_pairs={{0,24},{8,16},{16,8},{24,0},{1,25},{9,17},{17,9},{25,1},{2,26},{10... | collective-permute-start | bytes 344072 | tf_op jit(solution)/shard_map/ppermute | solution.py:27
  64.5 0.8 %collective-permute-start.21 = (bf16[448,128]{1,0:T(8,128)(2,1)S(1)}, bf16[448,128]{1,0:T(8,128)(2,1)S(1)}, u32[]{:S(2)}, u32[]{:S(2)}) collective-permute-start(bf16[448,128]{1,0:T(8,128)(2,1)S(1)} %added.3.after_ref.refs_0_), channel_id=1, source_target_pairs={{0,8},{8,0},{16,24},{24,16},{1,9},{9,1},{17,25},{25,17},{2,10},{10... | collective-permute-start | bytes 344072 | tf_op jit(solution)/shard_map/ppermute | solution.py:27
  65.3 2.0 %collective-permute-done.16.refs_1_ = bf16[448,128]{1,0:T(8,128)(2,1)S(1)} collective-permute-done((bf16[448,128]{1,0:T(8,128)(2,1)S(1)}, bf16[448,128]{1,0:T(8,128)(2,1)S(1)}, u32[]{:S(2)}, u32[]{:S(2)}) %collective-permute-start.16) | collective-permute-done | bytes 114720 | tf_op jit(solution)/shard_map/ppermute | solution.py:27
  67.3 1.7 %collective-permute-done.17.refs_2_ = bf16[448,128]{1,0:T(8,128)(2,1)S(1)} collective-permute-done((bf16[448,128]{1,0:T(8,128)(2,1)S(1)}, bf16[448,128]{1,0:T(8,128)(2,1)S(1)}, u32[]{:S(2)}, u32[]{:S(2)}) %collective-permute-start.17) | collective-permute-done | bytes 114720 | tf_op jit(solution)/shard_map/ppermute | solution.py:27
  69.0 0.3 collective-permute-done.21.refs_6_
  69.2 0.2 collective-permute-start.22
  69.5 2.0 %conv.15 = (bf16[2,4,128,128]{3,2,1,0:T(8,128)(2,1)S(1)}, bf16[1,4,16,128,128]{4,3,2,1,0:T(8,128)(2,1)}) custom-call(s32[7]{0:T(128)S(1)} %stack.39.info_ref, bf16[448,128]{1,0:T(8,128)(2,1)S(1)} %added.3.after_ref.refs_0_, bf16[6,18,10,16,128]{4,3,2,1,0:T(8,128)(2,1)S(1)} %get-tuple-element.50.act_ref, ...), custom_call_target="tpu_custom_call", output_to_operand_aliasing={{1}: (7, {})} | custom-call | tf_op jit(solution)/shard_map/conv/pallas_call | solution.py:500
  71.5 2.4 %collect.1 = (f32[1,128]{1,0:T(1,128)}, bf16[1,4,16,128,128]{4,3,2,1,0:T(8,128)(2,1)}, f32[8,432,128]{2,1,0:T(8,128)}) custom-call(s32[7]{0:T(128)S(1)} %stack.39.info_ref, bf16[448,128]{1,0:T(8,128)(2,1)S(1)} %added.3.after_ref.refs_0_, bf16[448,128]{1,0:T(8,128)(2,1)S(1)} %collective-permute-done.16.refs_1_, ...), custom_call_target="tpu_custom_call", output_to_operand_aliasing={{1}: (10, {})} | custom-call | tf_op jit(solution)/shard_map/collect/pallas_call | solution.py:571
  (26 shorter events, 0.1 us)
Async XLA Ops:
  4.3 21.9 %collective-permute-start = (bf16[1,2,16,128,128]{4,3,2,1,0:T(8,128)(2,1)S(1)}, bf16[1,2,16,128,128]{4,3,2,1,0:T(8,128)(2,1)S(1)}, u32[]{:S(2)}, u32[]{:S(2)}) collective-permute-start(bf16[1,2,16,128,128]{4,3,2,1,0:T(8,128)(2,1)S(1)} %get-tuple-element.45), channel_id=1, source_target_pairs={{0,4},{4,0},{1,5},{5,1},{2,6},{6,2},{3,7},{7,3},{8,12},{12,8},{9,1... | collective-permute-start | bytes 3145736 | tf_op jit(solution)/shard_map/ppermute | solution.py:405
  5.8 6.8 %collective-permute-start.1 = (bf16[4,128,128]{2,1,0:T(8,128)(2,1)S(1)}, bf16[4,128,128]{2,1,0:T(8,128)(2,1)S(1)}, u32[]{:S(2)}, u32[]{:S(2)}) collective-permute-start(bf16[4,128,128]{2,1,0:T(8,128)(2,1)S(1)} %get-tuple-element.46), channel_id=1, source_target_pairs={{0,1},{1,0},{2,3},{3,2},{4,5},{5,4},{6,7},{7,6},{8,9},{9,8},{10,11... | collective-permute-start | bytes 393224 | tf_op jit(solution)/shard_map/ppermute | solution.py:27
  8.5 4.2 %collective-permute-start.2 = (bf16[4,128,128]{2,1,0:T(8,128)(2,1)S(1)}, bf16[4,128,128]{2,1,0:T(8,128)(2,1)S(1)}, u32[]{:S(2)}, u32[]{:S(2)}) collective-permute-start(bf16[4,128,128]{2,1,0:T(8,128)(2,1)S(1)} %get-tuple-element.47), channel_id=1, source_target_pairs={{1,2},{2,1},{5,6},{6,5},{9,10},{10,9},{13,14},{14,13},{17,18},{18,... | collective-permute-start | bytes 393224 | tf_op jit(solution)/shard_map/ppermute | solution.py:388
  12.6 13.6 %collective-permute-start.3 = (bf16[4,128,128]{2,1,0:T(8,128)(2,1)S(1)}, bf16[4,128,128]{2,1,0:T(8,128)(2,1)S(1)}, u32[]{:S(2)}, u32[]{:S(2)}) collective-permute-start(bf16[4,128,128]{2,1,0:T(8,128)(2,1)S(1)} %collective-permute-done.1.near_ref), channel_id=1, source_target_pairs={{0,4},{4,0},{1,5},{5,1},{2,6},{6,2},{3,7},{7,3},{8,12},{12,8},{9,1... | collective-permute-start | bytes 393224 | tf_op jit(solution)/shard_map/ppermute | solution.py:419
  12.6 13.6 %collective-permute-start.4 = (bf16[4,128,128]{2,1,0:T(8,128)(2,1)S(1)}, bf16[4,128,128]{2,1,0:T(8,128)(2,1)S(1)}, u32[]{:S(2)}, u32[]{:S(2)}) collective-permute-start(bf16[4,128,128]{2,1,0:T(8,128)(2,1)S(1)} %collective-permute-done.2.refs_0_), channel_id=1, source_target_pairs={{0,4},{4,0},{1,5},{5,1},{2,6},{6,2},{3,7},{7,3},{8,12},{12,8},{9,1... | collective-permute-start | bytes 393224 | tf_op jit(solution)/shard_map/ppermute | solution.py:420
  13.1 1.2 %collective-permute-start.5 = (f32[3,8,128]{2,1,0:T(8,128)S(1)}, f32[3,8,128]{2,1,0:T(8,128)S(1)}, u32[]{:S(2)}, u32[]{:S(2)}) collective-permute-start(f32[3,8,128]{2,1,0:T(8,128)S(1)} %get-tuple-element.48.refs_0_), channel_id=1, source_target_pairs={{0,4},{4,0},{1,5},{5,1},{2,6},{6,2},{3,7},{7,3},{8,12},{12,8},{9,1... | collective-permute-start | bytes 36872 | tf_op jit(solution)/shard_map/ppermute | solution.py:27
  14.3 6.2 %collective-permute-start.6 = (f32[3,8,128]{2,1,0:T(8,128)S(1)}, f32[3,8,128]{2,1,0:T(8,128)S(1)}, u32[]{:S(2)}, u32[]{:S(2)}) collective-permute-start(f32[3,8,128]{2,1,0:T(8,128)S(1)} %merge.1.refs_5_.after_ref), channel_id=1, source_target_pairs={{0,1},{1,0},{2,3},{3,2},{4,5},{5,4},{6,7},{7,6},{8,9},{9,8},{10,11... | collective-permute-start | bytes 36872 | tf_op jit(solution)/shard_map/ppermute | solution.py:27
  18.8 7.3 %collective-permute-start.7 = (f32[3,8,128]{2,1,0:T(8,128)S(1)}, f32[3,8,128]{2,1,0:T(8,128)S(1)}, u32[]{:S(2)}, u32[]{:S(2)}) collective-permute-start(f32[3,8,128]{2,1,0:T(8,128)S(1)} %merge.1.refs_5_.after_ref), channel_id=1, source_target_pairs={{0,2},{1,3},{2,0},{3,1},{4,6},{5,7},{6,4},{7,5},{8,10},{9,11},{10,... | collective-permute-start | bytes 36872 | tf_op jit(solution)/shard_map/ppermute | solution.py:27
  20.5 5.7 %collective-permute-start.8 = (f32[3,8,128]{2,1,0:T(8,128)S(1)}, f32[3,8,128]{2,1,0:T(8,128)S(1)}, u32[]{:S(2)}, u32[]{:S(2)}) collective-permute-start(f32[3,8,128]{2,1,0:T(8,128)S(1)} %merge.1.refs_5_.after_ref), channel_id=1, source_target_pairs={{0,3},{1,2},{2,1},{3,0},{4,7},{5,6},{6,5},{7,4},{8,11},{9,10},{10,... | collective-permute-start | bytes 36872 | tf_op jit(solution)/shard_map/ppermute | solution.py:27
  23.1 3.1 %copy-start.2 = (f32[128]{0:T(128)S(1)}, f32[128]{0:T(128)}, u32[]{:S(2)}) copy-start(f32[128]{0:T(128)} %param.9) | copy-start | bytes 1540
  23.1 3.1 %copy-start.3 = (f32[128]{0:T(128)S(1)}, f32[128]{0:T(128)}, u32[]{:S(2)}) copy-start(f32[128]{0:T(128)} %param.10) | copy-start | bytes 1540
  26.2 10.5 %copy-start = (bf16[3,3,3,128,128]{4,3,2,1,0:T(8,128)(2,1)S(1)}, bf16[3,3,3,128,128]{4,3,2,1,0:T(8,128)(2,1)}, u32[]{:S(2)}) copy-start(bf16[3,3,3,128,128]{4,3,2,1,0:T(8,128)(2,1)} %kernel_ref.1) | copy-start | bytes 2654212
  36.7 0.7 copy-start.1
  36.7 2.6 %collective-permute-start.9 = (f32[4,448,128]{2,1,0:T(8,128)S(1)}, f32[4,448,128]{2,1,0:T(8,128)S(1)}, u32[]{:S(2)}, u32[]{:S(2)}) collective-permute-start(f32[4,448,128]{2,1,0:T(8,128)S(1)} %get-tuple-element.52), channel_id=1, source_target_pairs={{0,4},{4,0},{1,5},{5,1},{2,6},{6,2},{3,7},{7,3},{8,12},{12,8},{9,1... | collective-permute-start | bytes 2752520 | tf_op jit(solution)/shard_map/ppermute | solution.py:27
  40.0 8.1 %collective-permute-start.10 = (bf16[448,128]{1,0:T(8,128)(2,1)S(1)}, bf16[448,128]{1,0:T(8,128)(2,1)S(1)}, u32[]{:S(2)}, u32[]{:S(2)}) collective-permute-start(bf16[448,128]{1,0:T(8,128)(2,1)S(1)} %get-tuple-element.58), channel_id=1, source_target_pairs={{0,8},{8,0},{16,24},{24,16},{1,9},{9,1},{17,25},{25,17},{2,10},{10... | collective-permute-start | bytes 344072 | tf_op jit(solution)/shard_map/ppermute | solution.py:27
  41.5 7.5 %collective-permute-start.11 = (bf16[448,128]{1,0:T(8,128)(2,1)S(1)}, bf16[448,128]{1,0:T(8,128)(2,1)S(1)}, u32[]{:S(2)}, u32[]{:S(2)}) collective-permute-start(bf16[448,128]{1,0:T(8,128)(2,1)S(1)} %get-tuple-element.59), channel_id=1, source_target_pairs={{0,16},{8,24},{16,0},{24,8},{1,17},{9,25},{17,1},{25,9},{2,18},{10... | collective-permute-start | bytes 344072 | tf_op jit(solution)/shard_map/ppermute | solution.py:27
  43.1 6.0 %collective-permute-start.12 = (bf16[448,128]{1,0:T(8,128)(2,1)S(1)}, bf16[448,128]{1,0:T(8,128)(2,1)S(1)}, u32[]{:S(2)}, u32[]{:S(2)}) collective-permute-start(bf16[448,128]{1,0:T(8,128)(2,1)S(1)} %get-tuple-element.60), channel_id=1, source_target_pairs={{0,24},{8,16},{16,8},{24,0},{1,25},{9,17},{17,9},{25,1},{2,26},{10... | collective-permute-start | bytes 344072 | tf_op jit(solution)/shard_map/ppermute | solution.py:27
  49.2 12.4 %collective-permute-start.13 = (bf16[448,128]{1,0:T(8,128)(2,1)S(1)}, bf16[448,128]{1,0:T(8,128)(2,1)S(1)}, u32[]{:S(2)}, u32[]{:S(2)}) collective-permute-start(bf16[448,128]{1,0:T(8,128)(2,1)S(1)} %added.2.after_ref.refs_0_), channel_id=1, source_target_pairs={{0,1},{1,0},{2,3},{3,2},{4,5},{5,4},{6,7},{7,6},{8,9},{9,8},{10,11... | collective-permute-start | bytes 344072 | tf_op jit(solution)/shard_map/ppermute | solution.py:27
  50.4 11.3 %collective-permute-start.14 = (bf16[448,128]{1,0:T(8,128)(2,1)S(1)}, bf16[448,128]{1,0:T(8,128)(2,1)S(1)}, u32[]{:S(2)}, u32[]{:S(2)}) collective-permute-start(bf16[448,128]{1,0:T(8,128)(2,1)S(1)} %added.2.after_ref.refs_0_), channel_id=1, source_target_pairs={{0,2},{1,3},{2,0},{3,1},{4,6},{5,7},{6,4},{7,5},{8,10},{9,11},{10,... | collective-permute-start | bytes 344072 | tf_op jit(solution)/shard_map/ppermute | solution.py:27
  52.2 9.4 %collective-permute-start.15 = (bf16[448,128]{1,0:T(8,128)(2,1)S(1)}, bf16[448,128]{1,0:T(8,128)(2,1)S(1)}, u32[]{:S(2)}, u32[]{:S(2)}) collective-permute-start(bf16[448,128]{1,0:T(8,128)(2,1)S(1)} %added.2.after_ref.refs_0_), channel_id=1, source_target_pairs={{0,3},{1,2},{2,1},{3,0},{4,7},{5,6},{6,5},{7,4},{8,11},{9,10},{10,... | collective-permute-start | bytes 344072 | tf_op jit(solution)/shard_map/ppermute | solution.py:27
  61.7 5.6 %collective-permute-start.16 = (bf16[448,128]{1,0:T(8,128)(2,1)S(1)}, bf16[448,128]{1,0:T(8,128)(2,1)S(1)}, u32[]{:S(2)}, u32[]{:S(2)}) collective-permute-start(bf16[448,128]{1,0:T(8,128)(2,1)S(1)} %added.3.after_ref.refs_0_), channel_id=1, source_target_pairs={{0,16},{8,24},{16,0},{24,8},{1,17},{9,25},{17,1},{25,9},{2,18},{10... | collective-permute-start | bytes 344072 | tf_op jit(solution)/shard_map/ppermute | solution.py:27
  63.3 5.7 %collective-permute-start.17 = (bf16[448,128]{1,0:T(8,128)(2,1)S(1)}, bf16[448,128]{1,0:T(8,128)(2,1)S(1)}, u32[]{:S(2)}, u32[]{:S(2)}) collective-permute-start(bf16[448,128]{1,0:T(8,128)(2,1)S(1)} %added.3.after_ref.refs_0_), channel_id=1, source_target_pairs={{0,24},{8,16},{16,8},{24,0},{1,25},{9,17},{17,9},{25,1},{2,26},{10... | collective-permute-start | bytes 344072 | tf_op jit(solution)/shard_map/ppermute | solution.py:27
  64.5 4.8 %collective-permute-start.21 = (bf16[448,128]{1,0:T(8,128)(2,1)S(1)}, bf16[448,128]{1,0:T(8,128)(2,1)S(1)}, u32[]{:S(2)}, u32[]{:S(2)}) collective-permute-start(bf16[448,128]{1,0:T(8,128)(2,1)S(1)} %added.3.after_ref.refs_0_), channel_id=1, source_target_pairs={{0,8},{8,0},{16,24},{24,16},{1,9},{9,1},{17,25},{25,17},{2,10},{10... | collective-permute-start | bytes 344072 | tf_op jit(solution)/shard_map/ppermute | solution.py:27
  65.3 6.2 %collective-permute-start.18 = (bf16[448,128]{1,0:T(8,128)(2,1)S(1)}, bf16[448,128]{1,0:T(8,128)(2,1)S(1)}, u32[]{:S(2)}, u32[]{:S(2)}) collective-permute-start(bf16[448,128]{1,0:T(8,128)(2,1)S(1)} %added.3.after_ref.refs_0_), channel_id=1, source_target_pairs={{0,4},{4,0},{1,5},{5,1},{2,6},{6,2},{3,7},{7,3},{8,12},{12,8},{9,1... | collective-permute-start | bytes 344072 | tf_op jit(solution)/shard_map/ppermute | solution.py:27
  67.3 4.2 %collective-permute-start.19 = (bf16[448,128]{1,0:T(8,128)(2,1)S(1)}, bf16[448,128]{1,0:T(8,128)(2,1)S(1)}, u32[]{:S(2)}, u32[]{:S(2)}) collective-permute-start(bf16[448,128]{1,0:T(8,128)(2,1)S(1)} %collective-permute-done.16.refs_1_), channel_id=1, source_target_pairs={{0,4},{4,0},{1,5},{5,1},{2,6},{6,2},{3,7},{7,3},{8,12},{12,8},{9,1... | collective-permute-start | bytes 344072 | tf_op jit(solution)/shard_map/ppermute | solution.py:27
  69.0 2.5 %collective-permute-start.20 = (bf16[448,128]{1,0:T(8,128)(2,1)S(1)}, bf16[448,128]{1,0:T(8,128)(2,1)S(1)}, u32[]{:S(2)}, u32[]{:S(2)}) collective-permute-start(bf16[448,128]{1,0:T(8,128)(2,1)S(1)} %collective-permute-done.17.refs_2_), channel_id=1, source_target_pairs={{0,4},{4,0},{1,5},{5,1},{2,6},{6,2},{3,7},{7,3},{8,12},{12,8},{9,1... | collective-permute-start | bytes 344072 | tf_op jit(solution)/shard_map/ppermute | solution.py:27
  69.2 2.3 %collective-permute-start.22 = (bf16[448,128]{1,0:T(8,128)(2,1)S(1)}, bf16[448,128]{1,0:T(8,128)(2,1)S(1)}, u32[]{:S(2)}, u32[]{:S(2)}) collective-permute-start(bf16[448,128]{1,0:T(8,128)(2,1)S(1)} %collective-permute-done.21.refs_6_), channel_id=1, source_target_pairs={{0,4},{4,0},{1,5},{5,1},{2,6},{6,2},{3,7},{7,3},{8,12},{12,8},{9,1... | collective-permute-start | bytes 344072 | tf_op jit(solution)/shard_map/ppermute | solution.py:27
